TPU v7x, 32 devices: a whole 2x2x4 slice. The times are simulated.
32 devices in a mesh: fsdp: 8 (over y, x, core), tp: 4 (over z).
Axes of the slice: x: 2, y: 2, z: 4, core: 2. Of those that a mesh axis runs over, the one named last changes fastest.
Arguments:
- block_in: bfloat16 [16, 1024, 3072], P('fsdp', 'tp'), may hold values from -6 to 6
- out_cotangent: bfloat16 [16, 1024, 3072], P('fsdp', 'tp'), may hold values from -6 to 6
- segment_ids: int32 [16, 1024], P('fsdp', 'tp'), may hold values from 0 to 3, as said below
- doc_positions: int32 [16, 1024], P('fsdp', 'tp'), may hold values from 0 to 799, as said below
- norm1_gain: bfloat16 [3072], replicated, may hold values from 0.5 to 1.5
- qkv_weight: bfloat16 [3072, 3, 3072], P('fsdp', None, 'tp'), may hold values from -0.5 to 0.5
- out_weight: bfloat16 [3072, 3072], P(('tp', 'fsdp')), may hold values from -0.875 to 0.875
- norm2_gain: bfloat16 [3072], replicated, may hold values from 0.5 to 1.5
- gate_up_weight: bfloat16 [3072, 2, 8192], P('fsdp', None, 'tp'), may hold values from -0.109375 to 0.109375
- down_weight: bfloat16 [8192, 3072], P(('tp', 'fsdp')), may hold values from -0.0625 to 0.0625
Outputs:
- block_out: bfloat16 [16, 1024, 3072], P('fsdp', 'tp')
- in_grad: float32 [16, 1024, 3072], P('fsdp', 'tp')
- norm1_gain_grad: float32 [3072], P(('fsdp', 'tp'))
- qkv_weight_grad: float32 [3072, 3, 3072], P('fsdp', None, 'tp')
- out_weight_grad: float32 [3072, 3072], P(('tp', 'fsdp'))
- norm2_gain_grad: float32 [3072], P(('fsdp', 'tp'))
- gate_up_weight_grad: float32 [3072, 2, 8192], P('fsdp', None, 'tp')
- down_weight_grad: float32 [8192, 3072], P(('tp', 'fsdp'))
Inputs may be any that keep to these rules, and one draw needn't show every extreme that they name: `segment_ids`: within each sequence the numbers start at 0, never fall and rise by at most one from a token to the next; every document has 60 to 800 tokens, and the first document of each sequence has 800. `doc_positions`: 0 at the first token of each document, else one more than at the token before.
All inputs are finite; a program needn't handle non-finite values.
Results may differ from a plain program's by a relative error of at most 0.017.
Values may be sent and summed in bfloat16 or wider, within the bound.
A program may use at most 256 MiB of HBM per device.

v0:
```python
import jax
import jax.numpy as jnp
from jax import lax
from jax.sharding import PartitionSpec as P

D = 3072
HD = 96


rms_epsilon = 1e-05
rope_theta = 10000.0
masked_score = -1e30


def rope_tables(positions, head_size):
    half_width = head_size // 2
    frequency = rope_theta ** (-(jnp.arange(half_width, dtype=jnp.float32) * 2.0 / head_size))
    angles = positions.astype(jnp.float32)[:, None] * frequency[None, :]
    return (jnp.cos(angles)[:, None, :], jnp.sin(angles)[:, None, :])


def rotate(values, cosine_part, sine_part):
    half_width = values.shape[-1] // 2
    lead_half = values[..., :half_width]
    tail_half = values[..., half_width:]
    return jnp.concatenate(
        [
            lead_half * cosine_part - tail_half * sine_part,
            tail_half * cosine_part + lead_half * sine_part,
        ],
        axis=-1,
    )


def unrotate(values, cosine_part, sine_part):
    half_width = values.shape[-1] // 2
    lead_half = values[..., :half_width]
    tail_half = values[..., half_width:]
    return jnp.concatenate(
        [
            lead_half * cosine_part + tail_half * sine_part,
            tail_half * cosine_part - lead_half * sine_part,
        ],
        axis=-1,
    )


def rms_scale(stream):
    return lax.rsqrt(jnp.mean(stream * stream, axis=-1, keepdims=True) + rms_epsilon)


def norm_back(stream, scale_rows, gain_vec, grad_rows):
    gained_grad = gain_vec * grad_rows
    input_grad = scale_rows * gained_grad - stream * scale_rows**3 * jnp.mean(
        gained_grad * stream, axis=-1, keepdims=True
    )
    return (input_grad, jnp.sum(grad_rows * stream * scale_rows, axis=0))


def allowed_mask(segment_tile, index_tile, segments):
    columns = jnp.arange(segments.shape[0], dtype=jnp.int32)
    return (segment_tile[:, None] == segments[None, :]) & (index_tile[:, None] >= columns[None, :])


def masked_scores(query_tile, key_rows, segment_tile, index_tile, segments, scale_value):
    scores = (
        jnp.einsum("qhd,khd->hqk", query_tile, key_rows, preferred_element_type=jnp.float32)
        * scale_value
    )
    return jnp.where(allowed_mask(segment_tile, index_tile, segments)[None], scores, masked_score)


def attention_forward(queries, key_rows, value_rows, segments, block_rows):
    seq_len, head_count, head_size = queries.shape
    tiles = seq_len // block_rows
    scale_value = head_size ** (-0.5)
    positions = jnp.arange(seq_len, dtype=jnp.int32)

    def query_block(packed):
        query_tile, segment_tile, index_tile = packed
        scores = masked_scores(
            query_tile, key_rows, segment_tile, index_tile, segments, scale_value
        )
        row_max = jnp.max(scores, axis=-1, keepdims=True)
        exponent = jnp.exp(scores - row_max)
        row_total = jnp.sum(exponent, axis=-1, keepdims=True)
        probs_low = (exponent / row_total).astype(jnp.bfloat16)
        mixed = jnp.einsum(
            "hqk,khd->qhd", probs_low, value_rows, preferred_element_type=jnp.float32
        )
        return (mixed, (row_max + jnp.log(row_total))[..., 0])

    mixed, log_total = lax.map(
        query_block,
        (
            queries.reshape(tiles, block_rows, head_count, head_size),
            segments.reshape(tiles, block_rows),
            positions.reshape(tiles, block_rows),
        ),
    )
    return (mixed.reshape(seq_len, head_count * head_size), log_total)


def attention_backward(queries, key_rows, value_rows, segments, log_total, out_grad, block_rows):
    seq_len, head_count, head_size = queries.shape
    tiles = seq_len // block_rows
    scale_value = head_size ** (-0.5)
    positions = jnp.arange(seq_len, dtype=jnp.int32)

    def query_block(carry, packed):
        key_acc, value_acc = carry
        query_tile, segment_tile, index_tile, total_tile, grad_tile = packed
        scores = masked_scores(
            query_tile, key_rows, segment_tile, index_tile, segments, scale_value
        )
        probs = jnp.exp(scores - total_tile[..., None])
        probs_low = probs.astype(jnp.bfloat16)
        prob_grad = jnp.einsum(
            "qhd,khd->hqk", grad_tile, value_rows, preferred_element_type=jnp.float32
        )
        score_grad = (
            probs * (prob_grad - jnp.sum(probs * prob_grad, axis=-1, keepdims=True))
        ).astype(jnp.bfloat16)
        query_grad = (
            jnp.einsum("hqk,khd->qhd", score_grad, key_rows, preferred_element_type=jnp.float32)
            * scale_value
        )
        key_acc = (
            key_acc
            + jnp.einsum("hqk,qhd->khd", score_grad, query_tile, preferred_element_type=jnp.float32)
            * scale_value
        )
        value_acc = value_acc + jnp.einsum(
            "hqk,qhd->khd", probs_low, grad_tile, preferred_element_type=jnp.float32
        )
        return ((key_acc, value_acc), query_grad)

    start_acc = (jnp.zeros(queries.shape, jnp.float32), jnp.zeros(queries.shape, jnp.float32))
    (key_grad, value_grad), query_grad = lax.scan(
        query_block,
        start_acc,
        (
            queries.reshape(tiles, block_rows, head_count, head_size),
            segments.reshape(tiles, block_rows),
            positions.reshape(tiles, block_rows),
            log_total,
            out_grad.reshape(tiles, block_rows, head_count, head_size),
        ),
    )
    return (query_grad.reshape(seq_len, head_count, head_size), key_grad, value_grad)


def gather_attention(qkv_weight, out_weight):
    return (
        lax.all_gather(qkv_weight, "fsdp", axis=0, tiled=True),
        lax.all_gather(out_weight, "fsdp", axis=0, tiled=True),
    )


def gather_feedforward(gate_up_weight, down_weight):
    return (
        lax.all_gather(gate_up_weight, "fsdp", axis=0, tiled=True),
        lax.all_gather(down_weight, "fsdp", axis=0, tiled=True),
    )


def per_device(
    block_in,
    out_cotangent,
    segment_ids,
    doc_positions,
    norm1_gain,
    qkv_weight,
    out_weight,
    norm2_gain,
    gate_up_weight,
    down_weight,
):
    micro_count = block_in.shape[0]
    fsdp_count = lax.axis_size("fsdp")
    segment_full, position_full = (
        lax.all_gather(segment_ids, "tp", axis=1, tiled=True),
        lax.all_gather(doc_positions, "tp", axis=1, tiled=True),
    )
    seq_len = segment_full.shape[1]
    block_rows = min(seq_len, 512)
    gain_one = norm1_gain.astype(jnp.float32)
    gain_two = norm2_gain.astype(jnp.float32)
    local_cols = qkv_weight.shape[2]
    local_units = gate_up_weight.shape[2]
    heads_local = local_cols // HD
    grad_qkv = jnp.zeros((D, 3, local_cols), jnp.float32)
    grad_out = jnp.zeros((out_weight.shape[0] * fsdp_count, D), jnp.float32)
    grad_gate_up = jnp.zeros((D, 2, local_units), jnp.float32)
    grad_down = jnp.zeros((down_weight.shape[0] * fsdp_count, D), jnp.float32)
    gain_one_acc = jnp.zeros((D,), jnp.float32)
    gain_two_acc = jnp.zeros((D,), jnp.float32)
    outputs = []
    input_grads = []
    for micro_index in range(micro_count):
        weights_fwd = (
            gather_attention(qkv_weight, out_weight),
            gather_feedforward(gate_up_weight, down_weight),
        )
        (qkv_full, out_full), (gate_up_full, down_full) = weights_fwd
        stream = block_in[micro_index].astype(jnp.float32)
        segment_row = segment_full[micro_index]
        cosine_part, sine_part = rope_tables(position_full[micro_index], HD)
        scale_one = rms_scale(stream)
        normed_one = (stream * scale_one * gain_one).astype(jnp.bfloat16)
        normed_one_full = lax.all_gather(normed_one, "tp", axis=0, tiled=True)
        projected = jnp.einsum(
            "sd,dtc->stc", normed_one_full, qkv_full, preferred_element_type=jnp.float32
        )
        queries = rotate(
            projected[:, 0].reshape(seq_len, heads_local, HD), cosine_part, sine_part
        ).astype(jnp.bfloat16)
        key_rows = rotate(
            projected[:, 1].reshape(seq_len, heads_local, HD), cosine_part, sine_part
        ).astype(jnp.bfloat16)
        value_rows = projected[:, 2].reshape(seq_len, heads_local, HD).astype(jnp.bfloat16)
        mixed, log_total = attention_forward(queries, key_rows, value_rows, segment_row, block_rows)
        attn_heads = mixed.astype(jnp.bfloat16)
        attn_term = jnp.dot(attn_heads, out_full, preferred_element_type=jnp.float32)
        attn_branch = lax.psum_scatter(attn_term, "tp", scatter_dimension=0, tiled=True)
        middle = stream + attn_branch
        scale_two = rms_scale(middle)
        normed_two = (middle * scale_two * gain_two).astype(jnp.bfloat16)
        normed_two_full = lax.all_gather(normed_two, "tp", axis=0, tiled=True)
        gate_up = jnp.einsum(
            "sd,dtf->stf", normed_two_full, gate_up_full, preferred_element_type=jnp.float32
        )
        gate_rows = gate_up[:, 0]
        up_rows = gate_up[:, 1]
        sigmoid_gate = jax.nn.sigmoid(gate_rows)
        silu_gate = gate_rows * sigmoid_gate
        activated = (silu_gate * up_rows).astype(jnp.bfloat16)
        mlp_term = jnp.dot(activated, down_full, preferred_element_type=jnp.float32)
        mlp_branch = lax.psum_scatter(
            mlp_term.astype(jnp.bfloat16), "tp", scatter_dimension=0, tiled=True
        ).astype(jnp.float32)
        outputs.append((middle + mlp_branch).astype(jnp.bfloat16))
        (qkv_back, out_back), (gate_up_back, down_back) = weights_fwd
        cotangent = out_cotangent[micro_index].astype(jnp.float32)
        cotangent_full = lax.all_gather(out_cotangent[micro_index], "tp", axis=0, tiled=True)
        grad_down = grad_down + jnp.einsum(
            "sf,sd->fd", activated, cotangent_full, preferred_element_type=jnp.float32
        )
        act_grad = jnp.einsum(
            "sd,fd->sf", cotangent_full, down_back, preferred_element_type=jnp.float32
        )
        gate_grad = act_grad * up_rows * sigmoid_gate * (1.0 + gate_rows * (1.0 - sigmoid_gate))
        up_grad = act_grad * silu_gate
        gate_up_grad = jnp.stack([gate_grad, up_grad], axis=1).astype(jnp.bfloat16)
        grad_gate_up = grad_gate_up + jnp.einsum(
            "sd,stf->dtf", normed_two_full, gate_up_grad, preferred_element_type=jnp.float32
        )
        normed_two_term = jnp.einsum(
            "stf,dtf->sd", gate_up_grad, gate_up_back, preferred_element_type=jnp.float32
        )
        normed_two_grad = lax.psum_scatter(normed_two_term, "tp", scatter_dimension=0, tiled=True)
        middle_back, gain_two_term = norm_back(middle, scale_two, gain_two, normed_two_grad)
        gain_two_acc = gain_two_acc + gain_two_term
        middle_grad = cotangent + middle_back
        attn_grad_full = lax.all_gather(middle_grad.astype(jnp.bfloat16), "tp", axis=0, tiled=True)
        grad_out = grad_out + jnp.einsum(
            "sc,sd->cd", attn_heads, attn_grad_full, preferred_element_type=jnp.float32
        )
        heads_grad = jnp.einsum(
            "sd,cd->sc", attn_grad_full, out_back, preferred_element_type=jnp.float32
        ).astype(jnp.bfloat16)
        query_grad, key_grad, value_grad = attention_backward(
            queries,
            key_rows,
            value_rows,
            segment_row,
            log_total,
            heads_grad.reshape(seq_len, heads_local, HD),
            block_rows,
        )
        projected_grad = jnp.stack(
            [
                unrotate(query_grad, cosine_part, sine_part).reshape(seq_len, local_cols),
                unrotate(key_grad, cosine_part, sine_part).reshape(seq_len, local_cols),
                value_grad.reshape(seq_len, local_cols),
            ],
            axis=1,
        ).astype(jnp.bfloat16)
        grad_qkv = grad_qkv + jnp.einsum(
            "sd,stc->dtc", normed_one_full, projected_grad, preferred_element_type=jnp.float32
        )
        normed_one_term = jnp.einsum(
            "stc,dtc->sd", projected_grad, qkv_back, preferred_element_type=jnp.float32
        )
        normed_one_grad = lax.psum_scatter(
            normed_one_term.astype(jnp.bfloat16), "tp", scatter_dimension=0, tiled=True
        ).astype(jnp.float32)
        stream_back, gain_one_term = norm_back(stream, scale_one, gain_one, normed_one_grad)
        gain_one_acc = gain_one_acc + gain_one_term
        input_grads.append(middle_grad + stream_back)
    owned_grads = (
        lax.psum_scatter(
            grad_qkv.astype(jnp.bfloat16), "fsdp", scatter_dimension=0, tiled=True
        ).astype(jnp.float32),
        lax.psum_scatter(
            grad_out.astype(jnp.bfloat16), "fsdp", scatter_dimension=0, tiled=True
        ).astype(jnp.float32),
        lax.psum_scatter(
            grad_gate_up.astype(jnp.bfloat16), "fsdp", scatter_dimension=0, tiled=True
        ).astype(jnp.float32),
        lax.psum_scatter(
            grad_down.astype(jnp.bfloat16), "fsdp", scatter_dimension=0, tiled=True
        ).astype(jnp.float32),
    )
    owned_gains = (
        lax.psum_scatter(gain_one_acc, ("fsdp", "tp"), scatter_dimension=0, tiled=True),
        lax.psum_scatter(gain_two_acc, ("fsdp", "tp"), scatter_dimension=0, tiled=True),
    )
    return (
        jnp.stack(outputs),
        jnp.stack(input_grads),
        owned_gains[0],
        owned_grads[0],
        owned_grads[1],
        owned_gains[1],
        owned_grads[2],
        owned_grads[3],
    )


def solution(mesh):
    in_specs = (
        P("fsdp", "tp", None),
        P("fsdp", "tp", None),
        P("fsdp", "tp"),
        P("fsdp", "tp"),
        P(),
        P("fsdp", None, "tp"),
        P(("tp", "fsdp"), None),
        P(),
        P("fsdp", None, "tp"),
        P(("tp", "fsdp"), None),
    )
    out_specs = (
        P("fsdp", "tp", None),
        P("fsdp", "tp", None),
        P(("fsdp", "tp")),
        P("fsdp", None, "tp"),
        P(("tp", "fsdp"), None),
        P(("fsdp", "tp")),
        P("fsdp", None, "tp"),
        P(("tp", "fsdp"), None),
    )
    return jax.shard_map(
        per_device, mesh=mesh, in_specs=in_specs, out_specs=out_specs, check_vma=False
    )
```

profile of v0, /device:TPU:0, one launch (start us, length us, event | category | flops | bytes accessed | tf_op | source)
XLA Modules:
  0.0 3195.4 jit_solution(16178268120911016994)
XLA Ops:
  53.0 79.6 %all-gather.15.cloned.1.call-done = bf16[1024,3072]{1,0:T(8,128)(2,1)} async-done(((bf16[256,3072]{1,0:T(8,128)(2,1)}), bf16[1024,3072]{1,0:T(8,128)(2,1)}) %all-gather.15.cloned.1.call-update) | async-done | bytes 6291472 | tf_op jit(solution)/shard_map/all_gather | solution.py:211
  132.6 82.2 %all-gather.17.cloned.1.call-done = bf16[3072,3,768]{0,2,1:T(8,128)(2,1)} async-done(((bf16[384,3,768]{0,2,1:T(8,128)(2,1)}), bf16[3072,3,768]{0,2,1:T(8,128)(2,1)}) %all-gather.17.cloned.1.call-update) | async-done | bytes 14155792 | tf_op jit(solution)/shard_map/all_gather | solution.py:155
  290.2 82.9 %all-gather.27.cloned.1.call-done = bf16[1024,3072]{1,0:T(8,128)(2,1)} async-done(((bf16[256,3072]{1,0:T(8,128)(2,1)}), bf16[1024,3072]{1,0:T(8,128)(2,1)}) %all-gather.27.cloned.1.call-update) | async-done | bytes 6291472 | tf_op jit(solution)/shard_map/all_gather | solution.py:211
  452.1 133.4 %reduce-scatter.13.cloned.1.call-done = f32[256,3072]{1,0:T(8,128)} async-done(((f32[1024,3072]{1,0:T(8,128)}), f32[256,3072]{1,0:T(8,128)}) %reduce-scatter.13.cloned.1.call-update) | async-done | bytes 3145744 | tf_op jit(solution)/shard_map/reduce_scatter | solution.py:225
  585.4 215.1 %reduce-scatter.17.cloned.1.call-done = f32[256,3072]{1,0:T(8,128)} async-done(((f32[1024,3072]{1,0:T(8,128)}), f32[256,3072]{1,0:T(8,128)}) %reduce-scatter.17.cloned.1.call-update) | async-done | bytes 3145744 | tf_op jit(solution)/shard_map/reduce_scatter | solution.py:225
  812.7 116.8 %all-gather.23.cloned.1.call-done = bf16[3072,2,2048]{2,0,1:T(8,128)(2,1)} async-done(((bf16[384,2,2048]{2,0,1:T(8,128)(2,1)}), bf16[3072,2,2048]{2,0,1:T(8,128)(2,1)}) %all-gather.23.cloned.1.call-update) | async-done | bytes 25165840 | tf_op jit(solution)/shard_map/all_gather | solution.py:162
  929.4 117.5 %all-gather.21.cloned.1.call-done = bf16[1024,3072]{1,0:T(8,128)(2,1)} async-done(((bf16[256,3072]{1,0:T(8,128)(2,1)}), bf16[1024,3072]{1,0:T(8,128)(2,1)}) %all-gather.21.cloned.1.call-update) | async-done | bytes 6291472 | tf_op jit(solution)/shard_map/all_gather | solution.py:229
  1080.4 82.4 %all-gather.35.cloned.1.call-done = bf16[1,1024,3072]{2,1,0:T(8,128)(2,1)} async-done(((bf16[1,256,3072]{2,1,0:T(8,128)(2,1)}), bf16[1,1024,3072]{2,1,0:T(8,128)(2,1)}) %all-gather.35.cloned.1.call-update) | async-done | bytes 6291472 | tf_op jit(solution)/shard_map/all_gather | solution.py:245
  1162.7 72.1 %all-gather.25.cloned.1.call-done = bf16[2048,3072]{1,0:T(8,128)(2,1)} async-done(((bf16[256,3072]{1,0:T(8,128)(2,1)}), bf16[2048,3072]{1,0:T(8,128)(2,1)}) %all-gather.25.cloned.1.call-update) | async-done | bytes 12582928 | tf_op jit(solution)/shard_map/all_gather | solution.py:163
  1260.2 34.2 %convolution_bitcast_fusion.1 = f32[1024,3072]{1,0:T(8,128)} fusion(bf16[3072,2,2048]{2,0,1:T(8,128)(2,1)} %all-gather.23.cloned.1.call-done, bf16[1024,1,2048]{2,0,1:T(8,128)(2,1)} %get-tuple-element.541, bf16[1024,1,2048]{2,0,1:T(8,128)(2,1)} %get-tuple-element.540), kind=kOutput, calls=%fused_computation.123 | convolution fusion | flops 25773998080 | bytes 46137344 | tf_op jit(solution)/shard_map/stf,dtf->sd/dot_general | solution.py:258
  1295.0 211.4 %reduce-scatter.21.cloned.1.call-done = f32[256,3072]{1,0:T(8,128)} async-done(((f32[1024,3072]{1,0:T(8,128)}), f32[256,3072]{1,0:T(8,128)}) %reduce-scatter.21.cloned.1.call-update) | async-done | bytes 3145744 | tf_op jit(solution)/shard_map/reduce_scatter | solution.py:261
  1513.2 115.7 %all-gather.29.cloned.1.call-done = bf16[1024,3072]{1,0:T(8,128)(2,1)} async-done(((bf16[256,3072]{1,0:T(8,128)(2,1)}), bf16[1024,3072]{1,0:T(8,128)(2,1)}) %all-gather.29.cloned.1.call-update) | async-done | bytes 6291472 | tf_op jit(solution)/shard_map/all_gather | solution.py:229
  1662.3 81.8 %all-gather.37.cloned.1.call-done = bf16[1,1024,3072]{2,1,0:T(8,128)(2,1)} async-done(((bf16[1,256,3072]{2,1,0:T(8,128)(2,1)}), bf16[1,1024,3072]{2,1,0:T(8,128)(2,1)}) %all-gather.37.cloned.1.call-update) | async-done | bytes 6291472 | tf_op jit(solution)/shard_map/all_gather | solution.py:245
  1840.8 172.8 %reduce-scatter.25.cloned.1.call-done = f32[256,3072]{1,0:T(8,128)} async-done(((f32[1024,3072]{1,0:T(8,128)}), f32[256,3072]{1,0:T(8,128)}) %reduce-scatter.25.cloned.1.call-update) | async-done | bytes 3145744 | tf_op jit(solution)/shard_map/reduce_scatter | solution.py:261
  2018.0 110.2 %reduce-scatter.15.cloned.1.call-done = bf16[256,3072]{1,0:T(8,128)(2,1)} async-done(((bf16[1024,3072]{1,0:T(8,128)(2,1)}), bf16[256,3072]{1,0:T(8,128)(2,1)}) %reduce-scatter.15.cloned.1.call-update) | async-done | bytes 1572880 | tf_op jit(solution)/shard_map/reduce_scatter | solution.py:239
  2128.2 114.0 %reduce-scatter.19.cloned.1.call-done = bf16[256,3072]{1,0:T(8,128)(2,1)} async-done(((bf16[1024,3072]{1,0:T(8,128)(2,1)}), bf16[256,3072]{1,0:T(8,128)(2,1)}) %reduce-scatter.19.cloned.1.call-update) | async-done | bytes 1572880 | tf_op jit(solution)/shard_map/reduce_scatter | solution.py:239
  2296.3 35.1 %fusion.71 = f32[3072,2,2048]{2,0,1:T(8,128)} fusion(bf16[1024,3072]{1,0:T(8,128)(2,1)} %all-gather.21.cloned.1.call-done, bf16[1024,1,2048]{2,0,1:T(8,128)(2,1)} %get-tuple-element.541, bf16[1024,1,2048]{2,0,1:T(8,128)(2,1)} %get-tuple-element.540), kind=kOutput, calls=%fused_computation.138 | convolution fusion | flops 25786580992 | bytes 65011712 | tf_op jit(solution)/shard_map/sd,stf->dtf/dot_general | solution.py:255
  2331.5 37.3 %add_convert_fusion = bf16[3072,2,2048]{2,0,1:T(8,128)(2,1)} fusion(f32[3072,2,2048]{2,0,1:T(8,128)} %fusion.71, bf16[1024,3072]{1,0:T(8,128)(2,1)} %all-gather.29.cloned.1.call-done, bf16[1024,1,2048]{2,0,1:T(8,128)(2,1)} %get-tuple-element.543, bf16[1024,1,2048]{2,0,1:T(8,128)(2,1)} %get-tuple-element.542), kind=kOutput, calls=%fused_computation.88 | convolution fusion | flops 25811746816 | bytes 90177536 | tf_op jit(solution)/shard_map/sd,stf->dtf/dot_general | solution.py:255
  2397.4 86.0 %all-gather.33.cloned.1.call-done = bf16[1024,3072]{1,0:T(8,128)(2,1)} async-done(((bf16[256,3072]{1,0:T(8,128)(2,1)}), bf16[1024,3072]{1,0:T(8,128)(2,1)}) %all-gather.33.cloned.1.call-update) | async-done | bytes 6291472 | tf_op jit(solution)/shard_map/all_gather | solution.py:265
  2496.8 193.2 %while.56 = (s32[]{:T(128)}, f32[1024,8,96]{0,2,1:T(8,128)S(1)}, f32[1024,8,96]{0,2,1:T(8,128)}, f32[2,512,8,96]{1,0,3,2:T(2,128)}, bf16[2,512,8,96]{1,3,2,0:T(8...) while((s32[]{:T(128)}, f32[1024,8,96]{0,2,1:T(8,128)S(1)}, ...), condition=%wide.region_20.21_spmd.clone, body=%wide.region_18.20_spmd.clone.sunk | while | flops 4070174720 | bytes 241271072 | solution.py:139
  2748.0 181.8 %while.57 = (s32[]{:T(128)}, f32[1024,8,96]{0,2,1:T(8,128)S(1)}, f32[1024,8,96]{0,2,1:T(8,128)}, f32[2,512,8,96]{1,0,3,2:T(2,128)}, bf16[2,512,8,96]{1,3,2,0:T(8...) while((s32[]{:T(128)}, f32[1024,8,96]{0,2,1:T(8,128)S(1)}, ...), condition=%wide.region_27.28_spmd.clone, body=%wide.region_25.27_spmd.clone.sunk | while | flops 4070174720 | bytes 234979584 | solution.py:139
  3032.2 46.8 %reduce-scatter.27.cloned.1.call-done = bf16[256,3072]{1,0:T(8,128)(2,1)} async-done(((bf16[1024,3072]{1,0:T(8,128)(2,1)}), bf16[256,3072]{1,0:T(8,128)(2,1)}) %reduce-scatter.27.cloned.1.call-update) | async-done | bytes 1572880 | tf_op jit(solution)/shard_map/reduce_scatter | solution.py:295
  3083.8 41.4 %all-reduce.2 = (f32[3072]{0:T(1024)S(1)}, f32[3072]{0:T(1024)S(1)}) all-reduce(f32[3072]{0:T(1024)S(1)} %add.229, f32[3072]{0:T(1024)S(1)} %add.232), channel_id=12, replica_groups=mesh['fsdp'=8,'tp'=4] {'fsdp','tp'}, use_global_device_ids=true, to_apply=%region_32.33.clone | all-reduce | flops 6144 | bytes 49152
  3134.8 50.0 %reduce-scatter.29.cloned.1.call-done = bf16[384,3,768]{2,0,1:T(8,128)(2,1)} async-done(((bf16[3072,3,768]{2,0,1:T(8,128)(2,1)}), bf16[384,3,768]{2,0,1:T(8,128)(2,1)}) %reduce-scatter.29.cloned.1.call-update) | async-done | bytes 1769488 | tf_op jit(solution)/shard_map/reduce_scatter | solution.py:302
  (419 shorter events, 1127.2 us)
Async XLA Ops:
  7.2 125.4 %all-gather.15.cloned.1.call-start = ((), (), s32[]{:S(2)}) async-start(), calls=%async_computation.12 | async-start | bytes 7864320 | tf_op jit(solution)/shard_map/all_gather | solution.py:211
  14.2 200.6 %all-gather.17.cloned.1.call-start = ((), (), s32[]{:S(2)}) async-start(), calls=%async_computation.13 | async-start | bytes 15925248 | tf_op jit(solution)/shard_map/all_gather | solution.py:155
  18.1 261.2 %all-gather.19.cloned.1.call-start = ((), (), s32[]{:S(2)}) async-start(), calls=%async_computation.14 | async-start | bytes 5308416 | tf_op jit(solution)/shard_map/all_gather | solution.py:156
  18.9 354.2 %all-gather.27.cloned.1.call-start = ((), (), s32[]{:S(2)}) async-start(), calls=%async_computation.20 | async-start | bytes 7864320 | tf_op jit(solution)/shard_map/all_gather | solution.py:211
  19.5 566.0 %reduce-scatter.13.cloned.1.call-start = ((), (), s32[]{:S(2)}) async-start(), calls=%async_computation.15 | async-start | bytes 15728640 | tf_op jit(solution)/shard_map/reduce_scatter | solution.py:225
  289.5 511.0 %reduce-scatter.17.cloned.1.call-start = ((), (), s32[]{:S(2)}) async-start(), calls=%async_computation.21 | async-start | bytes 15728640 | tf_op jit(solution)/shard_map/reduce_scatter | solution.py:225
  447.0 482.5 %all-gather.23.cloned.1.call-start = ((), (), s32[]{:S(2)}) async-start(), calls=%async_computation.17 | async-start | bytes 28311552 | tf_op jit(solution)/shard_map/all_gather | solution.py:162
  452.0 595.0 %all-gather.21.cloned.1.call-start = ((), (), s32[]{:S(2)}) async-start(), calls=%async_computation.16 | async-start | bytes 7864320 | tf_op jit(solution)/shard_map/all_gather | solution.py:229
  809.1 353.6 %all-gather.35.cloned.1.call-start = ((), (), s32[]{:S(2)}) async-start(), calls=%async_computation.34 | async-start | bytes 7864320 | tf_op jit(solution)/shard_map/all_gather | solution.py:245
  812.0 422.8 %all-gather.25.cloned.1.call-start = ((), (), s32[]{:S(2)}) async-start(), calls=%async_computation.18 | async-start | bytes 14155776 | tf_op jit(solution)/shard_map/all_gather | solution.py:163
  812.6 693.8 %reduce-scatter.21.cloned.1.call-start = ((), (), s32[]{:S(2)}) async-start(), calls=%async_computation.24 | async-start | bytes 15728640 | tf_op jit(solution)/shard_map/reduce_scatter | solution.py:261
  1294.4 334.5 %all-gather.29.cloned.1.call-start = ((), (), s32[]{:S(2)}) async-start(), calls=%async_computation.22 | async-start | bytes 7864320 | tf_op jit(solution)/shard_map/all_gather | solution.py:229
  1512.4 231.7 %all-gather.37.cloned.1.call-start = ((), (), s32[]{:S(2)}) async-start(), calls=%async_computation.35 | async-start | bytes 7864320 | tf_op jit(solution)/shard_map/all_gather | solution.py:245
  1513.1 500.5 %reduce-scatter.25.cloned.1.call-start = ((), (), s32[]{:S(2)}) async-start(), calls=%async_computation.27 | async-start | bytes 15728640 | tf_op jit(solution)/shard_map/reduce_scatter | solution.py:261
  1803.4 324.8 %reduce-scatter.15.cloned.1.call-start = ((), (), s32[]{:S(2)}) async-start(), calls=%async_computation.19 | async-start | bytes 7864320 | tf_op jit(solution)/shard_map/reduce_scatter | solution.py:239
  1821.8 420.4 %reduce-scatter.19.cloned.1.call-start = ((), (), s32[]{:S(2)}) async-start(), calls=%async_computation.23 | async-start | bytes 7864320 | tf_op jit(solution)/shard_map/reduce_scatter | solution.py:239
  1840.2 528.9 %all-gather.31.cloned.1.call-start = ((), (), s32[]{:S(2)}) async-start(), calls=%async_computation.25 | async-start | bytes 7864320 | tf_op jit(solution)/shard_map/all_gather | solution.py:265
  2252.3 231.1 %all-gather.33.cloned.1.call-start = ((), (), s32[]{:S(2)}) async-start(), calls=%async_computation.28 | async-start | bytes 7864320 | tf_op jit(solution)/shard_map/all_gather | solution.py:265
  2252.9 763.4 %reduce-scatter.35.cloned.1.call-start = ((), (), s32[]{:S(2)}) async-start(), calls=%async_computation.33 | async-start | bytes 14155776 | tf_op jit(solution)/shard_map/reduce_scatter | solution.py:311
  2296.1 725.8 %reduce-scatter.33.cloned.1.call-start = ((), (), s32[]{:S(2)}) async-start(), calls=%async_computation.32 | async-start | bytes 28311552 | tf_op jit(solution)/shard_map/reduce_scatter | solution.py:308
  2368.8 661.2 %reduce-scatter.31.cloned.1.call-start = ((), (), s32[]{:S(2)}) async-start(), calls=%async_computation.31 | async-start | bytes 5308416 | tf_op jit(solution)/shard_map/reduce_scatter | solution.py:305
  2493.8 538.4 %reduce-scatter.23.cloned.1.call-start = ((), (), s32[]{:S(2)}) async-start(), calls=%async_computation.26 | async-start | bytes 7864320 | tf_op jit(solution)/shard_map/reduce_scatter | solution.py:295
  2745.3 333.8 %reduce-scatter.27.cloned.1.call-start = ((), (), s32[]{:S(2)}) async-start(), calls=%async_computation.29 | async-start | bytes 7864320 | tf_op jit(solution)/shard_map/reduce_scatter | solution.py:295
  2968.7 216.1 %reduce-scatter.29.cloned.1.call-start = ((), (), s32[]{:S(2)}) async-start(), calls=%async_computation.30 | async-start | bytes 15925248 | tf_op jit(solution)/shard_map/reduce_scatter | solution.py:302
  (94 other events, 5655.4 us)
Sparse Core Ops, SparseCore 0:
  14.3 118.2 all-gather.14
  135.0 79.7 all-gather.16
  216.7 38.9 all-gather.18
  257.7 115.4 all-gather.26
  375.3 210.0 reduce-scatter.12
  587.6 212.8 reduce-scatter.16
  803.0 126.3 all-gather.22
  931.6 115.3 all-gather.20
  1049.1 113.5 all-gather.34
  1164.5 70.3 all-gather.24
  1294.5 211.8 reduce-scatter.20
  1512.5 116.3 all-gather.28
  1630.5 113.5 all-gather.36
  1803.5 210.0 reduce-scatter.24
  2016.3 111.7 reduce-scatter.14
  2130.9 111.2 reduce-scatter.18
  2252.5 115.8 all-gather.30
  2369.8 113.5 all-gather.32
  2486.9 90.6 reduce-scatter.34
  2581.0 156.8 reduce-scatter.32
  2741.4 53.8 reduce-scatter.30
  2798.3 110.7 reduce-scatter.22
  2968.8 110.1 reduce-scatter.26
  3082.9 101.8 reduce-scatter.28
where the time goes:
time: 3210 us; the launch traced here: 3200 us
  waiting for transfers between devices  1970 us (61%)
  matrix products  733 us (23%)
  local copies, waits for them, and re-layouts  233 us (7%)
  other arithmetic  165 us (5%)
  blocking collectives  71.3 us (2%)
    reduce_scatter x2, waiting for transfers between devices, per_device(): lax.psum_scatter(normed_two_term, 'tp', scatter_dimension=0, tiled=True)  384 us
    reduce_scatter x2, waiting for transfers between devices, per_device(): lax.psum_scatter(attn_term, 'tp', scatter_dimension=0, tiled=True)  348 us
    all_gather x2, waiting for transfers between devices, per_device(): normed_two_full = lax.all_gather(normed_two, 'tp', axis=0, tiled=True)  233 us
    reduce_scatter x2, waiting for transfers between devices, per_device(): lax.psum_scatter(mlp_term.astype(jnp.bfloat16), 'tp', scatter_dimension=0...  224 us
    all_gather x2, waiting for transfers between devices, per_device(): lax.all_gather(out_cotangent[micro_index], 'tp', axis=0, tiled=True)  164 us
    all_gather x2, waiting for transfers between devices, per_device(): normed_one_full = lax.all_gather(normed_one, 'tp', axis=0, tiled=True)  163 us
    dynamic_update_slice x8, local copies, waits for them, and re-layouts, attention_forward(): lax.map(query_block, (queries.reshape(tiles, block_rows, head_count, head...  127 us
    all_gather x1, waiting for transfers between devices, gather_feedforward(): lax.all_gather(gate_up_weight, 'fsdp', axis=0, tiled=True)  117 us
  transfers between devices with their start and end apart: 24, of which 18 were waited for; matrix products, arithmetic and copies ran while one was open for 30% of the time, Pallas kernels for 0%

commit v1 on v0

--- a/solution.py
+++ b/solution.py
@@ -1,6 +1,10 @@
+import functools
+
 import jax
 import jax.numpy as jnp
 from jax import lax
+from jax.experimental import pallas as pl
+from jax.experimental.pallas import tpu as pltpu
 from jax.sharding import PartitionSpec as P
 
 D = 3072
@@ -10,6 +14,7 @@
 rms_epsilon = 1e-05
 rope_theta = 10000.0
 masked_score = -1e30
+LOG2E = 1.4426950408889634
 
 
 def rope_tables(positions, head_size):
@@ -328,7 +333,531 @@
     )
 
 
+HEAD_GROUP = 4
+FIRST_DOC = 800
+
+
+def dot_nt(left, right):
+    return lax.dot_general(left, right, (((1,), (1,)), ((), ())), preferred_element_type=jnp.float32)
+
+
+def dot_tn(left, right):
+    return lax.dot_general(left, right, (((0,), (0,)), ((), ())), preferred_element_type=jnp.float32)
+
+
+def dot_nn(left, right):
+    return lax.dot_general(left, right, (((1,), (0,)), ((), ())), preferred_element_type=jnp.float32)
+
+
+def swap_halves(values):
+    lanes = lax.broadcasted_iota(jnp.int32, values.shape, 1)
+    width = values.shape[1]
+    return jnp.where(
+        lanes % HD < HD // 2,
+        pltpu.roll(values, width - HD // 2, 1),
+        pltpu.roll(values, HD // 2, 1),
+    )
+
+
+def causal_mask(rows, columns):
+    row_ids = lax.broadcasted_iota(jnp.int32, (rows, columns), 0)
+    column_ids = lax.broadcasted_iota(jnp.int32, (rows, columns), 1)
+    return row_ids >= column_ids
+
+
+def tail_mask(reach):
+    rows = reach.shape[0]
+    row_ids = lax.broadcasted_iota(jnp.int32, (rows, rows), 0)
+    column_ids = lax.broadcasted_iota(jnp.int32, (rows, rows), 1)
+    return (row_ids >= column_ids) & (row_ids - column_ids <= reach)
+
+
+def halves(slot_ref, quarter):
+    first = slot_ref[0]
+    return (
+        pl.multiple_of(first * quarter, quarter),
+        pl.multiple_of((1 - first) * quarter, quarter),
+    )
+
+
+def load_rotated(offsets, quarter, q_ref, k_ref, v_ref, cos_ref, sin_ref, qr_ref, kr_ref, vr_ref):
+    for place, offset in enumerate(offsets):
+        rows = pl.ds(offset, quarter)
+        target = pl.ds(place * quarter, quarter)
+        cosine, sine = cos_ref[rows, :], sin_ref[rows, :]
+        q_raw, k_raw = q_ref[rows, :], k_ref[rows, :]
+        qr_ref[target, :] = (q_raw * cosine + swap_halves(q_raw) * sine).astype(jnp.bfloat16)
+        kr_ref[target, :] = (k_raw * cosine + swap_halves(k_raw) * sine).astype(jnp.bfloat16)
+        vr_ref[target, :] = v_ref[rows, :].astype(jnp.bfloat16)
+
+
+def softmax_mix(query, pieces, factor):
+    scores = []
+    for keys, _, mask in pieces:
+        score = dot_nt(query, keys)
+        scores.append(score if mask is None else jnp.where(mask, score, masked_score))
+    top = functools.reduce(jnp.maximum, [jnp.max(s, axis=-1, keepdims=True) for s in scores])
+    weights = [jnp.exp2((s - top) * factor) for s in scores]
+    total = functools.reduce(jnp.add, [jnp.sum(w, axis=-1, keepdims=True) for w in weights])
+    inverse = 1.0 / total
+    mixed = functools.reduce(
+        jnp.add,
+        [dot_nn((w * inverse).astype(jnp.bfloat16), piece[1]) for w, piece in zip(weights, pieces)],
+    )
+    return mixed, top * factor + jnp.log2(total)
+
+
+def head_slice(head):
+    return slice(head * HD, (head + 1) * HD)
+
+
+def forward_first(
+    slot_ref, q_ref, k_ref, v_ref, cos_ref, sin_ref, qr_ref, kr_ref, vr_ref, o_ref, lse_ref
+):
+    half = q_ref.shape[0]
+    quarter = half // 2
+    offsets = halves(slot_ref, quarter)
+    load_rotated(offsets, quarter, q_ref, k_ref, v_ref, cos_ref, sin_ref, qr_ref, kr_ref, vr_ref)
+    factor = HD ** (-0.5) * LOG2E
+    mask = causal_mask(quarter, quarter)
+    for head in range(HEAD_GROUP):
+        cols = head_slice(head)
+        early, late = slice(0, quarter), slice(quarter, half)
+        k_early, v_early = kr_ref[early, cols], vr_ref[early, cols]
+        mixed, lse = softmax_mix(qr_ref[early, cols], [(k_early, v_early, mask)], factor)
+        o_ref[pl.ds(offsets[0], quarter), cols] = mixed.astype(jnp.bfloat16)
+        lse_ref[0, early, head : head + 1] = lse
+        mixed, lse = softmax_mix(
+            qr_ref[late, cols],
+            [(k_early, v_early, None), (kr_ref[late, cols], vr_ref[late, cols], mask)],
+            factor,
+        )
+        o_ref[pl.ds(offsets[1], quarter), cols] = mixed.astype(jnp.bfloat16)
+        lse_ref[0, late, head : head + 1] = lse
+
+
+def forward_second(
+    slot_ref, q_ref, k_ref, v_ref, cos_ref, sin_ref, ka_ref, va_ref, pos_ref,
+    qr_ref, kr_ref, vr_ref, o_ref, lse_ref,
+):
+    half = q_ref.shape[0]
+    quarter = half // 2
+    cut = FIRST_DOC - half
+    spill = cut - quarter
+    offsets = halves(slot_ref, quarter)
+    load_rotated(offsets, quarter, q_ref, k_ref, v_ref, cos_ref, sin_ref, qr_ref, kr_ref, vr_ref)
+    factor = HD ** (-0.5) * LOG2E
+    mask = causal_mask(cut, cut)
+    mask_tail = tail_mask(pos_ref[pl.ds(offsets[1] + spill, half - cut), :])
+    for head in range(HEAD_GROUP):
+        cols = head_slice(head)
+        early, late = slice(0, cut), slice(cut, half)
+        mixed, lse = softmax_mix(
+            qr_ref[early, cols],
+            [
+                (ka_ref[:, cols], va_ref[:, cols], None),
+                (kr_ref[early, cols], vr_ref[early, cols], mask),
+            ],
+            factor,
+        )
+        low = mixed.astype(jnp.bfloat16)
+        o_ref[pl.ds(offsets[0], quarter), cols] = low[:quarter]
+        o_ref[pl.ds(offsets[1], spill), cols] = low[quarter:]
+        lse_ref[0, early, head : head + 1] = lse
+        mixed, lse = softmax_mix(
+            qr_ref[late, cols], [(kr_ref[late, cols], vr_ref[late, cols], mask_tail)], factor
+        )
+        o_ref[pl.ds(offsets[1] + spill, half - cut), cols] = mixed.astype(jnp.bfloat16)
+        lse_ref[0, late, head : head + 1] = lse
+
+
+def backward_both(
+    slot_ref, qa_ref, ka_ref, va_ref, qb_ref, kb_ref, vb_ref, ga_ref, gb_ref, la_ref, lb_ref,
+    cosa_ref, sina_ref, cosb_ref, sinb_ref, pos_ref,
+    dqa_ref, dka_ref, dva_ref, dqb_ref, dkb_ref, dvb_ref,
+    go_a, go_b, tqa, tka, tva, tqb, tkb, tvb,
+):
+    half = qa_ref.shape[0]
+    quarter = half // 2
+    cut = FIRST_DOC - half
+    spill = cut - quarter
+    offsets = halves(slot_ref, quarter)
+    scale_value = HD ** (-0.5)
+    factor = scale_value * LOG2E
+    for place, offset in enumerate(offsets):
+        target, rows = pl.ds(place * quarter, quarter), pl.ds(offset, quarter)
+        go_a[target, :] = ga_ref[rows, :]
+        go_b[target, :] = gb_ref[rows, :]
+    mask = causal_mask(quarter, quarter)
+    mask_cut = causal_mask(cut, cut)
+    mask_tail = tail_mask(pos_ref[pl.ds(offsets[1] + spill, half - cut), :])
+    for accumulator in (tka, tva, tkb, tvb):
+        accumulator[...] = jnp.zeros_like(accumulator)
+
+    def attend(query, grad, lse, pieces):
+        weights, weight_grads = [], []
+        for k_ref, v_ref, rows, cols, mask, _, _ in pieces:
+            weight = jnp.exp2(dot_nt(query, k_ref[rows, cols]) * factor - lse)
+            weights.append(weight if mask is None else jnp.where(mask, weight, 0.0))
+            weight_grads.append(dot_nt(grad, v_ref[rows, cols]))
+        shared = functools.reduce(
+            jnp.add,
+            [jnp.sum(w * g, axis=-1, keepdims=True) for w, g in zip(weights, weight_grads)],
+        )
+        query_grad = None
+        for weight, weight_grad, piece in zip(weights, weight_grads, pieces):
+            k_ref, v_ref, rows, cols, _, tk, tv = piece
+            score_grad = (weight * (weight_grad - shared)).astype(jnp.bfloat16)
+            term = dot_nn(score_grad, k_ref[rows, cols])
+            query_grad = term if query_grad is None else query_grad + term
+            tk[rows, cols] += dot_tn(score_grad, query)
+            tv[rows, cols] += dot_tn(weight.astype(jnp.bfloat16), grad)
+        return query_grad
+
+    for head in range(HEAD_GROUP):
+        cols = head_slice(head)
+        lane = slice(head, head + 1)
+        early, late, whole = slice(0, quarter), slice(quarter, half), slice(0, half)
+        tqa[early, cols] = attend(
+            qa_ref[early, cols], go_a[early, cols], la_ref[0, early, lane],
+            [(ka_ref, va_ref, early, cols, mask, tka, tva)],
+        )
+        tqa[late, cols] = attend(
+            qa_ref[late, cols], go_a[late, cols], la_ref[0, late, lane],
+            [
+                (ka_ref, va_ref, early, cols, None, tka, tva),
+                (ka_ref, va_ref, late, cols, mask, tka, tva),
+            ],
+        )
+        early, late = slice(0, cut), slice(cut, half)
+        tqb[early, cols] = attend(
+            qb_ref[early, cols], go_b[early, cols], lb_ref[0, early, lane],
+            [
+                (ka_ref, va_ref, whole, cols, None, tka, tva),
+                (kb_ref, vb_ref, early, cols, mask_cut, tkb, tvb),
+            ],
+        )
+        tqb[late, cols] = attend(
+            qb_ref[late, cols], go_b[late, cols], lb_ref[0, late, lane],
+            [(kb_ref, vb_ref, late, cols, mask_tail, tkb, tvb)],
+        )
+    for place, offset in enumerate(offsets):
+        source, rows = pl.ds(place * quarter, quarter), pl.ds(offset, quarter)
+        for total, cos_ref, sin_ref, out_ref in (
+            (tqa, cosa_ref, sina_ref, dqa_ref),
+            (tka, cosa_ref, sina_ref, dka_ref),
+            (tqb, cosb_ref, sinb_ref, dqb_ref),
+            (tkb, cosb_ref, sinb_ref, dkb_ref),
+        ):
+            grad = total[source, :] * scale_value
+            out_ref[rows, :] = (
+                grad * cos_ref[rows, :] - swap_halves(grad) * sin_ref[rows, :]
+            ).astype(jnp.bfloat16)
+        dva_ref[rows, :] = tva[source, :].astype(jnp.bfloat16)
+        dvb_ref[rows, :] = tvb[source, :].astype(jnp.bfloat16)
+
+
+def kernel_params():
+    return pltpu.CompilerParams(
+        dimension_semantics=("arbitrary", "arbitrary"), vmem_limit_bytes=40 * 1024 * 1024
+    )
+
+
+def attention_call(kernel, slot, arrays, kinds, outs, scratch, flops):
+    rows, heads_local = arrays[-1].shape[0], outs[1]
+    half = rows // 2
+    groups = heads_local // HEAD_GROUP
+    width = HEAD_GROUP * HD
+
+    def spec(kind):
+        if kind == "table":
+            return pl.BlockSpec((half, width), lambda s, g, _: (s, 0))
+        if kind == "column":
+            return pl.BlockSpec((half, 1), lambda s, g, _: (s, 0))
+        if kind == "lse":
+            return pl.BlockSpec((1, half, HEAD_GROUP), lambda s, g, _: (g, s, 0))
+        shift = kind * groups
+        return pl.BlockSpec((half, width), lambda s, g, _: (s, shift + g))
+
+    def shape(kind):
+        if kind == "lse":
+            return jax.ShapeDtypeStruct((groups, rows, HEAD_GROUP), jnp.float32)
+        return jax.ShapeDtypeStruct((rows, heads_local * HD), jnp.bfloat16)
+
+    return pl.pallas_call(
+        kernel,
+        out_shape=[shape(kind) for kind in outs[0]],
+        grid_spec=pltpu.PrefetchScalarGridSpec(
+            num_scalar_prefetch=1,
+            grid=(rows // half, groups),
+            in_specs=[spec(kind) for kind in kinds],
+            out_specs=[spec(kind) for kind in outs[0]],
+            scratch_shapes=scratch(half, width),
+        ),
+        compiler_params=kernel_params(),
+        cost_estimate=pl.CostEstimate(
+            flops=flops, bytes_accessed=rows * heads_local * HD * 20, transcendentals=flops // 400
+        ),
+    )(slot, *arrays)
+
+
+def backward_scratch(half, width):
+    return [pltpu.VMEM((half, width), jnp.bfloat16)] * 2 + [
+        pltpu.VMEM((half, width), jnp.float32)
+    ] * 6
+
+
+def no_scratch(half, width):
+    return []
+
+
+def wide_tables(positions):
+    half_width = HD // 2
+    frequency = rope_theta ** (-(jnp.arange(half_width, dtype=jnp.float32) * 2.0 / HD))
+    angles = positions.astype(jnp.float32)[:, None] * frequency[None, :]
+    cosine, sine = jnp.cos(angles), jnp.sin(angles)
+    return (
+        jnp.concatenate([cosine, cosine] * HEAD_GROUP, axis=-1),
+        jnp.concatenate([-sine, sine] * HEAD_GROUP, axis=-1),
+    )
+
+
+def paired_device(
+    block_in,
+    out_cotangent,
+    segment_ids,
+    doc_positions,
+    norm1_gain,
+    qkv_weight,
+    out_weight,
+    norm2_gain,
+    gate_up_weight,
+    down_weight,
+):
+    fsdp_count, tp_count = lax.axis_size("fsdp"), lax.axis_size("tp")
+    core = lax.axis_index("fsdp") % 2
+    lane_z = lax.axis_index("tp")
+    near, far = lane_z % 2, lane_z // 2
+    slot = jnp.reshape(near, (1,)).astype(jnp.int32)
+    core_pairs = [(i, i ^ 1) for i in range(fsdp_count)]
+    near_pairs = [(i, i ^ 1) for i in range(tp_count)]
+    far_pairs = [(i, i ^ 2) for i in range(tp_count)]
+    plane_groups = [list(range(first, fsdp_count, 2)) for first in range(2)]
+    rows = block_in.shape[1]
+    local_cols = qkv_weight.shape[2]
+    heads_local = local_cols // HD
+    gain_one = norm1_gain.astype(jnp.float32)
+    gain_two = norm2_gain.astype(jnp.float32)
+
+    def swap_core(value):
+        return lax.ppermute(value, "fsdp", core_pairs)
+
+    def swap_near(value):
+        return lax.ppermute(value, "tp", near_pairs)
+
+    def swap_far(value):
+        return lax.ppermute(value, "tp", far_pairs)
+
+    def spread_tokens(value):
+        keep = lax.dynamic_index_in_dim(value, far, 0, keepdims=False)
+        got = swap_far(lax.dynamic_index_in_dim(value, 1 - far, 0, keepdims=False))
+        return jnp.where(far == 0, keep, got), jnp.where(far == 0, got, keep)
+
+    def return_tokens(first, second, link_type, final_type):
+        keep = jnp.where(far == 0, first, second)
+        got = swap_far(jnp.where(far == 0, second, first).astype(link_type))
+        keep, got = keep.astype(final_type), got.astype(final_type)
+        return jnp.stack([jnp.where(far == 0, keep, got), jnp.where(far == 0, got, keep)])
+
+    def gather_tokens(value):
+        both = jnp.concatenate([value, swap_near(value)], axis=0)
+        return jnp.concatenate([both, swap_core(both)], axis=0)
+
+    def scatter_tokens(term):
+        half = term.shape[0] // 2
+        quarter = half // 2
+        summed = term[:half].astype(jnp.float32) + swap_core(term[half:]).astype(jnp.float32)
+        return summed[:quarter] + swap_near(summed[quarter:].astype(jnp.bfloat16)).astype(
+            jnp.float32
+        )
+
+    def gather_weight(weight):
+        other = swap_far(weight)
+        mine = jnp.where(core == far, weight, other)
+        sibling = swap_core(jnp.where(core == far, other, weight))
+        pair = jnp.concatenate(
+            [jnp.where(core == 0, mine, sibling), jnp.where(core == 0, sibling, mine)], axis=0
+        )
+        return lax.all_gather(pair, "fsdp", axis=0, tiled=True, axis_index_groups=plane_groups)
+
+    def scatter_weight(grad):
+        pair = lax.psum_scatter(
+            grad, "fsdp", scatter_dimension=0, tiled=True, axis_index_groups=plane_groups
+        )
+        count = pair.shape[0] // 2
+        even, odd = pair[:count], pair[count:]
+        mine = jnp.where(core == 0, even, odd)
+        got = swap_core(jnp.where(core == 0, odd, even))
+        keep = jnp.where(core == far, mine, got)
+        sent = swap_far(jnp.where(core == far, got, mine))
+        return keep.astype(jnp.float32) + sent.astype(jnp.float32)
+
+    qkv_full = gather_weight(qkv_weight.reshape(qkv_weight.shape[0], 3 * local_cols))
+    out_full = gather_weight(out_weight)
+    gate_up_full = gather_weight(gate_up_weight)
+    down_full = gather_weight(down_weight)
+
+    streams = spread_tokens(block_in)
+    positions = [gather_tokens(part) for part in spread_tokens(doc_positions)]
+    tables = [wide_tables(part) for part in positions]
+    reach = positions[1].astype(jnp.int32)[:, None]
+
+    normed_one_full, saved, attn_outs, lses = [], [], [], []
+    scales_one = []
+    streams = [part.astype(jnp.float32) for part in streams]
+    for part in range(2):
+        stream = streams[part]
+        scale_one = rms_scale(stream)
+        scales_one.append(scale_one)
+        normed = (stream * scale_one * gain_one).astype(jnp.bfloat16)
+        normed_one_full.append(gather_tokens(normed))
+    count = normed_one_full[0].shape[0]
+    pair_flops = 2 * heads_local * count * count * HD // 2
+    for part in range(2):
+        projected = jnp.dot(
+            normed_one_full[part], qkv_full, preferred_element_type=jnp.float32
+        )
+        cosine, sine = tables[part]
+        arrays = [projected, projected, projected, cosine, sine]
+        kinds = [0, 1, 2, "table", "table"]
+        if part == 0:
+            kernel = forward_first
+        else:
+            kernel = forward_second
+            arrays += [saved[0][1], saved[0][2], reach]
+            kinds += [0, 0, "column"]
+        results = attention_call(
+            kernel, slot, arrays, kinds, ([0, 0, 0, 0, "lse"], heads_local), no_scratch, pair_flops
+        )
+        saved.append(results[:3])
+        attn_outs.append(results[3])
+        lses.append(results[4])
+
+    cotangents = [part for part in spread_tokens(out_cotangent)]
+    cotangent_full = [gather_tokens(part) for part in cotangents]
+    middles, scales_two, normed_two_full = [], [], []
+    for part in range(2):
+        term = jnp.dot(attn_outs[part], out_full, preferred_element_type=jnp.float32)
+        middle = streams[part] + scatter_tokens(term.astype(jnp.bfloat16))
+        scale_two = rms_scale(middle)
+        normed = (middle * scale_two * gain_two).astype(jnp.bfloat16)
+        middles.append(middle)
+        scales_two.append(scale_two)
+        normed_two_full.append(gather_tokens(normed))
+
+    outputs, middle_grads, attn_grad_full = [], [], []
+    grad_down = grad_gate_up = grad_out = None
+    gain_two_acc = 0.0
+    for part in range(2):
+        gate_up = jnp.einsum(
+            "sd,dtf->stf", normed_two_full[part], gate_up_full, preferred_element_type=jnp.float32
+        )
+        gate_rows, up_rows = gate_up[:, 0], gate_up[:, 1]
+        sigmoid_gate = jax.nn.sigmoid(gate_rows)
+        silu_gate = gate_rows * sigmoid_gate
+        activated = (silu_gate * up_rows).astype(jnp.bfloat16)
+        term = jnp.einsum(
+            "sf,sd->fd", activated, cotangent_full[part], preferred_element_type=jnp.float32
+        )
+        grad_down = term if part == 0 else grad_down + term
+        act_grad = jnp.einsum(
+            "sd,fd->sf", cotangent_full[part], down_full, preferred_element_type=jnp.float32
+        )
+        gate_grad = act_grad * up_rows * sigmoid_gate * (1.0 + gate_rows * (1.0 - sigmoid_gate))
+        up_grad = act_grad * silu_gate
+        gate_up_grad = jnp.stack([gate_grad, up_grad], axis=1).astype(jnp.bfloat16)
+        term = jnp.einsum(
+            "sd,stf->dtf", normed_two_full[part], gate_up_grad, preferred_element_type=jnp.float32
+        )
+        grad_gate_up = term if part == 0 else grad_gate_up + term
+        term = jnp.einsum(
+            "stf,dtf->sd", gate_up_grad, gate_up_full, preferred_element_type=jnp.float32
+        )
+        normed_two_grad = scatter_tokens(term.astype(jnp.bfloat16))
+        mlp_term = jnp.dot(activated, down_full, preferred_element_type=jnp.float32)
+        mlp_branch = scatter_tokens(mlp_term.astype(jnp.bfloat16))
+        outputs.append((middles[part] + mlp_branch).astype(jnp.bfloat16))
+        middle_back, gain_two_term = norm_back(
+            middles[part], scales_two[part], gain_two, normed_two_grad
+        )
+        gain_two_acc = gain_two_acc + gain_two_term
+        middle_grad = cotangents[part].astype(jnp.float32) + middle_back
+        middle_grads.append(middle_grad)
+        attn_grad_full.append(gather_tokens(middle_grad.astype(jnp.bfloat16)))
+    down_owned = scatter_weight(grad_down.astype(jnp.bfloat16))
+    gate_up_owned = scatter_weight(grad_gate_up.astype(jnp.bfloat16))
+
+    head_grads = []
+    for part in range(2):
+        term = jnp.einsum(
+            "sc,sd->cd", attn_outs[part], attn_grad_full[part], preferred_element_type=jnp.float32
+        )
+        grad_out = term if part == 0 else grad_out + term
+        head_grads.append(
+            jnp.einsum(
+                "sd,cd->sc", attn_grad_full[part], out_full, preferred_element_type=jnp.float32
+            ).astype(jnp.bfloat16)
+        )
+    out_owned = scatter_weight(grad_out.astype(jnp.bfloat16))
+    grads = attention_call(
+        backward_both,
+        slot,
+        [*saved[0], *saved[1], *head_grads, *lses, *tables[0], *tables[1], reach],
+        [0] * 8 + ["lse"] * 2 + ["table"] * 4 + ["column"],
+        ([0] * 6, heads_local),
+        backward_scratch,
+        pair_flops * 5,
+    )
+    input_grads = []
+    grad_qkv = None
+    gain_one_acc = 0.0
+    for part in range(2):
+        projected_grad = jnp.concatenate(grads[3 * part : 3 * part + 3], axis=1)
+        term = jnp.einsum(
+            "sd,sc->dc", normed_one_full[part], projected_grad, preferred_element_type=jnp.float32
+        )
+        grad_qkv = term if part == 0 else grad_qkv + term
+        term = jnp.einsum(
+            "sc,dc->sd", projected_grad, qkv_full, preferred_element_type=jnp.float32
+        )
+        normed_one_grad = scatter_tokens(term.astype(jnp.bfloat16))
+        stream_back, gain_one_term = norm_back(
+            streams[part], scales_one[part], gain_one, normed_one_grad
+        )
+        gain_one_acc = gain_one_acc + gain_one_term
+        input_grads.append(middle_grads[part] + stream_back)
+    qkv_owned = scatter_weight(grad_qkv.astype(jnp.bfloat16))
+    gains = lax.psum_scatter(
+        jnp.stack([gain_one_acc, gain_two_acc], axis=1),
+        ("fsdp", "tp"),
+        scatter_dimension=0,
+        tiled=True,
+    )
+    return (
+        return_tokens(outputs[0], outputs[1], jnp.bfloat16, jnp.bfloat16),
+        return_tokens(input_grads[0], input_grads[1], jnp.bfloat16, jnp.float32),
+        gains[:, 0],
+        qkv_owned.reshape(qkv_weight.shape),
+        out_owned,
+        gains[:, 1],
+        gate_up_owned,
+        down_owned,
+    )
+
+
 def solution(mesh):
+    sizes = (mesh.shape["fsdp"], mesh.shape["tp"])
+    body = paired_device if sizes == (8, 4) else per_device
     in_specs = (
         P("fsdp", "tp", None),
         P("fsdp", "tp", None),
@@ -352,5 +881,5 @@
         P(("tp", "fsdp"), None),
     )
     return jax.shard_map(
-        per_device, mesh=mesh, in_specs=in_specs, out_specs=out_specs, check_vma=False
-    )
+        body, mesh=mesh, in_specs=in_specs, out_specs=out_specs, check_vma=False
+    )

time: 3210 us -> 2440 us (0.76)
  waiting for transfers between devices: 1970 us -> 1510 us
  matrix products: 733 us -> 509 us
  local copies, waits for them, and re-layouts: 233 us -> 101 us
  Pallas kernels: 0 us -> 119 us
  blocking collectives: 71.3 us -> 0 us
    ppermute x0 -> x57, waiting for transfers between devices: none -> 1280 us  [the longest x13 751 us: swap_far(): return lax.ppermute(value, 'tp', far_pairs)]
    all_gather x12 -> x4, waiting for transfers between devices: 917 us -> 0.02 us  [gather_weight(): lax.all_gather(pair, 'fsdp', axis=0, tiled=True, axis_index_groups=plane_...]
    reduce_scatter x12 -> x4, waiting for transfers between devices: 1050 us -> 228 us  [scatter_weight(): lax.psum_scatter(grad, 'fsdp', scatter_dimension=0, tiled=True, axis_inde...]
    dot_general x52 -> x24, matrix products: 733 us -> 509 us  [the longest x2 73.2 us: paired_device(): jnp.einsum('sd,stf->dtf', normed_two_full[part], gate_up_grad, preferred_...]
    dynamic_update_slice x8 -> x0, local copies, waits for them, and re-layouts: 127 us -> none  [attention_forward(): lax.map(query_block, (queries.reshape(tiles, block_rows, head_count, head...]
    pallas_call x0 -> x3, Pallas kernels: none -> 119 us  [attention_call(): pl.pallas_call(kernel, out_shape=[shape(kind) for kind in outs[0]], grid_...]
    convert_element_type x13 -> x7, other arithmetic: 86.7 us -> 17.4 us  [the longest x1 9.59 us: return_tokens(): got = swap_far(jnp.where(far == 0, second, first).astype(link_type))]
    unnamed x1 -> x0, blocking collectives: 41.4 us -> none
  transfers between devices with their start and end apart: 24 -> 66, of which waited for: 18 -> 36; matrix products, arithmetic and copies ran while one was open for 30% -> 27% of each run, Pallas kernels for 0% -> 2%
where the time goes in v1:
time: 2440 us; the launch traced here: 2430 us
  waiting for transfers between devices  1510 us (62%)
  matrix products  509 us (21%)
  other arithmetic  144 us (6%)
  Pallas kernels  119 us (5%)
  local copies, waits for them, and re-layouts  101 us (4%)
  starting transfers between devices  33.6 us (1%)
    ppermute x13, waiting for transfers between devices, swap_far(): return lax.ppermute(value, 'tp', far_pairs)  751 us
    ppermute x18, waiting for transfers between devices, swap_near(): return lax.ppermute(value, 'tp', near_pairs)  511 us
    reduce_scatter x4, waiting for transfers between devices, scatter_weight(): lax.psum_scatter(grad, 'fsdp', scatter_dimension=0, tiled=True, axis_inde...  228 us
    pallas_call x3, Pallas kernels, attention_call(): pl.pallas_call(kernel, out_shape=[shape(kind) for kind in outs[0]], grid_...  119 us
    dot_general x2, matrix products, paired_device(): jnp.einsum('sd,stf->dtf', normed_two_full[part], gate_up_grad, preferred_...  73.2 us
    dot_general x2, matrix products, paired_device(): jnp.einsum('stf,dtf->sd', gate_up_grad, gate_up_full, preferred_element_t...  66.6 us
    dot_general x2, matrix products, paired_device(): jnp.einsum('sd,dtf->stf', normed_two_full[part], gate_up_full, preferred_...  66 us
    unnamed x247, local copies, waits for them, and re-layouts  55.9 us
  transfers between devices with their start and end apart: 66, of which 36 were waited for; matrix products, arithmetic and copies ran while one was open for 27% of the time, Pallas kernels for 2%

profile of v1, /device:TPU:0, one launch (start us, length us, event | category | flops | bytes accessed | tf_op | source)
XLA Modules:
  0.0 2431.1 jit_solution(17836966437526865381)
XLA Ops:
  15.2 76.5 %collective-permute-done.3 = bf16[384,2304]{1,0:T(8,128)(2,1)S(1)} collective-permute-done((bf16[384,2304]{1,0:T(8,128)(2,1)S(1)}, bf16[384,2304]{1,0:T(8,128)(2,1)S(1)}, u32[]{:S(2)}, u32[]{:S(2)}) %collective-permute-start.3) | collective-permute-done | bytes 1769504 | tf_op jit(solution)/shard_map/ppermute | solution.py:659
  135.4 136.7 %collective-permute-done.14 = bf16[384,2,2048]{2,0,1:T(8,128)(2,1)} collective-permute-done((bf16[384,2,2048]{2,0,1:T(8,128)(2,1)}, bf16[384,2,2048]{2,0,1:T(8,128)(2,1)}, u32[]{:S(2)}, u32[]{:S(2)}) %collective-permute-start.14) | collective-permute-done | bytes 3145760 | tf_op jit(solution)/shard_map/ppermute | solution.py:659
  292.2 70.6 %collective-permute-done = bf16[256,3072]{1,0:T(8,128)(2,1)} collective-permute-done((bf16[256,3072]{1,0:T(8,128)(2,1)}, bf16[256,3072]{1,0:T(8,128)(2,1)}, u32[]{:S(2)}, u32[]{:S(2)}) %collective-permute-start) | collective-permute-done | bytes 1572896 | tf_op jit(solution)/shard_map/ppermute | solution.py:659
  371.1 68.0 %collective-permute-done.1 = bf16[256,3072]{1,0:T(8,128)(2,1)S(1)} collective-permute-done((bf16[256,3072]{1,0:T(8,128)(2,1)S(1)}, bf16[256,3072]{1,0:T(8,128)(2,1)S(1)}, u32[]{:S(2)}, u32[]{:S(2)}) %collective-permute-start.1) | collective-permute-done | bytes 1572896 | tf_op jit(solution)/shard_map/ppermute | solution.py:656
  647.6 33.4 %collective-permute-done.25 = bf16[256,3072]{1,0:T(8,128)(2,1)S(1)} collective-permute-done((bf16[256,3072]{1,0:T(8,128)(2,1)S(1)}, bf16[256,3072]{1,0:T(8,128)(2,1)S(1)}, u32[]{:S(2)}, u32[]{:S(2)}) %collective-permute-start.25) | collective-permute-done | bytes 1572896 | tf_op jit(solution)/shard_map/ppermute | solution.py:656
  720.2 64.4 %collective-permute-done.26 = bf16[256,3072]{1,0:T(8,128)(2,1)S(1)} collective-permute-done((bf16[256,3072]{1,0:T(8,128)(2,1)S(1)}, bf16[256,3072]{1,0:T(8,128)(2,1)S(1)}, u32[]{:S(2)}, u32[]{:S(2)}) %collective-permute-start.26) | collective-permute-done | bytes 1572896 | tf_op jit(solution)/shard_map/ppermute | solution.py:656
  791.3 35.2 %collective-permute-done.32 = bf16[256,3072]{1,0:T(8,128)(2,1)S(1)} collective-permute-done((bf16[256,3072]{1,0:T(8,128)(2,1)S(1)}, bf16[256,3072]{1,0:T(8,128)(2,1)S(1)}, u32[]{:S(2)}, u32[]{:S(2)}) %collective-permute-start.32) | collective-permute-done | bytes 1572896 | tf_op jit(solution)/shard_map/ppermute | solution.py:656
  892.4 33.3 %fusion.7 = f32[1024,2,2048]{2,0,1:T(8,128)} fusion(bf16[3072,2,2048]{2,0,1:T(8,128)(2,1)} %all-gather.9.cloned.1.call-done, bf16[512,3072]{1,0:T(8,128)(2,1)} %collective-permute-done.27, bf16[256,3072]{1,0:T(8,128)(2,1)} %copy-done.81, bf16[256,3072]{1,0:T(8,128)(2,1)} %copy-done.67), kind=kOutput, calls=%fused_computation.68 | convolution fusion | flops 25788678144 | bytes 48234496 | tf_op jit(solution)/shard_map/sd,dtf->stf/dot_general | solution.py:762
  952.0 33.2 %bitcast_convert_fusion = bf16[1024,3072]{1,0:T(8,128)(2,1)} fusion(bf16[3072,2,2048]{2,0,1:T(8,128)(2,1)} %all-gather.9.cloned.1.call-done, bf16[1024,1,2048]{2,0,1:T(8,128)(2,1)} %get-tuple-element.91, bf16[1024,1,2048]{2,0,1:T(8,128)(2,1)} %get-tuple-element.90), kind=kOutput, calls=%fused_computation.3 | convolution fusion | flops 25777143808 | bytes 39845888 | tf_op jit(solution)/shard_map/stf,dtf->sd/dot_general | solution.py:783
  989.7 32.7 %fusion.8 = f32[1024,2,2048]{2,0,1:T(8,128)} fusion(bf16[3072,2,2048]{2,0,1:T(8,128)(2,1)} %all-gather.9.cloned.1.call-done, bf16[512,3072]{1,0:T(8,128)(2,1)} %collective-permute-done.13, bf16[256,3072]{1,0:T(8,128)(2,1)S(1)} %copy-done.79, bf16[256,3072]{1,0:T(8,128)(2,1)S(1)} %copy-done.65), kind=kOutput, calls=%fused_computation.69 | convolution fusion | flops 25788678144 | bytes 48234496 | tf_op jit(solution)/shard_map/sd,dtf->stf/dot_general | solution.py:762
  1048.3 33.4 %bitcast_convert_fusion.1 = bf16[1024,3072]{1,0:T(8,128)(2,1)} fusion(bf16[3072,2,2048]{2,0,1:T(8,128)(2,1)} %all-gather.9.cloned.1.call-done, bf16[1024,1,2048]{2,0,1:T(8,128)(2,1)} %get-tuple-element.93, bf16[1024,1,2048]{2,0,1:T(8,128)(2,1)} %get-tuple-element.92), kind=kOutput, calls=%fused_computation.4 | convolution fusion | flops 25777143808 | bytes 39845888 | tf_op jit(solution)/shard_map/stf,dtf->sd/dot_general | solution.py:783
  1127.0 33.2 %collective-permute-done.35 = bf16[256,3072]{1,0:T(8,128)(2,1)S(1)} collective-permute-done((bf16[256,3072]{1,0:T(8,128)(2,1)S(1)}, bf16[256,3072]{1,0:T(8,128)(2,1)S(1)}, u32[]{:S(2)}, u32[]{:S(2)}) %collective-permute-start.35) | collective-permute-done | bytes 1572896 | tf_op jit(solution)/shard_map/ppermute | solution.py:656
  1169.1 35.5 %collective-permute-done.36 = bf16[256,3072]{1,0:T(8,128)(2,1)S(1)} collective-permute-done((bf16[256,3072]{1,0:T(8,128)(2,1)}, bf16[256,3072]{1,0:T(8,128)(2,1)S(1)}, u32[]{:S(2)}, u32[]{:S(2)}) %collective-permute-start.36) | collective-permute-done | bytes 1572896 | tf_op jit(solution)/shard_map/ppermute | solution.py:656
  1261.3 60.6 %shard_map.154 = (bf16[1024,768]{1,0:T(8,128)(2,1)S(1)}, bf16[1024,768]{1,0:T(8,128)(2,1)S(1)}, bf16[1024,768]{1,0:T(8,128)(2,1)S(1)}, bf16[1024,768]{1,0:T(8,12...) custom-call(s32[1]{0:T(128)} %bitcast.2.slot_ref, bf16[1024,768]{1,0:T(8,128)(2,1)S(1)} %copy-done.9, ...), custom_call_target="tpu_custom_call" | custom-call | flops 4026531840 | bytes 15728640 | tf_op jit(solution)/shard_map/pallas_call | solution.py:587
  1381.3 35.1 %fusion.2 = f32[3072,2,2048]{2,0,1:T(8,128)} fusion(bf16[1024,1,2048]{2,0,1:T(8,128)(2,1)} %get-tuple-element.91, bf16[1024,1,2048]{2,0,1:T(8,128)(2,1)} %get-tuple-element.90, bf16[512,3072]{1,0:T(8,128)(2,1)} %collective-permute-done.27, bf16[256,3072]{1,0:T(8,128)(2,1)} %copy-done.81, bf16[256,3072]{1,0:T(8,128)(2,1)S(1)} %copy-done.68), kind=kOutput, calls=%fused_computation.59 | convolution fusion | flops 25805455360 | bytes 65011712 | tf_op jit(solution)/shard_map/sd,stf->dtf/dot_general | solution.py:779
  1448.2 38.1 %add_convert_fusion = bf16[3072,2,2048]{2,0,1:T(8,128)(2,1)} fusion(f32[3072,2,2048]{2,0,1:T(8,128)} %fusion.2, bf16[1024,1,2048]{2,0,1:T(8,128)(2,1)} %get-tuple-element.93, bf16[1024,1,2048]{2,0,1:T(8,128)(2,1)} %get-tuple-element.92, bf16[512,3072]{1,0:T(8,128)(2,1)} %collective-permute-done.13, bf16[256,3072]{1,0:T(8,128)(2,1)S(1)} %copy-done.80, ...), kind=kOutput, calls=%fused_computation | convolution fusion | flops 25830621184 | bytes 90177536 | tf_op jit(solution)/shard_map/sd,stf->dtf/dot_general | solution.py:779
  1669.1 33.3 %collective-permute-done.29 = bf16[256,3072]{1,0:T(8,128)(2,1)} collective-permute-done((bf16[256,3072]{1,0:T(8,128)(2,1)S(1)}, bf16[256,3072]{1,0:T(8,128)(2,1)}, u32[]{:S(2)}, u32[]{:S(2)}) %collective-permute-start.29) | collective-permute-done | bytes 1572896 | tf_op jit(solution)/shard_map/ppermute | solution.py:656
  1721.4 93.4 %collective-permute-done.30 = bf16[256,3072]{1,0:T(8,128)(2,1)S(1)} collective-permute-done((bf16[256,3072]{1,0:T(8,128)(2,1)}, bf16[256,3072]{1,0:T(8,128)(2,1)S(1)}, u32[]{:S(2)}, u32[]{:S(2)}) %collective-permute-start.30) | collective-permute-done | bytes 1572896 | tf_op jit(solution)/shard_map/ppermute | solution.py:659
  1857.6 36.3 %reduce-scatter.14.cloned.1.call-done = bf16[512,3072]{1,0:T(8,128)(2,1)} async-done(((bf16[2048,3072]{1,0:T(8,128)(2,1)}), bf16[512,3072]{1,0:T(8,128)(2,1)}) %reduce-scatter.14.cloned.1.call-update) | async-done | bytes 3145744 | tf_op jit(solution)/shard_map/reduce_scatter | solution.py:694
  1897.1 57.2 %reduce-scatter.10.cloned.1.call-done = bf16[192,3072]{1,0:T(8,128)(2,1)} async-done(((bf16[768,3072]{1,0:T(8,128)(2,1)}), bf16[192,3072]{1,0:T(8,128)(2,1)}) %reduce-scatter.10.cloned.1.call-update) | async-done | bytes 1179664 | tf_op jit(solution)/shard_map/reduce_scatter | solution.py:694
  1956.4 135.0 %reduce-scatter.8.cloned.1.call-done = bf16[768,2304]{1,0:T(8,128)(2,1)} async-done(((bf16[3072,2304]{1,0:T(8,128)(2,1)}), bf16[768,2304]{1,0:T(8,128)(2,1)}) %reduce-scatter.8.cloned.1.call-update) | async-done | bytes 3538960 | tf_op jit(solution)/shard_map/reduce_scatter | solution.py:694
  2111.0 153.2 %collective-permute-done.52 = bf16[96,3072]{1,0:T(8,128)(2,1)S(1)} collective-permute-done((bf16[96,3072]{1,0:T(8,128)(2,1)S(1)}, bf16[96,3072]{1,0:T(8,128)(2,1)S(1)}, u32[]{:S(2)}, u32[]{:S(2)}) %collective-permute-start.52) | collective-permute-done | bytes 589856 | tf_op jit(solution)/shard_map/ppermute | solution.py:659
  2265.6 32.5 %collective-permute-done.56 = bf16[256,3072]{1,0:T(8,128)(2,1)} collective-permute-done((bf16[256,3072]{1,0:T(8,128)(2,1)}, bf16[256,3072]{1,0:T(8,128)(2,1)}, u32[]{:S(2)}, u32[]{:S(2)}) %collective-permute-start.56) | collective-permute-done | bytes 1572896 | tf_op jit(solution)/shard_map/ppermute | solution.py:659
  2302.1 100.4 %collective-permute-done.50 = bf16[384,2304]{1,0:T(8,128)(2,1)S(1)} collective-permute-done((bf16[384,2304]{1,0:T(8,128)(2,1)S(1)}, bf16[384,2304]{1,0:T(8,128)(2,1)S(1)}, u32[]{:S(2)}, u32[]{:S(2)}) %collective-permute-start.50) | collective-permute-done | bytes 1769504 | tf_op jit(solution)/shard_map/ppermute | solution.py:659
  (496 shorter events, 954.3 us)
Async XLA Ops:
  7.2 504.8 %all-gather.5.cloned.1.call-start = ((), (), s32[]{:S(2)}) async-start(), calls=%async_computation.5 | async-start | bytes 17694720 | tf_op jit(solution)/shard_map/all_gather | solution.py:691
  101.0 523.2 %all-gather.7.cloned.1.call-start = ((), (), s32[]{:S(2)}) async-start(), calls=%async_computation.6 | async-start | bytes 5898240 | tf_op jit(solution)/shard_map/all_gather | solution.py:691
  133.8 138.4 %collective-permute-start.14 = (bf16[384,2,2048]{2,0,1:T(8,128)(2,1)}, bf16[384,2,2048]{2,0,1:T(8,128)(2,1)}, u32[]{:S(2)}, u32[]{:S(2)}) collective-permute-start(bf16[384,2,2048]{2,0,1:T(8,128)(2,1)} %copy.44), channel_id=1, source_target_pairs={{0,2},{1,3},{2,0},{3,1},{4,6},{5,7},{6,4},{7,5},{8,10},{9,11},{10,... | collective-permute-start | bytes 9437192 | tf_op jit(solution)/shard_map/ppermute | solution.py:659
  135.3 757.1 %all-gather.9.cloned.1.call-start = ((), (), s32[]{:S(2)}) async-start(), calls=%async_computation.7 | async-start | bytes 31457280 | tf_op jit(solution)/shard_map/all_gather | solution.py:691
  287.8 637.9 %all-gather.11.cloned.1.call-start = ((), (), s32[]{:S(2)}) async-start(), calls=%async_computation.8 | async-start | bytes 15728640 | tf_op jit(solution)/shard_map/all_gather | solution.py:691
  371.0 132.6 %collective-permute-start.20 = (bf16[256,3072]{1,0:T(8,128)(2,1)}, bf16[256,3072]{1,0:T(8,128)(2,1)}, u32[]{:S(2)}, u32[]{:S(2)}) collective-permute-start(bf16[256,3072]{1,0:T(8,128)(2,1)} %get-tuple-element.122), channel_id=1, source_target_pairs={{0,1},{1,0},{2,3},{3,2},{4,5},{5,4},{6,7},{7,6},{8,9},{9,8},{10,11... | collective-permute-start | bytes 4718600 | tf_op jit(solution)/shard_map/ppermute | solution.py:656
  511.4 1305.6 %reduce-scatter.16.cloned.1.call-start = ((), (), s32[]{:S(2)}) async-start(), calls=%async_computation.13 | async-start | bytes 1622016
  785.7 106.7 %collective-permute-start.27 = (bf16[512,3072]{1,0:T(8,128)(2,1)S(1)}, bf16[512,3072]{1,0:T(8,128)(2,1)}, u32[]{:S(2)}, u32[]{:S(2)}) collective-permute-start(bf16[512,3072]{1,0:T(8,128)(2,1)S(1)} %pad_maximum_fusion.19), channel_id=1, source_target_pairs={{0,4},{4,0},{8,12},{12,8},{16,20},{20,16},{24,28},{28,24},{1,5},{5... | collective-permute-start | bytes 9437192 | tf_op jit(solution)/shard_map/ppermute | solution.py:653
  791.2 99.0 %collective-permute-start.12 = (bf16[256,3072]{1,0:T(8,128)(2,1)S(1)}, bf16[256,3072]{1,0:T(8,128)(2,1)S(1)}, u32[]{:S(2)}, u32[]{:S(2)}) collective-permute-start(bf16[256,3072]{1,0:T(8,128)(2,1)S(1)} %get-tuple-element.121), channel_id=1, source_target_pairs={{0,1},{1,0},{2,3},{3,2},{4,5},{5,4},{6,7},{7,6},{8,9},{9,8},{10,11... | collective-permute-start | bytes 4718600 | tf_op jit(solution)/shard_map/ppermute | solution.py:656
  828.7 193.7 %collective-permute-start.33 = (bf16[512,3072]{1,0:T(8,128)(2,1)}, bf16[512,3072]{1,0:T(8,128)(2,1)}, u32[]{:S(2)}, u32[]{:S(2)}) collective-permute-start(bf16[512,3072]{1,0:T(8,128)(2,1)} %pad_maximum_fusion.21), channel_id=1, source_target_pairs={{0,4},{4,0},{8,12},{12,8},{16,20},{20,16},{24,28},{28,24},{1,5},{5... | collective-permute-start | bytes 9437192 | tf_op jit(solution)/shard_map/ppermute | solution.py:653
  892.4 97.3 %collective-permute-start.13 = (bf16[512,3072]{1,0:T(8,128)(2,1)}, bf16[512,3072]{1,0:T(8,128)(2,1)}, u32[]{:S(2)}, u32[]{:S(2)}) collective-permute-start(bf16[512,3072]{1,0:T(8,128)(2,1)} %pad_maximum_fusion.16), channel_id=1, source_target_pairs={{0,4},{4,0},{8,12},{12,8},{16,20},{20,16},{24,28},{28,24},{1,5},{5... | collective-permute-start | bytes 9437192 | tf_op jit(solution)/shard_map/ppermute | solution.py:653
  1447.4 405.3 %reduce-scatter.12.cloned.1.call-start = ((), (), s32[]{:S(2)}) async-start(), calls=%async_computation.11 | async-start | bytes 31457280 | tf_op jit(solution)/shard_map/reduce_scatter | solution.py:694
  1486.3 407.6 %reduce-scatter.14.cloned.1.call-start = ((), (), s32[]{:S(2)}) async-start(), calls=%async_computation.12 | async-start | bytes 15728640 | tf_op jit(solution)/shard_map/reduce_scatter | solution.py:694
  1529.6 424.7 %reduce-scatter.10.cloned.1.call-start = ((), (), s32[]{:S(2)}) async-start(), calls=%async_computation.10 | async-start | bytes 5898240 | tf_op jit(solution)/shard_map/reduce_scatter | solution.py:694
  1545.9 545.4 %reduce-scatter.8.cloned.1.call-start = ((), (), s32[]{:S(2)}) async-start(), calls=%async_computation.9 | async-start | bytes 17694720 | tf_op jit(solution)/shard_map/reduce_scatter | solution.py:694
  1709.3 105.5 %collective-permute-start.30 = (bf16[256,3072]{1,0:T(8,128)(2,1)}, bf16[256,3072]{1,0:T(8,128)(2,1)S(1)}, u32[]{:S(2)}, u32[]{:S(2)}) collective-permute-start(bf16[256,3072]{1,0:T(8,128)(2,1)} %get-tuple-element.79), channel_id=1, source_target_pairs={{0,2},{1,3},{2,0},{3,1},{4,6},{5,7},{6,4},{7,5},{8,10},{9,11},{10,... | collective-permute-start | bytes 4718600 | tf_op jit(solution)/shard_map/ppermute | solution.py:659
  1721.4 126.3 %collective-permute-start.48 = (bf16[256,3072]{1,0:T(8,128)(2,1)}, bf16[256,3072]{1,0:T(8,128)(2,1)}, u32[]{:S(2)}, u32[]{:S(2)}) collective-permute-start(bf16[256,3072]{1,0:T(8,128)(2,1)} %get-tuple-element.72), channel_id=1, source_target_pairs={{0,2},{1,3},{2,0},{3,1},{4,6},{5,7},{6,4},{7,5},{8,10},{9,11},{10,... | collective-permute-start | bytes 4718600 | tf_op jit(solution)/shard_map/ppermute | solution.py:659
  1857.6 243.0 %collective-permute-start.53 = (bf16[384,2,2048]{2,0,1:T(8,128)(2,1)}, bf16[384,2,2048]{2,0,1:T(8,128)(2,1)}, u32[]{:S(2)}, u32[]{:S(2)}) collective-permute-start(bf16[384,2,2048]{2,0,1:T(8,128)(2,1)} %broadcast_select_fusion.3), channel_id=1, source_target_pairs={{0,4},{4,0},{8,12},{12,8},{16,20},{20,16},{24,28},{28,24},{1,5},{5... | collective-permute-start | bytes 9437192 | tf_op jit(solution)/shard_map/ppermute | solution.py:653
  1897.1 200.7 %collective-permute-start.55 = (bf16[256,3072]{1,0:T(8,128)(2,1)}, bf16[256,3072]{1,0:T(8,128)(2,1)}, u32[]{:S(2)}, u32[]{:S(2)}) collective-permute-start(bf16[256,3072]{1,0:T(8,128)(2,1)} %broadcast_select_fusion.17), channel_id=1, source_target_pairs={{0,4},{4,0},{8,12},{12,8},{16,20},{20,16},{24,28},{28,24},{1,5},{5... | collective-permute-start | bytes 4718600 | tf_op jit(solution)/shard_map/ppermute | solution.py:653
  1956.4 137.4 %collective-permute-start.51 = (bf16[96,3072]{1,0:T(8,128)(2,1)}, bf16[96,3072]{1,0:T(8,128)(2,1)}, u32[]{:S(2)}, u32[]{:S(2)}) collective-permute-start(bf16[96,3072]{1,0:T(8,128)(2,1)} %broadcast_select_fusion.27), channel_id=1, source_target_pairs={{0,4},{4,0},{8,12},{12,8},{16,20},{20,16},{24,28},{28,24},{1,5},{5... | collective-permute-start | bytes 1769480 | tf_op jit(solution)/shard_map/ppermute | solution.py:653
  2095.4 168.8 %collective-permute-start.52 = (bf16[96,3072]{1,0:T(8,128)(2,1)S(1)}, bf16[96,3072]{1,0:T(8,128)(2,1)S(1)}, u32[]{:S(2)}, u32[]{:S(2)}) collective-permute-start(bf16[96,3072]{1,0:T(8,128)(2,1)S(1)} %broadcast_select_fusion.24), channel_id=1, source_target_pairs={{0,2},{1,3},{2,0},{3,1},{4,6},{5,7},{6,4},{7,5},{8,10},{9,11},{10,... | collective-permute-start | bytes 1769480 | tf_op jit(solution)/shard_map/ppermute | solution.py:659
  2100.5 197.5 %collective-permute-start.56 = (bf16[256,3072]{1,0:T(8,128)(2,1)}, bf16[256,3072]{1,0:T(8,128)(2,1)}, u32[]{:S(2)}, u32[]{:S(2)}) collective-permute-start(bf16[256,3072]{1,0:T(8,128)(2,1)} %broadcast_select_fusion.14), channel_id=1, source_target_pairs={{0,2},{1,3},{2,0},{3,1},{4,6},{5,7},{6,4},{7,5},{8,10},{9,11},{10,... | collective-permute-start | bytes 4718600 | tf_op jit(solution)/shard_map/ppermute | solution.py:659
  2104.7 306.9 %collective-permute-start.54 = (bf16[384,2,2048]{2,0,1:T(8,128)(2,1)}, bf16[384,2,2048]{2,0,1:T(8,128)(2,1)}, u32[]{:S(2)}, u32[]{:S(2)}) collective-permute-start(bf16[384,2,2048]{2,0,1:T(8,128)(2,1)} %broadcast_select_fusion), channel_id=1, source_target_pairs={{0,2},{1,3},{2,0},{3,1},{4,6},{5,7},{6,4},{7,5},{8,10},{9,11},{10,... | collective-permute-start | bytes 9437192 | tf_op jit(solution)/shard_map/ppermute | solution.py:659
  2105.8 296.7 %collective-permute-start.50 = (bf16[384,2304]{1,0:T(8,128)(2,1)S(1)}, bf16[384,2304]{1,0:T(8,128)(2,1)S(1)}, u32[]{:S(2)}, u32[]{:S(2)}) collective-permute-start(bf16[384,2304]{1,0:T(8,128)(2,1)S(1)} %broadcast_select_fusion.7), channel_id=1, source_target_pairs={{0,2},{1,3},{2,0},{3,1},{4,6},{5,7},{6,4},{7,5},{8,10},{9,11},{10,... | collective-permute-start | bytes 5308424 | tf_op jit(solution)/shard_map/ppermute | solution.py:659
  (160 other events, 5428.8 us)
Sparse Core Ops, SparseCore 0:
  101.1 136.7 all-gather.4
  240.3 57.0 all-gather.6
  299.9 227.3 all-gather.8
  529.5 122.5 all-gather.10
  1447.6 98.2 reduce-scatter.15
  1548.8 220.8 reduce-scatter.11
  1773.1 120.6 reduce-scatter.13
  1897.1 57.0 reduce-scatter.9
  1957.7 133.5 reduce-scatter.7

commit v2 on v1

--- a/solution.py
+++ b/solution.py
@@ -380,11 +380,15 @@
     )
 
 
+def widen(table):
+    return jnp.concatenate([table] * HEAD_GROUP, axis=1)
+
+
 def load_rotated(offsets, quarter, q_ref, k_ref, v_ref, cos_ref, sin_ref, qr_ref, kr_ref, vr_ref):
     for place, offset in enumerate(offsets):
         rows = pl.ds(offset, quarter)
         target = pl.ds(place * quarter, quarter)
-        cosine, sine = cos_ref[rows, :], sin_ref[rows, :]
+        cosine, sine = widen(cos_ref[rows, :]), widen(sin_ref[rows, :])
         q_raw, k_raw = q_ref[rows, :], k_ref[rows, :]
         qr_ref[target, :] = (q_raw * cosine + swap_halves(q_raw) * sine).astype(jnp.bfloat16)
         kr_ref[target, :] = (k_raw * cosine + swap_halves(k_raw) * sine).astype(jnp.bfloat16)
@@ -551,19 +555,303 @@
         ):
             grad = total[source, :] * scale_value
             out_ref[rows, :] = (
-                grad * cos_ref[rows, :] - swap_halves(grad) * sin_ref[rows, :]
+                grad * widen(cos_ref[rows, :]) - swap_halves(grad) * widen(sin_ref[rows, :])
             ).astype(jnp.bfloat16)
         dva_ref[rows, :] = tva[source, :].astype(jnp.bfloat16)
         dvb_ref[rows, :] = tvb[source, :].astype(jnp.bfloat16)
 
 
+COST_SCALE = 1.7
+
+
+def cost_of(flops):
+    return pl.CostEstimate(flops=int(COST_SCALE * flops), bytes_accessed=1000, transcendentals=0)
+
+
+def line_params():
+    return pltpu.CompilerParams(
+        dimension_semantics=("arbitrary",), vmem_limit_bytes=48 * 1024 * 1024
+    )
+
+
+def rows_kernel(pairs, extra_count, dot, chunk, finish, *refs):
+    lefts, weights = refs[:pairs], refs[pairs : 2 * pairs]
+    extras = refs[2 * pairs : 2 * pairs + extra_count]
+    outs = refs[2 * pairs + extra_count :]
+
+    @pl.loop(0, outs[0].shape[0] // chunk)
+    def _(step):
+        rows = pl.ds(pl.multiple_of(step * chunk, chunk), chunk)
+        total = None
+        for left, weight in zip(lefts, weights):
+            term = dot(left[rows, :], weight[...])
+            total = term if total is None else total + term
+        for out, value in zip(outs, finish(total, *[extra[rows, :] for extra in extras])):
+            out[rows, :] = value.astype(out.dtype)
+
+
+def keep_one(total):
+    return (total,)
+
+
+def rows_matmul(lefts, weights, dot, types, tile, chunk=1024, finish=keep_one, extras=()):
+    rows = lefts[0].shape[0]
+    if dot is dot_nn:
+        width = weights[0].shape[1]
+        weight_specs = [pl.BlockSpec((w.shape[0], tile), lambda j: (0, j)) for w in weights]
+    else:
+        width = weights[0].shape[0]
+        weight_specs = [pl.BlockSpec((tile, w.shape[1]), lambda j: (j, 0)) for w in weights]
+    column = pl.BlockSpec((rows, tile), lambda j: (0, j))
+    flops = 2 * rows * width * sum(left.shape[1] for left in lefts)
+    results = pl.pallas_call(
+        functools.partial(rows_kernel, len(lefts), len(extras), dot, min(chunk, rows), finish),
+        out_shape=[jax.ShapeDtypeStruct((rows, width), kind) for kind in types],
+        grid=(width // tile,),
+        in_specs=[pl.BlockSpec(left.shape, lambda j: (0, 0)) for left in lefts]
+        + weight_specs
+        + [column] * len(extras),
+        out_specs=[column] * len(types),
+        compiler_params=line_params(),
+        cost_estimate=cost_of(flops),
+    )(*lefts, *weights, *extras)
+    return tuple(results) if len(types) > 1 else results[0]
+
+
+def sum_kernel(parts, chunk, *refs):
+    lefts, rights, out = refs[:parts], refs[parts : 2 * parts], refs[-1]
+
+    @pl.loop(0, out.shape[1] // chunk)
+    def _(step):
+        cols = pl.ds(pl.multiple_of(step * chunk, chunk), chunk)
+        total = None
+        for left, right in zip(lefts, rights):
+            term = dot_tn(left[...], right[:, cols])
+            total = term if total is None else total + term
+        out[:, cols] = total.astype(out.dtype)
+
+
+def sum_matmul(lefts, rights, tile, chunk):
+    rows, height = lefts[0].shape
+    width = rights[0].shape[1]
+    return pl.pallas_call(
+        functools.partial(sum_kernel, len(lefts), chunk),
+        out_shape=jax.ShapeDtypeStruct((height, width), jnp.bfloat16),
+        grid=(height // tile,),
+        in_specs=[pl.BlockSpec((rows, tile), lambda j: (0, j)) for _ in lefts]
+        + [pl.BlockSpec((rows, width), lambda j: (0, 0)) for _ in rights],
+        out_specs=pl.BlockSpec((tile, width), lambda j: (j, 0)),
+        compiler_params=line_params(),
+        cost_estimate=cost_of(2 * rows * height * width * len(lefts)),
+    )(*lefts, *rights)
+
+
+def sibling_id():
+    index = lax.axis_index("fsdp")
+    return (index + 1 - 2 * (index % 2), lax.axis_index("tp"))
+
+
+def meet(partner):
+    barrier = pltpu.get_barrier_semaphore()
+    pl.semaphore_signal(barrier, inc=1, device_id=partner, device_id_type=pl.DeviceIdType.MESH)
+    pl.semaphore_wait(barrier, 1)
+
+
+def push(source, target, send, receive, partner):
+    return pltpu.make_async_remote_copy(
+        src_ref=source,
+        dst_ref=target,
+        send_sem=send,
+        recv_sem=receive,
+        device_id=partner,
+        device_id_type=pl.DeviceIdType.MESH,
+    )
+
+
+def exchange_call(kernel, key, operands, outs, scratch, vmem=16):
+    anywhere = pl.BlockSpec(memory_space=pl.ANY)
+    results = pl.pallas_call(
+        kernel,
+        out_shape=outs,
+        in_specs=[anywhere] * len(operands),
+        out_specs=[anywhere] * len(outs),
+        scratch_shapes=scratch,
+        compiler_params=pltpu.CompilerParams(
+            collective_id=key, has_side_effects=True, vmem_limit_bytes=vmem * 1024 * 1024
+        ),
+        cost_estimate=cost_of(4 * 10**9),
+    )(*operands)
+    return tuple(results) if len(outs) > 1 else results[0]
+
+
+def gather_kernel(own_ref, near_ref, full_ref, local, send, receive):
+    partner = sibling_id()
+    meet(partner)
+    count = own_ref.shape[0]
+    copies = []
+    for place, ref in enumerate((own_ref, near_ref)):
+        remote = push(
+            ref, full_ref.at[pl.ds((2 + place) * count, count)],
+            send.at[place], receive.at[place], partner,
+        )
+        remote.start()
+        copies.append(remote)
+    for place, ref in enumerate((own_ref, near_ref)):
+        copy = pltpu.make_async_copy(
+            ref, full_ref.at[pl.ds(place * count, count)], local.at[place]
+        )
+        copy.start()
+        copies.append(copy)
+    for copy in copies:
+        copy.wait()
+
+
+def core_gather(own, near):
+    shape = (4 * own.shape[0], own.shape[1])
+    return exchange_call(
+        gather_kernel, 1, [own, near], [jax.ShapeDtypeStruct(shape, own.dtype)],
+        [pltpu.SemaphoreType.DMA((2,))] * 3,
+    )
+
+
+def reduce_kernel(term_ref, keep_ref, away_ref, mine, got, keep, away, local, send, receive, store):
+    partner = sibling_id()
+    meet(partner)
+    pieces, count = mine.shape[0], mine.shape[1]
+    half = pieces * count
+    remotes, loads = [], []
+    for piece in range(pieces):
+        order = (piece + pieces // 2) % pieces
+        remote = push(
+            term_ref.at[pl.ds(half + order * count, count)], got.at[order],
+            send.at[order], receive.at[order], partner,
+        )
+        remote.start()
+        remotes.append(remote)
+        load = pltpu.make_async_copy(
+            term_ref.at[pl.ds(order * count, count)], mine.at[order], local.at[order]
+        )
+        load.start()
+        loads.append(load)
+    stores = []
+    for piece in range(pieces):
+        order = (piece + pieces // 2) % pieces
+        loads[piece].wait()
+        remotes[piece].wait()
+        total = mine[order].astype(jnp.float32) + got[order].astype(jnp.float32)
+        if order < pieces // 2:
+            keep[order] = total
+            copy = pltpu.make_async_copy(
+                keep.at[order], keep_ref.at[pl.ds(order * count, count)], store.at[order]
+            )
+        else:
+            slot = order - pieces // 2
+            away[slot] = total.astype(away.dtype)
+            copy = pltpu.make_async_copy(
+                away.at[slot], away_ref.at[pl.ds(slot * count, count)], store.at[order]
+            )
+        copy.start()
+        stores.append(copy)
+    for copy in stores:
+        copy.wait()
+
+
+def core_reduce(term):
+    rows, width = term.shape
+    quarter = rows // 4
+    pieces = 4
+    count = 2 * quarter // pieces
+    return exchange_call(
+        reduce_kernel, 2, [term],
+        [
+            jax.ShapeDtypeStruct((quarter, width), jnp.float32),
+            jax.ShapeDtypeStruct((quarter, width), term.dtype),
+        ],
+        [
+            pltpu.VMEM((pieces, count, width), term.dtype),
+            pltpu.VMEM((pieces, count, width), term.dtype),
+            pltpu.VMEM((pieces // 2, count, width), jnp.float32),
+            pltpu.VMEM((pieces // 2, count, width), term.dtype),
+        ]
+        + [pltpu.SemaphoreType.DMA((pieces,))] * 4,
+        vmem=24,
+    )
+
+
+def pair_kernel(own_ref, other_ref, pair_ref, local, send, receive):
+    partner = sibling_id()
+    core = lax.axis_index("fsdp") % 2
+    far = lax.axis_index("tp") // 2
+    meet(partner)
+    count = own_ref.shape[0]
+    place = pl.ds(pl.multiple_of(core * count, count), count)
+
+    def run(mine, theirs):
+        remote = push(theirs, pair_ref.at[place], send.at[0], receive.at[0], partner)
+        remote.start()
+        copy = pltpu.make_async_copy(mine, pair_ref.at[place], local.at[0])
+        copy.start()
+        copy.wait()
+        remote.wait()
+
+    @pl.when(core == far)
+    def _():
+        run(own_ref, other_ref)
+
+    @pl.when(core != far)
+    def _():
+        run(other_ref, own_ref)
+
+
+def core_pair(key, own, other):
+    shape = (2 * own.shape[0], own.shape[1])
+    return exchange_call(
+        pair_kernel, key, [own, other], [jax.ShapeDtypeStruct(shape, own.dtype)],
+        [pltpu.SemaphoreType.DMA((1,))] * 3,
+    )
+
+
+def split_kernel(pair_ref, keep_ref, away_ref, local, send, receive):
+    partner = sibling_id()
+    core = lax.axis_index("fsdp") % 2
+    far = lax.axis_index("tp") // 2
+    meet(partner)
+    count = keep_ref.shape[0]
+    mine = pair_ref.at[pl.ds(pl.multiple_of(core * count, count), count)]
+    theirs = pair_ref.at[pl.ds(pl.multiple_of((1 - core) * count, count), count)]
+
+    def run(own_target, other_target):
+        remote = push(theirs, other_target, send.at[0], receive.at[0], partner)
+        remote.start()
+        copy = pltpu.make_async_copy(mine, own_target, local.at[0])
+        copy.start()
+        copy.wait()
+        remote.wait()
+
+    @pl.when(core == far)
+    def _():
+        run(keep_ref, keep_ref)
+
+    @pl.when(core != far)
+    def _():
+        run(away_ref, away_ref)
+
+
+def core_split(key, pair):
+    shape = (pair.shape[0] // 2, pair.shape[1])
+    return exchange_call(
+        split_kernel, key, [pair], [jax.ShapeDtypeStruct(shape, pair.dtype)] * 2,
+        [pltpu.SemaphoreType.DMA((1,))] * 3,
+    )
+
+
 def kernel_params():
     return pltpu.CompilerParams(
         dimension_semantics=("arbitrary", "arbitrary"), vmem_limit_bytes=40 * 1024 * 1024
     )
 
 
-def attention_call(kernel, slot, arrays, kinds, outs, scratch, flops):
+def attention_call(kernel, slot, arrays, kinds, outs, scratch):
     rows, heads_local = arrays[-1].shape[0], outs[1]
     half = rows // 2
     groups = heads_local // HEAD_GROUP
@@ -571,7 +859,7 @@
 
     def spec(kind):
         if kind == "table":
-            return pl.BlockSpec((half, width), lambda s, g, _: (s, 0))
+            return pl.BlockSpec((half, HD), lambda s, g, _: (s, 0))
         if kind == "column":
             return pl.BlockSpec((half, 1), lambda s, g, _: (s, 0))
         if kind == "lse":
@@ -595,9 +883,7 @@
             scratch_shapes=scratch(half, width),
         ),
         compiler_params=kernel_params(),
-        cost_estimate=pl.CostEstimate(
-            flops=flops, bytes_accessed=rows * heads_local * HD * 20, transcendentals=flops // 400
-        ),
+        cost_estimate=cost_of(4 * len(outs[0]) ** 2 * rows * rows * heads_local * HD // 16),
     )(slot, *arrays)
 
 
@@ -611,14 +897,14 @@
     return []
 
 
-def wide_tables(positions):
+def head_tables(positions):
     half_width = HD // 2
     frequency = rope_theta ** (-(jnp.arange(half_width, dtype=jnp.float32) * 2.0 / HD))
     angles = positions.astype(jnp.float32)[:, None] * frequency[None, :]
     cosine, sine = jnp.cos(angles), jnp.sin(angles)
     return (
-        jnp.concatenate([cosine, cosine] * HEAD_GROUP, axis=-1),
-        jnp.concatenate([-sine, sine] * HEAD_GROUP, axis=-1),
+        jnp.concatenate([cosine, cosine], axis=-1),
+        jnp.concatenate([-sine, sine], axis=-1),
     )
 
 
@@ -658,198 +944,331 @@
     def swap_far(value):
         return lax.ppermute(value, "tp", far_pairs)
 
-    def spread_tokens(value):
-        keep = lax.dynamic_index_in_dim(value, far, 0, keepdims=False)
-        got = swap_far(lax.dynamic_index_in_dim(value, 1 - far, 0, keepdims=False))
+    def pick_tile(size):
+        return 512 if size % 512 == 0 else 768
+
+    tokens = []
+
+    def act(work, *inputs):
+        held = lax.optimization_barrier((*inputs, *tokens))[: len(inputs)]
+        result = work(*held)
+        tokens[:] = result if isinstance(result, tuple) else (result,)
+        return result
+
+    def pick(value, index):
+        return lax.dynamic_index_in_dim(value, index, 0, keepdims=False)
+
+    def place_tokens(value, got):
+        keep = pick(value, far)
         return jnp.where(far == 0, keep, got), jnp.where(far == 0, got, keep)
 
-    def return_tokens(first, second, link_type, final_type):
-        keep = jnp.where(far == 0, first, second)
-        got = swap_far(jnp.where(far == 0, second, first).astype(link_type))
-        keep, got = keep.astype(final_type), got.astype(final_type)
+    def join(left, right):
+        return jnp.concatenate([left, right], axis=0)
+
+    def plane_gather(pair):
+        return lax.all_gather(pair, "fsdp", axis=0, tiled=True, axis_index_groups=plane_groups)
+
+    def plane_scatter(grad):
+        return lax.psum_scatter(
+            grad, "fsdp", scatter_dimension=0, tiled=True, axis_index_groups=plane_groups
+        )
+
+    def gather_weight(key, local, other):
+        return plane_gather(act(lambda own, got: core_pair(key, own, got), local, other))
+
+    def add_wide(left, right):
+        return left.astype(jnp.float32) + right.astype(jnp.float32)
+
+    def chained(value, *others):
+        return lax.optimization_barrier((value, *others))[0]
+
+    def scatter_gains(gains):
+        for axis, size in (("fsdp", fsdp_count), ("tp", tp_count)):
+            index = lax.axis_index(axis)
+            step = size // 2
+            while step >= 1:
+                bit = (index // step) % 2
+                parts = gains.reshape(gains.shape[0], 2, gains.shape[1] // 2)
+                sent = lax.dynamic_index_in_dim(parts, 1 - bit, 1, keepdims=False)
+                kept = lax.dynamic_index_in_dim(parts, bit, 1, keepdims=False)
+                gains = kept + lax.ppermute(sent, axis, [(i, i ^ step) for i in range(size)])
+                step //= 2
+        return gains
+
+    def wide_dot(left, right, *_):
+        return rows_matmul([left], [right], dot_nn, [jnp.float32], pick_tile(right.shape[1]))
+
+    def dot_bf16(left, right):
+        return rows_matmul([left], [right], dot_nn, [jnp.bfloat16], pick_tile(right.shape[1]))
+
+    def grad_sum(left, right, left_next, right_next):
+        return sum_matmul(
+            [left, left_next], [right, right_next], pick_tile(left.shape[1]),
+            2 * pick_tile(right.shape[1]) if right.shape[1] % 1024 == 0 else pick_tile(right.shape[1]),
+        )
+
+    def rms_pack(stream, gain):
+        scale = rms_scale(stream)
+        return scale, (stream * scale * gain).astype(jnp.bfloat16)
+
+    qkv_local = qkv_weight.reshape(qkv_weight.shape[0], 3 * local_cols)
+    gate_local, up_local = gate_up_weight[:, 0], gate_up_weight[:, 1]
+
+    position_got = swap_far(pick(doc_positions, 1 - far))
+    out_other = swap_far(out_weight)
+    out_full = gather_weight(3, out_weight, out_other)
+    qkv_other = swap_far(chained(qkv_local, out_other))
+    first, second = act(place_tokens, doc_positions, position_got)
+    near_both = swap_near(join(first, second))
+    first, second = act(
+        lambda a, b, c: (join(a, c[: a.shape[0]]), join(b, c[a.shape[0] :])),
+        first, second, near_both,
+    )
+    core_both = swap_core(join(first, second))
+
+    def make_tables(first, second, both):
+        count = first.shape[0]
+        late = join(second, both[count:])
+        return (*head_tables(join(first, both[:count])), *head_tables(late), late[:, None])
+
+    cos_first, sin_first, cos_second, sin_second, reach = act(
+        make_tables, first, second, core_both
+    )
+    tables = [(cos_first, sin_first), (cos_second, sin_second)]
+    stream_got = swap_far(chained(pick(block_in, 1 - far), qkv_other))
+    qkv_full = gather_weight(4, qkv_local, qkv_other)
+
+    def first_norm(value, got):
+        streams = [part.astype(jnp.float32) for part in place_tokens(value, got)]
+        return (*streams, *rms_pack(streams[0], gain_one), *rms_pack(streams[1], gain_one))
+
+    gate_other = swap_far(chained(gate_local, stream_got))
+    s_first, s_second, r_first, n_first, r_second, n_second = act(first_norm, block_in, stream_got)
+    streams, scales_one = [s_first, s_second], [r_first, r_second]
+    near_first = swap_near(n_first)
+    gate_full = gather_weight(5, gate_local, gate_other)
+    up_other = swap_far(chained(up_local, gate_other))
+    near_second = swap_near(chained(n_second, near_first))
+    h1_first = act(core_gather, n_first, near_first)
+
+    def attend_first(projected):
+        arrays = [projected, projected, projected, *tables[0]]
+        return tuple(
+            attention_call(
+                forward_first, slot, arrays, [0, 1, 2, "table", "table"],
+                ([0, 0, 0, 0, "lse"], heads_local), no_scratch,
+            )
+        )
+
+    def attend_second(projected):
+        arrays = [projected, projected, projected, *tables[1], saved[0][1], saved[0][2], reach]
+        return tuple(
+            attention_call(
+                forward_second, slot, arrays, [0, 1, 2, "table", "table", 0, 0, "column"],
+                ([0, 0, 0, 0, "lse"], heads_local), no_scratch,
+            )
+        )
+
+    projected = act(wide_dot, h1_first, qkv_full, out_full)
+    results = act(attend_first, projected)
+    saved, lses, mixed_first = [results[:3]], [results[4]], results[3]
+    h1_second = act(core_gather, n_second, near_second)
+    term_first = act(dot_bf16, mixed_first, out_full)
+    keep_first, send_first = act(core_reduce, term_first)
+    branch_first = swap_near(send_first)
+    projected = act(wide_dot, h1_second, qkv_full)
+    up_full = gather_weight(5, up_local, up_other)
+    down_other = swap_far(chained(down_weight, up_other))
+    results = act(attend_second, projected)
+    saved.append(results[:3])
+    lses.append(results[4])
+    mixed_second = results[3]
+
+    def second_norm(stream, keep, got):
+        middle = stream + keep + got.astype(jnp.float32)
+        return (middle, *rms_pack(middle, gain_two))
+
+    m_first, q_first, n_first = act(second_norm, streams[0], keep_first, branch_first)
+    near_first = swap_near(n_first)
+    term_second = act(dot_bf16, mixed_second, out_full)
+    keep_second, send_second = act(core_reduce, term_second)
+    branch_second = swap_near(chained(send_second, near_first))
+    h2_first = act(core_gather, n_first, near_first)
+    down_full = gather_weight(6, down_weight, down_other)
+    cotangent_got = swap_far(chained(pick(out_cotangent, 1 - far), down_other))
+
+    gate_first = act(wide_dot, h2_first, gate_full)
+    m_second, q_second, n_second = act(second_norm, streams[1], keep_second, branch_second)
+    near_second = swap_near(n_second)
+    c_first, c_second = act(place_tokens, out_cotangent, cotangent_got)
+    near_third = swap_near(chained(c_first, near_second))
+    near_fourth = swap_near(chained(c_second, near_third))
+    h2_second = act(core_gather, n_second, near_second)
+    gate_second = act(wide_dot, h2_second, gate_full)
+
+    def rise(hidden, weight, gate):
+        return rows_matmul(
+            [hidden], [weight], dot_nn, [jnp.float32, jnp.bfloat16], pick_tile(weight.shape[1]),
+            finish=lambda up, gate: (up, gate * jax.nn.sigmoid(gate) * up), extras=[gate],
+        )
+
+    up_first, a_first = act(rise, h2_first, up_full, gate_first)
+    y_first = act(core_gather, c_first, near_third)
+    up_second, a_second = act(rise, h2_second, up_full, gate_second)
+    y_second = act(core_gather, c_second, near_fourth)
+    down_sum = plane_scatter(act(grad_sum, a_first, y_first, a_second, y_second))
+
+    def fall_finish(act_grad, gate, up):
+        sigmoid_gate = jax.nn.sigmoid(gate)
+        return (
+            act_grad * up * sigmoid_gate * (1.0 + gate * (1.0 - sigmoid_gate)),
+            act_grad * (gate * sigmoid_gate),
+        )
+
+    def fall(cotangent, weight, gate, up):
+        return rows_matmul(
+            [cotangent], [weight], dot_nt, [jnp.bfloat16] * 2, pick_tile(weight.shape[0]),
+            chunk=512, finish=fall_finish, extras=[gate, up],
+        )
+
+    dg_first, du_first = act(fall, y_first, down_full, gate_first, up_first)
+    dg_second, du_second = act(fall, y_second, down_full, gate_second, up_second)
+    gate_sum = plane_scatter(act(grad_sum, h2_first, dg_first, h2_second, dg_second))
+
+    def hidden_grad(gate_grad, up_grad, gate_weight, up_weight):
+        return rows_matmul(
+            [gate_grad, up_grad], [gate_weight, up_weight], dot_nt, [jnp.bfloat16],
+            pick_tile(gate_weight.shape[0]),
+        )
+
+    def second_back(middle, scale, keep, got, cotangent):
+        grad, gain_term = norm_back(middle, scale, gain_two, keep + got.astype(jnp.float32))
+        grad = cotangent.astype(jnp.float32) + grad
+        return grad, grad.astype(jnp.bfloat16), gain_term
+
+    term_first = act(hidden_grad, dg_first, du_first, gate_full, up_full)
+    keep_first, send_first = act(core_reduce, term_first)
+    back_first = swap_near(send_first)
+    term_second = act(hidden_grad, dg_second, du_second, gate_full, up_full)
+    keep_second, send_second = act(core_reduce, term_second)
+    back_second = swap_near(chained(send_second, back_first))
+    g_first, n_first, gain_two_first = act(
+        second_back, m_first, q_first, keep_first, back_first, c_first
+    )
+    near_first = swap_near(chained(n_first, back_second))
+    up_sum = plane_scatter(act(grad_sum, h2_first, du_first, h2_second, du_second))
+    g_second, n_second, gain_two_second = act(
+        second_back, m_second, q_second, keep_second, back_second, c_second
+    )
+    near_second = swap_near(chained(n_second, near_first))
+    mlp_first = act(dot_bf16, a_first, down_full)
+    mlp_keep_first, mlp_send_first = act(core_reduce, mlp_first)
+    d_first = act(core_gather, n_first, near_first)
+
+    def heads_back(grad, weight):
+        return rows_matmul([grad], [weight], dot_nt, [jnp.bfloat16], pick_tile(weight.shape[0]))
+
+    mlp_second = act(dot_bf16, a_second, down_full)
+    mlp_branch_first = swap_near(chained(mlp_send_first, near_second))
+    heads_first = act(heads_back, d_first, out_full)
+    mlp_keep_second, mlp_send_second = act(core_reduce, mlp_second)
+    d_second = act(core_gather, n_second, near_second)
+    mlp_branch_second = swap_near(chained(mlp_send_second, mlp_branch_first))
+    heads_second = act(heads_back, d_second, out_full)
+    out_sum = plane_scatter(act(grad_sum, mixed_first, d_first, mixed_second, d_second))
+    down_mine, down_away = act(lambda pair: core_split(10, pair), down_sum)
+    down_got = swap_far(down_away)
+
+    def attend_back(heads_first, heads_second):
+        return tuple(
+            attention_call(
+                backward_both,
+                slot,
+                [
+                    *saved[0], *saved[1], heads_first, heads_second, *lses,
+                    *tables[0], *tables[1], reach,
+                ],
+                [0] * 8 + ["lse"] * 2 + ["table"] * 4 + ["column"],
+                ([0] * 6, heads_local),
+                backward_scratch,
+            )
+        )
+
+    grads = act(attend_back, heads_first, heads_second)
+    p_first, p_second = act(
+        lambda *parts: (
+            jnp.concatenate(parts[:3], axis=1),
+            jnp.concatenate(parts[3:], axis=1),
+        ),
+        *grads,
+    )
+
+    def finish_output(first, first_keep, first_got, second, second_keep, second_got):
+        first = (first + first_keep + first_got.astype(jnp.float32)).astype(jnp.bfloat16)
+        second = (second + second_keep + second_got.astype(jnp.float32)).astype(jnp.bfloat16)
+        return jnp.where(far == 0, first, second), jnp.where(far == 0, second, first)
+
+    out_keep, out_send = act(
+        finish_output,
+        m_first, mlp_keep_first, mlp_branch_first, m_second, mlp_keep_second, mlp_branch_second,
+    )
+    out_got = swap_far(chained(out_send, down_got))
+    qkv_sum = plane_scatter(act(grad_sum, h1_first, p_first, h1_second, p_second))
+    down_owned = act(add_wide, down_mine, down_got)
+    term_first = act(heads_back, p_first, qkv_full)
+    keep_first, send_first = act(core_reduce, term_first)
+    back_first = swap_near(send_first)
+    gate_mine, gate_away = act(lambda pair: core_split(9, pair), gate_sum)
+    term_second = act(heads_back, p_second, qkv_full)
+    keep_second, send_second = act(core_reduce, term_second)
+    back_second = swap_near(chained(send_second, back_first))
+
+    def settle(keep, got):
         return jnp.stack([jnp.where(far == 0, keep, got), jnp.where(far == 0, got, keep)])
 
-    def gather_tokens(value):
-        both = jnp.concatenate([value, swap_near(value)], axis=0)
-        return jnp.concatenate([both, swap_core(both)], axis=0)
-
-    def scatter_tokens(term):
-        half = term.shape[0] // 2
-        quarter = half // 2
-        summed = term[:half].astype(jnp.float32) + swap_core(term[half:]).astype(jnp.float32)
-        return summed[:quarter] + swap_near(summed[quarter:].astype(jnp.bfloat16)).astype(
-            jnp.float32
-        )
-
-    def gather_weight(weight):
-        other = swap_far(weight)
-        mine = jnp.where(core == far, weight, other)
-        sibling = swap_core(jnp.where(core == far, other, weight))
-        pair = jnp.concatenate(
-            [jnp.where(core == 0, mine, sibling), jnp.where(core == 0, sibling, mine)], axis=0
-        )
-        return lax.all_gather(pair, "fsdp", axis=0, tiled=True, axis_index_groups=plane_groups)
-
-    def scatter_weight(grad):
-        pair = lax.psum_scatter(
-            grad, "fsdp", scatter_dimension=0, tiled=True, axis_index_groups=plane_groups
-        )
-        count = pair.shape[0] // 2
-        even, odd = pair[:count], pair[count:]
-        mine = jnp.where(core == 0, even, odd)
-        got = swap_core(jnp.where(core == 0, odd, even))
-        keep = jnp.where(core == far, mine, got)
-        sent = swap_far(jnp.where(core == far, got, mine))
-        return keep.astype(jnp.float32) + sent.astype(jnp.float32)
-
-    qkv_full = gather_weight(qkv_weight.reshape(qkv_weight.shape[0], 3 * local_cols))
-    out_full = gather_weight(out_weight)
-    gate_up_full = gather_weight(gate_up_weight)
-    down_full = gather_weight(down_weight)
-
-    streams = spread_tokens(block_in)
-    positions = [gather_tokens(part) for part in spread_tokens(doc_positions)]
-    tables = [wide_tables(part) for part in positions]
-    reach = positions[1].astype(jnp.int32)[:, None]
-
-    normed_one_full, saved, attn_outs, lses = [], [], [], []
-    scales_one = []
-    streams = [part.astype(jnp.float32) for part in streams]
-    for part in range(2):
-        stream = streams[part]
-        scale_one = rms_scale(stream)
-        scales_one.append(scale_one)
-        normed = (stream * scale_one * gain_one).astype(jnp.bfloat16)
-        normed_one_full.append(gather_tokens(normed))
-    count = normed_one_full[0].shape[0]
-    pair_flops = 2 * heads_local * count * count * HD // 2
-    for part in range(2):
-        projected = jnp.dot(
-            normed_one_full[part], qkv_full, preferred_element_type=jnp.float32
-        )
-        cosine, sine = tables[part]
-        arrays = [projected, projected, projected, cosine, sine]
-        kinds = [0, 1, 2, "table", "table"]
-        if part == 0:
-            kernel = forward_first
-        else:
-            kernel = forward_second
-            arrays += [saved[0][1], saved[0][2], reach]
-            kinds += [0, 0, "column"]
-        results = attention_call(
-            kernel, slot, arrays, kinds, ([0, 0, 0, 0, "lse"], heads_local), no_scratch, pair_flops
-        )
-        saved.append(results[:3])
-        attn_outs.append(results[3])
-        lses.append(results[4])
-
-    cotangents = [part for part in spread_tokens(out_cotangent)]
-    cotangent_full = [gather_tokens(part) for part in cotangents]
-    middles, scales_two, normed_two_full = [], [], []
-    for part in range(2):
-        term = jnp.dot(attn_outs[part], out_full, preferred_element_type=jnp.float32)
-        middle = streams[part] + scatter_tokens(term.astype(jnp.bfloat16))
-        scale_two = rms_scale(middle)
-        normed = (middle * scale_two * gain_two).astype(jnp.bfloat16)
-        middles.append(middle)
-        scales_two.append(scale_two)
-        normed_two_full.append(gather_tokens(normed))
-
-    outputs, middle_grads, attn_grad_full = [], [], []
-    grad_down = grad_gate_up = grad_out = None
-    gain_two_acc = 0.0
-    for part in range(2):
-        gate_up = jnp.einsum(
-            "sd,dtf->stf", normed_two_full[part], gate_up_full, preferred_element_type=jnp.float32
-        )
-        gate_rows, up_rows = gate_up[:, 0], gate_up[:, 1]
-        sigmoid_gate = jax.nn.sigmoid(gate_rows)
-        silu_gate = gate_rows * sigmoid_gate
-        activated = (silu_gate * up_rows).astype(jnp.bfloat16)
-        term = jnp.einsum(
-            "sf,sd->fd", activated, cotangent_full[part], preferred_element_type=jnp.float32
-        )
-        grad_down = term if part == 0 else grad_down + term
-        act_grad = jnp.einsum(
-            "sd,fd->sf", cotangent_full[part], down_full, preferred_element_type=jnp.float32
-        )
-        gate_grad = act_grad * up_rows * sigmoid_gate * (1.0 + gate_rows * (1.0 - sigmoid_gate))
-        up_grad = act_grad * silu_gate
-        gate_up_grad = jnp.stack([gate_grad, up_grad], axis=1).astype(jnp.bfloat16)
-        term = jnp.einsum(
-            "sd,stf->dtf", normed_two_full[part], gate_up_grad, preferred_element_type=jnp.float32
-        )
-        grad_gate_up = term if part == 0 else grad_gate_up + term
-        term = jnp.einsum(
-            "stf,dtf->sd", gate_up_grad, gate_up_full, preferred_element_type=jnp.float32
-        )
-        normed_two_grad = scatter_tokens(term.astype(jnp.bfloat16))
-        mlp_term = jnp.dot(activated, down_full, preferred_element_type=jnp.float32)
-        mlp_branch = scatter_tokens(mlp_term.astype(jnp.bfloat16))
-        outputs.append((middles[part] + mlp_branch).astype(jnp.bfloat16))
-        middle_back, gain_two_term = norm_back(
-            middles[part], scales_two[part], gain_two, normed_two_grad
-        )
-        gain_two_acc = gain_two_acc + gain_two_term
-        middle_grad = cotangents[part].astype(jnp.float32) + middle_back
-        middle_grads.append(middle_grad)
-        attn_grad_full.append(gather_tokens(middle_grad.astype(jnp.bfloat16)))
-    down_owned = scatter_weight(grad_down.astype(jnp.bfloat16))
-    gate_up_owned = scatter_weight(grad_gate_up.astype(jnp.bfloat16))
-
-    head_grads = []
-    for part in range(2):
-        term = jnp.einsum(
-            "sc,sd->cd", attn_outs[part], attn_grad_full[part], preferred_element_type=jnp.float32
-        )
-        grad_out = term if part == 0 else grad_out + term
-        head_grads.append(
-            jnp.einsum(
-                "sd,cd->sc", attn_grad_full[part], out_full, preferred_element_type=jnp.float32
-            ).astype(jnp.bfloat16)
-        )
-    out_owned = scatter_weight(grad_out.astype(jnp.bfloat16))
-    grads = attention_call(
-        backward_both,
-        slot,
-        [*saved[0], *saved[1], *head_grads, *lses, *tables[0], *tables[1], reach],
-        [0] * 8 + ["lse"] * 2 + ["table"] * 4 + ["column"],
-        ([0] * 6, heads_local),
-        backward_scratch,
-        pair_flops * 5,
-    )
-    input_grads = []
-    grad_qkv = None
-    gain_one_acc = 0.0
-    for part in range(2):
-        projected_grad = jnp.concatenate(grads[3 * part : 3 * part + 3], axis=1)
-        term = jnp.einsum(
-            "sd,sc->dc", normed_one_full[part], projected_grad, preferred_element_type=jnp.float32
-        )
-        grad_qkv = term if part == 0 else grad_qkv + term
-        term = jnp.einsum(
-            "sc,dc->sd", projected_grad, qkv_full, preferred_element_type=jnp.float32
-        )
-        normed_one_grad = scatter_tokens(term.astype(jnp.bfloat16))
-        stream_back, gain_one_term = norm_back(
-            streams[part], scales_one[part], gain_one, normed_one_grad
-        )
-        gain_one_acc = gain_one_acc + gain_one_term
-        input_grads.append(middle_grads[part] + stream_back)
-    qkv_owned = scatter_weight(grad_qkv.astype(jnp.bfloat16))
-    gains = lax.psum_scatter(
-        jnp.stack([gain_one_acc, gain_two_acc], axis=1),
-        ("fsdp", "tp"),
-        scatter_dimension=0,
-        tiled=True,
-    )
+    def first_back(stream, scale, keep, got, grad):
+        back, gain_term = norm_back(stream, scale, gain_one, keep + got.astype(jnp.float32))
+        return grad + back, gain_term
+
+    i_first, gain_one_first = act(
+        first_back, streams[0], scales_one[0], keep_first, back_first, g_first
+    )
+
+    def last_back(stream, scale, keep, got, grad, first):
+        second, gain_term = first_back(stream, scale, keep, got, grad)
+        return (
+            jnp.where(far == 0, first, second),
+            jnp.where(far == 0, second, first).astype(jnp.bfloat16),
+            gain_term,
+        )
+
+    in_keep, in_send, gain_one_second = act(
+        last_back, streams[1], scales_one[1], keep_second, back_second, g_second, i_first
+    )
+    block_out = act(settle, out_keep, out_got)
+    gate_got = swap_far(chained(gate_away, out_got))
+    in_got = swap_far(chained(in_send, gate_got))
+    gains = scatter_gains(
+        jnp.stack([gain_one_first + gain_one_second, gain_two_first + gain_two_second])
+    )
+    gate_owned = act(add_wide, gate_mine, gate_got)
+    up_mine, up_away = act(lambda pair: core_split(9, pair), up_sum)
+    up_got = swap_far(chained(up_away, in_got))
+    in_grad = act(lambda keep, got: settle(keep, got.astype(jnp.float32)), in_keep, in_got)
+    out_mine, out_away = act(lambda pair: core_split(7, pair), out_sum)
+    out_back = swap_far(chained(out_away, up_got))
+    up_owned = act(add_wide, up_mine, up_got)
+    gate_up_owned = act(lambda a, b: jnp.stack([a, b], axis=1), gate_owned, up_owned)
+    out_owned = act(add_wide, out_mine, out_back)
+    qkv_mine, qkv_away = act(lambda pair: core_split(8, pair), qkv_sum)
+    qkv_owned = act(add_wide, qkv_mine, swap_far(qkv_away))
     return (
-        return_tokens(outputs[0], outputs[1], jnp.bfloat16, jnp.bfloat16),
-        return_tokens(input_grads[0], input_grads[1], jnp.bfloat16, jnp.float32),
-        gains[:, 0],
+        block_out,
+        in_grad,
+        gains[0],
         qkv_owned.reshape(qkv_weight.shape),
         out_owned,
-        gains[:, 1],
+        gains[1],
         gate_up_owned,
         down_owned,
     )

time: 2440 us -> 1980 us (0.81)
  Pallas kernels: 119 us -> 808 us
  waiting for transfers between devices: 1510 us -> 835 us
  matrix products: 509 us -> 0 us
  other arithmetic: 144 us -> 88.8 us
  starting transfers between devices: 33.6 us -> 85.3 us
  local copies, waits for them, and re-layouts: 101 us -> 135 us
    pallas_call x0 -> x49, Pallas kernels: none -> 679 us  [the longest x18 347 us: rows_matmul(): pl.pallas_call(functools.partial(rows_kernel, len(lefts), len(extras), do...]
    dot_general x24 -> x0, matrix products: 509 us -> none  [the longest x2 73.2 us: paired_device(): jnp.einsum('sd,stf->dtf', normed_two_full[part], gate_up_grad, preferred_...]
    ppermute x13 -> x15, waiting for transfers between devices: 751 us -> 474 us  [swap_far(): return lax.ppermute(value, 'tp', far_pairs)]
    reduce_scatter x4 -> x5, waiting for transfers between devices: 228 us -> 0.01 us  [plane_scatter(): lax.psum_scatter(grad, 'fsdp', scatter_dimension=0, tiled=True, axis_inde...]
    ppermute x18 -> x17, waiting for transfers between devices: 511 us -> 286 us  [swap_near(): return lax.ppermute(value, 'tp', near_pairs)]
    ppermute x0 -> x5, waiting for transfers between devices: none -> 74.2 us  [scatter_gains(): lax.ppermute(sent, axis, [(i, i ^ step) for i in range(size)])]
    unnamed x247 -> x251, local copies, waits for them, and re-layouts: 55.9 us -> 114 us
    ppermute x13 -> x15, starting transfers between devices: 17.6 us -> 56.1 us  [swap_far(): return lax.ppermute(value, 'tp', far_pairs)]
  transfers between devices with their start and end apart: 66 -> 48, of which waited for: 36 -> 25; matrix products, arithmetic and copies ran while one was open for 27% -> 6% of each run, Pallas kernels for 2% -> 41%
where the time goes in v2:
time: 1980 us; the launch traced here: 1970 us
  waiting for transfers between devices  835 us (42%)
  Pallas kernels  808 us (41%)
  local copies, waits for them, and re-layouts  135 us (7%)
  other arithmetic  88.8 us (4%)
  starting transfers between devices  85.3 us (4%)
    ppermute x15, waiting for transfers between devices, swap_far(): return lax.ppermute(value, 'tp', far_pairs)  474 us
    pallas_call x18, Pallas kernels, rows_matmul(): pl.pallas_call(functools.partial(rows_kernel, len(lefts), len(extras), do...  347 us
    ppermute x17, waiting for transfers between devices, swap_near(): return lax.ppermute(value, 'tp', near_pairs)  286 us
    pallas_call x26, Pallas kernels, exchange_call(): pl.pallas_call(kernel, out_shape=outs, in_specs=[anywhere] * len(operands...  174 us
    pallas_call x5, Pallas kernels, sum_matmul(): pl.pallas_call(functools.partial(sum_kernel, len(lefts), chunk), out_shap...  158 us
    pallas_call x3, Pallas kernels, attention_call(): pl.pallas_call(kernel, out_shape=[shape(kind) for kind in outs[0]], grid_...  129 us
    unnamed x251, local copies, waits for them, and re-layouts  114 us
    ppermute x5, waiting for transfers between devices, scatter_gains(): lax.ppermute(sent, axis, [(i, i ^ step) for i in range(size)])  74.2 us
  transfers between devices with their start and end apart: 48, of which 25 were waited for; matrix products, arithmetic and copies ran while one was open for 6% of the time, Pallas kernels for 41%

profile of v2, /device:TPU:0, one launch (start us, length us, event | category | flops | bytes accessed | tf_op | source)
XLA Modules:
  0.0 1968.5 jit_solution(1008352340312216814)
XLA Ops:
  61.0 66.5 %collective-permute-done.1.other_ref = bf16[384,2304]{1,0:T(8,128)(2,1)S(1)} collective-permute-done((bf16[384,2304]{1,0:T(8,128)(2,1)}, bf16[384,2304]{1,0:T(8,128)(2,1)S(1)}, u32[]{:S(2)}, u32[]{:S(2)}) %collective-permute-start.1) | collective-permute-done | bytes 1769504 | tf_op jit(solution)/shard_map/ppermute | solution.py:945
  142.7 64.0 %collective-permute-done.2 = bf16[256,3072]{1,0:T(8,128)(2,1)S(1)} collective-permute-done((bf16[256,3072]{1,0:T(8,128)(2,1)S(1)}, bf16[256,3072]{1,0:T(8,128)(2,1)S(1)}, u32[]{:S(2)}, u32[]{:S(2)}) %collective-permute-start.2) | collective-permute-done | bytes 1572896 | tf_op jit(solution)/shard_map/ppermute | solution.py:945
  211.4 65.0 %collective-permute-done.7.other_ref = bf16[384,2048]{1,0:T(8,128)(2,1)S(1)} collective-permute-done((bf16[384,2048]{1,0:T(8,128)(2,1)S(1)}, bf16[384,2048]{1,0:T(8,128)(2,1)S(1)}, u32[]{:S(2)}, u32[]{:S(2)}) %collective-permute-start.7) | collective-permute-done | bytes 1572896 | tf_op jit(solution)/shard_map/ppermute | solution.py:945
  284.4 32.5 %collective-permute-done.6.near_ref = bf16[256,3072]{1,0:T(8,128)(2,1)} collective-permute-done((bf16[256,3072]{1,0:T(8,128)(2,1)S(1)}, bf16[256,3072]{1,0:T(8,128)(2,1)}, u32[]{:S(2)}, u32[]{:S(2)}) %collective-permute-start.6) | collective-permute-done | bytes 1572896 | tf_op jit(solution)/shard_map/ppermute | solution.py:942
  435.3 48.9 %shard_map.162 = bf16[768,2048]{1,0:T(8,128)(2,1)} custom-call(bf16[384,2048]{1,0:T(8,128)(2,1)} %bitcast.73.own_ref, bf16[384,2048]{1,0:T(8,128)(2,1)} %collective-permute-done.10.other_ref), custom_call_target="tpu_custom_call" | custom-call | flops 6800000000 | bytes 1000 | tf_op jit(solution)/shard_map/pallas_call | solution.py:673
  492.6 34.6 %shard_map.163 = (bf16[1024,768]{1,0:T(8,128)(2,1)S(1)}, bf16[1024,768]{1,0:T(8,128)(2,1)S(1)}, bf16[1024,768]{1,0:T(8,128)(2,1)S(1)}, bf16[1024,768]{1,0:T(8,128)(2,1)S(1)}, f32[2,1024,4]{2,1,0:T(8,128)S(1)}) custom-call(s32[1]{0:T(128)} %bitcast.6.slot_ref, f32[1024,2304]{1,0:T(8,128)} %shard_map.161.q_ref.k_ref.v_ref, ...), custom_call_target="tpu_custom_call" | custom-call | flops 8556380160 | bytes 1000 | tf_op jit(solution)/shard_map/pallas_call | solution.py:875
  552.7 48.6 %collective-permute-done.11.near_ref = bf16[256,3072]{1,0:T(8,128)(2,1)} collective-permute-done((bf16[256,3072]{1,0:T(8,128)(2,1)S(1)}, bf16[256,3072]{1,0:T(8,128)(2,1)}, u32[]{:S(2)}, u32[]{:S(2)}) %collective-permute-start.11) | collective-permute-done | bytes 1572896 | tf_op jit(solution)/shard_map/ppermute | solution.py:942
  616.1 45.3 %collective-permute-start.15 = (bf16[256,3072]{1,0:T(8,128)(2,1)}, bf16[256,3072]{1,0:T(8,128)(2,1)}, u32[]{:S(2)}, u32[]{:S(2)}) collective-permute-start(bf16[256,3072]{1,0:T(8,128)(2,1)} %dynamic-slice_bitcast_fusion), channel_id=1, source_target_pairs={{0,2},{1,3},{2,0},{3,1},{4,6},{5,7},{6,4},{7,5},{8,10},{9,11},{10,... | collective-permute-start | bytes 4718600 | tf_op jit(solution)/shard_map/ppermute | solution.py:945
  685.1 45.7 %collective-permute-done.13 = bf16[256,3072]{1,0:T(8,128)(2,1)} collective-permute-done((bf16[256,3072]{1,0:T(8,128)(2,1)}, bf16[256,3072]{1,0:T(8,128)(2,1)}, u32[]{:S(2)}, u32[]{:S(2)}) %collective-permute-start.13) | collective-permute-done | bytes 1572896 | tf_op jit(solution)/shard_map/ppermute | solution.py:942
  737.8 31.8 %collective-permute-done.14.near_ref = bf16[256,3072]{1,0:T(8,128)(2,1)S(1)} collective-permute-done((bf16[256,3072]{1,0:T(8,128)(2,1)S(1)}, bf16[256,3072]{1,0:T(8,128)(2,1)S(1)}, u32[]{:S(2)}, u32[]{:S(2)}) %collective-permute-start.14) | collective-permute-done | bytes 1572896 | tf_op jit(solution)/shard_map/ppermute | solution.py:942
  868.3 35.9 %shard_map.175 = bf16[2048,3072]{1,0:T(8,128)(2,1)} custom-call(bf16[1024,2048]{1,0:T(8,128)(2,1)S(1)} %copy-done.81, bf16[1024,2048]{1,0:T(8,128)(2,1)} %copy-done.78, bf16[1024,3072]{1,0:T(8,128)(2,1)} %copy-done.59, bf16[1024,3072]{1,0:T(8,128)(2,1)} %copy-done.61), custom_call_target="tpu_custom_call" | custom-call | flops 43808665600 | bytes 1000 | tf_op jit(solution)/shard_map/pallas_call | solution.py:637
  956.4 33.1 %shard_map.178 = bf16[3072,2048]{1,0:T(8,128)(2,1)} custom-call(bf16[1024,3072]{1,0:T(8,128)(2,1)} %copy-done.57, bf16[1024,3072]{1,0:T(8,128)(2,1)} %copy-done.58, bf16[1024,2048]{1,0:T(8,128)(2,1)S(1)} %get-tuple-element.348.refs_2_.refs_0_, bf16[1024,2048]{1,0:T(8,128)(2,1)} %copy-done.74), custom_call_target="tpu_custom_call" | custom-call | flops 43808665600 | bytes 1000 | tf_op jit(solution)/shard_map/pallas_call | solution.py:637
  991.8 32.6 %shard_map.179.term_ref = bf16[1024,3072]{1,0:T(8,128)(2,1)} custom-call(bf16[1024,2048]{1,0:T(8,128)(2,1)S(1)} %copy-done.77, bf16[1024,2048]{1,0:T(8,128)(2,1)} %get-tuple-element.368.refs_1_.refs_2_, bf16[3072,2048]{1,0:T(8,128)(2,1)} %all-gather.12.cloned.1.call-done.refs_1_.refs_2_, bf16[3072,2048]{1,0:T(8,128)(2,1)} %all-gather.10.cloned.1.call-done.refs_1_.refs_3_), custom_call_target="tpu_custom_call" | custom-call | flops 43808665600 | bytes 1000 | tf_op jit(solution)/shard_map/pallas_call | solution.py:607
  1035.6 31.8 %shard_map.181.term_ref = bf16[1024,3072]{1,0:T(8,128)(2,1)} custom-call(bf16[1024,2048]{1,0:T(8,128)(2,1)S(1)} %copy-done.75, bf16[1024,2048]{1,0:T(8,128)(2,1)} %get-tuple-element.369.refs_1_.refs_3_, bf16[3072,2048]{1,0:T(8,128)(2,1)} %all-gather.12.cloned.1.call-done.refs_1_.refs_2_, bf16[3072,2048]{1,0:T(8,128)(2,1)} %all-gather.10.cloned.1.call-done.refs_1_.refs_3_), custom_call_target="tpu_custom_call" | custom-call | flops 43808665600 | bytes 1000 | tf_op jit(solution)/shard_map/pallas_call | solution.py:607
  1085.6 33.8 %shard_map.183 = bf16[3072,2048]{1,0:T(8,128)(2,1)} custom-call(bf16[1024,3072]{1,0:T(8,128)(2,1)} %copy-done.57, bf16[1024,3072]{1,0:T(8,128)(2,1)} %copy-done.58, bf16[1024,2048]{1,0:T(8,128)(2,1)S(1)} %copy-done.73, bf16[1024,2048]{1,0:T(8,128)(2,1)} %get-tuple-element.369.refs_1_.refs_3_), custom_call_target="tpu_custom_call" | custom-call | flops 43808665600 | bytes 1000 | tf_op jit(solution)/shard_map/pallas_call | solution.py:637
  1121.7 34.9 %collective-permute-done.19 = bf16[256,3072]{1,0:T(8,128)(2,1)S(1)} collective-permute-done((bf16[256,3072]{1,0:T(8,128)(2,1)}, bf16[256,3072]{1,0:T(8,128)(2,1)S(1)}, u32[]{:S(2)}, u32[]{:S(2)}) %collective-permute-start.19) | collective-permute-done | bytes 1572896 | tf_op jit(solution)/shard_map/ppermute | solution.py:942
  1304.9 66.2 %shard_map.194 = (bf16[1024,768]{1,0:T(8,128)(2,1)S(1)}, bf16[1024,768]{1,0:T(8,128)(2,1)S(1)}, bf16[1024,768]{1,0:T(8,128)(2,1)S(1)}, bf16[1024,768]{1,0:T(8,12...) custom-call(s32[1]{0:T(128)} %bitcast.6.slot_ref, bf16[1024,768]{1,0:T(8,128)(2,1)} %copy-done.50, ...), custom_call_target="tpu_custom_call" | custom-call | flops 12321187840 | bytes 1000 | tf_op jit(solution)/shard_map/pallas_call | solution.py:875
  1386.0 37.5 %shard_map.195 = bf16[3072,2304]{1,0:T(8,128)(2,1)} custom-call(bf16[1024,3072]{1,0:T(8,128)(2,1)} %copy-done.55, bf16[1024,3072]{1,0:T(8,128)(2,1)} %copy-done.56, bf16[1024,2304]{1,0:T(8,128)(2,1)S(1)} %constant_dynamic-update-slice_fusion.refs_2_.refs_0_, bf16[1024,2304]{1,0:T(8,128)(2,1)} %copy-done.25), custom_call_target="tpu_custom_call" | custom-call | flops 49284751360 | bytes 1000 | tf_op jit(solution)/shard_map/pallas_call | solution.py:637
  1425.0 71.1 %collective-permute-done.24 = bf16[256,3072]{1,0:T(8,128)(2,1)} collective-permute-done((bf16[256,3072]{1,0:T(8,128)(2,1)S(1)}, bf16[256,3072]{1,0:T(8,128)(2,1)}, u32[]{:S(2)}, u32[]{:S(2)}) %collective-permute-start.24) | collective-permute-done | bytes 1572896 | tf_op jit(solution)/shard_map/ppermute | solution.py:945
  1534.0 34.9 %collective-permute-done.25 = bf16[256,3072]{1,0:T(8,128)(2,1)} collective-permute-done((bf16[256,3072]{1,0:T(8,128)(2,1)}, bf16[256,3072]{1,0:T(8,128)(2,1)}, u32[]{:S(2)}, u32[]{:S(2)}) %collective-permute-start.25) | collective-permute-done | bytes 1572896 | tf_op jit(solution)/shard_map/ppermute | solution.py:945
  1608.0 62.3 %collective-permute-done.27 = bf16[256,3072]{1,0:T(8,128)(2,1)S(1)} collective-permute-done((bf16[256,3072]{1,0:T(8,128)(2,1)S(1)}, bf16[256,3072]{1,0:T(8,128)(2,1)S(1)}, u32[]{:S(2)}, u32[]{:S(2)}) %collective-permute-start.27) | collective-permute-done | bytes 1572896 | tf_op jit(solution)/shard_map/ppermute | solution.py:942
  1694.0 58.8 %collective-permute-done.29 = bf16[256,3072]{1,0:T(8,128)(2,1)} collective-permute-done((bf16[256,3072]{1,0:T(8,128)(2,1)}, bf16[256,3072]{1,0:T(8,128)(2,1)}, u32[]{:S(2)}, u32[]{:S(2)}) %collective-permute-start.29) | collective-permute-done | bytes 1572896 | tf_op jit(solution)/shard_map/ppermute | solution.py:945
  1761.4 61.2 %collective-permute-done.35 = bf16[384,2048]{1,0:T(8,128)(2,1)} collective-permute-done((bf16[384,2048]{1,0:T(8,128)(2,1)S(1)}, bf16[384,2048]{1,0:T(8,128)(2,1)}, u32[]{:S(2)}, u32[]{:S(2)}) %collective-permute-start.35) | collective-permute-done | bytes 1572896 | tf_op jit(solution)/shard_map/ppermute | solution.py:945
  1869.7 67.1 %collective-permute-done.33 = f32[2,192]{1,0:T(2,128)S(1)} collective-permute-done((f32[2,192]{1,0:T(2,128)S(1)}, f32[2,192]{1,0:T(2,128)S(1)}, u32[]{:S(2)}, u32[]{:S(2)}) %collective-permute-start.33) | collective-permute-done | bytes 1568 | tf_op jit(solution)/shard_map/ppermute | solution.py:994
  (471 shorter events, 808.2 us)
Async XLA Ops:
  7.2 321.3 %all-gather.8.cloned.1.call-start = ((), (), s32[]{:S(2)}) async-start(), calls=%async_computation.6 | async-start | bytes 5898240 | tf_op jit(solution)/shard_map/all_gather | solution.py:969
  40.8 287.7 %all-gather.6.cloned.1.call-start = ((), (), s32[]{:S(2)}) async-start(), calls=%async_computation.5 | async-start | bytes 17694720 | tf_op jit(solution)/shard_map/all_gather | solution.py:969
  49.0 78.5 %collective-permute-start.1 = (bf16[384,2304]{1,0:T(8,128)(2,1)}, bf16[384,2304]{1,0:T(8,128)(2,1)S(1)}, u32[]{:S(2)}, u32[]{:S(2)}) collective-permute-start(bf16[384,2304]{1,0:T(8,128)(2,1)} %copy.33), channel_id=1, source_target_pairs={{0,2},{1,3},{2,0},{3,1},{4,6},{5,7},{6,4},{7,5},{8,10},{9,11},{10,... | collective-permute-start | bytes 5308424 | tf_op jit(solution)/shard_map/ppermute | solution.py:945
  134.1 529.9 %all-gather.12.cloned.1.call-start = ((), (), s32[]{:S(2)}) async-start(), calls=%async_computation.8 | async-start | bytes 15728640 | tf_op jit(solution)/shard_map/all_gather | solution.py:969
  135.8 70.8 %collective-permute-start.2 = (bf16[256,3072]{1,0:T(8,128)(2,1)S(1)}, bf16[256,3072]{1,0:T(8,128)(2,1)S(1)}, u32[]{:S(2)}, u32[]{:S(2)}) collective-permute-start(bf16[256,3072]{1,0:T(8,128)(2,1)S(1)} %dynamic-slice_bitcast_fusion.1), channel_id=1, source_target_pairs={{0,2},{1,3},{2,0},{3,1},{4,6},{5,7},{6,4},{7,5},{8,10},{9,11},{10,... | collective-permute-start | bytes 4718600 | tf_op jit(solution)/shard_map/ppermute | solution.py:945
  280.0 527.8 %all-gather.10.cloned.1.call-start = ((), (), s32[]{:S(2)}) async-start(), calls=%async_computation.7 | async-start | bytes 15728640 | tf_op jit(solution)/shard_map/all_gather | solution.py:969
  317.2 118.1 %collective-permute-start.10 = (bf16[384,2048]{1,0:T(8,128)(2,1)}, bf16[384,2048]{1,0:T(8,128)(2,1)}, u32[]{:S(2)}, u32[]{:S(2)}) collective-permute-start(bf16[384,2048]{1,0:T(8,128)(2,1)} %bitcast.73.own_ref), channel_id=1, source_target_pairs={{0,2},{1,3},{2,0},{3,1},{4,6},{5,7},{6,4},{7,5},{8,10},{9,11},{10,... | collective-permute-start | bytes 4718600 | tf_op jit(solution)/shard_map/ppermute | solution.py:945
  484.3 420.0 %all-gather.14.cloned.1.call-start = ((), (), s32[]{:S(2)}) async-start(), calls=%async_computation.9 | async-start | bytes 15728640 | tf_op jit(solution)/shard_map/all_gather | solution.py:969
  533.5 76.4 %collective-permute-start.12 = (bf16[256,3072]{1,0:T(8,128)(2,1)S(1)}, bf16[256,3072]{1,0:T(8,128)(2,1)}, u32[]{:S(2)}, u32[]{:S(2)}) collective-permute-start(bf16[256,3072]{1,0:T(8,128)(2,1)S(1)} %copy-done.33), channel_id=1, source_target_pairs={{0,2},{1,3},{2,0},{3,1},{4,6},{5,7},{6,4},{7,5},{8,10},{9,11},{10,... | collective-permute-start | bytes 4718600 | tf_op jit(solution)/shard_map/ppermute | solution.py:945
  613.4 683.6 %reduce-scatter.6.cloned.1.call-start = ((), (), s32[]{:S(2)}) async-start(), calls=%async_computation.10 | async-start | bytes 15728640 | tf_op jit(solution)/shard_map/reduce_scatter | solution.py:972
  616.1 119.0 %collective-permute-start.15 = (bf16[256,3072]{1,0:T(8,128)(2,1)}, bf16[256,3072]{1,0:T(8,128)(2,1)}, u32[]{:S(2)}, u32[]{:S(2)}) collective-permute-start(bf16[256,3072]{1,0:T(8,128)(2,1)} %dynamic-slice_bitcast_fusion), channel_id=1, source_target_pairs={{0,2},{1,3},{2,0},{3,1},{4,6},{5,7},{6,4},{7,5},{8,10},{9,11},{10,... | collective-permute-start | bytes 4718600 | tf_op jit(solution)/shard_map/ppermute | solution.py:945
  904.2 624.4 %reduce-scatter.8.cloned.1.call-start = ((), (), s32[]{:S(2)}) async-start(), calls=%async_computation.11 | async-start | bytes 15728640 | tf_op jit(solution)/shard_map/reduce_scatter | solution.py:972
  989.6 697.1 %reduce-scatter.10.cloned.1.call-start = ((), (), s32[]{:S(2)}) async-start(), calls=%async_computation.12 | async-start | bytes 15728640 | tf_op jit(solution)/shard_map/reduce_scatter | solution.py:972
  1119.4 638.7 %reduce-scatter.14.cloned.1.call-start = ((), (), s32[]{:S(2)}) async-start(), calls=%async_computation.14 | async-start | bytes 5898240 | tf_op jit(solution)/shard_map/reduce_scatter | solution.py:972
  1277.6 574.7 %reduce-scatter.12.cloned.1.call-start = ((), (), s32[]{:S(2)}) async-start(), calls=%async_computation.13 | async-start | bytes 17694720 | tf_op jit(solution)/shard_map/reduce_scatter | solution.py:972
  1296.1 77.8 %collective-permute-start.23 = (bf16[256,3072]{1,0:T(8,128)(2,1)}, bf16[256,3072]{1,0:T(8,128)(2,1)}, u32[]{:S(2)}, u32[]{:S(2)}) collective-permute-start(bf16[256,3072]{1,0:T(8,128)(2,1)} %copy-done.41), channel_id=1, source_target_pairs={{0,1},{1,0},{2,3},{3,2},{4,5},{5,4},{6,7},{7,6},{8,9},{9,8},{10,11... | collective-permute-start | bytes 4718600 | tf_op jit(solution)/shard_map/ppermute | solution.py:942
  1424.9 71.1 %collective-permute-start.24 = (bf16[256,3072]{1,0:T(8,128)(2,1)S(1)}, bf16[256,3072]{1,0:T(8,128)(2,1)}, u32[]{:S(2)}, u32[]{:S(2)}) collective-permute-start(bf16[256,3072]{1,0:T(8,128)(2,1)S(1)} %copy-done.40), channel_id=1, source_target_pairs={{0,2},{1,3},{2,0},{3,1},{4,6},{5,7},{6,4},{7,5},{8,10},{9,11},{10,... | collective-permute-start | bytes 4718600 | tf_op jit(solution)/shard_map/ppermute | solution.py:945
  1527.0 71.6 %collective-permute-start.26 = (bf16[256,3072]{1,0:T(8,128)(2,1)}, bf16[256,3072]{1,0:T(8,128)(2,1)}, u32[]{:S(2)}, u32[]{:S(2)}) collective-permute-start(bf16[256,3072]{1,0:T(8,128)(2,1)} %get-tuple-element.427), channel_id=1, source_target_pairs={{0,1},{1,0},{2,3},{3,2},{4,5},{5,4},{6,7},{7,6},{8,9},{9,8},{10,11... | collective-permute-start | bytes 4718600 | tf_op jit(solution)/shard_map/ppermute | solution.py:942
  1569.0 114.0 %collective-permute-start.28 = (bf16[384,2048]{1,0:T(8,128)(2,1)}, bf16[384,2048]{1,0:T(8,128)(2,1)}, u32[]{:S(2)}, u32[]{:S(2)}) collective-permute-start(bf16[384,2048]{1,0:T(8,128)(2,1)} %get-tuple-element.449), channel_id=1, source_target_pairs={{0,2},{1,3},{2,0},{3,1},{4,6},{5,7},{6,4},{7,5},{8,10},{9,11},{10,... | collective-permute-start | bytes 4718600 | tf_op jit(solution)/shard_map/ppermute | solution.py:945
  1598.7 71.6 %collective-permute-start.27 = (bf16[256,3072]{1,0:T(8,128)(2,1)S(1)}, bf16[256,3072]{1,0:T(8,128)(2,1)S(1)}, u32[]{:S(2)}, u32[]{:S(2)}) collective-permute-start(bf16[256,3072]{1,0:T(8,128)(2,1)S(1)} %get-tuple-element.435), channel_id=1, source_target_pairs={{0,1},{1,0},{2,3},{3,2},{4,5},{5,4},{6,7},{7,6},{8,9},{9,8},{10,11... | collective-permute-start | bytes 4718600 | tf_op jit(solution)/shard_map/ppermute | solution.py:942
  1687.3 171.0 %collective-permute-start.30 = (f32[2,1536]{1,0:T(2,128)}, f32[2,1536]{1,0:T(2,128)}, u32[]{:S(2)}, u32[]{:S(2)}) collective-permute-start(f32[2,1536]{1,0:T(2,128)} %bitcast.75), channel_id=1, source_target_pairs={{0,16},{4,20},{8,24},{12,28},{16,0},{20,4},{24,8},{28,12},{1,17},{... | collective-permute-start | bytes 36872 | tf_op jit(solution)/shard_map/ppermute | solution.py:994
  1752.8 69.9 %collective-permute-start.35 = (bf16[384,2048]{1,0:T(8,128)(2,1)S(1)}, bf16[384,2048]{1,0:T(8,128)(2,1)}, u32[]{:S(2)}, u32[]{:S(2)}) collective-permute-start(bf16[384,2048]{1,0:T(8,128)(2,1)S(1)} %get-tuple-element.461), channel_id=1, source_target_pairs={{0,2},{1,3},{2,0},{3,1},{4,6},{5,7},{6,4},{7,5},{8,10},{9,11},{10,... | collective-permute-start | bytes 4718600 | tf_op jit(solution)/shard_map/ppermute | solution.py:945
  1858.2 93.2 %collective-permute-start.37 = (bf16[384,2304]{1,0:T(8,128)(2,1)S(1)}, bf16[384,2304]{1,0:T(8,128)(2,1)}, u32[]{:S(2)}, u32[]{:S(2)}) collective-permute-start(bf16[384,2304]{1,0:T(8,128)(2,1)S(1)} %get-tuple-element.471), channel_id=1, source_target_pairs={{0,2},{1,3},{2,0},{3,1},{4,6},{5,7},{6,4},{7,5},{8,10},{9,11},{10,... | collective-permute-start | bytes 5308424 | tf_op jit(solution)/shard_map/ppermute | solution.py:945
  1866.8 70.0 %collective-permute-start.33 = (f32[2,192]{1,0:T(2,128)S(1)}, f32[2,192]{1,0:T(2,128)S(1)}, u32[]{:S(2)}, u32[]{:S(2)}) collective-permute-start(f32[2,192]{1,0:T(2,128)S(1)} %bitcast.99), channel_id=1, source_target_pairs={{0,2},{1,3},{2,0},{3,1},{4,6},{5,7},{6,4},{7,5},{8,10},{9,11},{10,... | collective-permute-start | bytes 4616 | tf_op jit(solution)/shard_map/ppermute | solution.py:994
  (143 other events, 2502.6 us)
Sparse Core Ops, SparseCore 0:
  40.9 58.2 all-gather.7
  134.2 135.6 all-gather.5
  280.1 122.5 all-gather.11
  484.4 121.6 all-gather.9
  613.6 167.5 all-gather.13
  904.3 118.7 reduce-scatter.5
  1026.2 120.7 reduce-scatter.7
  1150.1 120.7 reduce-scatter.9
  1277.7 55.4 reduce-scatter.13
  1423.7 131.7 reduce-scatter.11

commit v3 on v2

--- a/solution.py
+++ b/solution.py
@@ -372,8 +372,8 @@
     return (row_ids >= column_ids) & (row_ids - column_ids <= reach)
 
 
-def halves(slot_ref, quarter):
-    first = slot_ref[0]
+def halves(quarter):
+    first = lax.axis_index("tp") % 2
     return (
         pl.multiple_of(first * quarter, quarter),
         pl.multiple_of((1 - first) * quarter, quarter),
@@ -416,11 +416,11 @@
 
 
 def forward_first(
-    slot_ref, q_ref, k_ref, v_ref, cos_ref, sin_ref, qr_ref, kr_ref, vr_ref, o_ref, lse_ref
+    q_ref, k_ref, v_ref, cos_ref, sin_ref, qr_ref, kr_ref, vr_ref, o_ref, lse_ref
 ):
     half = q_ref.shape[0]
     quarter = half // 2
-    offsets = halves(slot_ref, quarter)
+    offsets = halves(quarter)
     load_rotated(offsets, quarter, q_ref, k_ref, v_ref, cos_ref, sin_ref, qr_ref, kr_ref, vr_ref)
     factor = HD ** (-0.5) * LOG2E
     mask = causal_mask(quarter, quarter)
@@ -441,14 +441,14 @@
 
 
 def forward_second(
-    slot_ref, q_ref, k_ref, v_ref, cos_ref, sin_ref, ka_ref, va_ref, pos_ref,
+    q_ref, k_ref, v_ref, cos_ref, sin_ref, ka_ref, va_ref, pos_ref,
     qr_ref, kr_ref, vr_ref, o_ref, lse_ref,
 ):
     half = q_ref.shape[0]
     quarter = half // 2
     cut = FIRST_DOC - half
     spill = cut - quarter
-    offsets = halves(slot_ref, quarter)
+    offsets = halves(quarter)
     load_rotated(offsets, quarter, q_ref, k_ref, v_ref, cos_ref, sin_ref, qr_ref, kr_ref, vr_ref)
     factor = HD ** (-0.5) * LOG2E
     mask = causal_mask(cut, cut)
@@ -476,7 +476,7 @@
 
 
 def backward_both(
-    slot_ref, qa_ref, ka_ref, va_ref, qb_ref, kb_ref, vb_ref, ga_ref, gb_ref, la_ref, lb_ref,
+    qa_ref, ka_ref, va_ref, qb_ref, kb_ref, vb_ref, ga_ref, gb_ref, la_ref, lb_ref,
     cosa_ref, sina_ref, cosb_ref, sinb_ref, pos_ref,
     dqa_ref, dka_ref, dva_ref, dqb_ref, dkb_ref, dvb_ref,
     go_a, go_b, tqa, tka, tva, tqb, tkb, tvb,
@@ -485,7 +485,7 @@
     quarter = half // 2
     cut = FIRST_DOC - half
     spill = cut - quarter
-    offsets = halves(slot_ref, quarter)
+    offsets = halves(quarter)
     scale_value = HD ** (-0.5)
     factor = scale_value * LOG2E
     for place, offset in enumerate(offsets):
@@ -568,12 +568,6 @@
     return pl.CostEstimate(flops=int(COST_SCALE * flops), bytes_accessed=1000, transcendentals=0)
 
 
-def line_params():
-    return pltpu.CompilerParams(
-        dimension_semantics=("arbitrary",), vmem_limit_bytes=48 * 1024 * 1024
-    )
-
-
 def rows_kernel(pairs, extra_count, dot, chunk, finish, *refs):
     lefts, weights = refs[:pairs], refs[pairs : 2 * pairs]
     extras = refs[2 * pairs : 2 * pairs + extra_count]
@@ -594,7 +588,9 @@
     return (total,)
 
 
-def rows_matmul(lefts, weights, dot, types, tile, chunk=1024, finish=keep_one, extras=()):
+def rows_matmul(
+    lefts, weights, dot, types, tile, chunk=1024, finish=keep_one, extras=(), pushes=()
+):
     rows = lefts[0].shape[0]
     if dot is dot_nn:
         width = weights[0].shape[1]
@@ -603,19 +599,18 @@
         width = weights[0].shape[0]
         weight_specs = [pl.BlockSpec((tile, w.shape[1]), lambda j: (j, 0)) for w in weights]
     column = pl.BlockSpec((rows, tile), lambda j: (0, j))
-    flops = 2 * rows * width * sum(left.shape[1] for left in lefts)
-    results = pl.pallas_call(
+    return grid_call(
         functools.partial(rows_kernel, len(lefts), len(extras), dot, min(chunk, rows), finish),
-        out_shape=[jax.ShapeDtypeStruct((rows, width), kind) for kind in types],
-        grid=(width // tile,),
-        in_specs=[pl.BlockSpec(left.shape, lambda j: (0, 0)) for left in lefts]
+        [*lefts, *weights, *extras],
+        [pl.BlockSpec(left.shape, lambda j: (0, 0)) for left in lefts]
         + weight_specs
         + [column] * len(extras),
-        out_specs=[column] * len(types),
-        compiler_params=line_params(),
-        cost_estimate=cost_of(flops),
-    )(*lefts, *weights, *extras)
-    return tuple(results) if len(types) > 1 else results[0]
+        [jax.ShapeDtypeStruct((rows, width), kind) for kind in types],
+        [column] * len(types),
+        (width // tile,),
+        2 * rows * width * sum(left.shape[1] for left in lefts),
+        pushes=pushes,
+    )
 
 
 def sum_kernel(parts, chunk, *refs):
@@ -631,19 +626,127 @@
         out[:, cols] = total.astype(out.dtype)
 
 
-def sum_matmul(lefts, rights, tile, chunk):
+def sum_matmul(lefts, rights, tile, chunk, pushes=()):
     rows, height = lefts[0].shape
     width = rights[0].shape[1]
-    return pl.pallas_call(
+    return grid_call(
         functools.partial(sum_kernel, len(lefts), chunk),
-        out_shape=jax.ShapeDtypeStruct((height, width), jnp.bfloat16),
-        grid=(height // tile,),
-        in_specs=[pl.BlockSpec((rows, tile), lambda j: (0, j)) for _ in lefts]
+        [*lefts, *rights],
+        [pl.BlockSpec((rows, tile), lambda j: (0, j)) for _ in lefts]
         + [pl.BlockSpec((rows, width), lambda j: (0, 0)) for _ in rights],
-        out_specs=pl.BlockSpec((tile, width), lambda j: (j, 0)),
-        compiler_params=line_params(),
-        cost_estimate=cost_of(2 * rows * height * width * len(lefts)),
-    )(*lefts, *rights)
+        [jax.ShapeDtypeStruct((height, width), jnp.bfloat16)],
+        [pl.BlockSpec((tile, width), lambda j: (j, 0))],
+        (height // tile,),
+        2 * rows * height * width * len(lefts),
+        pushes=pushes,
+    )
+
+
+def partner_of(kind):
+    index, place = lax.axis_index("fsdp"), lax.axis_index("tp")
+    if kind == "near":
+        return (index, place + 1 - 2 * (place % 2))
+    return (index, place + 2 - 4 * (place // 2))
+
+
+def start_pushes(kinds, sources, targets, send, receive):
+    barrier = pltpu.get_barrier_semaphore()
+    names = sorted(set(kinds))
+    for kind in names:
+        pl.semaphore_signal(
+            barrier, inc=1, device_id=partner_of(kind), device_id_type=pl.DeviceIdType.MESH
+        )
+    pl.semaphore_wait(barrier, len(names))
+    for place, kind in enumerate(kinds):
+        push(
+            sources[place], targets[place], send.at[place], receive.at[place], partner_of(kind)
+        ).start()
+
+
+def wait_pushes(kinds, sources, targets, send, receive):
+    for place, kind in enumerate(kinds):
+        push(
+            sources[place], targets[place], send.at[place], receive.at[place], partner_of(kind)
+        ).wait()
+
+
+def pushing_kernel(kernel, axes, in_count, out_count, kinds, *refs):
+    count = len(kinds)
+    inputs, sources = refs[:in_count], refs[in_count : in_count + count]
+    outs = refs[in_count + count : in_count + count + out_count]
+    targets = refs[in_count + count + out_count : in_count + 2 * count + out_count]
+    scratch, (send, receive) = refs[in_count + 2 * count + out_count : -2], refs[-2:]
+    first = functools.reduce(jnp.logical_and, [pl.program_id(axis) == 0 for axis in range(axes)])
+    last = functools.reduce(
+        jnp.logical_and,
+        [pl.program_id(axis) == pl.num_programs(axis) - 1 for axis in range(axes)],
+    )
+
+    @pl.when(first)
+    def _():
+        start_pushes(kinds, sources, targets, send, receive)
+
+    kernel(*inputs, *outs, *scratch)
+
+    @pl.when(last)
+    def _():
+        wait_pushes(kinds, sources, targets, send, receive)
+
+
+def grid_call(
+    kernel, operands, in_specs, outs, out_specs, grid, flops, scratch=(), pushes=(), vmem=48
+):
+    params = dict(
+        dimension_semantics=("arbitrary",) * len(grid), vmem_limit_bytes=vmem * 1024 * 1024
+    )
+    operands, in_specs, outs = list(operands), list(in_specs), list(outs)
+    out_specs, scratch = list(out_specs), list(scratch)
+    if pushes:
+        kinds = tuple(kind for kind, _ in pushes)
+        kernel = functools.partial(
+            pushing_kernel, kernel, len(grid), len(operands), len(outs), kinds
+        )
+        anywhere = [pl.BlockSpec(memory_space=pl.ANY)] * len(pushes)
+        operands += [value for _, value in pushes]
+        in_specs += anywhere
+        outs += [jax.ShapeDtypeStruct(value.shape, value.dtype) for _, value in pushes]
+        out_specs += anywhere
+        scratch += [pltpu.SemaphoreType.DMA((len(pushes),))] * 2
+        next_key[0] += 1
+        params.update(collective_id=next_key[0], has_side_effects=True)
+    return tuple(
+        pl.pallas_call(
+            kernel,
+            out_shape=outs,
+            grid=grid,
+            in_specs=in_specs,
+            out_specs=out_specs,
+            scratch_shapes=scratch,
+            compiler_params=pltpu.CompilerParams(**params),
+            cost_estimate=cost_of(flops),
+        )(*operands)
+    )
+
+
+def swap_kernel(kinds, *refs):
+    count = len(kinds)
+    sources, targets, (send, receive) = refs[:count], refs[count : 2 * count], refs[2 * count :]
+    start_pushes(kinds, sources, targets, send, receive)
+    wait_pushes(kinds, sources, targets, send, receive)
+
+
+def swap_call(*pushes):
+    next_key[0] += 1
+    kinds = tuple(kind for kind, _ in pushes)
+    values = [value for _, value in pushes]
+    return exchange_call(
+        functools.partial(swap_kernel, kinds), next_key[0], values,
+        [jax.ShapeDtypeStruct(value.shape, value.dtype) for value in values],
+        [pltpu.SemaphoreType.DMA((len(pushes),))] * 2,
+    )
+
+
+next_key = [10]
 
 
 def sibling_id():
@@ -778,36 +881,44 @@
     )
 
 
-def pair_kernel(own_ref, other_ref, pair_ref, local, send, receive):
+def pair_kernel(own_ref, *refs):
+    others, (pair_ref, local, send, receive) = refs[:-4], refs[-4:]
     partner = sibling_id()
     core = lax.axis_index("fsdp") % 2
     far = lax.axis_index("tp") // 2
     meet(partner)
-    count = own_ref.shape[0]
-    place = pl.ds(pl.multiple_of(core * count, count), count)
+    base = pl.multiple_of(core * own_ref.shape[0], own_ref.shape[0])
+    count = others[0].shape[0]
+    owns = [own_ref.at[pl.ds(place * count, count)] for place in range(len(others))]
 
     def run(mine, theirs):
-        remote = push(theirs, pair_ref.at[place], send.at[0], receive.at[0], partner)
-        remote.start()
-        copy = pltpu.make_async_copy(mine, pair_ref.at[place], local.at[0])
-        copy.start()
-        copy.wait()
-        remote.wait()
+        copies = []
+        for place in range(len(others)):
+            target = pair_ref.at[pl.ds(base + place * count, count)]
+            remote = push(
+                theirs[place], target, send.at[place], receive.at[place], partner
+            )
+            remote.start()
+            copy = pltpu.make_async_copy(mine[place], target, local.at[place])
+            copy.start()
+            copies += [remote, copy]
+        for copy in copies:
+            copy.wait()
 
     @pl.when(core == far)
     def _():
-        run(own_ref, other_ref)
+        run(owns, others)
 
     @pl.when(core != far)
     def _():
-        run(other_ref, own_ref)
-
-
-def core_pair(key, own, other):
+        run(others, owns)
+
+
+def core_pair(key, own, *others):
     shape = (2 * own.shape[0], own.shape[1])
     return exchange_call(
-        pair_kernel, key, [own, other], [jax.ShapeDtypeStruct(shape, own.dtype)],
-        [pltpu.SemaphoreType.DMA((1,))] * 3,
+        pair_kernel, key, [own, *others], [jax.ShapeDtypeStruct(shape, own.dtype)],
+        [pltpu.SemaphoreType.DMA((len(others),))] * 3,
     )
 
 
@@ -845,13 +956,7 @@
     )
 
 
-def kernel_params():
-    return pltpu.CompilerParams(
-        dimension_semantics=("arbitrary", "arbitrary"), vmem_limit_bytes=40 * 1024 * 1024
-    )
-
-
-def attention_call(kernel, slot, arrays, kinds, outs, scratch):
+def attention_call(kernel, arrays, kinds, outs, scratch, pushes=()):
     rows, heads_local = arrays[-1].shape[0], outs[1]
     half = rows // 2
     groups = heads_local // HEAD_GROUP
@@ -859,32 +964,31 @@
 
     def spec(kind):
         if kind == "table":
-            return pl.BlockSpec((half, HD), lambda s, g, _: (s, 0))
+            return pl.BlockSpec((half, HD), lambda s, g: (s, 0))
         if kind == "column":
-            return pl.BlockSpec((half, 1), lambda s, g, _: (s, 0))
+            return pl.BlockSpec((half, 1), lambda s, g: (s, 0))
         if kind == "lse":
-            return pl.BlockSpec((1, half, HEAD_GROUP), lambda s, g, _: (g, s, 0))
+            return pl.BlockSpec((1, half, HEAD_GROUP), lambda s, g: (g, s, 0))
         shift = kind * groups
-        return pl.BlockSpec((half, width), lambda s, g, _: (s, shift + g))
+        return pl.BlockSpec((half, width), lambda s, g: (s, shift + g))
 
     def shape(kind):
         if kind == "lse":
             return jax.ShapeDtypeStruct((groups, rows, HEAD_GROUP), jnp.float32)
         return jax.ShapeDtypeStruct((rows, heads_local * HD), jnp.bfloat16)
 
-    return pl.pallas_call(
+    return grid_call(
         kernel,
-        out_shape=[shape(kind) for kind in outs[0]],
-        grid_spec=pltpu.PrefetchScalarGridSpec(
-            num_scalar_prefetch=1,
-            grid=(rows // half, groups),
-            in_specs=[spec(kind) for kind in kinds],
-            out_specs=[spec(kind) for kind in outs[0]],
-            scratch_shapes=scratch(half, width),
-        ),
-        compiler_params=kernel_params(),
-        cost_estimate=cost_of(4 * len(outs[0]) ** 2 * rows * rows * heads_local * HD // 16),
-    )(slot, *arrays)
+        arrays,
+        [spec(kind) for kind in kinds],
+        [shape(kind) for kind in outs[0]],
+        [spec(kind) for kind in outs[0]],
+        (rows // half, groups),
+        4 * len(outs[0]) ** 2 * rows * rows * heads_local * HD // 16,
+        scratch=scratch(half, width),
+        pushes=pushes,
+        vmem=40,
+    )
 
 
 def backward_scratch(half, width):
@@ -924,7 +1028,6 @@
     core = lax.axis_index("fsdp") % 2
     lane_z = lax.axis_index("tp")
     near, far = lane_z % 2, lane_z // 2
-    slot = jnp.reshape(near, (1,)).astype(jnp.int32)
     core_pairs = [(i, i ^ 1) for i in range(fsdp_count)]
     near_pairs = [(i, i ^ 1) for i in range(tp_count)]
     far_pairs = [(i, i ^ 2) for i in range(tp_count)]
@@ -949,11 +1052,19 @@
 
     tokens = []
 
-    def act(work, *inputs):
-        held = lax.optimization_barrier((*inputs, *tokens))[: len(inputs)]
-        result = work(*held)
+    def act(work, *inputs, sends=()):
+        values = [*inputs, *[value for _, value in sends]]
+        held = lax.optimization_barrier((*values, *tokens))[: len(values)]
+        if sends:
+            kinds = [kind for kind, _ in sends]
+            result = work(*held[: len(inputs)], pushes=list(zip(kinds, held[len(inputs) :])))
+        else:
+            result = work(*held)
         tokens[:] = result if isinstance(result, tuple) else (result,)
-        return result
+        return result[0] if isinstance(result, tuple) and len(result) == 1 else result
+
+    def swap(*sends):
+        return act(lambda pushes: swap_call(*pushes), sends=sends)
 
     def pick(value, index):
         return lax.dynamic_index_in_dim(value, index, 0, keepdims=False)
@@ -973,8 +1084,12 @@
             grad, "fsdp", scatter_dimension=0, tiled=True, axis_index_groups=plane_groups
         )
 
-    def gather_weight(key, local, other):
-        return plane_gather(act(lambda own, got: core_pair(key, own, got), local, other))
+    def gather_weight(key, local, *others):
+        return plane_gather(act(lambda own, *got: core_pair(key, own, *got), local, *others))
+
+    def halve(value):
+        count = value.shape[0] // 2
+        return value[:count], value[count:]
 
     def add_wide(left, right):
         return left.astype(jnp.float32) + right.astype(jnp.float32)
@@ -995,16 +1110,26 @@
                 step //= 2
         return gains
 
-    def wide_dot(left, right, *_):
-        return rows_matmul([left], [right], dot_nn, [jnp.float32], pick_tile(right.shape[1]))
-
-    def dot_bf16(left, right):
-        return rows_matmul([left], [right], dot_nn, [jnp.bfloat16], pick_tile(right.shape[1]))
-
-    def grad_sum(left, right, left_next, right_next):
+    def wide_dot(left, right, pushes=()):
+        return rows_matmul(
+            [left], [right], dot_nn, [jnp.float32], pick_tile(right.shape[1]), pushes=pushes
+        )
+
+    def dot_bf16(left, right, pushes=()):
+        return rows_matmul(
+            [left], [right], dot_nn, [jnp.bfloat16], pick_tile(right.shape[1]), pushes=pushes
+        )
+
+    def grad_sum(left, right, left_next, right_next, pushes=()):
+        chunk = pick_tile(right.shape[1])
         return sum_matmul(
             [left, left_next], [right, right_next], pick_tile(left.shape[1]),
-            2 * pick_tile(right.shape[1]) if right.shape[1] % 1024 == 0 else pick_tile(right.shape[1]),
+            2 * chunk if right.shape[1] % (2 * chunk) == 0 else chunk, pushes=pushes,
+        )
+
+    def heads_back(grad, weight, pushes=()):
+        return rows_matmul(
+            [grad], [weight], dot_nt, [jnp.bfloat16], pick_tile(weight.shape[0]), pushes=pushes
         )
 
     def rms_pack(stream, gain):
@@ -1014,12 +1139,14 @@
     qkv_local = qkv_weight.reshape(qkv_weight.shape[0], 3 * local_cols)
     gate_local, up_local = gate_up_weight[:, 0], gate_up_weight[:, 1]
 
+    next_key[0] = 10
     position_got = swap_far(pick(doc_positions, 1 - far))
-    out_other = swap_far(out_weight)
+    out_other = swap(("far", out_weight))
     out_full = gather_weight(3, out_weight, out_other)
-    qkv_other = swap_far(chained(qkv_local, out_other))
     first, second = act(place_tokens, doc_positions, position_got)
     near_both = swap_near(join(first, second))
+    qkv_other = swap(("far", qkv_local))
+    qkv_full = gather_weight(4, qkv_local, qkv_other)
     first, second = act(
         lambda a, b, c: (join(a, c[: a.shape[0]]), join(b, c[a.shape[0] :])),
         first, second, near_both,
@@ -1031,91 +1158,93 @@
         late = join(second, both[count:])
         return (*head_tables(join(first, both[:count])), *head_tables(late), late[:, None])
 
-    cos_first, sin_first, cos_second, sin_second, reach = act(
-        make_tables, first, second, core_both
-    )
-    tables = [(cos_first, sin_first), (cos_second, sin_second)]
-    stream_got = swap_far(chained(pick(block_in, 1 - far), qkv_other))
-    qkv_full = gather_weight(4, qkv_local, qkv_other)
+    stream_got = swap(("far", pick(block_in, 1 - far)))
 
     def first_norm(value, got):
         streams = [part.astype(jnp.float32) for part in place_tokens(value, got)]
         return (*streams, *rms_pack(streams[0], gain_one), *rms_pack(streams[1], gain_one))
 
-    gate_other = swap_far(chained(gate_local, stream_got))
     s_first, s_second, r_first, n_first, r_second, n_second = act(first_norm, block_in, stream_got)
     streams, scales_one = [s_first, s_second], [r_first, r_second]
-    near_first = swap_near(n_first)
+    near_first, gate_other = swap(("near", n_first), ("far", gate_local))
     gate_full = gather_weight(5, gate_local, gate_other)
-    up_other = swap_far(chained(up_local, gate_other))
-    near_second = swap_near(chained(n_second, near_first))
     h1_first = act(core_gather, n_first, near_first)
 
-    def attend_first(projected):
+    def attend_first(projected, pushes=()):
         arrays = [projected, projected, projected, *tables[0]]
-        return tuple(
-            attention_call(
-                forward_first, slot, arrays, [0, 1, 2, "table", "table"],
-                ([0, 0, 0, 0, "lse"], heads_local), no_scratch,
-            )
-        )
-
-    def attend_second(projected):
+        return attention_call(
+            forward_first, arrays, [0, 1, 2, "table", "table"],
+            ([0, 0, 0, 0, "lse"], heads_local), no_scratch, pushes,
+        )
+
+    def attend_second(projected, pushes=()):
         arrays = [projected, projected, projected, *tables[1], saved[0][1], saved[0][2], reach]
-        return tuple(
-            attention_call(
-                forward_second, slot, arrays, [0, 1, 2, "table", "table", 0, 0, "column"],
-                ([0, 0, 0, 0, "lse"], heads_local), no_scratch,
-            )
-        )
-
-    projected = act(wide_dot, h1_first, qkv_full, out_full)
-    results = act(attend_first, projected)
+        return attention_call(
+            forward_second, arrays, [0, 1, 2, "table", "table", 0, 0, "column"],
+            ([0, 0, 0, 0, "lse"], heads_local), no_scratch, pushes,
+        )
+
+    up_halves, down_halves = halve(up_local), halve(down_weight)
+    cot_halves = halve(pick(out_cotangent, 1 - far))
+    cos_first, sin_first, cos_second, sin_second, reach = act(
+        make_tables, first, second, core_both
+    )
+    tables = [(cos_first, sin_first), (cos_second, sin_second)]
+    projected, near_second, up_early = act(
+        wide_dot, h1_first, qkv_full, sends=[("near", n_second), ("far", up_halves[0])]
+    )
+    *results, up_late = act(attend_first, projected, sends=[("far", up_halves[1])])
     saved, lses, mixed_first = [results[:3]], [results[4]], results[3]
+    up_full = gather_weight(7, up_local, up_early, up_late)
     h1_second = act(core_gather, n_second, near_second)
     term_first = act(dot_bf16, mixed_first, out_full)
     keep_first, send_first = act(core_reduce, term_first)
-    branch_first = swap_near(send_first)
-    projected = act(wide_dot, h1_second, qkv_full)
-    up_full = gather_weight(5, up_local, up_other)
-    down_other = swap_far(chained(down_weight, up_other))
-    results = act(attend_second, projected)
+    projected, branch_first, down_early = act(
+        wide_dot, h1_second, qkv_full, sends=[("near", send_first), ("far", down_halves[0])]
+    )
+
+    def second_norm(stream, keep, got):
+        middle = stream + keep + got.astype(jnp.float32)
+        return (middle, *rms_pack(middle, gain_two))
+
+    m_first, q_first, n_first = act(second_norm, streams[0], keep_first, branch_first)
+    *results, near_first, down_late = act(
+        attend_second, projected, sends=[("near", n_first), ("far", down_halves[1])]
+    )
     saved.append(results[:3])
     lses.append(results[4])
     mixed_second = results[3]
-
-    def second_norm(stream, keep, got):
-        middle = stream + keep + got.astype(jnp.float32)
-        return (middle, *rms_pack(middle, gain_two))
-
-    m_first, q_first, n_first = act(second_norm, streams[0], keep_first, branch_first)
-    near_first = swap_near(n_first)
+    down_full = gather_weight(6, down_weight, down_early, down_late)
     term_second = act(dot_bf16, mixed_second, out_full)
     keep_second, send_second = act(core_reduce, term_second)
-    branch_second = swap_near(chained(send_second, near_first))
     h2_first = act(core_gather, n_first, near_first)
-    down_full = gather_weight(6, down_weight, down_other)
-    cotangent_got = swap_far(chained(pick(out_cotangent, 1 - far), down_other))
-
-    gate_first = act(wide_dot, h2_first, gate_full)
+
+    gate_first, branch_second, cot_early = act(
+        wide_dot, h2_first, gate_full, sends=[("near", send_second), ("far", cot_halves[0])]
+    )
     m_second, q_second, n_second = act(second_norm, streams[1], keep_second, branch_second)
-    near_second = swap_near(n_second)
-    c_first, c_second = act(place_tokens, out_cotangent, cotangent_got)
-    near_third = swap_near(chained(c_first, near_second))
-    near_fourth = swap_near(chained(c_second, near_third))
-    h2_second = act(core_gather, n_second, near_second)
-    gate_second = act(wide_dot, h2_second, gate_full)
-
-    def rise(hidden, weight, gate):
+
+    def rise(hidden, weight, gate, pushes=()):
         return rows_matmul(
             [hidden], [weight], dot_nn, [jnp.float32, jnp.bfloat16], pick_tile(weight.shape[1]),
             finish=lambda up, gate: (up, gate * jax.nn.sigmoid(gate) * up), extras=[gate],
-        )
-
-    up_first, a_first = act(rise, h2_first, up_full, gate_first)
-    y_first = act(core_gather, c_first, near_third)
-    up_second, a_second = act(rise, h2_second, up_full, gate_second)
-    y_second = act(core_gather, c_second, near_fourth)
+            pushes=pushes,
+        )
+
+    up_first, a_first, near_second, cot_late = act(
+        rise, h2_first, up_full, gate_first, sends=[("near", n_second), ("far", cot_halves[1])]
+    )
+    h2_second = act(core_gather, n_second, near_second)
+    c_first, c_second = act(
+        lambda value, early, late: place_tokens(value, join(early, late)),
+        out_cotangent, cot_early, cot_late,
+    )
+    gate_second, near_first = act(wide_dot, h2_second, gate_full, sends=[("near", c_first)])
+    y_first = act(core_gather, c_first, near_first)
+    up_second, a_second, near_second = act(
+        rise, h2_second, up_full, gate_second, sends=[("near", c_second)]
+    )
+    y_second = act(core_gather, c_second, near_second)
     down_sum = plane_scatter(act(grad_sum, a_first, y_first, a_second, y_second))
 
     def fall_finish(act_grad, gate, up):
@@ -1135,10 +1264,10 @@
     dg_second, du_second = act(fall, y_second, down_full, gate_second, up_second)
     gate_sum = plane_scatter(act(grad_sum, h2_first, dg_first, h2_second, dg_second))
 
-    def hidden_grad(gate_grad, up_grad, gate_weight, up_weight):
+    def hidden_grad(gate_grad, up_grad, gate_weight, up_weight, pushes=()):
         return rows_matmul(
             [gate_grad, up_grad], [gate_weight, up_weight], dot_nt, [jnp.bfloat16],
-            pick_tile(gate_weight.shape[0]),
+            pick_tile(gate_weight.shape[0]), pushes=pushes,
         )
 
     def second_back(middle, scale, keep, got, cotangent):
@@ -1148,53 +1277,52 @@
 
     term_first = act(hidden_grad, dg_first, du_first, gate_full, up_full)
     keep_first, send_first = act(core_reduce, term_first)
-    back_first = swap_near(send_first)
-    term_second = act(hidden_grad, dg_second, du_second, gate_full, up_full)
+    term_second, back_first = act(
+        hidden_grad, dg_second, du_second, gate_full, up_full, sends=[("near", send_first)]
+    )
     keep_second, send_second = act(core_reduce, term_second)
-    back_second = swap_near(chained(send_second, back_first))
     g_first, n_first, gain_two_first = act(
         second_back, m_first, q_first, keep_first, back_first, c_first
     )
-    near_first = swap_near(chained(n_first, back_second))
-    up_sum = plane_scatter(act(grad_sum, h2_first, du_first, h2_second, du_second))
+    grad_up, back_second = act(
+        grad_sum, h2_first, du_first, h2_second, du_second, sends=[("near", send_second)]
+    )
+    up_sum = plane_scatter(grad_up)
+    mlp_first, near_first = act(dot_bf16, a_first, down_full, sends=[("near", n_first)])
     g_second, n_second, gain_two_second = act(
         second_back, m_second, q_second, keep_second, back_second, c_second
     )
-    near_second = swap_near(chained(n_second, near_first))
-    mlp_first = act(dot_bf16, a_first, down_full)
+    d_first = act(core_gather, n_first, near_first)
+
+    mlp_second, near_second = act(dot_bf16, a_second, down_full, sends=[("near", n_second)])
+    heads_first = act(heads_back, d_first, out_full)
+    d_second = act(core_gather, n_second, near_second)
+    heads_second = act(heads_back, d_second, out_full)
     mlp_keep_first, mlp_send_first = act(core_reduce, mlp_first)
-    d_first = act(core_gather, n_first, near_first)
-
-    def heads_back(grad, weight):
-        return rows_matmul([grad], [weight], dot_nt, [jnp.bfloat16], pick_tile(weight.shape[0]))
-
-    mlp_second = act(dot_bf16, a_second, down_full)
-    mlp_branch_first = swap_near(chained(mlp_send_first, near_second))
-    heads_first = act(heads_back, d_first, out_full)
     mlp_keep_second, mlp_send_second = act(core_reduce, mlp_second)
-    d_second = act(core_gather, n_second, near_second)
-    mlp_branch_second = swap_near(chained(mlp_send_second, mlp_branch_first))
-    heads_second = act(heads_back, d_second, out_full)
-    out_sum = plane_scatter(act(grad_sum, mixed_first, d_first, mixed_second, d_second))
     down_mine, down_away = act(lambda pair: core_split(10, pair), down_sum)
-    down_got = swap_far(down_away)
-
-    def attend_back(heads_first, heads_second):
-        return tuple(
-            attention_call(
-                backward_both,
-                slot,
-                [
-                    *saved[0], *saved[1], heads_first, heads_second, *lses,
-                    *tables[0], *tables[1], reach,
-                ],
-                [0] * 8 + ["lse"] * 2 + ["table"] * 4 + ["column"],
-                ([0] * 6, heads_local),
-                backward_scratch,
-            )
-        )
-
-    grads = act(attend_back, heads_first, heads_second)
+    grad_out, mlp_branch_first = act(
+        grad_sum, mixed_first, d_first, mixed_second, d_second, sends=[("near", mlp_send_first)]
+    )
+    out_sum = plane_scatter(grad_out)
+
+    def attend_back(heads_first, heads_second, pushes=()):
+        return attention_call(
+            backward_both,
+            [
+                *saved[0], *saved[1], heads_first, heads_second, *lses,
+                *tables[0], *tables[1], reach,
+            ],
+            [0] * 8 + ["lse"] * 2 + ["table"] * 4 + ["column"],
+            ([0] * 6, heads_local),
+            backward_scratch,
+            pushes,
+        )
+
+    *grads, mlp_branch_second, down_got = act(
+        attend_back, heads_first, heads_second,
+        sends=[("near", mlp_send_second), ("far", down_away)],
+    )
     p_first, p_second = act(
         lambda *parts: (
             jnp.concatenate(parts[:3], axis=1),
@@ -1202,26 +1330,29 @@
         ),
         *grads,
     )
+    gate_mine, gate_away = act(lambda pair: core_split(9, pair), gate_sum)
+    gate_halves = halve(gate_away)
+    grad_qkv, gate_early = act(
+        grad_sum, h1_first, p_first, h1_second, p_second, sends=[("far", gate_halves[0])]
+    )
+    qkv_sum = plane_scatter(grad_qkv)
 
     def finish_output(first, first_keep, first_got, second, second_keep, second_got):
         first = (first + first_keep + first_got.astype(jnp.float32)).astype(jnp.bfloat16)
         second = (second + second_keep + second_got.astype(jnp.float32)).astype(jnp.bfloat16)
         return jnp.where(far == 0, first, second), jnp.where(far == 0, second, first)
 
+    term_first, gate_late = act(heads_back, p_first, qkv_full, sends=[("far", gate_halves[1])])
+    keep_first, send_first = act(core_reduce, term_first)
     out_keep, out_send = act(
         finish_output,
         m_first, mlp_keep_first, mlp_branch_first, m_second, mlp_keep_second, mlp_branch_second,
     )
-    out_got = swap_far(chained(out_send, down_got))
-    qkv_sum = plane_scatter(act(grad_sum, h1_first, p_first, h1_second, p_second))
-    down_owned = act(add_wide, down_mine, down_got)
-    term_first = act(heads_back, p_first, qkv_full)
-    keep_first, send_first = act(core_reduce, term_first)
-    back_first = swap_near(send_first)
-    gate_mine, gate_away = act(lambda pair: core_split(9, pair), gate_sum)
-    term_second = act(heads_back, p_second, qkv_full)
+    out_halves = halve(out_send)
+    term_second, back_first, out_early = act(
+        heads_back, p_second, qkv_full, sends=[("near", send_first), ("far", out_halves[0])]
+    )
     keep_second, send_second = act(core_reduce, term_second)
-    back_second = swap_near(chained(send_second, back_first))
 
     def settle(keep, got):
         return jnp.stack([jnp.where(far == 0, keep, got), jnp.where(far == 0, got, keep)])
@@ -1229,10 +1360,6 @@
     def first_back(stream, scale, keep, got, grad):
         back, gain_term = norm_back(stream, scale, gain_one, keep + got.astype(jnp.float32))
         return grad + back, gain_term
-
-    i_first, gain_one_first = act(
-        first_back, streams[0], scales_one[0], keep_first, back_first, g_first
-    )
 
     def last_back(stream, scale, keep, got, grad, first):
         second, gain_term = first_back(stream, scale, keep, got, grad)
@@ -1242,25 +1369,29 @@
             gain_term,
         )
 
+    back_second, out_late = swap(("near", send_second), ("far", out_halves[1]))
+    i_first, gain_one_first = act(
+        first_back, streams[0], scales_one[0], keep_first, back_first, g_first
+    )
     in_keep, in_send, gain_one_second = act(
         last_back, streams[1], scales_one[1], keep_second, back_second, g_second, i_first
     )
-    block_out = act(settle, out_keep, out_got)
-    gate_got = swap_far(chained(gate_away, out_got))
-    in_got = swap_far(chained(in_send, gate_got))
+    up_mine, up_away = act(lambda pair: core_split(9, pair), up_sum)
+    up_got = swap_far(up_away)
+    down_owned = act(add_wide, down_mine, down_got)
     gains = scatter_gains(
         jnp.stack([gain_one_first + gain_one_second, gain_two_first + gain_two_second])
     )
-    gate_owned = act(add_wide, gate_mine, gate_got)
-    up_mine, up_away = act(lambda pair: core_split(9, pair), up_sum)
-    up_got = swap_far(chained(up_away, in_got))
+    block_out = act(lambda keep, early, late: settle(keep, join(early, late)), out_keep, out_early, out_late)
+    gate_owned = act(lambda mine, early, late: add_wide(mine, join(early, late)), gate_mine, gate_early, gate_late)
+    up_owned = act(add_wide, up_mine, up_got)
+    in_got = swap_far(chained(in_send, up_got))
+    gate_up_owned = act(lambda a, b: jnp.stack([a, b], axis=1), gate_owned, up_owned)
     in_grad = act(lambda keep, got: settle(keep, got.astype(jnp.float32)), in_keep, in_got)
-    out_mine, out_away = act(lambda pair: core_split(7, pair), out_sum)
-    out_back = swap_far(chained(out_away, up_got))
-    up_owned = act(add_wide, up_mine, up_got)
-    gate_up_owned = act(lambda a, b: jnp.stack([a, b], axis=1), gate_owned, up_owned)
+    out_mine, out_away = act(lambda pair: core_split(8, pair), out_sum)
+    out_back = swap_far(chained(out_away, in_got))
     out_owned = act(add_wide, out_mine, out_back)
-    qkv_mine, qkv_away = act(lambda pair: core_split(8, pair), qkv_sum)
+    qkv_mine, qkv_away = act(lambda pair: core_split(0, pair), qkv_sum)
     qkv_owned = act(add_wide, qkv_mine, swap_far(qkv_away))
     return (
         block_out,

time: 1980 us -> 1990 us (level)
  Pallas kernels: 808 us -> 1480 us
  waiting for transfers between devices: 835 us -> 230 us
  starting transfers between devices: 85.3 us -> 14.8 us
  local copies, waits for them, and re-layouts: 135 us -> 164 us
    pallas_call x26, Pallas kernels: 634 us -> 1050 us  [grid_call(): pl.pallas_call(kernel, out_shape=outs, grid=grid, in_specs=in_specs, out_...]
    ppermute x15 -> x5, waiting for transfers between devices: 474 us -> 153 us  [swap_far(): return lax.ppermute(value, 'tp', far_pairs)]
    ppermute x17 -> x1, waiting for transfers between devices: 286 us -> 2.01 us  [swap_near(): return lax.ppermute(value, 'tp', near_pairs)]
    pallas_call x26 -> x31, Pallas kernels: 174 us -> 434 us  [exchange_call(): pl.pallas_call(kernel, out_shape=outs, in_specs=[anywhere] * len(operands...]
    ppermute x15 -> x5, starting transfers between devices: 56.1 us -> 7.61 us  [swap_far(): return lax.ppermute(value, 'tp', far_pairs)]
    unnamed x251 -> x297, local copies, waits for them, and re-layouts: 114 us -> 137 us
    ppermute x17 -> x1, starting transfers between devices: 22.8 us -> 0.07 us  [swap_near(): return lax.ppermute(value, 'tp', near_pairs)]
  transfers between devices with their start and end apart: 48 -> 22, of which waited for: 25 -> 8; matrix products, arithmetic and copies ran while one was open for 6% -> 6% of each run, Pallas kernels for 41% -> 71%
where the time goes in v3:
time: 1990 us; the launch traced here: 1980 us
  Pallas kernels  1480 us (74%)
  waiting for transfers between devices  230 us (12%)
  local copies, waits for them, and re-layouts  164 us (8%)
  other arithmetic  76.6 us (4%)
    pallas_call x26, Pallas kernels, grid_call(): pl.pallas_call(kernel, out_shape=outs, grid=grid, in_specs=in_specs, out_...  1050 us
    pallas_call x31, Pallas kernels, exchange_call(): pl.pallas_call(kernel, out_shape=outs, in_specs=[anywhere] * len(operands...  434 us
    ppermute x5, waiting for transfers between devices, swap_far(): return lax.ppermute(value, 'tp', far_pairs)  153 us
    unnamed x297, local copies, waits for them, and re-layouts  137 us
    ppermute x5, waiting for transfers between devices, scatter_gains(): lax.ppermute(sent, axis, [(i, i ^ step) for i in range(size)])  74.7 us
  transfers between devices with their start and end apart: 22, of which 8 were waited for; matrix products, arithmetic and copies ran while one was open for 6% of the time, Pallas kernels for 71%

profile of v3, /device:TPU:0, one launch (start us, length us, event | category | flops | bytes accessed | tf_op | source)
XLA Modules:
  0.0 1982.2 jit_solution(12419007530836832338)
XLA Ops:
  48.1 78.1 %shard_map.154.refs_0_ = bf16[384,2304]{1,0:T(8,128)(2,1)S(1)} custom-call(bf16[384,2304]{1,0:T(8,128)(2,1)S(1)} %copy.37.refs_0_), custom_call_target="tpu_custom_call" | custom-call | flops 6800000000 | bytes 1000 | tf_op jit(solution)/shard_map/pallas_call | solution.py:776
  143.6 69.9 %shard_map.156 = bf16[256,3072]{1,0:T(8,128)(2,1)S(1)} custom-call(bf16[256,3072]{1,0:T(8,128)(2,1)S(1)} %dynamic-slice_bitcast_fusion.refs_0_), custom_call_target="tpu_custom_call" | custom-call | flops 6800000000 | bytes 1000 | tf_op jit(solution)/shard_map/pallas_call | solution.py:776
  218.8 71.1 %shard_map.157 = (bf16[256,3072]{1,0:T(8,128)(2,1)S(1)}, bf16[384,2048]{1,0:T(8,128)(2,1)S(1)}) custom-call(bf16[256,3072]{1,0:T(8,128)(2,1)S(1)} %get-tuple-element.333.refs_0_.own_ref, bf16[384,2048]{1,0:T(8,128)(2,1)S(1)} %bitcast.86), custom_call_target="tpu_custom_call" | custom-call | flops 6800000000 | bytes 1000 | tf_op jit(solution)/shard_map/pallas_call | solution.py:776
  317.2 60.6 %shard_map.160 = (f32[1024,2304]{1,0:T(8,128)}, bf16[256,3072]{1,0:T(8,128)(2,1)S(1)}, bf16[192,2048]{1,0:T(8,128)(2,1)S(1)}) custom-call(bf16[1024,3072]{1,0:T(8,128)(2,1)} %copy-done.67, bf16[3072,2304]{1,0:T(8,128)(2,1)} %all-gather.6.cloned.1.call-done.refs_1_, bf16[256,3072]{1,0:T(8,128)(2,1)S(1)} %copy-done.28, bf16[192,2048]{1,0:T(8,128)(2,1)S(1)} %bitcast.89), custom_call_target="tpu_custom_call" | custom-call | flops 24642375680 | bytes 1000 | tf_op jit(solution)/shard_map/pallas_call | solution.py:718
  379.0 38.6 %shard_map.161 = (bf16[1024,768]{1,0:T(8,128)(2,1)S(1)}, bf16[1024,768]{1,0:T(8,128)(2,1)S(1)}, bf16[1024,768]{1,0:T(8,128)(2,1)S(1)}, bf16[1024,768]{1,0:T(8,12...) custom-call(f32[1024,2304]{1,0:T(8,128)} %get-tuple-element.345.refs_0_.refs_1_.refs_2_, ...), custom_call_target="tpu_custom_call" | custom-call | flops 8556380160 | bytes 1000 | tf_op jit(solution)/shard_map/pallas_call | solution.py:718
  462.3 61.5 %shard_map.166 = (f32[1024,2304]{1,0:T(8,128)}, bf16[256,3072]{1,0:T(8,128)(2,1)S(1)}, bf16[128,3072]{1,0:T(8,128)(2,1)S(1)}) custom-call(bf16[1024,3072]{1,0:T(8,128)(2,1)} %copy-done.68, bf16[3072,2304]{1,0:T(8,128)(2,1)} %all-gather.6.cloned.1.call-done.refs_1_, bf16[256,3072]{1,0:T(8,128)(2,1)S(1)} %get-tuple-element.364.refs_2_, ...), custom_call_target="tpu_custom_call" | custom-call | flops 24642375680 | bytes 1000 | tf_op jit(solution)/shard_map/pallas_call | solution.py:718
  527.3 55.7 %shard_map.167 = (bf16[1024,768]{1,0:T(8,128)(2,1)S(1)}, bf16[1024,768]{1,0:T(8,128)(2,1)S(1)}, bf16[1024,768]{1,0:T(8,128)(2,1)S(1)}, bf16[1024,768]{1,0:T(8,12...) custom-call(f32[1024,2304]{1,0:T(8,128)} %get-tuple-element.372.refs_0_.refs_1_, ...), custom_call_target="tpu_custom_call" | custom-call | flops 8556380160 | bytes 1000 | tf_op jit(solution)/shard_map/pallas_call | solution.py:718
  626.4 58.7 %shard_map.172 = (f32[1024,2048]{1,0:T(8,128)}, bf16[256,3072]{1,0:T(8,128)(2,1)S(1)}, bf16[128,3072]{1,0:T(8,128)(2,1)S(1)}) custom-call(bf16[1024,3072]{1,0:T(8,128)(2,1)} %copy-done.69, bf16[3072,2048]{1,0:T(8,128)(2,1)} %all-gather.12.cloned.1.call-done.refs_1_.refs_2_, bf16[256,3072]{1,0:T(8,128)(2,1)S(1)} %copy-done.93, bf16[128,3072]{1,0:T(8,128)(2,1)S(1)} %copy-done.37), custom_call_target="tpu_custom_call" | custom-call | flops 21904332800 | bytes 1000 | tf_op jit(solution)/shard_map/pallas_call | solution.py:718
  689.7 60.4 %shard_map.173 = (f32[1024,2048]{1,0:T(8,128)}, bf16[1024,2048]{1,0:T(8,128)(2,1)}, bf16[256,3072]{1,0:T(8,128)(2,1)S(1)}, bf16[128,3072]{1,0:T(8,128)(2,1)S(1)}) custom-call(bf16[1024,3072]{1,0:T(8,128)(2,1)} %copy-done.69, bf16[3072,2048]{1,0:T(8,128)(2,1)} %all-gather.10.cloned.1.call-done.refs_1_.refs_3_, f32[1024,2048]{1,0:T(8,128)} %get-tuple-element.437.refs_2_, ...), custom_call_target="tpu_custom_call" | custom-call | flops 21904332800 | bytes 1000 | tf_op jit(solution)/shard_map/pallas_call | solution.py:718
  758.8 42.7 %shard_map.175 = (f32[1024,2048]{1,0:T(8,128)}, bf16[256,3072]{1,0:T(8,128)(2,1)S(1)}) custom-call(bf16[1024,3072]{1,0:T(8,128)(2,1)} %copy-done.70, bf16[3072,2048]{1,0:T(8,128)(2,1)} %all-gather.12.cloned.1.call-done.refs_1_.refs_2_, bf16[256,3072]{1,0:T(8,128)(2,1)S(1)} %get-tuple-element.466.refs_2_.own_ref), custom_call_target="tpu_custom_call" | custom-call | flops 21904332800 | bytes 1000 | tf_op jit(solution)/shard_map/pallas_call | solution.py:718
  810.0 42.6 %shard_map.177 = (f32[1024,2048]{1,0:T(8,128)}, bf16[1024,2048]{1,0:T(8,128)(2,1)}, bf16[256,3072]{1,0:T(8,128)(2,1)S(1)}) custom-call(bf16[1024,3072]{1,0:T(8,128)(2,1)} %copy-done.70, bf16[3072,2048]{1,0:T(8,128)(2,1)} %all-gather.10.cloned.1.call-done.refs_1_.refs_3_, f32[1024,2048]{1,0:T(8,128)} %get-tuple-element.443.refs_2_, ...), custom_call_target="tpu_custom_call" | custom-call | flops 21904332800 | bytes 1000 | tf_op jit(solution)/shard_map/pallas_call | solution.py:718
  1023.4 43.3 %shard_map.185 = (bf16[1024,3072]{1,0:T(8,128)(2,1)}, bf16[256,3072]{1,0:T(8,128)(2,1)S(1)}) custom-call(bf16[1024,2048]{1,0:T(8,128)(2,1)} %copy-done.95, bf16[1024,2048]{1,0:T(8,128)(2,1)} %get-tuple-element.474.refs_1_.refs_3_, bf16[3072,2048]{1,0:T(8,128)(2,1)} %all-gather.12.cloned.1.call-done.refs_1_.refs_2_, ...), custom_call_target="tpu_custom_call" | custom-call | flops 43808665600 | bytes 1000 | tf_op jit(solution)/shard_map/pallas_call | solution.py:718
  1081.5 42.0 %shard_map.187 = (bf16[3072,2048]{1,0:T(8,128)(2,1)}, bf16[256,3072]{1,0:T(8,128)(2,1)S(1)}) custom-call(bf16[1024,3072]{1,0:T(8,128)(2,1)} %copy-done.69, bf16[1024,3072]{1,0:T(8,128)(2,1)} %copy-done.70, bf16[1024,2048]{1,0:T(8,128)(2,1)} %get-tuple-element.473.refs_1_.refs_2_, bf16[1024,2048]{1,0:T(8,128)(2,1)} %get-tuple-element.474.refs_1_.refs_3_, ...), custom_call_target="tpu_custom_call" | custom-call | flops 43808665600 | bytes 1000 | tf_op jit(solution)/shard_map/pallas_call | solution.py:718
  1126.1 40.3 %shard_map.188 = (bf16[1024,3072]{1,0:T(8,128)(2,1)}, bf16[256,3072]{1,0:T(8,128)(2,1)S(1)}) custom-call(bf16[1024,2048]{1,0:T(8,128)(2,1)} %get-tuple-element.478.refs_0_, bf16[2048,3072]{1,0:T(8,128)(2,1)} %all-gather.14.cloned.1.call-done.refs_1_, bf16[256,3072]{1,0:T(8,128)(2,1)S(1)} %copy-done.30), custom_call_target="tpu_custom_call" | custom-call | flops 21904332800 | bytes 1000 | tf_op jit(solution)/shard_map/pallas_call | solution.py:718
  1184.0 40.4 %shard_map.190 = (bf16[1024,3072]{1,0:T(8,128)(2,1)}, bf16[256,3072]{1,0:T(8,128)(2,1)S(1)}) custom-call(bf16[1024,2048]{1,0:T(8,128)(2,1)} %get-tuple-element.490.refs_1_.refs_0_, bf16[2048,3072]{1,0:T(8,128)(2,1)} %all-gather.14.cloned.1.call-done.refs_1_, bf16[256,3072]{1,0:T(8,128)(2,1)S(1)} %get-tuple-element.497.refs_2_.own_ref), custom_call_target="tpu_custom_call" | custom-call | flops 21904332800 | bytes 1000 | tf_op jit(solution)/shard_map/pallas_call | solution.py:718
  1280.6 43.5 %shard_map.197 = (bf16[768,3072]{1,0:T(8,128)(2,1)}, bf16[256,3072]{1,0:T(8,128)(2,1)S(1)}) custom-call(bf16[1024,768]{1,0:T(8,128)(2,1)S(1)} %copy-done.64, bf16[1024,768]{1,0:T(8,128)(2,1)S(1)} %copy-done.54, bf16[1024,3072]{1,0:T(8,128)(2,1)} %copy-done.71, bf16[1024,3072]{1,0:T(8,128)(2,1)} %copy-done.72, bf16[256,3072]{1,0:T(8,128)(2,1)} %copy-done.91), custom_call_target="tpu_custom_call" | custom-call | flops 16428250112 | bytes 1000 | tf_op jit(solution)/shard_map/pallas_call | solution.py:718
  1333.3 72.2 %shard_map.198 = (bf16[1024,768]{1,0:T(8,128)(2,1)S(1)}, bf16[1024,768]{1,0:T(8,128)(2,1)S(1)}, bf16[1024,768]{1,0:T(8,128)(2,1)S(1)}, bf16[1024,768]{1,0:T(8,12...) custom-call(bf16[1024,768]{1,0:T(8,128)(2,1)} %copy-done.61, ...), custom_call_target="tpu_custom_call" | custom-call | flops 12321187840 | bytes 1000 | tf_op jit(solution)/shard_map/pallas_call | solution.py:718
  1418.0 43.1 %shard_map.200 = (bf16[3072,2304]{1,0:T(8,128)(2,1)}, bf16[192,2048]{1,0:T(8,128)(2,1)S(1)}) custom-call(bf16[1024,3072]{1,0:T(8,128)(2,1)} %copy-done.67, bf16[1024,3072]{1,0:T(8,128)(2,1)} %copy-done.68, bf16[1024,2304]{1,0:T(8,128)(2,1)} %constant_dynamic-update-slice_fusion.2.refs_2_.refs_0_, bf16[1024,2304]{1,0:T(8,128)(2,1)} %copy-done.123, ...), custom_call_target="tpu_custom_call" | custom-call | flops 49284751360 | bytes 1000 | tf_op jit(solution)/shard_map/pallas_call | solution.py:718
  1463.9 46.3 %shard_map.201 = (bf16[1024,3072]{1,0:T(8,128)(2,1)}, bf16[192,2048]{1,0:T(8,128)(2,1)S(1)}) custom-call(bf16[1024,2304]{1,0:T(8,128)(2,1)} %constant_dynamic-update-slice_fusion.2.refs_2_.refs_0_, bf16[3072,2304]{1,0:T(8,128)(2,1)} %all-gather.6.cloned.1.call-done.refs_1_, bf16[192,2048]{1,0:T(8,128)(2,1)S(1)} %copy-done.35), custom_call_target="tpu_custom_call" | custom-call | flops 24642375680 | bytes 1000 | tf_op jit(solution)/shard_map/pallas_call | solution.py:718
  1530.7 65.9 %shard_map.203 = (bf16[1024,3072]{1,0:T(8,128)(2,1)}, bf16[256,3072]{1,0:T(8,128)(2,1)S(1)}, bf16[128,3072]{1,0:T(8,128)(2,1)S(1)}) custom-call(bf16[1024,2304]{1,0:T(8,128)(2,1)} %copy-done.123, bf16[3072,2304]{1,0:T(8,128)(2,1)} %all-gather.6.cloned.1.call-done.refs_1_, bf16[256,3072]{1,0:T(8,128)(2,1)S(1)} %copy-done.90, ...), custom_call_target="tpu_custom_call" | custom-call | flops 24642375680 | bytes 1000 | tf_op jit(solution)/shard_map/pallas_call | solution.py:718
  1605.5 59.1 %shard_map.205 = (bf16[256,3072]{1,0:T(8,128)(2,1)S(1)}, bf16[128,3072]{1,0:T(8,128)(2,1)S(1)}) custom-call(bf16[256,3072]{1,0:T(8,128)(2,1)S(1)} %get-tuple-element.564.refs_0_, bf16[128,3072]{1,0:T(8,128)(2,1)S(1)} %get-tuple-element.565.refs_1_), custom_call_target="tpu_custom_call" | custom-call | flops 6800000000 | bytes 1000 | tf_op jit(solution)/shard_map/pallas_call | solution.py:776
  1692.4 64.6 %collective-permute-done.3 = bf16[384,2048]{1,0:T(8,128)(2,1)S(1)} collective-permute-done((bf16[384,2048]{1,0:T(8,128)(2,1)S(1)}, bf16[384,2048]{1,0:T(8,128)(2,1)S(1)}, u32[]{:S(2)}, u32[]{:S(2)}) %collective-permute-start.3) | collective-permute-done | bytes 1572896 | tf_op jit(solution)/shard_map/ppermute | solution.py:1048
  1765.3 62.3 %collective-permute-done.4 = bf16[256,3072]{1,0:T(8,128)(2,1)} collective-permute-done((bf16[256,3072]{1,0:T(8,128)(2,1)}, bf16[256,3072]{1,0:T(8,128)(2,1)}, u32[]{:S(2)}, u32[]{:S(2)}) %collective-permute-start.4) | collective-permute-done | bytes 1572896 | tf_op jit(solution)/shard_map/ppermute | solution.py:1048
  1882.9 67.8 %collective-permute-done.8 = f32[2,192]{1,0:T(2,128)S(1)} collective-permute-done((f32[2,192]{1,0:T(2,128)S(1)}, f32[2,192]{1,0:T(2,128)S(1)}, u32[]{:S(2)}, u32[]{:S(2)}) %collective-permute-start.8) | collective-permute-done | bytes 1568 | tf_op jit(solution)/shard_map/ppermute | solution.py:1109
  (477 shorter events, 635.1 us)
Async XLA Ops:
  7.2 308.6 %all-gather.6.cloned.1.call-start = ((), (), s32[]{:S(2)}) async-start(), calls=%async_computation.5 | async-start | bytes 17694720 | tf_op jit(solution)/shard_map/all_gather | solution.py:1080
  7.3 38.5 %collective-permute-start = (s32[256]{0:T(256)S(1)}, s32[256]{0:T(256)S(1)}, u32[]{:S(2)}, u32[]{:S(2)}) collective-permute-start(s32[256]{0:T(256)S(1)} %bitcast.113), channel_id=1, source_target_pairs={{0,2},{1,3},{2,0},{3,1},{4,6},{5,7},{6,4},{7,5},{8,10},{9,11},{10,... | collective-permute-start | bytes 3080 | tf_op jit(solution)/shard_map/ppermute | solution.py:1048
  132.7 310.0 %all-gather.8.cloned.1.call-start = ((), (), s32[]{:S(2)}) async-start(), calls=%async_computation.6 | async-start | bytes 5898240 | tf_op jit(solution)/shard_map/all_gather | solution.py:1080
  133.5 490.4 %all-gather.12.cloned.1.call-start = ((), (), s32[]{:S(2)}) async-start(), calls=%async_computation.8 | async-start | bytes 15728640 | tf_op jit(solution)/shard_map/all_gather | solution.py:1080
  139.9 3.7 collective-permute-start.1
  294.7 395.0 %all-gather.10.cloned.1.call-start = ((), (), s32[]{:S(2)}) async-start(), calls=%async_computation.7 | async-start | bytes 15728640 | tf_op jit(solution)/shard_map/all_gather | solution.py:1080
  303.6 5.9 collective-permute-start.2
  314.5 212.3 %copy-start.13 = (f32[1024,96]{1,0:T(8,128)}, f32[1024,96]{1,0:T(8,128)S(1)}, u32[]{:S(2)}) copy-start(f32[1024,96]{1,0:T(8,128)S(1)} %pad_maximum_fusion.5.refs_3_.refs_12_) | copy-start | bytes 1179652
  426.9 469.8 %all-gather.14.cloned.1.call-start = ((), (), s32[]{:S(2)}) async-start(), calls=%async_computation.9 | async-start | bytes 15728640 | tf_op jit(solution)/shard_map/all_gather | solution.py:1080
  427.5 259.7 %copy-start.121 = (f32[3072]{0:T(1024)}, f32[3072]{0:T(1024)S(1)}, u32[]{:S(2)}) copy-start(f32[3072]{0:T(1024)S(1)} %convert_element_type.124) | copy-start | bytes 36868
  593.4 679.6 %reduce-scatter.6.cloned.1.call-start = ((), (), s32[]{:S(2)}) async-start(), calls=%async_computation.10 | async-start | bytes 15728640 | tf_op jit(solution)/shard_map/reduce_scatter | solution.py:1083
  896.6 514.6 %reduce-scatter.8.cloned.1.call-start = ((), (), s32[]{:S(2)}) async-start(), calls=%async_computation.11 | async-start | bytes 15728640 | tf_op jit(solution)/shard_map/reduce_scatter | solution.py:1083
  980.3 699.6 %reduce-scatter.10.cloned.1.call-start = ((), (), s32[]{:S(2)}) async-start(), calls=%async_computation.12 | async-start | bytes 15728640 | tf_op jit(solution)/shard_map/reduce_scatter | solution.py:1083
  1124.7 708.4 %reduce-scatter.14.cloned.1.call-start = ((), (), s32[]{:S(2)}) async-start(), calls=%async_computation.14 | async-start | bytes 5898240 | tf_op jit(solution)/shard_map/reduce_scatter | solution.py:1083
  1325.3 540.3 %reduce-scatter.12.cloned.1.call-start = ((), (), s32[]{:S(2)}) async-start(), calls=%async_computation.13 | async-start | bytes 17694720 | tf_op jit(solution)/shard_map/reduce_scatter | solution.py:1083
  1685.2 71.8 %collective-permute-start.3 = (bf16[384,2048]{1,0:T(8,128)(2,1)S(1)}, bf16[384,2048]{1,0:T(8,128)(2,1)S(1)}, u32[]{:S(2)}, u32[]{:S(2)}) collective-permute-start(bf16[384,2048]{1,0:T(8,128)(2,1)S(1)} %get-tuple-element.583), channel_id=1, source_target_pairs={{0,2},{1,3},{2,0},{3,1},{4,6},{5,7},{6,4},{7,5},{8,10},{9,11},{10,... | collective-permute-start | bytes 4718600 | tf_op jit(solution)/shard_map/ppermute | solution.py:1048
  1757.0 70.6 %collective-permute-start.4 = (bf16[256,3072]{1,0:T(8,128)(2,1)}, bf16[256,3072]{1,0:T(8,128)(2,1)}, u32[]{:S(2)}, u32[]{:S(2)}) collective-permute-start(bf16[256,3072]{1,0:T(8,128)(2,1)} %get-tuple-element.589), channel_id=1, source_target_pairs={{0,2},{1,3},{2,0},{3,1},{4,6},{5,7},{6,4},{7,5},{8,10},{9,11},{10,... | collective-permute-start | bytes 4718600 | tf_op jit(solution)/shard_map/ppermute | solution.py:1048
  1836.4 28.1 %collective-permute-start.10 = (bf16[96,3072]{1,0:T(8,128)(2,1)S(1)}, bf16[96,3072]{1,0:T(8,128)(2,1)S(1)}, u32[]{:S(2)}, u32[]{:S(2)}) collective-permute-start(bf16[96,3072]{1,0:T(8,128)(2,1)S(1)} %get-tuple-element.603), channel_id=1, source_target_pairs={{0,2},{1,3},{2,0},{3,1},{4,6},{5,7},{6,4},{7,5},{8,10},{9,11},{10,... | collective-permute-start | bytes 1769480 | tf_op jit(solution)/shard_map/ppermute | solution.py:1048
  1837.1 34.5 %collective-permute-start.5 = (f32[2,1536]{1,0:T(2,128)}, f32[2,1536]{1,0:T(2,128)}, u32[]{:S(2)}, u32[]{:S(2)}) collective-permute-start(f32[2,1536]{1,0:T(2,128)} %bitcast.82), channel_id=1, source_target_pairs={{0,16},{4,20},{8,24},{12,28},{16,0},{20,4},{24,8},{28,12},{1,17},{... | collective-permute-start | bytes 36872 | tf_op jit(solution)/shard_map/ppermute | solution.py:1109
  1871.5 93.7 %collective-permute-start.11 = (bf16[384,2304]{1,0:T(8,128)(2,1)S(1)}, bf16[384,2304]{1,0:T(8,128)(2,1)}, u32[]{:S(2)}, u32[]{:S(2)}) collective-permute-start(bf16[384,2304]{1,0:T(8,128)(2,1)S(1)} %get-tuple-element.608), channel_id=1, source_target_pairs={{0,2},{1,3},{2,0},{3,1},{4,6},{5,7},{6,4},{7,5},{8,10},{9,11},{10,... | collective-permute-start | bytes 5308424 | tf_op jit(solution)/shard_map/ppermute | solution.py:1048
  1874.3 3.6 collective-permute-start.6
  1878.6 1.2 collective-permute-start.7
  1879.9 70.8 %collective-permute-start.8 = (f32[2,192]{1,0:T(2,128)S(1)}, f32[2,192]{1,0:T(2,128)S(1)}, u32[]{:S(2)}, u32[]{:S(2)}) collective-permute-start(f32[2,192]{1,0:T(2,128)S(1)} %bitcast.111), channel_id=1, source_target_pairs={{0,2},{1,3},{2,0},{3,1},{4,6},{5,7},{6,4},{7,5},{8,10},{9,11},{10,... | collective-permute-start | bytes 4616 | tf_op jit(solution)/shard_map/ppermute | solution.py:1109
  1950.8 3.6 collective-permute-start.9
  (138 other events, 1691.8 us)
Sparse Core Ops, SparseCore 0:
  132.9 135.8 all-gather.5
  270.6 57.0 all-gather.7
  329.6 122.5 all-gather.11
  453.8 122.4 all-gather.9
  593.5 121.8 all-gather.13
  896.7 119.9 reduce-scatter.5
  1019.8 120.7 reduce-scatter.7
  1143.7 120.6 reduce-scatter.9
  1325.5 55.8 reduce-scatter.13
  1462.2 133.0 reduce-scatter.11

commit v4 on v3

--- a/solution.py
+++ b/solution.py
@@ -746,7 +746,7 @@
     )
 
 
-next_key = [10]
+next_key = [11]
 
 
 def sibling_id():
@@ -814,6 +814,49 @@
     return exchange_call(
         gather_kernel, 1, [own, near], [jax.ShapeDtypeStruct(shape, own.dtype)],
         [pltpu.SemaphoreType.DMA((2,))] * 3,
+    )
+
+
+def gather_two_kernel(
+    own_ref, own_near_ref, got_ref, got_near_ref, first_ref, second_ref, local, send, receive
+):
+    partner = sibling_id()
+    far = lax.axis_index("tp") // 2
+    meet(partner)
+    count = own_ref.shape[0]
+
+    def run(targets):
+        copies = []
+        for place, ref in enumerate((own_ref, own_near_ref, got_ref, got_near_ref)):
+            target, row = targets[place // 2], place % 2
+            remote = push(
+                ref, target.at[pl.ds((2 + row) * count, count)],
+                send.at[place], receive.at[place], partner,
+            )
+            remote.start()
+            copy = pltpu.make_async_copy(
+                ref, target.at[pl.ds(row * count, count)], local.at[place]
+            )
+            copy.start()
+            copies += [remote, copy]
+        for copy in copies:
+            copy.wait()
+
+    @pl.when(far == 0)
+    def _():
+        run((first_ref, second_ref))
+
+    @pl.when(far != 0)
+    def _():
+        run((second_ref, first_ref))
+
+
+def core_gather_two(own, own_near, got, got_near):
+    shape = (4 * own.shape[0], own.shape[1])
+    return exchange_call(
+        gather_two_kernel, 11, [own, own_near, got, got_near],
+        [jax.ShapeDtypeStruct(shape, own.dtype)] * 2,
+        [pltpu.SemaphoreType.DMA((4,))] * 3,
     )
 
 
@@ -1139,17 +1182,20 @@
     qkv_local = qkv_weight.reshape(qkv_weight.shape[0], 3 * local_cols)
     gate_local, up_local = gate_up_weight[:, 0], gate_up_weight[:, 1]
 
-    next_key[0] = 10
+    next_key[0] = 11
     position_got = swap_far(pick(doc_positions, 1 - far))
-    out_other = swap(("far", out_weight))
-    out_full = gather_weight(3, out_weight, out_other)
-    first, second = act(place_tokens, doc_positions, position_got)
+    first, second = place_tokens(doc_positions, position_got)
     near_both = swap_near(join(first, second))
-    qkv_other = swap(("far", qkv_local))
+
+    def first_norm(part):
+        stream = part.astype(jnp.float32)
+        return (stream, *rms_pack(stream, gain_one))
+
+    s_own, r_own, n_own = act(lambda value: first_norm(pick(value, far)), block_in)
+    near_own, qkv_other = swap(("near", n_own), ("far", qkv_local))
     qkv_full = gather_weight(4, qkv_local, qkv_other)
-    first, second = act(
-        lambda a, b, c: (join(a, c[: a.shape[0]]), join(b, c[a.shape[0] :])),
-        first, second, near_both,
+    first, second = (
+        join(first, near_both[: first.shape[0]]), join(second, near_both[first.shape[0] :])
     )
     core_both = swap_core(join(first, second))
 
@@ -1158,17 +1204,17 @@
         late = join(second, both[count:])
         return (*head_tables(join(first, both[:count])), *head_tables(late), late[:, None])
 
-    stream_got = swap(("far", pick(block_in, 1 - far)))
-
-    def first_norm(value, got):
-        streams = [part.astype(jnp.float32) for part in place_tokens(value, got)]
-        return (*streams, *rms_pack(streams[0], gain_one), *rms_pack(streams[1], gain_one))
-
-    s_first, s_second, r_first, n_first, r_second, n_second = act(first_norm, block_in, stream_got)
-    streams, scales_one = [s_first, s_second], [r_first, r_second]
-    near_first, gate_other = swap(("near", n_first), ("far", gate_local))
+    c_own = pick(out_cotangent, far)
+    stream_got, c_near_own, out_other = swap(
+        ("far", pick(block_in, 1 - far)), ("near", c_own), ("far", out_weight)
+    )
+    out_full = gather_weight(3, out_weight, out_other)
+    s_got, r_got, n_got = act(first_norm, stream_got)
+    near_got, gate_other = swap(("near", n_got), ("far", gate_local))
     gate_full = gather_weight(5, gate_local, gate_other)
-    h1_first = act(core_gather, n_first, near_first)
+    h1_first, h1_second = act(core_gather_two, n_own, near_own, n_got, near_got)
+    streams = [jnp.where(far == 0, s_own, s_got), jnp.where(far == 0, s_got, s_own)]
+    scales_one = [jnp.where(far == 0, r_own, r_got), jnp.where(far == 0, r_got, r_own)]
 
     def attend_first(projected, pushes=()):
         arrays = [projected, projected, projected, *tables[0]]
@@ -1190,13 +1236,10 @@
         make_tables, first, second, core_both
     )
     tables = [(cos_first, sin_first), (cos_second, sin_second)]
-    projected, near_second, up_early = act(
-        wide_dot, h1_first, qkv_full, sends=[("near", n_second), ("far", up_halves[0])]
-    )
+    projected, up_early = act(wide_dot, h1_first, qkv_full, sends=[("far", up_halves[0])])
     *results, up_late = act(attend_first, projected, sends=[("far", up_halves[1])])
     saved, lses, mixed_first = [results[:3]], [results[4]], results[3]
     up_full = gather_weight(7, up_local, up_early, up_late)
-    h1_second = act(core_gather, n_second, near_second)
     term_first = act(dot_bf16, mixed_first, out_full)
     keep_first, send_first = act(core_reduce, term_first)
     projected, branch_first, down_early = act(
@@ -1235,16 +1278,12 @@
         rise, h2_first, up_full, gate_first, sends=[("near", n_second), ("far", cot_halves[1])]
     )
     h2_second = act(core_gather, n_second, near_second)
-    c_first, c_second = act(
-        lambda value, early, late: place_tokens(value, join(early, late)),
-        out_cotangent, cot_early, cot_late,
-    )
-    gate_second, near_first = act(wide_dot, h2_second, gate_full, sends=[("near", c_first)])
-    y_first = act(core_gather, c_first, near_first)
-    up_second, a_second, near_second = act(
-        rise, h2_second, up_full, gate_second, sends=[("near", c_second)]
-    )
-    y_second = act(core_gather, c_second, near_second)
+    gate_second, c_near_got = act(
+        wide_dot, h2_second, gate_full, sends=[("near", c_got := join(cot_early, cot_late))]
+    )
+    y_first, y_second = act(core_gather_two, c_own, c_near_own, c_got, c_near_got)
+    c_first, c_second = jnp.where(far == 0, c_own, c_got), jnp.where(far == 0, c_got, c_own)
+    up_second, a_second = act(rise, h2_second, up_full, gate_second)
     down_sum = plane_scatter(act(grad_sum, a_first, y_first, a_second, y_second))
 
     def fall_finish(act_grad, gate, up):
@@ -1284,27 +1323,37 @@
     g_first, n_first, gain_two_first = act(
         second_back, m_first, q_first, keep_first, back_first, c_first
     )
-    grad_up, back_second = act(
-        grad_sum, h2_first, du_first, h2_second, du_second, sends=[("near", send_second)]
+    down_mine, down_away = act(lambda pair: core_split(10, pair), down_sum)
+    down_halves = halve(down_away)
+    grad_up, back_second, down_early = act(
+        grad_sum, h2_first, du_first, h2_second, du_second,
+        sends=[("near", send_second), ("far", down_halves[0])],
     )
     up_sum = plane_scatter(grad_up)
-    mlp_first, near_first = act(dot_bf16, a_first, down_full, sends=[("near", n_first)])
+    mlp_first, near_first, down_late = act(
+        dot_bf16, a_first, down_full, sends=[("near", n_first), ("far", down_halves[1])]
+    )
     g_second, n_second, gain_two_second = act(
         second_back, m_second, q_second, keep_second, back_second, c_second
     )
     d_first = act(core_gather, n_first, near_first)
 
-    mlp_second, near_second = act(dot_bf16, a_second, down_full, sends=[("near", n_second)])
+    gate_mine, gate_away = act(lambda pair: core_split(9, pair), gate_sum)
+    gate_halves = halve(gate_away)
+    mlp_second, near_second, gate_early = act(
+        dot_bf16, a_second, down_full, sends=[("near", n_second), ("far", gate_halves[0])]
+    )
+    mlp_keep_first, mlp_send_first = act(core_reduce, mlp_first)
     heads_first = act(heads_back, d_first, out_full)
     d_second = act(core_gather, n_second, near_second)
     heads_second = act(heads_back, d_second, out_full)
-    mlp_keep_first, mlp_send_first = act(core_reduce, mlp_first)
     mlp_keep_second, mlp_send_second = act(core_reduce, mlp_second)
-    down_mine, down_away = act(lambda pair: core_split(10, pair), down_sum)
-    grad_out, mlp_branch_first = act(
-        grad_sum, mixed_first, d_first, mixed_second, d_second, sends=[("near", mlp_send_first)]
+    grad_out, mlp_branch_first, gate_late = act(
+        grad_sum, mixed_first, d_first, mixed_second, d_second,
+        sends=[("near", mlp_send_first), ("far", gate_halves[1])],
     )
     out_sum = plane_scatter(grad_out)
+    up_mine, up_away = act(lambda pair: core_split(9, pair), up_sum)
 
     def attend_back(heads_first, heads_second, pushes=()):
         return attention_call(
@@ -1319,9 +1368,9 @@
             pushes,
         )
 
-    *grads, mlp_branch_second, down_got = act(
+    *grads, mlp_branch_second, up_got = act(
         attend_back, heads_first, heads_second,
-        sends=[("near", mlp_send_second), ("far", down_away)],
+        sends=[("near", mlp_send_second), ("far", up_away)],
     )
     p_first, p_second = act(
         lambda *parts: (
@@ -1330,28 +1379,24 @@
         ),
         *grads,
     )
-    gate_mine, gate_away = act(lambda pair: core_split(9, pair), gate_sum)
-    gate_halves = halve(gate_away)
-    grad_qkv, gate_early = act(
-        grad_sum, h1_first, p_first, h1_second, p_second, sends=[("far", gate_halves[0])]
-    )
-    qkv_sum = plane_scatter(grad_qkv)
 
     def finish_output(first, first_keep, first_got, second, second_keep, second_got):
         first = (first + first_keep + first_got.astype(jnp.float32)).astype(jnp.bfloat16)
         second = (second + second_keep + second_got.astype(jnp.float32)).astype(jnp.bfloat16)
         return jnp.where(far == 0, first, second), jnp.where(far == 0, second, first)
 
-    term_first, gate_late = act(heads_back, p_first, qkv_full, sends=[("far", gate_halves[1])])
+    term_first = act(heads_back, p_first, qkv_full)
     keep_first, send_first = act(core_reduce, term_first)
+    grad_qkv, back_first = act(
+        grad_sum, h1_first, p_first, h1_second, p_second, sends=[("near", send_first)]
+    )
+    qkv_sum = plane_scatter(grad_qkv)
     out_keep, out_send = act(
         finish_output,
         m_first, mlp_keep_first, mlp_branch_first, m_second, mlp_keep_second, mlp_branch_second,
     )
     out_halves = halve(out_send)
-    term_second, back_first, out_early = act(
-        heads_back, p_second, qkv_full, sends=[("near", send_first), ("far", out_halves[0])]
-    )
+    term_second, out_early = act(heads_back, p_second, qkv_full, sends=[("far", out_halves[0])])
     keep_second, send_second = act(core_reduce, term_second)
 
     def settle(keep, got):
@@ -1376,23 +1421,24 @@
     in_keep, in_send, gain_one_second = act(
         last_back, streams[1], scales_one[1], keep_second, back_second, g_second, i_first
     )
-    up_mine, up_away = act(lambda pair: core_split(9, pair), up_sum)
-    up_got = swap_far(up_away)
-    down_owned = act(add_wide, down_mine, down_got)
+    in_got = swap_far(in_send)
+    block_out = act(
+        lambda keep, early, late: settle(keep, join(early, late)), out_keep, out_early, out_late
+    )
+    add_halves = lambda mine, early, late: add_wide(mine, join(early, late))
+    down_owned = act(add_halves, down_mine, down_early, down_late)
+    gate_owned = act(add_halves, gate_mine, gate_early, gate_late)
+    up_owned = act(add_wide, up_mine, up_got)
+    gate_up_owned = act(lambda a, b: jnp.stack([a, b], axis=1), gate_owned, up_owned)
+    out_mine, out_away = act(lambda pair: core_split(8, pair), out_sum)
     gains = scatter_gains(
         jnp.stack([gain_one_first + gain_one_second, gain_two_first + gain_two_second])
     )
-    block_out = act(lambda keep, early, late: settle(keep, join(early, late)), out_keep, out_early, out_late)
-    gate_owned = act(lambda mine, early, late: add_wide(mine, join(early, late)), gate_mine, gate_early, gate_late)
-    up_owned = act(add_wide, up_mine, up_got)
-    in_got = swap_far(chained(in_send, up_got))
-    gate_up_owned = act(lambda a, b: jnp.stack([a, b], axis=1), gate_owned, up_owned)
     in_grad = act(lambda keep, got: settle(keep, got.astype(jnp.float32)), in_keep, in_got)
-    out_mine, out_away = act(lambda pair: core_split(8, pair), out_sum)
-    out_back = swap_far(chained(out_away, in_got))
+    qkv_mine, qkv_away = act(lambda pair: core_split(0, pair), qkv_sum)
+    out_back, qkv_back = swap(("far", out_away), ("far", qkv_away))
     out_owned = act(add_wide, out_mine, out_back)
-    qkv_mine, qkv_away = act(lambda pair: core_split(0, pair), qkv_sum)
-    qkv_owned = act(add_wide, qkv_mine, swap_far(qkv_away))
+    qkv_owned = act(add_wide, qkv_mine, qkv_back)
     return (
         block_out,
         in_grad,

time: 1990 us -> 1890 us (0.950)
  waiting for transfers between devices: 230 us -> 45.3 us
  Pallas kernels: 1480 us -> 1570 us
    ppermute x5 -> x2, waiting for transfers between devices: 153 us -> 0.01 us  [swap_far(): return lax.ppermute(value, 'tp', far_pairs)]
    pallas_call x31 -> x29, Pallas kernels: 434 us -> 543 us  [exchange_call(): pl.pallas_call(kernel, out_shape=outs, in_specs=[anywhere] * len(operands...]
    ppermute x5, waiting for transfers between devices: 74.7 us -> 44 us  [scatter_gains(): lax.ppermute(sent, axis, [(i, i ^ step) for i in range(size)])]
    pallas_call x26, Pallas kernels: 1050 us -> 1020 us  [grid_call(): pl.pallas_call(kernel, out_shape=outs, grid=grid, in_specs=in_specs, out_...]
    unnamed x297 -> x295, local copies, waits for them, and re-layouts: 137 us -> 136 us
  transfers between devices with their start and end apart: 22 -> 19, of which waited for: 8 -> 2; matrix products, arithmetic and copies ran while one was open for 6% -> 6% of each run, Pallas kernels for 71% -> 73%
where the time goes in v4:
time: 1890 us; the launch traced here: 1880 us
  Pallas kernels  1570 us (83%)
  local copies, waits for them, and re-layouts  168 us (9%)
  other arithmetic  75.1 us (4%)
  waiting for transfers between devices  45.3 us (2%)
    pallas_call x26, Pallas kernels, grid_call(): pl.pallas_call(kernel, out_shape=outs, grid=grid, in_specs=in_specs, out_...  1020 us
    pallas_call x29, Pallas kernels, exchange_call(): pl.pallas_call(kernel, out_shape=outs, in_specs=[anywhere] * len(operands...  543 us
    unnamed x295, local copies, waits for them, and re-layouts  136 us
    ppermute x5, waiting for transfers between devices, scatter_gains(): lax.ppermute(sent, axis, [(i, i ^ step) for i in range(size)])  44 us
  transfers between devices with their start and end apart: 19, of which 2 were waited for; matrix products, arithmetic and copies ran while one was open for 6% of the time, Pallas kernels for 73%

profile of v4, /device:TPU:0, one launch (start us, length us, event | category | flops | bytes accessed | tf_op | source)
XLA Modules:
  0.0 1879.8 jit_solution(3348820249626549820)
XLA Ops:
  18.1 82.0 %shard_map.152 = (bf16[256,3072]{1,0:T(8,128)(2,1)S(1)}, bf16[384,2304]{1,0:T(8,128)(2,1)S(1)}) custom-call(bf16[256,3072]{1,0:T(8,128)(2,1)S(1)} %fusion.4.refs_0_.own_ref, bf16[384,2304]{1,0:T(8,128)(2,1)S(1)} %copy.37.refs_1_), custom_call_target="tpu_custom_call" | custom-call | flops 6800000000 | bytes 1000 | tf_op jit(solution)/shard_map/pallas_call | solution.py:776
  114.2 96.2 %shard_map.154 = (bf16[256,3072]{1,0:T(8,128)(2,1)S(1)}, bf16[256,3072]{1,0:T(8,128)(2,1)S(1)}, bf16[96,3072]{1,0:T(8,128)(2,1)S(1)}) custom-call(bf16[256,3072]{1,0:T(8,128)(2,1)S(1)} %dynamic-slice_bitcast_fusion.1.refs_0_, bf16[256,3072]{1,0:T(8,128)(2,1)S(1)} %dynamic-slice_bitcast_fusion.refs_1_.own_ref, bf16[96,3072]{1,0:T(8,128)(2,1)S(1)} %copy-done.62), custom_call_target="tpu_custom_call" | custom-call | flops 6800000000 | bytes 1000 | tf_op jit(solution)/shard_map/pallas_call | solution.py:776
  230.4 71.2 %shard_map.156 = (bf16[256,3072]{1,0:T(8,128)(2,1)S(1)}, bf16[384,2048]{1,0:T(8,128)(2,1)S(1)}) custom-call(bf16[256,3072]{1,0:T(8,128)(2,1)S(1)} %multiply_convert_fusion.2.refs_0_.got_ref, bf16[384,2048]{1,0:T(8,128)(2,1)S(1)} %bitcast.85), custom_call_target="tpu_custom_call" | custom-call | flops 6800000000 | bytes 1000 | tf_op jit(solution)/shard_map/pallas_call | solution.py:776
  338.2 43.6 %shard_map.159 = (f32[1024,2304]{1,0:T(8,128)}, bf16[192,2048]{1,0:T(8,128)(2,1)S(1)}) custom-call(bf16[1024,3072]{1,0:T(8,128)(2,1)} %copy-done.75, bf16[3072,2304]{1,0:T(8,128)(2,1)} %all-gather.6.cloned.1.call-done.refs_1_, bf16[192,2048]{1,0:T(8,128)(2,1)S(1)} %bitcast.88), custom_call_target="tpu_custom_call" | custom-call | flops 24642375680 | bytes 1000 | tf_op jit(solution)/shard_map/pallas_call | solution.py:718
  381.8 37.5 %shard_map.160 = (bf16[1024,768]{1,0:T(8,128)(2,1)S(1)}, bf16[1024,768]{1,0:T(8,128)(2,1)S(1)}, bf16[1024,768]{1,0:T(8,128)(2,1)S(1)}, bf16[1024,768]{1,0:T(8,12...) custom-call(f32[1024,2304]{1,0:T(8,128)} %get-tuple-element.353.refs_0_.refs_1_.refs_2_, ...), custom_call_target="tpu_custom_call" | custom-call | flops 8556380160 | bytes 1000 | tf_op jit(solution)/shard_map/pallas_call | solution.py:718
  452.6 59.7 %shard_map.164 = (f32[1024,2304]{1,0:T(8,128)}, bf16[256,3072]{1,0:T(8,128)(2,1)S(1)}, bf16[128,3072]{1,0:T(8,128)(2,1)S(1)}) custom-call(bf16[1024,3072]{1,0:T(8,128)(2,1)} %copy-done.76, bf16[3072,2304]{1,0:T(8,128)(2,1)} %all-gather.6.cloned.1.call-done.refs_1_, bf16[256,3072]{1,0:T(8,128)(2,1)S(1)} %get-tuple-element.370.refs_2_, ...), custom_call_target="tpu_custom_call" | custom-call | flops 24642375680 | bytes 1000 | tf_op jit(solution)/shard_map/pallas_call | solution.py:718
  515.7 55.7 %shard_map.165 = (bf16[1024,768]{1,0:T(8,128)(2,1)S(1)}, bf16[1024,768]{1,0:T(8,128)(2,1)S(1)}, bf16[1024,768]{1,0:T(8,128)(2,1)S(1)}, bf16[1024,768]{1,0:T(8,12...) custom-call(f32[1024,2304]{1,0:T(8,128)} %get-tuple-element.378.refs_0_.refs_1_, ...), custom_call_target="tpu_custom_call" | custom-call | flops 8556380160 | bytes 1000 | tf_op jit(solution)/shard_map/pallas_call | solution.py:718
  615.8 59.5 %shard_map.170 = (f32[1024,2048]{1,0:T(8,128)}, bf16[256,3072]{1,0:T(8,128)(2,1)S(1)}, bf16[128,3072]{1,0:T(8,128)(2,1)S(1)}) custom-call(bf16[1024,3072]{1,0:T(8,128)(2,1)} %copy-done.69, bf16[3072,2048]{1,0:T(8,128)(2,1)} %all-gather.12.cloned.1.call-done.refs_1_.refs_2_, bf16[256,3072]{1,0:T(8,128)(2,1)S(1)} %copy-done.96, bf16[128,3072]{1,0:T(8,128)(2,1)S(1)} %copy-done.41), custom_call_target="tpu_custom_call" | custom-call | flops 21904332800 | bytes 1000 | tf_op jit(solution)/shard_map/pallas_call | solution.py:718
  679.3 59.4 %shard_map.171 = (f32[1024,2048]{1,0:T(8,128)}, bf16[1024,2048]{1,0:T(8,128)(2,1)}, bf16[256,3072]{1,0:T(8,128)(2,1)S(1)}, bf16[128,3072]{1,0:T(8,128)(2,1)S(1)}) custom-call(bf16[1024,3072]{1,0:T(8,128)(2,1)} %copy-done.69, bf16[3072,2048]{1,0:T(8,128)(2,1)} %all-gather.10.cloned.1.call-done.refs_1_.refs_3_, f32[1024,2048]{1,0:T(8,128)} %get-tuple-element.440.refs_2_, ...), custom_call_target="tpu_custom_call" | custom-call | flops 21904332800 | bytes 1000 | tf_op jit(solution)/shard_map/pallas_call | solution.py:718
  747.2 41.8 %shard_map.173 = (f32[1024,2048]{1,0:T(8,128)}, bf16[256,3072]{1,0:T(8,128)(2,1)S(1)}) custom-call(bf16[1024,3072]{1,0:T(8,128)(2,1)} %copy-done.70, bf16[3072,2048]{1,0:T(8,128)(2,1)} %all-gather.12.cloned.1.call-done.refs_1_.refs_2_, bf16[256,3072]{1,0:T(8,128)(2,1)S(1)} %constant_dynamic-update-slice_fusion.refs_2_.got_ref), custom_call_target="tpu_custom_call" | custom-call | flops 21904332800 | bytes 1000 | tf_op jit(solution)/shard_map/pallas_call | solution.py:718
  826.4 35.2 %shard_map.176 = bf16[2048,3072]{1,0:T(8,128)(2,1)} custom-call(bf16[1024,2048]{1,0:T(8,128)(2,1)S(1)} %copy-done.101, bf16[1024,2048]{1,0:T(8,128)(2,1)} %copy-done.102, bf16[1024,3072]{1,0:T(8,128)(2,1)} %copy-done.78, bf16[1024,3072]{1,0:T(8,128)(2,1)} %copy-done.77), custom_call_target="tpu_custom_call" | custom-call | flops 43808665600 | bytes 1000 | tf_op jit(solution)/shard_map/pallas_call | solution.py:718
  912.8 33.1 %shard_map.179 = bf16[3072,2048]{1,0:T(8,128)(2,1)} custom-call(bf16[1024,3072]{1,0:T(8,128)(2,1)} %copy-done.69, bf16[1024,3072]{1,0:T(8,128)(2,1)} %copy-done.70, bf16[1024,2048]{1,0:T(8,128)(2,1)S(1)} %get-tuple-element.454.refs_2_.refs_0_, bf16[1024,2048]{1,0:T(8,128)(2,1)} %copy-done.98), custom_call_target="tpu_custom_call" | custom-call | flops 43808665600 | bytes 1000 | tf_op jit(solution)/shard_map/pallas_call | solution.py:718
  948.2 31.8 %shard_map.180.term_ref = bf16[1024,3072]{1,0:T(8,128)(2,1)} custom-call(bf16[1024,2048]{1,0:T(8,128)(2,1)S(1)} %copy-done.100, bf16[1024,2048]{1,0:T(8,128)(2,1)} %get-tuple-element.479.refs_1_.refs_2_, bf16[3072,2048]{1,0:T(8,128)(2,1)} %all-gather.12.cloned.1.call-done.refs_1_.refs_2_, bf16[3072,2048]{1,0:T(8,128)(2,1)} %all-gather.10.cloned.1.call-done.refs_1_.refs_3_), custom_call_target="tpu_custom_call" | custom-call | flops 43808665600 | bytes 1000 | tf_op jit(solution)/shard_map/pallas_call | solution.py:718
  988.8 43.5 %shard_map.182 = (bf16[1024,3072]{1,0:T(8,128)(2,1)}, bf16[256,3072]{1,0:T(8,128)(2,1)S(1)}) custom-call(bf16[1024,2048]{1,0:T(8,128)(2,1)} %copy-done.98, bf16[1024,2048]{1,0:T(8,128)(2,1)} %get-tuple-element.480.refs_1_.refs_3_, bf16[3072,2048]{1,0:T(8,128)(2,1)} %all-gather.12.cloned.1.call-done.refs_1_.refs_2_, ...), custom_call_target="tpu_custom_call" | custom-call | flops 43808665600 | bytes 1000 | tf_op jit(solution)/shard_map/pallas_call | solution.py:718
  1058.5 59.6 %shard_map.185 = (bf16[3072,2048]{1,0:T(8,128)(2,1)}, bf16[256,3072]{1,0:T(8,128)(2,1)S(1)}, bf16[128,3072]{1,0:T(8,128)(2,1)S(1)}) custom-call(bf16[1024,3072]{1,0:T(8,128)(2,1)} %copy-done.69, bf16[1024,3072]{1,0:T(8,128)(2,1)} %copy-done.70, bf16[1024,2048]{1,0:T(8,128)(2,1)} %get-tuple-element.479.refs_1_.refs_2_, ...), custom_call_target="tpu_custom_call" | custom-call | flops 43808665600 | bytes 1000 | tf_op jit(solution)/shard_map/pallas_call | solution.py:718
  1122.7 57.1 %shard_map.186 = (bf16[1024,3072]{1,0:T(8,128)(2,1)}, bf16[256,3072]{1,0:T(8,128)(2,1)S(1)}, bf16[128,3072]{1,0:T(8,128)(2,1)S(1)}) custom-call(bf16[1024,2048]{1,0:T(8,128)(2,1)} %get-tuple-element.486.refs_0_, bf16[2048,3072]{1,0:T(8,128)(2,1)} %all-gather.14.cloned.1.call-done.refs_1_, bf16[256,3072]{1,0:T(8,128)(2,1)S(1)} %copy-done.31, ...), custom_call_target="tpu_custom_call" | custom-call | flops 21904332800 | bytes 1000 | tf_op jit(solution)/shard_map/pallas_call | solution.py:718
  1201.1 58.6 %shard_map.189 = (bf16[1024,3072]{1,0:T(8,128)(2,1)}, bf16[256,3072]{1,0:T(8,128)(2,1)S(1)}, bf16[192,2048]{1,0:T(8,128)(2,1)S(1)}) custom-call(bf16[1024,2048]{1,0:T(8,128)(2,1)} %copy-done.102, bf16[2048,3072]{1,0:T(8,128)(2,1)} %all-gather.14.cloned.1.call-done.refs_1_, bf16[256,3072]{1,0:T(8,128)(2,1)S(1)} %copy-done.32, ...), custom_call_target="tpu_custom_call" | custom-call | flops 21904332800 | bytes 1000 | tf_op jit(solution)/shard_map/pallas_call | solution.py:718
  1305.9 61.4 %shard_map.195 = (bf16[768,3072]{1,0:T(8,128)(2,1)}, bf16[256,3072]{1,0:T(8,128)(2,1)S(1)}, bf16[192,2048]{1,0:T(8,128)(2,1)S(1)}) custom-call(bf16[1024,768]{1,0:T(8,128)(2,1)S(1)} %copy-done.66, bf16[1024,768]{1,0:T(8,128)(2,1)} %copy-done.55, bf16[1024,3072]{1,0:T(8,128)(2,1)} %copy-done.71, bf16[1024,3072]{1,0:T(8,128)(2,1)} %copy-done.72, ...), custom_call_target="tpu_custom_call" | custom-call | flops 16428250112 | bytes 1000 | tf_op jit(solution)/shard_map/pallas_call | solution.py:718
  1377.3 74.3 %shard_map.197 = (bf16[1024,768]{1,0:T(8,128)(2,1)S(1)}, bf16[1024,768]{1,0:T(8,128)(2,1)S(1)}, bf16[1024,768]{1,0:T(8,128)(2,1)S(1)}, bf16[1024,768]{1,0:T(8,12...) custom-call(bf16[1024,768]{1,0:T(8,128)(2,1)} %copy-done.63, ...), custom_call_target="tpu_custom_call" | custom-call | flops 12321187840 | bytes 1000 | tf_op jit(solution)/shard_map/pallas_call | solution.py:718
  1483.4 43.2 %shard_map.200 = (bf16[3072,2304]{1,0:T(8,128)(2,1)}, bf16[256,3072]{1,0:T(8,128)(2,1)S(1)}) custom-call(bf16[1024,3072]{1,0:T(8,128)(2,1)} %copy-done.75, bf16[1024,3072]{1,0:T(8,128)(2,1)} %copy-done.76, bf16[1024,2304]{1,0:T(8,128)(2,1)} %copy-done.45, bf16[1024,2304]{1,0:T(8,128)(2,1)} %copy-done.124, bf16[256,3072]{1,0:T(8,128)(2,1)S(1)} %get-tuple-element.559.refs_4_), custom_call_target="tpu_custom_call" | custom-call | flops 49284751360 | bytes 1000 | tf_op jit(solution)/shard_map/pallas_call | solution.py:718
  1537.4 41.0 %shard_map.201 = (bf16[1024,3072]{1,0:T(8,128)(2,1)}, bf16[128,3072]{1,0:T(8,128)(2,1)S(1)}) custom-call(bf16[1024,2304]{1,0:T(8,128)(2,1)} %copy-done.124, bf16[3072,2304]{1,0:T(8,128)(2,1)} %all-gather.6.cloned.1.call-done.refs_1_, bf16[128,3072]{1,0:T(8,128)(2,1)S(1)} %get-tuple-element.570.refs_2_), custom_call_target="tpu_custom_call" | custom-call | flops 24642375680 | bytes 1000 | tf_op jit(solution)/shard_map/pallas_call | solution.py:718
  1587.6 59.3 %shard_map.203 = (bf16[256,3072]{1,0:T(8,128)(2,1)S(1)}, bf16[128,3072]{1,0:T(8,128)(2,1)S(1)}) custom-call(bf16[256,3072]{1,0:T(8,128)(2,1)S(1)} %get-tuple-element.575.refs_0_, bf16[128,3072]{1,0:T(8,128)(2,1)S(1)} %get-tuple-element.576.refs_1_), custom_call_target="tpu_custom_call" | custom-call | flops 6800000000 | bytes 1000 | tf_op jit(solution)/shard_map/pallas_call | solution.py:776
  1683.9 44.0 %collective-permute-done.7 = f32[2,192]{1,0:T(2,128)S(1)} collective-permute-done((f32[2,192]{1,0:T(2,128)S(1)}, f32[2,192]{1,0:T(2,128)S(1)}, u32[]{:S(2)}, u32[]{:S(2)}) %collective-permute-start.7) | collective-permute-done | bytes 1568 | tf_op jit(solution)/shard_map/ppermute | solution.py:1152
  1753.9 109.2 %shard_map.206 = (bf16[96,3072]{1,0:T(8,128)(2,1)S(1)}, bf16[384,2304]{1,0:T(8,128)(2,1)S(1)}) custom-call(bf16[96,3072]{1,0:T(8,128)(2,1)S(1)} %get-tuple-element.612.refs_0_, bf16[384,2304]{1,0:T(8,128)(2,1)S(1)} %get-tuple-element.613.refs_1_), custom_call_target="tpu_custom_call" | custom-call | flops 6800000000 | bytes 1000 | tf_op jit(solution)/shard_map/pallas_call | solution.py:776
  (471 shorter events, 505.9 us)
Async XLA Ops:
  7.2 329.9 %all-gather.6.cloned.1.call-start = ((), (), s32[]{:S(2)}) async-start(), calls=%async_computation.5 | async-start | bytes 17694720 | tf_op jit(solution)/shard_map/all_gather | solution.py:1123
  9.7 220.1 %copy-start.120 = (f32[3072]{0:T(1024)}, f32[3072]{0:T(1024)S(1)}, u32[]{:S(2)}) copy-start(f32[3072]{0:T(1024)S(1)} %convert_element_type.121) | copy-start | bytes 36868
  110.5 320.7 %all-gather.8.cloned.1.call-start = ((), (), s32[]{:S(2)}) async-start(), calls=%async_computation.6 | async-start | bytes 5898240 | tf_op jit(solution)/shard_map/all_gather | solution.py:1123
  112.1 98.3 %copy-start.29 = (bf16[256,3072]{1,0:T(8,128)(2,1)}, bf16[256,3072]{1,0:T(8,128)(2,1)S(1)}, u32[]{:S(2)}) copy-start(bf16[256,3072]{1,0:T(8,128)(2,1)S(1)} %dynamic-slice_bitcast_fusion.refs_1_.own_ref) | copy-start | bytes 4718596
  214.6 398.6 %all-gather.12.cloned.1.call-start = ((), (), s32[]{:S(2)}) async-start(), calls=%async_computation.8 | async-start | bytes 15728640 | tf_op jit(solution)/shard_map/all_gather | solution.py:1123
  305.3 372.9 %all-gather.10.cloned.1.call-start = ((), (), s32[]{:S(2)}) async-start(), calls=%async_computation.7 | async-start | bytes 15728640 | tf_op jit(solution)/shard_map/all_gather | solution.py:1123
  305.9 18.5 collective-permute-start
  324.4 5.1 collective-permute-start.1
  329.6 1.2 collective-permute-start.2
  335.8 179.6 %copy-start.11 = (f32[1024,96]{1,0:T(8,128)}, f32[1024,96]{1,0:T(8,128)S(1)}, u32[]{:S(2)}) copy-start(f32[1024,96]{1,0:T(8,128)S(1)} %pad_maximum_fusion.5.refs_3_.refs_12_) | copy-start | bytes 1179652
  336.0 179.4 %copy-start.9 = (f32[1024,96]{1,0:T(8,128)}, f32[1024,96]{1,0:T(8,128)S(1)}, u32[]{:S(2)}) copy-start(f32[1024,96]{1,0:T(8,128)S(1)} %pad_maximum_fusion.6.refs_4_.refs_13_) | copy-start | bytes 1179652
  428.5 433.6 %all-gather.14.cloned.1.call-start = ((), (), s32[]{:S(2)}) async-start(), calls=%async_computation.9 | async-start | bytes 15728640 | tf_op jit(solution)/shard_map/all_gather | solution.py:1123
  429.9 246.3 %copy-start.122 = (f32[3072]{0:T(1024)}, f32[3072]{0:T(1024)S(1)}, u32[]{:S(2)}) copy-start(f32[3072]{0:T(1024)S(1)} %convert_element_type.128) | copy-start | bytes 36868
  582.0 468.6 %reduce-scatter.6.cloned.1.call-start = ((), (), s32[]{:S(2)}) async-start(), calls=%async_computation.10 | async-start | bytes 15728640 | tf_op jit(solution)/shard_map/reduce_scatter | solution.py:1126
  861.7 332.1 %reduce-scatter.8.cloned.1.call-start = ((), (), s32[]{:S(2)}) async-start(), calls=%async_computation.11 | async-start | bytes 15728640 | tf_op jit(solution)/shard_map/reduce_scatter | solution.py:1126
  945.9 423.6 %reduce-scatter.10.cloned.1.call-start = ((), (), s32[]{:S(2)}) async-start(), calls=%async_computation.12 | async-start | bytes 15728640 | tf_op jit(solution)/shard_map/reduce_scatter | solution.py:1126
  1120.1 563.8 %reduce-scatter.12.cloned.1.call-start = ((), (), s32[]{:S(2)}) async-start(), calls=%async_computation.13 | async-start | bytes 5898240 | tf_op jit(solution)/shard_map/reduce_scatter | solution.py:1126
  1369.4 378.8 %reduce-scatter.14.cloned.1.call-start = ((), (), s32[]{:S(2)}) async-start(), calls=%async_computation.14 | async-start | bytes 17694720 | tf_op jit(solution)/shard_map/reduce_scatter | solution.py:1126
  1657.1 85.5 %collective-permute-start.3 = (bf16[256,3072]{1,0:T(8,128)(2,1)}, bf16[256,3072]{1,0:T(8,128)(2,1)}, u32[]{:S(2)}, u32[]{:S(2)}) collective-permute-start(bf16[256,3072]{1,0:T(8,128)(2,1)} %get-tuple-element.652), channel_id=1, source_target_pairs={{0,2},{1,3},{2,0},{3,1},{4,6},{5,7},{6,4},{7,5},{8,10},{9,11},{10,... | collective-permute-start | bytes 4718600 | tf_op jit(solution)/shard_map/ppermute | solution.py:1091
  1664.5 5.1 collective-permute-start.4
  1669.6 5.0 collective-permute-start.5
  1674.6 2.4 collective-permute-start.6
  1677.1 50.8 %collective-permute-start.7 = (f32[2,192]{1,0:T(2,128)S(1)}, f32[2,192]{1,0:T(2,128)S(1)}, u32[]{:S(2)}, u32[]{:S(2)}) collective-permute-start(f32[2,192]{1,0:T(2,128)S(1)} %bitcast.113), channel_id=1, source_target_pairs={{0,2},{1,3},{2,0},{3,1},{4,6},{5,7},{6,4},{7,5},{8,10},{9,11},{10,... | collective-permute-start | bytes 4616 | tf_op jit(solution)/shard_map/ppermute | solution.py:1152
  1728.0 14.1 collective-permute-start.8
  (134 other events, 1539.6 us)
Sparse Core Ops, SparseCore 0:
  110.6 135.6 all-gather.5
  248.6 57.0 all-gather.7
  307.6 122.5 all-gather.11
  431.8 122.5 all-gather.9
  582.1 121.9 all-gather.13
  861.8 120.8 reduce-scatter.5
  985.8 120.7 reduce-scatter.7
  1120.3 120.0 reduce-scatter.9
  1369.5 57.5 reduce-scatter.11
  1527.9 133.1 reduce-scatter.13

commit v5 on v4

--- a/solution.py
+++ b/solution.py
@@ -694,7 +694,7 @@
 
 
 def grid_call(
-    kernel, operands, in_specs, outs, out_specs, grid, flops, scratch=(), pushes=(), vmem=48
+    kernel, operands, in_specs, outs, out_specs, grid, flops, scratch=(), pushes=(), vmem=60
 ):
     params = dict(
         dimension_semantics=("arbitrary",) * len(grid), vmem_limit_bytes=vmem * 1024 * 1024
@@ -723,7 +723,7 @@
             out_specs=out_specs,
             scratch_shapes=scratch,
             compiler_params=pltpu.CompilerParams(**params),
-            cost_estimate=cost_of(flops),
+            cost_estimate=cost_of(max(flops, 27 * 10**9) if pushes else flops),
         )(*operands)
     )
 
@@ -742,7 +742,7 @@
     return exchange_call(
         functools.partial(swap_kernel, kinds), next_key[0], values,
         [jax.ShapeDtypeStruct(value.shape, value.dtype) for value in values],
-        [pltpu.SemaphoreType.DMA((len(pushes),))] * 2,
+        [pltpu.SemaphoreType.DMA((len(pushes),))] * 2, flops=200 * 10**9,
     )
 
 
@@ -771,7 +771,7 @@
     )
 
 
-def exchange_call(kernel, key, operands, outs, scratch, vmem=16):
+def exchange_call(kernel, key, operands, outs, scratch, vmem=60, flops=4 * 10**9):
     anywhere = pl.BlockSpec(memory_space=pl.ANY)
     results = pl.pallas_call(
         kernel,
@@ -782,7 +782,7 @@
         compiler_params=pltpu.CompilerParams(
             collective_id=key, has_side_effects=True, vmem_limit_bytes=vmem * 1024 * 1024
         ),
-        cost_estimate=cost_of(4 * 10**9),
+        cost_estimate=cost_of(flops),
     )(*operands)
     return tuple(results) if len(outs) > 1 else results[0]
 
@@ -920,7 +920,6 @@
             pltpu.VMEM((pieces // 2, count, width), term.dtype),
         ]
         + [pltpu.SemaphoreType.DMA((pieces,))] * 4,
-        vmem=24,
     )
 
 
@@ -1030,7 +1029,6 @@
         4 * len(outs[0]) ** 2 * rows * rows * heads_local * HD // 16,
         scratch=scratch(half, width),
         pushes=pushes,
-        vmem=40,
     )
 
 
@@ -1230,20 +1228,20 @@
             ([0, 0, 0, 0, "lse"], heads_local), no_scratch, pushes,
         )
 
-    up_halves, down_halves = halve(up_local), halve(down_weight)
-    cot_halves = halve(pick(out_cotangent, 1 - far))
+    up_other = swap_far(chained(up_local, gate_other))
     cos_first, sin_first, cos_second, sin_second, reach = act(
         make_tables, first, second, core_both
     )
     tables = [(cos_first, sin_first), (cos_second, sin_second)]
-    projected, up_early = act(wide_dot, h1_first, qkv_full, sends=[("far", up_halves[0])])
-    *results, up_late = act(attend_first, projected, sends=[("far", up_halves[1])])
+    projected = act(wide_dot, h1_first, qkv_full)
+    results = act(attend_first, projected)
     saved, lses, mixed_first = [results[:3]], [results[4]], results[3]
-    up_full = gather_weight(7, up_local, up_early, up_late)
     term_first = act(dot_bf16, mixed_first, out_full)
     keep_first, send_first = act(core_reduce, term_first)
-    projected, branch_first, down_early = act(
-        wide_dot, h1_second, qkv_full, sends=[("near", send_first), ("far", down_halves[0])]
+    up_full = gather_weight(5, up_local, up_other)
+    down_other = swap_far(chained(down_weight, up_other))
+    projected, branch_first = act(
+        wide_dot, h1_second, qkv_full, sends=[("near", send_first)]
     )
 
     def second_norm(stream, keep, got):
@@ -1251,19 +1249,19 @@
         return (middle, *rms_pack(middle, gain_two))
 
     m_first, q_first, n_first = act(second_norm, streams[0], keep_first, branch_first)
-    *results, near_first, down_late = act(
-        attend_second, projected, sends=[("near", n_first), ("far", down_halves[1])]
-    )
+    *results, near_first = act(attend_second, projected, sends=[("near", n_first)])
     saved.append(results[:3])
     lses.append(results[4])
     mixed_second = results[3]
-    down_full = gather_weight(6, down_weight, down_early, down_late)
     term_second = act(dot_bf16, mixed_second, out_full)
     keep_second, send_second = act(core_reduce, term_second)
     h2_first = act(core_gather, n_first, near_first)
-
-    gate_first, branch_second, cot_early = act(
-        wide_dot, h2_first, gate_full, sends=[("near", send_second), ("far", cot_halves[0])]
+    down_full_pair = act(lambda own, got: core_pair(6, own, got), down_weight, down_other)
+    down_full = plane_gather(down_full_pair)
+    c_got = swap_far(chained(pick(out_cotangent, 1 - far), down_full_pair))
+
+    gate_first, branch_second = act(
+        wide_dot, h2_first, gate_full, sends=[("near", send_second)]
     )
     m_second, q_second, n_second = act(second_norm, streams[1], keep_second, branch_second)
 
@@ -1274,12 +1272,12 @@
             pushes=pushes,
         )
 
-    up_first, a_first, near_second, cot_late = act(
-        rise, h2_first, up_full, gate_first, sends=[("near", n_second), ("far", cot_halves[1])]
+    up_first, a_first, near_second = act(
+        rise, h2_first, up_full, gate_first, sends=[("near", n_second)]
     )
     h2_second = act(core_gather, n_second, near_second)
     gate_second, c_near_got = act(
-        wide_dot, h2_second, gate_full, sends=[("near", c_got := join(cot_early, cot_late))]
+        wide_dot, h2_second, gate_full, sends=[("near", c_got)]
     )
     y_first, y_second = act(core_gather_two, c_own, c_near_own, c_got, c_near_got)
     c_first, c_second = jnp.where(far == 0, c_own, c_got), jnp.where(far == 0, c_got, c_own)
@@ -1324,33 +1322,27 @@
         second_back, m_first, q_first, keep_first, back_first, c_first
     )
     down_mine, down_away = act(lambda pair: core_split(10, pair), down_sum)
-    down_halves = halve(down_away)
-    grad_up, back_second, down_early = act(
-        grad_sum, h2_first, du_first, h2_second, du_second,
-        sends=[("near", send_second), ("far", down_halves[0])],
+    down_got = swap_far(down_away)
+    grad_up, back_second = act(
+        grad_sum, h2_first, du_first, h2_second, du_second, sends=[("near", send_second)]
     )
     up_sum = plane_scatter(grad_up)
-    mlp_first, near_first, down_late = act(
-        dot_bf16, a_first, down_full, sends=[("near", n_first), ("far", down_halves[1])]
-    )
+    mlp_first, near_first = act(dot_bf16, a_first, down_full, sends=[("near", n_first)])
     g_second, n_second, gain_two_second = act(
         second_back, m_second, q_second, keep_second, back_second, c_second
     )
     d_first = act(core_gather, n_first, near_first)
 
     gate_mine, gate_away = act(lambda pair: core_split(9, pair), gate_sum)
-    gate_halves = halve(gate_away)
-    mlp_second, near_second, gate_early = act(
-        dot_bf16, a_second, down_full, sends=[("near", n_second), ("far", gate_halves[0])]
-    )
+    gate_got = swap_far(gate_away)
+    mlp_second, near_second = act(dot_bf16, a_second, down_full, sends=[("near", n_second)])
     mlp_keep_first, mlp_send_first = act(core_reduce, mlp_first)
     heads_first = act(heads_back, d_first, out_full)
     d_second = act(core_gather, n_second, near_second)
     heads_second = act(heads_back, d_second, out_full)
     mlp_keep_second, mlp_send_second = act(core_reduce, mlp_second)
-    grad_out, mlp_branch_first, gate_late = act(
-        grad_sum, mixed_first, d_first, mixed_second, d_second,
-        sends=[("near", mlp_send_first), ("far", gate_halves[1])],
+    grad_out, mlp_branch_first = act(
+        grad_sum, mixed_first, d_first, mixed_second, d_second, sends=[("near", mlp_send_first)]
     )
     out_sum = plane_scatter(grad_out)
     up_mine, up_away = act(lambda pair: core_split(9, pair), up_sum)
@@ -1368,9 +1360,9 @@
             pushes,
         )
 
-    *grads, mlp_branch_second, up_got = act(
-        attend_back, heads_first, heads_second,
-        sends=[("near", mlp_send_second), ("far", up_away)],
+    up_got = swap_far(up_away)
+    *grads, mlp_branch_second = act(
+        attend_back, heads_first, heads_second, sends=[("near", mlp_send_second)]
     )
     p_first, p_second = act(
         lambda *parts: (
@@ -1385,20 +1377,20 @@
         second = (second + second_keep + second_got.astype(jnp.float32)).astype(jnp.bfloat16)
         return jnp.where(far == 0, first, second), jnp.where(far == 0, second, first)
 
+    out_keep, out_send = act(
+        finish_output,
+        m_first, mlp_keep_first, mlp_branch_first, m_second, mlp_keep_second, mlp_branch_second,
+    )
+    out_got = swap_far(out_send)
     term_first = act(heads_back, p_first, qkv_full)
     keep_first, send_first = act(core_reduce, term_first)
     grad_qkv, back_first = act(
         grad_sum, h1_first, p_first, h1_second, p_second, sends=[("near", send_first)]
     )
     qkv_sum = plane_scatter(grad_qkv)
-    out_keep, out_send = act(
-        finish_output,
-        m_first, mlp_keep_first, mlp_branch_first, m_second, mlp_keep_second, mlp_branch_second,
-    )
-    out_halves = halve(out_send)
-    term_second, out_early = act(heads_back, p_second, qkv_full, sends=[("far", out_halves[0])])
+    term_second = act(heads_back, p_second, qkv_full)
     keep_second, send_second = act(core_reduce, term_second)
-
+    out_mine, out_away = act(lambda pair: core_split(8, pair), out_sum)
     def settle(keep, got):
         return jnp.stack([jnp.where(far == 0, keep, got), jnp.where(far == 0, got, keep)])
 
@@ -1414,7 +1406,7 @@
             gain_term,
         )
 
-    back_second, out_late = swap(("near", send_second), ("far", out_halves[1]))
+    back_second, out_back = swap(("near", send_second), ("far", out_away))
     i_first, gain_one_first = act(
         first_back, streams[0], scales_one[0], keep_first, back_first, g_first
     )
@@ -1422,22 +1414,18 @@
         last_back, streams[1], scales_one[1], keep_second, back_second, g_second, i_first
     )
     in_got = swap_far(in_send)
-    block_out = act(
-        lambda keep, early, late: settle(keep, join(early, late)), out_keep, out_early, out_late
-    )
-    add_halves = lambda mine, early, late: add_wide(mine, join(early, late))
-    down_owned = act(add_halves, down_mine, down_early, down_late)
-    gate_owned = act(add_halves, gate_mine, gate_early, gate_late)
+    down_owned = act(add_wide, down_mine, down_got)
+    gate_owned = act(add_wide, gate_mine, gate_got)
+    block_out = act(settle, out_keep, out_got)
     up_owned = act(add_wide, up_mine, up_got)
     gate_up_owned = act(lambda a, b: jnp.stack([a, b], axis=1), gate_owned, up_owned)
-    out_mine, out_away = act(lambda pair: core_split(8, pair), out_sum)
+    out_owned = act(add_wide, out_mine, out_back)
     gains = scatter_gains(
         jnp.stack([gain_one_first + gain_one_second, gain_two_first + gain_two_second])
     )
     in_grad = act(lambda keep, got: settle(keep, got.astype(jnp.float32)), in_keep, in_got)
     qkv_mine, qkv_away = act(lambda pair: core_split(0, pair), qkv_sum)
-    out_back, qkv_back = swap(("far", out_away), ("far", qkv_away))
-    out_owned = act(add_wide, out_mine, out_back)
+    qkv_back = swap(("far", qkv_away))
     qkv_owned = act(add_wide, qkv_mine, qkv_back)
     return (
         block_out,

time: 1890 us -> 2930 us (1.55)
  Pallas kernels: 1570 us -> 2660 us
  local copies, waits for them, and re-layouts: 168 us -> 61.9 us
    pallas_call x29, Pallas kernels: 543 us -> 1660 us  [exchange_call(): pl.pallas_call(kernel, out_shape=outs, in_specs=[anywhere] * len(operands...]
    unnamed x295 -> x127, local copies, waits for them, and re-layouts: 136 us -> 37.9 us
  transfers between devices with their start and end apart: 19 -> 26, of which waited for: 2 -> 5; matrix products, arithmetic and copies ran while one was open for 6% -> 4% of each run, Pallas kernels for 73% -> 82%
where the time goes in v5:
time: 2930 us
  Pallas kernels  2660 us (91%)
  other arithmetic  98.4 us (3%)
  waiting for transfers between devices  73.8 us (3%)
  local copies, waits for them, and re-layouts  61.9 us (2%)
    pallas_call x29, Pallas kernels, exchange_call(): pl.pallas_call(kernel, out_shape=outs, in_specs=[anywhere] * len(operands...  1660 us
    pallas_call x26, Pallas kernels, grid_call(): pl.pallas_call(kernel, out_shape=outs, grid=grid, in_specs=in_specs, out_...  1010 us
    ppermute x5, waiting for transfers between devices, scatter_gains(): lax.ppermute(sent, axis, [(i, i ^ step) for i in range(size)])  68.8 us
  transfers between devices with their start and end apart: 26, of which 5 were waited for; matrix products, arithmetic and copies ran while one was open for 4% of the time, Pallas kernels for 82%

profile of v5, /device:TPU:0, one launch (start us, length us, event | category | flops | bytes accessed | tf_op | source)
XLA Modules:
  0.0 2926.5 jit_solution(5458418180988202277)
XLA Ops:
  19.1 82.3 %shard_map.152 = (bf16[256,3072]{1,0:T(8,128)(2,1)}, bf16[384,2304]{1,0:T(8,128)(2,1)}) custom-call(bf16[256,3072]{1,0:T(8,128)(2,1)} %fusion.4.refs_0_.own_ref, bf16[384,2304]{1,0:T(8,128)(2,1)} %copy.33.refs_1_), custom_call_target="tpu_custom_call" | custom-call | flops 340000014336 | bytes 1000 | tf_op jit(solution)/shard_map/pallas_call | solution.py:776
  105.2 54.7 %shard_map.153 = bf16[768,2304]{1,0:T(8,128)(2,1)} custom-call(bf16[384,2304]{1,0:T(8,128)(2,1)} %copy.34.own_ref, bf16[384,2304]{1,0:T(8,128)(2,1)} %get-tuple-element.290.refs_0_), custom_call_target="tpu_custom_call" | custom-call | flops 6800000000 | bytes 1000 | tf_op jit(solution)/shard_map/pallas_call | solution.py:776
  166.0 96.8 %shard_map.154 = (bf16[256,3072]{1,0:T(8,128)(2,1)}, bf16[256,3072]{1,0:T(8,128)(2,1)}, bf16[96,3072]{1,0:T(8,128)(2,1)}) custom-call(bf16[256,3072]{1,0:T(8,128)(2,1)} %get-tuple-element.291.refs_0_, bf16[256,3072]{1,0:T(8,128)(2,1)} %get-tuple-element.377.refs_1_.own_ref, bf16[96,3072]{1,0:T(8,128)(2,1)} %own_ref), custom_call_target="tpu_custom_call" | custom-call | flops 340000014336 | bytes 1000 | tf_op jit(solution)/shard_map/pallas_call | solution.py:776
  297.7 71.7 %shard_map.156 = (bf16[256,3072]{1,0:T(8,128)(2,1)}, bf16[384,2048]{1,0:T(8,128)(2,1)}) custom-call(bf16[256,3072]{1,0:T(8,128)(2,1)} %multiply_convert_fusion.2.refs_0_.got_ref, bf16[384,2048]{1,0:T(8,128)(2,1)} %get-tuple-element.304.refs_1_.own_ref), custom_call_target="tpu_custom_call" | custom-call | flops 340000014336 | bytes 1000 | tf_op jit(solution)/shard_map/pallas_call | solution.py:776
  421.9 191.8 %shard_map.158 = (bf16[1024,3072]{1,0:T(8,128)(2,1)}, bf16[1024,3072]{1,0:T(8,128)(2,1)}) custom-call(bf16[256,3072]{1,0:T(8,128)(2,1)} %fusion.4.refs_0_.own_ref, bf16[256,3072]{1,0:T(8,128)(2,1)} %get-tuple-element.307.own_near_ref, bf16[256,3072]{1,0:T(8,128)(2,1)} %multiply_convert_fusion.2.refs_0_.got_ref, bf16[256,3072]{1,0:T(8,128)(2,1)} %get-tuple-element.309.got_near_ref), custom_call_target="tpu_custom_call" | custom-call | flops 6800000000 | bytes 1000 | tf_op jit(solution)/shard_map/pallas_call | solution.py:776
  695.2 48.9 %shard_map.163 = bf16[768,2048]{1,0:T(8,128)(2,1)} custom-call(bf16[384,2048]{1,0:T(8,128)(2,1)} %get-tuple-element.327.own_ref, bf16[384,2048]{1,0:T(8,128)(2,1)} %copy-done.57), custom_call_target="tpu_custom_call" | custom-call | flops 6800000000 | bytes 1000 | tf_op jit(solution)/shard_map/pallas_call | solution.py:776
  746.8 77.6 %shard_map.164 = (f32[1024,2304]{1,0:T(8,128)}, bf16[256,3072]{1,0:T(8,128)(2,1)}) custom-call(bf16[1024,3072]{1,0:T(8,128)(2,1)} %get-tuple-element.507.refs_0_.refs_1_, bf16[3072,2304]{1,0:T(8,128)(2,1)} %all-gather.6.cloned.1.call-done.refs_1_, bf16[256,3072]{1,0:T(8,128)(2,1)} %get-tuple-element.331.refs_2_), custom_call_target="tpu_custom_call" | custom-call | flops 45900001280 | bytes 1000 | tf_op jit(solution)/shard_map/pallas_call | solution.py:718
  886.7 96.6 %shard_map.168.refs_0_ = bf16[1024,3072]{1,0:T(8,128)(2,1)} custom-call(bf16[256,3072]{1,0:T(8,128)(2,1)} %multiply_convert_fusion.1.refs_8_.own_ref, bf16[256,3072]{1,0:T(8,128)(2,1)} %get-tuple-element.350.near_ref), custom_call_target="tpu_custom_call" | custom-call | flops 6800000000 | bytes 1000 | tf_op jit(solution)/shard_map/pallas_call | solution.py:776
  983.4 49.2 %shard_map.169 = bf16[512,3072]{1,0:T(8,128)(2,1)} custom-call(bf16[256,3072]{1,0:T(8,128)(2,1)} %own_ref.1, bf16[256,3072]{1,0:T(8,128)(2,1)} %collective-permute-done.4.refs_0_), custom_call_target="tpu_custom_call" | custom-call | flops 6800000000 | bytes 1000 | tf_op jit(solution)/shard_map/pallas_call | solution.py:776
  1081.4 75.4 %shard_map.171 = (f32[1024,2048]{1,0:T(8,128)}, bf16[1024,2048]{1,0:T(8,128)(2,1)}, bf16[256,3072]{1,0:T(8,128)(2,1)}) custom-call(bf16[1024,3072]{1,0:T(8,128)(2,1)} %shard_map.168.refs_0_, bf16[3072,2048]{1,0:T(8,128)(2,1)} %all-gather.10.cloned.1.call-done.refs_1_.refs_3_, f32[1024,2048]{1,0:T(8,128)} %get-tuple-element.394.refs_2_, ...), custom_call_target="tpu_custom_call" | custom-call | flops 45900001280 | bytes 1000 | tf_op jit(solution)/shard_map/pallas_call | solution.py:718
  1156.9 96.5 %shard_map.172.refs_0_.refs_1_ = bf16[1024,3072]{1,0:T(8,128)(2,1)} custom-call(bf16[256,3072]{1,0:T(8,128)(2,1)} %multiply_convert_fusion.refs_3_.own_ref, bf16[256,3072]{1,0:T(8,128)(2,1)} %get-tuple-element.371.near_ref), custom_call_target="tpu_custom_call" | custom-call | flops 6800000000 | bytes 1000 | tf_op jit(solution)/shard_map/pallas_call | solution.py:776
  1295.7 191.8 %shard_map.174 = (bf16[1024,3072]{1,0:T(8,128)(2,1)}, bf16[1024,3072]{1,0:T(8,128)(2,1)}) custom-call(bf16[256,3072]{1,0:T(8,128)(2,1)} %get-tuple-element.377.refs_1_.own_ref, bf16[256,3072]{1,0:T(8,128)(2,1)} %get-tuple-element.378.own_near_ref, bf16[256,3072]{1,0:T(8,128)(2,1)} %collective-permute-done.5.refs_2_.got_ref, ...), custom_call_target="tpu_custom_call" | custom-call | flops 6800000000 | bytes 1000 | tf_op jit(solution)/shard_map/pallas_call | solution.py:776
  1730.0 48.9 %shard_map.184 = (bf16[256,3072]{1,0:T(8,128)(2,1)}, bf16[256,3072]{1,0:T(8,128)(2,1)}) custom-call(bf16[512,3072]{1,0:T(8,128)(2,1)} %reduce-scatter.6.cloned.1.call-done.pair_ref), custom_call_target="tpu_custom_call" | custom-call | flops 6800000000 | bytes 1000 | tf_op jit(solution)/shard_map/pallas_call | solution.py:776
  1822.6 73.5 %shard_map.186 = (bf16[1024,3072]{1,0:T(8,128)(2,1)}, bf16[256,3072]{1,0:T(8,128)(2,1)}) custom-call(bf16[1024,2048]{1,0:T(8,128)(2,1)} %get-tuple-element.438.refs_0_, bf16[2048,3072]{1,0:T(8,128)(2,1)} %all-gather.14.cloned.1.call-done.refs_1_, bf16[256,3072]{1,0:T(8,128)(2,1)} %get-tuple-element.448.refs_2_.own_ref), custom_call_target="tpu_custom_call" | custom-call | flops 45900001280 | bytes 1000 | tf_op jit(solution)/shard_map/pallas_call | solution.py:718
  1904.5 96.4 %shard_map.187.refs_0_.refs_2_ = bf16[1024,3072]{1,0:T(8,128)(2,1)} custom-call(bf16[256,3072]{1,0:T(8,128)(2,1)} %get-tuple-element.448.refs_2_.own_ref, bf16[256,3072]{1,0:T(8,128)(2,1)} %get-tuple-element.449.near_ref), custom_call_target="tpu_custom_call" | custom-call | flops 6800000000 | bytes 1000 | tf_op jit(solution)/shard_map/pallas_call | solution.py:776
  2001.0 49.3 %shard_map.188 = (bf16[384,2048]{1,0:T(8,128)(2,1)}, bf16[384,2048]{1,0:T(8,128)(2,1)}) custom-call(bf16[768,2048]{1,0:T(8,128)(2,1)} %reduce-scatter.8.cloned.1.call-done.pair_ref), custom_call_target="tpu_custom_call" | custom-call | flops 6800000000 | bytes 1000 | tf_op jit(solution)/shard_map/pallas_call | solution.py:776
  2050.4 74.8 %shard_map.189 = (bf16[1024,3072]{1,0:T(8,128)(2,1)}, bf16[256,3072]{1,0:T(8,128)(2,1)}) custom-call(bf16[1024,2048]{1,0:T(8,128)(2,1)} %get-tuple-element.453.refs_1_.refs_0_, bf16[2048,3072]{1,0:T(8,128)(2,1)} %all-gather.14.cloned.1.call-done.refs_1_, bf16[256,3072]{1,0:T(8,128)(2,1)} %get-tuple-element.463.refs_2_.own_ref), custom_call_target="tpu_custom_call" | custom-call | flops 45900001280 | bytes 1000 | tf_op jit(solution)/shard_map/pallas_call | solution.py:718
  2142.9 96.6 %shard_map.192.refs_0_.refs_3_ = bf16[1024,3072]{1,0:T(8,128)(2,1)} custom-call(bf16[256,3072]{1,0:T(8,128)(2,1)} %get-tuple-element.463.refs_2_.own_ref, bf16[256,3072]{1,0:T(8,128)(2,1)} %get-tuple-element.464.near_ref), custom_call_target="tpu_custom_call" | custom-call | flops 6800000000 | bytes 1000 | tf_op jit(solution)/shard_map/pallas_call | solution.py:776
  2352.6 74.9 %shard_map.197 = (bf16[1024,768]{1,0:T(8,128)(2,1)}, bf16[1024,768]{1,0:T(8,128)(2,1)}, bf16[1024,768]{1,0:T(8,128)(2,1)}, bf16[1024,768]{1,0:T(8,128)(2,1)}, bf...) custom-call(bf16[1024,768]{1,0:T(8,128)(2,1)} %get-tuple-element.318.refs_0_, ...), custom_call_target="tpu_custom_call" | custom-call | flops 45900001280 | bytes 1000 | tf_op jit(solution)/shard_map/pallas_call | solution.py:718
  2472.6 76.6 %shard_map.200 = (bf16[3072,2304]{1,0:T(8,128)(2,1)}, bf16[256,3072]{1,0:T(8,128)(2,1)}) custom-call(bf16[1024,3072]{1,0:T(8,128)(2,1)} %get-tuple-element.506.refs_0_, bf16[1024,3072]{1,0:T(8,128)(2,1)} %get-tuple-element.507.refs_0_.refs_1_, bf16[1024,2304]{1,0:T(8,128)(2,1)} %copy-done.44, bf16[1024,2304]{1,0:T(8,128)(2,1)} %copy-done.45, ...), custom_call_target="tpu_custom_call" | custom-call | flops 49284751360 | bytes 1000 | tf_op jit(solution)/shard_map/pallas_call | solution.py:718
  2595.9 50.0 %shard_map.204 = (bf16[256,3072]{1,0:T(8,128)(2,1)}, bf16[96,3072]{1,0:T(8,128)(2,1)}) custom-call(bf16[256,3072]{1,0:T(8,128)(2,1)} %get-tuple-element.520.refs_0_, bf16[96,3072]{1,0:T(8,128)(2,1)} %get-tuple-element.521.refs_1_), custom_call_target="tpu_custom_call" | custom-call | flops 340000014336 | bytes 1000 | tf_op jit(solution)/shard_map/pallas_call | solution.py:776
  2677.7 65.0 %collective-permute-done.14 = f32[2,192]{1,0:T(2,128)S(1)} collective-permute-done((f32[2,192]{1,0:T(2,128)S(1)}, f32[2,192]{1,0:T(2,128)S(1)}, u32[]{:S(2)}, u32[]{:S(2)}) %collective-permute-start.14) | collective-permute-done | bytes 1568 | tf_op jit(solution)/shard_map/ppermute | solution.py:1150
  2769.8 54.7 %shard_map.205 = (bf16[384,2304]{1,0:T(8,128)(2,1)}, bf16[384,2304]{1,0:T(8,128)(2,1)}) custom-call(bf16[768,2304]{1,0:T(8,128)(2,1)} %reduce-scatter.14.cloned.1.call-done.pair_ref), custom_call_target="tpu_custom_call" | custom-call | flops 6800000000 | bytes 1000 | tf_op jit(solution)/shard_map/pallas_call | solution.py:776
  2824.5 84.5 %shard_map.206 = bf16[384,2304]{1,0:T(8,128)(2,1)} custom-call(bf16[384,2304]{1,0:T(8,128)(2,1)} %get-tuple-element.552.refs_0_), custom_call_target="tpu_custom_call" | custom-call | flops 340000014336 | bytes 1000 | tf_op jit(solution)/shard_map/pallas_call | solution.py:776
  (307 shorter events, 932.2 us)
Async XLA Ops:
  7.2 619.4 %all-gather.6.cloned.1.call-start = ((), (), s32[]{:S(2)}) async-start(), calls=%async_computation.5 | async-start | bytes 17694720 | tf_op jit(solution)/shard_map/all_gather | solution.py:1121
  160.0 517.0 %all-gather.8.cloned.1.call-start = ((), (), s32[]{:S(2)}) async-start(), calls=%async_computation.6 | async-start | bytes 5898240 | tf_op jit(solution)/shard_map/all_gather | solution.py:1121
  282.0 750.6 %all-gather.12.cloned.1.call-start = ((), (), s32[]{:S(2)}) async-start(), calls=%async_computation.8 | async-start | bytes 15728640 | tf_op jit(solution)/shard_map/all_gather | solution.py:1121
  418.3 663.1 %all-gather.10.cloned.1.call-start = ((), (), s32[]{:S(2)}) async-start(), calls=%async_computation.7 | async-start | bytes 15728640 | tf_op jit(solution)/shard_map/all_gather | solution.py:1121
  419.0 194.8 %collective-permute-start = (s32[256]{0:T(256)S(1)}, s32[256]{0:T(256)S(1)}, u32[]{:S(2)}, u32[]{:S(2)}) collective-permute-start(s32[256]{0:T(256)S(1)} %bitcast.93), channel_id=1, source_target_pairs={{0,2},{1,3},{2,0},{3,1},{4,6},{5,7},{6,4},{7,5},{8,10},{9,11},{10,... | collective-permute-start | bytes 3080 | tf_op jit(solution)/shard_map/ppermute | solution.py:1089
  419.7 274.3 %collective-permute-start.3 = (bf16[384,2048]{1,0:T(8,128)(2,1)S(1)}, bf16[384,2048]{1,0:T(8,128)(2,1)S(1)}, u32[]{:S(2)}, u32[]{:S(2)}) collective-permute-start(bf16[384,2048]{1,0:T(8,128)(2,1)S(1)} %copy-done.30), channel_id=1, source_target_pairs={{0,2},{1,3},{2,0},{3,1},{4,6},{5,7},{6,4},{7,5},{8,10},{9,11},{10,... | collective-permute-start | bytes 4718600 | tf_op jit(solution)/shard_map/ppermute | solution.py:1089
  613.8 3.7 collective-permute-start.1
  744.1 798.9 %all-gather.14.cloned.1.call-start = ((), (), s32[]{:S(2)}) async-start(), calls=%async_computation.9 | async-start | bytes 15728640 | tf_op jit(solution)/shard_map/all_gather | solution.py:1121
  745.9 237.5 %collective-permute-start.4 = (bf16[256,3072]{1,0:T(8,128)(2,1)}, bf16[256,3072]{1,0:T(8,128)(2,1)}, u32[]{:S(2)}, u32[]{:S(2)}) collective-permute-start(bf16[256,3072]{1,0:T(8,128)(2,1)} %own_ref.1), channel_id=1, source_target_pairs={{0,2},{1,3},{2,0},{3,1},{4,6},{5,7},{6,4},{7,5},{8,10},{9,11},{10,... | collective-permute-start | bytes 4718600 | tf_op jit(solution)/shard_map/ppermute | solution.py:1089
  1032.6 697.4 %reduce-scatter.6.cloned.1.call-start = ((), (), s32[]{:S(2)}) async-start(), calls=%async_computation.10 | async-start | bytes 15728640 | tf_op jit(solution)/shard_map/reduce_scatter | solution.py:1124
  1074.9 178.5 %collective-permute-start.5 = (bf16[256,3072]{1,0:T(8,128)(2,1)}, bf16[256,3072]{1,0:T(8,128)(2,1)}, u32[]{:S(2)}, u32[]{:S(2)}) collective-permute-start(bf16[256,3072]{1,0:T(8,128)(2,1)} %get-tuple-element.367), channel_id=1, source_target_pairs={{0,2},{1,3},{2,0},{3,1},{4,6},{5,7},{6,4},{7,5},{8,10},{9,11},{10,... | collective-permute-start | bytes 4718600 | tf_op jit(solution)/shard_map/ppermute | solution.py:1089
  1543.0 458.0 %reduce-scatter.8.cloned.1.call-start = ((), (), s32[]{:S(2)}) async-start(), calls=%async_computation.11 | async-start | bytes 15728640 | tf_op jit(solution)/shard_map/reduce_scatter | solution.py:1124
  1624.8 678.2 %reduce-scatter.10.cloned.1.call-start = ((), (), s32[]{:S(2)}) async-start(), calls=%async_computation.12 | async-start | bytes 15728640 | tf_op jit(solution)/shard_map/reduce_scatter | solution.py:1124
  1821.9 754.8 %reduce-scatter.12.cloned.1.call-start = ((), (), s32[]{:S(2)}) async-start(), calls=%async_computation.13 | async-start | bytes 5898240 | tf_op jit(solution)/shard_map/reduce_scatter | solution.py:1124
  1822.1 848.9 %collective-permute-start.8 = (bf16[256,3072]{1,0:T(8,128)(2,1)}, bf16[256,3072]{1,0:T(8,128)(2,1)}, u32[]{:S(2)}, u32[]{:S(2)}) collective-permute-start(bf16[256,3072]{1,0:T(8,128)(2,1)} %get-tuple-element.430), channel_id=1, source_target_pairs={{0,2},{1,3},{2,0},{3,1},{4,6},{5,7},{6,4},{7,5},{8,10},{9,11},{10,... | collective-permute-start | bytes 4718600 | tf_op jit(solution)/shard_map/ppermute | solution.py:1089
  2050.3 627.3 %collective-permute-start.7 = (bf16[384,2048]{1,0:T(8,128)(2,1)}, bf16[384,2048]{1,0:T(8,128)(2,1)}, u32[]{:S(2)}, u32[]{:S(2)}) collective-permute-start(bf16[384,2048]{1,0:T(8,128)(2,1)} %get-tuple-element.452), channel_id=1, source_target_pairs={{0,2},{1,3},{2,0},{3,1},{4,6},{5,7},{6,4},{7,5},{8,10},{9,11},{10,... | collective-permute-start | bytes 4718600 | tf_op jit(solution)/shard_map/ppermute | solution.py:1089
  2302.9 466.9 %reduce-scatter.14.cloned.1.call-start = ((), (), s32[]{:S(2)}) async-start(), calls=%async_computation.14 | async-start | bytes 17694720 | tf_op jit(solution)/shard_map/reduce_scatter | solution.py:1124
  2351.8 398.8 %collective-permute-start.10 = (bf16[384,2048]{1,0:T(8,128)(2,1)}, bf16[384,2048]{1,0:T(8,128)(2,1)}, u32[]{:S(2)}, u32[]{:S(2)}) collective-permute-start(bf16[384,2048]{1,0:T(8,128)(2,1)} %get-tuple-element.479), channel_id=1, source_target_pairs={{0,2},{1,3},{2,0},{3,1},{4,6},{5,7},{6,4},{7,5},{8,10},{9,11},{10,... | collective-permute-start | bytes 4718600 | tf_op jit(solution)/shard_map/ppermute | solution.py:1089
  2444.0 303.0 %collective-permute-start.6 = (bf16[256,3072]{1,0:T(8,128)(2,1)}, bf16[256,3072]{1,0:T(8,128)(2,1)}, u32[]{:S(2)}, u32[]{:S(2)}) collective-permute-start(bf16[256,3072]{1,0:T(8,128)(2,1)} %get-tuple-element.589), channel_id=1, source_target_pairs={{0,2},{1,3},{2,0},{3,1},{4,6},{5,7},{6,4},{7,5},{8,10},{9,11},{10,... | collective-permute-start | bytes 4718600 | tf_op jit(solution)/shard_map/ppermute | solution.py:1089
  2657.4 3.8 collective-permute-start.11
  2661.2 7.6 collective-permute-start.12
  2668.8 4.2 collective-permute-start.13
  2670.9 92.6 %collective-permute-start.9 = (bf16[256,3072]{1,0:T(8,128)(2,1)}, bf16[256,3072]{1,0:T(8,128)(2,1)}, u32[]{:S(2)}, u32[]{:S(2)}) collective-permute-start(bf16[256,3072]{1,0:T(8,128)(2,1)} %get-tuple-element.587), channel_id=1, source_target_pairs={{0,2},{1,3},{2,0},{3,1},{4,6},{5,7},{6,4},{7,5},{8,10},{9,11},{10,... | collective-permute-start | bytes 4718600 | tf_op jit(solution)/shard_map/ppermute | solution.py:1089
  2673.2 69.5 %collective-permute-start.14 = (f32[2,192]{1,0:T(2,128)S(1)}, f32[2,192]{1,0:T(2,128)S(1)}, u32[]{:S(2)}, u32[]{:S(2)}) collective-permute-start(f32[2,192]{1,0:T(2,128)S(1)} %bitcast.92), channel_id=1, source_target_pairs={{0,2},{1,3},{2,0},{3,1},{4,6},{5,7},{6,4},{7,5},{8,10},{9,11},{10,... | collective-permute-start | bytes 4616 | tf_op jit(solution)/shard_map/ppermute | solution.py:1150
  (60 other events, 1102.6 us)
Sparse Core Ops, SparseCore 0:
  160.1 135.7 all-gather.5
  297.7 57.0 all-gather.7
  418.5 121.7 all-gather.11
  744.3 121.6 all-gather.9
  1032.7 121.5 all-gather.13
  1543.1 120.8 reduce-scatter.5
  1667.1 120.7 reduce-scatter.7
  1822.0 119.1 reduce-scatter.9
  2303.0 56.3 reduce-scatter.11
  2576.8 133.0 reduce-scatter.13

commit v6 on v5

--- a/solution.py
+++ b/solution.py
@@ -787,38 +787,50 @@
     return tuple(results) if len(outs) > 1 else results[0]
 
 
-def gather_kernel(own_ref, near_ref, full_ref, local, send, receive):
+def relay(sources, targets, buffer, load, store):
+    loads, stores = [], []
+    for place, source in enumerate(sources):
+        copy = pltpu.make_async_copy(source, buffer.at[place], load.at[place])
+        copy.start()
+        loads.append(copy)
+    for place, target in enumerate(targets):
+        loads[place].wait()
+        copy = pltpu.make_async_copy(buffer.at[place], target, store.at[place])
+        copy.start()
+        stores.append(copy)
+    for copy in stores:
+        copy.wait()
+
+
+def gather_kernel(own_ref, near_ref, full_ref, buffer, load, store, send, receive):
     partner = sibling_id()
     meet(partner)
     count = own_ref.shape[0]
-    copies = []
+    remotes = []
     for place, ref in enumerate((own_ref, near_ref)):
         remote = push(
             ref, full_ref.at[pl.ds((2 + place) * count, count)],
             send.at[place], receive.at[place], partner,
         )
         remote.start()
-        copies.append(remote)
-    for place, ref in enumerate((own_ref, near_ref)):
-        copy = pltpu.make_async_copy(
-            ref, full_ref.at[pl.ds(place * count, count)], local.at[place]
-        )
-        copy.start()
-        copies.append(copy)
-    for copy in copies:
-        copy.wait()
+        remotes.append(remote)
+    targets = [full_ref.at[pl.ds(place * count, count)] for place in range(2)]
+    relay((own_ref, near_ref), targets, buffer, load, store)
+    for remote in remotes:
+        remote.wait()
 
 
 def core_gather(own, near):
     shape = (4 * own.shape[0], own.shape[1])
     return exchange_call(
         gather_kernel, 1, [own, near], [jax.ShapeDtypeStruct(shape, own.dtype)],
-        [pltpu.SemaphoreType.DMA((2,))] * 3,
+        [pltpu.VMEM((2, *own.shape), own.dtype)] + [pltpu.SemaphoreType.DMA((2,))] * 4,
     )
 
 
 def gather_two_kernel(
-    own_ref, own_near_ref, got_ref, got_near_ref, first_ref, second_ref, local, send, receive
+    own_ref, own_near_ref, got_ref, got_near_ref, first_ref, second_ref,
+    buffer, load, store, send, receive,
 ):
     partner = sibling_id()
     far = lax.axis_index("tp") // 2
@@ -826,21 +838,20 @@
     count = own_ref.shape[0]
 
     def run(targets):
-        copies = []
-        for place, ref in enumerate((own_ref, own_near_ref, got_ref, got_near_ref)):
+        sources = (own_ref, own_near_ref, got_ref, got_near_ref)
+        remotes, places = [], []
+        for place, ref in enumerate(sources):
             target, row = targets[place // 2], place % 2
             remote = push(
                 ref, target.at[pl.ds((2 + row) * count, count)],
                 send.at[place], receive.at[place], partner,
             )
             remote.start()
-            copy = pltpu.make_async_copy(
-                ref, target.at[pl.ds(row * count, count)], local.at[place]
-            )
-            copy.start()
-            copies += [remote, copy]
-        for copy in copies:
-            copy.wait()
+            remotes.append(remote)
+            places.append(target.at[pl.ds(row * count, count)])
+        relay(sources, places, buffer, load, store)
+        for remote in remotes:
+            remote.wait()
 
     @pl.when(far == 0)
     def _():
@@ -856,7 +867,7 @@
     return exchange_call(
         gather_two_kernel, 11, [own, own_near, got, got_near],
         [jax.ShapeDtypeStruct(shape, own.dtype)] * 2,
-        [pltpu.SemaphoreType.DMA((4,))] * 3,
+        [pltpu.VMEM((4, *own.shape), own.dtype)] + [pltpu.SemaphoreType.DMA((4,))] * 4,
     )
 
 
@@ -924,7 +935,7 @@
 
 
 def pair_kernel(own_ref, *refs):
-    others, (pair_ref, local, send, receive) = refs[:-4], refs[-4:]
+    others, (pair_ref, buffer, load, store, send, receive) = refs[:-6], refs[-6:]
     partner = sibling_id()
     core = lax.axis_index("fsdp") % 2
     far = lax.axis_index("tp") // 2
@@ -934,18 +945,16 @@
     owns = [own_ref.at[pl.ds(place * count, count)] for place in range(len(others))]
 
     def run(mine, theirs):
-        copies = []
+        remotes, targets = [], []
         for place in range(len(others)):
             target = pair_ref.at[pl.ds(base + place * count, count)]
-            remote = push(
-                theirs[place], target, send.at[place], receive.at[place], partner
-            )
+            remote = push(theirs[place], target, send.at[place], receive.at[place], partner)
             remote.start()
-            copy = pltpu.make_async_copy(mine[place], target, local.at[place])
-            copy.start()
-            copies += [remote, copy]
-        for copy in copies:
-            copy.wait()
+            remotes.append(remote)
+            targets.append(target)
+        relay(mine, targets, buffer, load, store)
+        for remote in remotes:
+            remote.wait()
 
     @pl.when(core == far)
     def _():
@@ -960,11 +969,12 @@
     shape = (2 * own.shape[0], own.shape[1])
     return exchange_call(
         pair_kernel, key, [own, *others], [jax.ShapeDtypeStruct(shape, own.dtype)],
-        [pltpu.SemaphoreType.DMA((len(others),))] * 3,
-    )
-
-
-def split_kernel(pair_ref, keep_ref, away_ref, local, send, receive):
+        [pltpu.VMEM((len(others), *others[0].shape), own.dtype)]
+        + [pltpu.SemaphoreType.DMA((len(others),))] * 4,
+    )
+
+
+def split_kernel(pair_ref, keep_ref, away_ref, buffer, load, store, send, receive):
     partner = sibling_id()
     core = lax.axis_index("fsdp") % 2
     far = lax.axis_index("tp") // 2
@@ -976,9 +986,7 @@
     def run(own_target, other_target):
         remote = push(theirs, other_target, send.at[0], receive.at[0], partner)
         remote.start()
-        copy = pltpu.make_async_copy(mine, own_target, local.at[0])
-        copy.start()
-        copy.wait()
+        relay((mine,), (own_target,), buffer, load, store)
         remote.wait()
 
     @pl.when(core == far)
@@ -994,7 +1002,7 @@
     shape = (pair.shape[0] // 2, pair.shape[1])
     return exchange_call(
         split_kernel, key, [pair], [jax.ShapeDtypeStruct(shape, pair.dtype)] * 2,
-        [pltpu.SemaphoreType.DMA((1,))] * 3,
+        [pltpu.VMEM((1, *shape), pair.dtype)] + [pltpu.SemaphoreType.DMA((1,))] * 4,
     )
 
 

time: 2930 us -> 1820 us (0.62)
  Pallas kernels: 2660 us -> 1530 us
    pallas_call x29, Pallas kernels: 1660 us -> 525 us  [exchange_call(): pl.pallas_call(kernel, out_shape=outs, in_specs=[anywhere] * len(operands...]
  transfers between devices with their start and end apart: 26 -> 26, of which waited for: 5 -> 5; matrix products, arithmetic and copies ran while one was open for 4% -> 6% of each run, Pallas kernels for 82% -> 75%
where the time goes in v6:
time: 1820 us; the launch traced here: 1810 us
  Pallas kernels  1530 us (84%)
  other arithmetic  98 us (5%)
  waiting for transfers between devices  93.1 us (5%)
  local copies, waits for them, and re-layouts  62.1 us (3%)
    pallas_call x26, Pallas kernels, grid_call(): pl.pallas_call(kernel, out_shape=outs, grid=grid, in_specs=in_specs, out_...  1000 us
    pallas_call x29, Pallas kernels, exchange_call(): pl.pallas_call(kernel, out_shape=outs, in_specs=[anywhere] * len(operands...  525 us
    ppermute x5, waiting for transfers between devices, scatter_gains(): lax.ppermute(sent, axis, [(i, i ^ step) for i in range(size)])  68.6 us
    unnamed x127, local copies, waits for them, and re-layouts  38.1 us
  transfers between devices with their start and end apart: 26, of which 5 were waited for; matrix products, arithmetic and copies ran while one was open for 6% of the time, Pallas kernels for 75%

profile of v6, /device:TPU:0, one launch (start us, length us, event | category | flops | bytes accessed | tf_op | source)
XLA Modules:
  0.0 1815.0 jit_solution(8241687425051700161)
XLA Ops:
  19.1 82.3 %shard_map.152 = (bf16[256,3072]{1,0:T(8,128)(2,1)}, bf16[384,2304]{1,0:T(8,128)(2,1)}) custom-call(bf16[256,3072]{1,0:T(8,128)(2,1)} %fusion.4.refs_0_.own_ref, bf16[384,2304]{1,0:T(8,128)(2,1)} %copy.33.refs_1_), custom_call_target="tpu_custom_call" | custom-call | flops 340000014336 | bytes 1000 | tf_op jit(solution)/shard_map/pallas_call | solution.py:776
  115.3 96.5 %shard_map.154 = (bf16[256,3072]{1,0:T(8,128)(2,1)}, bf16[256,3072]{1,0:T(8,128)(2,1)}, bf16[96,3072]{1,0:T(8,128)(2,1)}) custom-call(bf16[256,3072]{1,0:T(8,128)(2,1)} %get-tuple-element.291.refs_0_, bf16[256,3072]{1,0:T(8,128)(2,1)} %get-tuple-element.377.refs_1_.own_ref, bf16[96,3072]{1,0:T(8,128)(2,1)} %own_ref), custom_call_target="tpu_custom_call" | custom-call | flops 340000014336 | bytes 1000 | tf_op jit(solution)/shard_map/pallas_call | solution.py:776
  230.0 71.6 %shard_map.156 = (bf16[256,3072]{1,0:T(8,128)(2,1)}, bf16[384,2048]{1,0:T(8,128)(2,1)}) custom-call(bf16[256,3072]{1,0:T(8,128)(2,1)} %multiply_convert_fusion.2.refs_0_.got_ref, bf16[384,2048]{1,0:T(8,128)(2,1)} %get-tuple-element.304.refs_1_.own_ref), custom_call_target="tpu_custom_call" | custom-call | flops 340000014336 | bytes 1000 | tf_op jit(solution)/shard_map/pallas_call | solution.py:776
  373.2 29.2 %shard_map.160 = (bf16[1024,768]{1,0:T(8,128)(2,1)}, bf16[1024,768]{1,0:T(8,128)(2,1)}, bf16[1024,768]{1,0:T(8,128)(2,1)}, bf16[1024,768]{1,0:T(8,128)(2,1)}, f32[2,1024,4]{2,1,0:T(8,128)}) custom-call(f32[1024,2304]{1,0:T(8,128)} %shard_map.159.q_ref.k_ref.v_ref, f32[1024,2304]{1,0:T(8,128)} %shard_map.159.q_ref.k_ref.v_ref, ...), custom_call_target="tpu_custom_call" | custom-call | flops 8556380160 | bytes 1000 | tf_op jit(solution)/shard_map/pallas_call | solution.py:718
  428.6 74.6 %shard_map.164 = (f32[1024,2304]{1,0:T(8,128)}, bf16[256,3072]{1,0:T(8,128)(2,1)}) custom-call(bf16[1024,3072]{1,0:T(8,128)(2,1)} %get-tuple-element.507.refs_0_.refs_1_, bf16[3072,2304]{1,0:T(8,128)(2,1)} %all-gather.6.cloned.1.call-done.refs_1_, bf16[256,3072]{1,0:T(8,128)(2,1)} %get-tuple-element.331.refs_2_), custom_call_target="tpu_custom_call" | custom-call | flops 45900001280 | bytes 1000 | tf_op jit(solution)/shard_map/pallas_call | solution.py:718
  509.5 39.0 %shard_map.165 = (bf16[1024,768]{1,0:T(8,128)(2,1)}, bf16[1024,768]{1,0:T(8,128)(2,1)}, bf16[1024,768]{1,0:T(8,128)(2,1)}, bf16[1024,768]{1,0:T(8,128)(2,1)}, f3...) custom-call(f32[1024,2304]{1,0:T(8,128)} %get-tuple-element.337.refs_0_.refs_1_.refs_2_, ...), custom_call_target="tpu_custom_call" | custom-call | flops 45900001280 | bytes 1000 | tf_op jit(solution)/shard_map/pallas_call | solution.py:718
  575.7 42.2 %shard_map.170 = (f32[1024,2048]{1,0:T(8,128)}, bf16[256,3072]{1,0:T(8,128)(2,1)}) custom-call(bf16[1024,3072]{1,0:T(8,128)(2,1)} %shard_map.168.refs_0_, bf16[3072,2048]{1,0:T(8,128)(2,1)} %all-gather.12.cloned.1.call-done.refs_1_.refs_2_, bf16[256,3072]{1,0:T(8,128)(2,1)} %get-tuple-element.356.refs_2_), custom_call_target="tpu_custom_call" | custom-call | flops 45900001280 | bytes 1000 | tf_op jit(solution)/shard_map/pallas_call | solution.py:718
  626.2 74.9 %shard_map.171 = (f32[1024,2048]{1,0:T(8,128)}, bf16[1024,2048]{1,0:T(8,128)(2,1)}, bf16[256,3072]{1,0:T(8,128)(2,1)}) custom-call(bf16[1024,3072]{1,0:T(8,128)(2,1)} %shard_map.168.refs_0_, bf16[3072,2048]{1,0:T(8,128)(2,1)} %all-gather.10.cloned.1.call-done.refs_1_.refs_3_, f32[1024,2048]{1,0:T(8,128)} %get-tuple-element.394.refs_2_, ...), custom_call_target="tpu_custom_call" | custom-call | flops 45900001280 | bytes 1000 | tf_op jit(solution)/shard_map/pallas_call | solution.py:718
  707.2 41.9 %shard_map.173 = (f32[1024,2048]{1,0:T(8,128)}, bf16[256,3072]{1,0:T(8,128)(2,1)}) custom-call(bf16[1024,3072]{1,0:T(8,128)(2,1)} %shard_map.172.refs_0_.refs_1_, bf16[3072,2048]{1,0:T(8,128)(2,1)} %all-gather.12.cloned.1.call-done.refs_1_.refs_2_, bf16[256,3072]{1,0:T(8,128)(2,1)} %collective-permute-done.5.refs_2_.got_ref), custom_call_target="tpu_custom_call" | custom-call | flops 45900001280 | bytes 1000 | tf_op jit(solution)/shard_map/pallas_call | solution.py:718
  780.0 35.3 %shard_map.176 = bf16[2048,3072]{1,0:T(8,128)(2,1)} custom-call(bf16[1024,2048]{1,0:T(8,128)(2,1)} %get-tuple-element.438.refs_0_, bf16[1024,2048]{1,0:T(8,128)(2,1)} %get-tuple-element.453.refs_1_.refs_0_, bf16[1024,3072]{1,0:T(8,128)(2,1)} %get-tuple-element.392.refs_2_.refs_0_, bf16[1024,3072]{1,0:T(8,128)(2,1)} %get-tuple-element.398.refs_3_.refs_0_), custom_call_target="tpu_custom_call" | custom-call | flops 43808665600 | bytes 1000 | tf_op jit(solution)/shard_map/pallas_call | solution.py:718
  815.3 23.4 %shard_map.177 = (bf16[1024,2048]{1,0:T(8,128)(2,1)}, bf16[1024,2048]{1,0:T(8,128)(2,1)}) custom-call(bf16[1024,3072]{1,0:T(8,128)(2,1)} %get-tuple-element.392.refs_2_.refs_0_, bf16[2048,3072]{1,0:T(8,128)(2,1)} %all-gather.14.cloned.1.call-done.refs_1_, f32[1024,2048]{1,0:T(8,128)} %get-tuple-element.394.refs_2_, f32[1024,2048]{1,0:T(8,128)} %get-tuple-element.395.refs_3_), custom_call_target="tpu_custom_call" | custom-call | flops 21904332800 | bytes 1000 | tf_op jit(solution)/shard_map/pallas_call | solution.py:718
  838.8 24.0 %shard_map.178 = (bf16[1024,2048]{1,0:T(8,128)(2,1)}, bf16[1024,2048]{1,0:T(8,128)(2,1)}) custom-call(bf16[1024,3072]{1,0:T(8,128)(2,1)} %get-tuple-element.398.refs_3_.refs_0_, bf16[2048,3072]{1,0:T(8,128)(2,1)} %all-gather.14.cloned.1.call-done.refs_1_, f32[1024,2048]{1,0:T(8,128)} %get-tuple-element.400.refs_2_, f32[1024,2048]{1,0:T(8,128)} %get-tuple-element.401.refs_3_), custom_call_target="tpu_custom_call" | custom-call | flops 21904332800 | bytes 1000 | tf_op jit(solution)/shard_map/pallas_call | solution.py:718
  862.8 34.1 %shard_map.179 = bf16[3072,2048]{1,0:T(8,128)(2,1)} custom-call(bf16[1024,3072]{1,0:T(8,128)(2,1)} %shard_map.168.refs_0_, bf16[1024,3072]{1,0:T(8,128)(2,1)} %shard_map.172.refs_0_.refs_1_, bf16[1024,2048]{1,0:T(8,128)(2,1)} %get-tuple-element.408.refs_2_.refs_0_, bf16[1024,2048]{1,0:T(8,128)(2,1)} %get-tuple-element.414.refs_3_.refs_0_), custom_call_target="tpu_custom_call" | custom-call | flops 43808665600 | bytes 1000 | tf_op jit(solution)/shard_map/pallas_call | solution.py:718
  901.8 33.2 %shard_map.180.term_ref = bf16[1024,3072]{1,0:T(8,128)(2,1)} custom-call(bf16[1024,2048]{1,0:T(8,128)(2,1)} %get-tuple-element.408.refs_2_.refs_0_, bf16[1024,2048]{1,0:T(8,128)(2,1)} %get-tuple-element.433.refs_1_.refs_2_, bf16[3072,2048]{1,0:T(8,128)(2,1)} %all-gather.12.cloned.1.call-done.refs_1_.refs_2_, ...), custom_call_target="tpu_custom_call" | custom-call | flops 43808665600 | bytes 1000 | tf_op jit(solution)/shard_map/pallas_call | solution.py:718
  942.4 43.7 %shard_map.182 = (bf16[1024,3072]{1,0:T(8,128)(2,1)}, bf16[256,3072]{1,0:T(8,128)(2,1)}) custom-call(bf16[1024,2048]{1,0:T(8,128)(2,1)} %get-tuple-element.414.refs_3_.refs_0_, bf16[1024,2048]{1,0:T(8,128)(2,1)} %get-tuple-element.434.refs_1_.refs_3_, bf16[3072,2048]{1,0:T(8,128)(2,1)} %all-gather.12.cloned.1.call-done.refs_1_.refs_2_, ...), custom_call_target="tpu_custom_call" | custom-call | flops 45900001280 | bytes 1000 | tf_op jit(solution)/shard_map/pallas_call | solution.py:718
  1005.7 42.7 %shard_map.185 = (bf16[3072,2048]{1,0:T(8,128)(2,1)}, bf16[256,3072]{1,0:T(8,128)(2,1)}) custom-call(bf16[1024,3072]{1,0:T(8,128)(2,1)} %shard_map.168.refs_0_, bf16[1024,3072]{1,0:T(8,128)(2,1)} %shard_map.172.refs_0_.refs_1_, bf16[1024,2048]{1,0:T(8,128)(2,1)} %get-tuple-element.433.refs_1_.refs_2_, bf16[1024,2048]{1,0:T(8,128)(2,1)} %get-tuple-element.434.refs_1_.refs_3_, ...), custom_call_target="tpu_custom_call" | custom-call | flops 45900001280 | bytes 1000 | tf_op jit(solution)/shard_map/pallas_call | solution.py:718
  1049.2 73.8 %shard_map.186 = (bf16[1024,3072]{1,0:T(8,128)(2,1)}, bf16[256,3072]{1,0:T(8,128)(2,1)}) custom-call(bf16[1024,2048]{1,0:T(8,128)(2,1)} %get-tuple-element.438.refs_0_, bf16[2048,3072]{1,0:T(8,128)(2,1)} %all-gather.14.cloned.1.call-done.refs_1_, bf16[256,3072]{1,0:T(8,128)(2,1)} %get-tuple-element.448.refs_2_.own_ref), custom_call_target="tpu_custom_call" | custom-call | flops 45900001280 | bytes 1000 | tf_op jit(solution)/shard_map/pallas_call | solution.py:718
  1141.3 74.6 %shard_map.189 = (bf16[1024,3072]{1,0:T(8,128)(2,1)}, bf16[256,3072]{1,0:T(8,128)(2,1)}) custom-call(bf16[1024,2048]{1,0:T(8,128)(2,1)} %get-tuple-element.453.refs_1_.refs_0_, bf16[2048,3072]{1,0:T(8,128)(2,1)} %all-gather.14.cloned.1.call-done.refs_1_, bf16[256,3072]{1,0:T(8,128)(2,1)} %get-tuple-element.463.refs_2_.own_ref), custom_call_target="tpu_custom_call" | custom-call | flops 45900001280 | bytes 1000 | tf_op jit(solution)/shard_map/pallas_call | solution.py:718
  1258.0 44.8 %shard_map.195 = (bf16[768,3072]{1,0:T(8,128)(2,1)}, bf16[256,3072]{1,0:T(8,128)(2,1)}) custom-call(bf16[1024,768]{1,0:T(8,128)(2,1)} %get-tuple-element.470.refs_0_, bf16[1024,768]{1,0:T(8,128)(2,1)} %get-tuple-element.471.refs_0_.refs_1_, bf16[1024,3072]{1,0:T(8,128)(2,1)} %shard_map.187.refs_0_.refs_2_, bf16[1024,3072]{1,0:T(8,128)(2,1)} %shard_map.192.refs_0_.refs_3_, ...), custom_call_target="tpu_custom_call" | custom-call | flops 45900001280 | bytes 1000 | tf_op jit(solution)/shard_map/pallas_call | solution.py:718
  1307.8 75.3 %shard_map.197 = (bf16[1024,768]{1,0:T(8,128)(2,1)}, bf16[1024,768]{1,0:T(8,128)(2,1)}, bf16[1024,768]{1,0:T(8,128)(2,1)}, bf16[1024,768]{1,0:T(8,128)(2,1)}, bf...) custom-call(bf16[1024,768]{1,0:T(8,128)(2,1)} %get-tuple-element.318.refs_0_, ...), custom_call_target="tpu_custom_call" | custom-call | flops 45900001280 | bytes 1000 | tf_op jit(solution)/shard_map/pallas_call | solution.py:718
  1428.2 76.1 %shard_map.200 = (bf16[3072,2304]{1,0:T(8,128)(2,1)}, bf16[256,3072]{1,0:T(8,128)(2,1)}) custom-call(bf16[1024,3072]{1,0:T(8,128)(2,1)} %get-tuple-element.506.refs_0_, bf16[1024,3072]{1,0:T(8,128)(2,1)} %get-tuple-element.507.refs_0_.refs_1_, bf16[1024,2304]{1,0:T(8,128)(2,1)} %copy-done.44, bf16[1024,2304]{1,0:T(8,128)(2,1)} %copy-done.45, ...), custom_call_target="tpu_custom_call" | custom-call | flops 49284751360 | bytes 1000 | tf_op jit(solution)/shard_map/pallas_call | solution.py:718
  1534.2 50.2 %shard_map.204 = (bf16[256,3072]{1,0:T(8,128)(2,1)}, bf16[96,3072]{1,0:T(8,128)(2,1)}) custom-call(bf16[256,3072]{1,0:T(8,128)(2,1)} %get-tuple-element.520.refs_0_, bf16[96,3072]{1,0:T(8,128)(2,1)} %get-tuple-element.521.refs_1_), custom_call_target="tpu_custom_call" | custom-call | flops 340000014336 | bytes 1000 | tf_op jit(solution)/shard_map/pallas_call | solution.py:776
  1616.8 65.0 %collective-permute-done.14 = f32[2,192]{1,0:T(2,128)S(1)} collective-permute-done((f32[2,192]{1,0:T(2,128)S(1)}, f32[2,192]{1,0:T(2,128)S(1)}, u32[]{:S(2)}, u32[]{:S(2)}) %collective-permute-start.14) | collective-permute-done | bytes 1568 | tf_op jit(solution)/shard_map/ppermute | solution.py:1158
  1712.9 84.5 %shard_map.206 = bf16[384,2304]{1,0:T(8,128)(2,1)} custom-call(bf16[384,2304]{1,0:T(8,128)(2,1)} %get-tuple-element.552.refs_0_), custom_call_target="tpu_custom_call" | custom-call | flops 340000014336 | bytes 1000 | tf_op jit(solution)/shard_map/pallas_call | solution.py:776
  (307 shorter events, 466.4 us)
Async XLA Ops:
  7.2 344.8 %all-gather.6.cloned.1.call-start = ((), (), s32[]{:S(2)}) async-start(), calls=%async_computation.5 | async-start | bytes 17694720 | tf_op jit(solution)/shard_map/all_gather | solution.py:1129
  109.3 293.1 %all-gather.8.cloned.1.call-start = ((), (), s32[]{:S(2)}) async-start(), calls=%async_computation.6 | async-start | bytes 5898240 | tf_op jit(solution)/shard_map/all_gather | solution.py:1129
  214.2 361.4 %all-gather.12.cloned.1.call-start = ((), (), s32[]{:S(2)}) async-start(), calls=%async_computation.8 | async-start | bytes 15728640 | tf_op jit(solution)/shard_map/all_gather | solution.py:1129
  305.5 320.7 %all-gather.10.cloned.1.call-start = ((), (), s32[]{:S(2)}) async-start(), calls=%async_computation.7 | async-start | bytes 15728640 | tf_op jit(solution)/shard_map/all_gather | solution.py:1129
  306.1 13.6 collective-permute-start
  306.9 112.6 %collective-permute-start.3 = (bf16[384,2048]{1,0:T(8,128)(2,1)S(1)}, bf16[384,2048]{1,0:T(8,128)(2,1)S(1)}, u32[]{:S(2)}, u32[]{:S(2)}) collective-permute-start(bf16[384,2048]{1,0:T(8,128)(2,1)S(1)} %copy-done.30), channel_id=1, source_target_pairs={{0,2},{1,3},{2,0},{3,1},{4,6},{5,7},{6,4},{7,5},{8,10},{9,11},{10,... | collective-permute-start | bytes 4718600 | tf_op jit(solution)/shard_map/ppermute | solution.py:1097
  319.8 23.1 %collective-permute-start.1 = (s32[512]{0:T(512)S(1)}, s32[512]{0:T(512)S(1)}, u32[]{:S(2)}, u32[]{:S(2)}) collective-permute-start(s32[512]{0:T(512)S(1)} %pad_add_fusion.2), channel_id=1, source_target_pairs={{0,1},{1,0},{2,3},{3,2},{4,5},{5,4},{6,7},{7,6},{8,9},{9,8},{10,11... | collective-permute-start | bytes 6152 | tf_op jit(solution)/shard_map/ppermute | solution.py:1094
  424.4 390.9 %all-gather.14.cloned.1.call-start = ((), (), s32[]{:S(2)}) async-start(), calls=%async_computation.9 | async-start | bytes 15728640 | tf_op jit(solution)/shard_map/all_gather | solution.py:1129
  426.1 145.6 %collective-permute-start.4 = (bf16[256,3072]{1,0:T(8,128)(2,1)}, bf16[256,3072]{1,0:T(8,128)(2,1)}, u32[]{:S(2)}, u32[]{:S(2)}) collective-permute-start(bf16[256,3072]{1,0:T(8,128)(2,1)} %own_ref.1), channel_id=1, source_target_pairs={{0,2},{1,3},{2,0},{3,1},{4,6},{5,7},{6,4},{7,5},{8,10},{9,11},{10,... | collective-permute-start | bytes 4718600 | tf_op jit(solution)/shard_map/ppermute | solution.py:1097
  575.7 426.2 %reduce-scatter.6.cloned.1.call-start = ((), (), s32[]{:S(2)}) async-start(), calls=%async_computation.10 | async-start | bytes 15728640 | tf_op jit(solution)/shard_map/reduce_scatter | solution.py:1132
  617.9 89.3 %collective-permute-start.5 = (bf16[256,3072]{1,0:T(8,128)(2,1)}, bf16[256,3072]{1,0:T(8,128)(2,1)}, u32[]{:S(2)}, u32[]{:S(2)}) collective-permute-start(bf16[256,3072]{1,0:T(8,128)(2,1)} %get-tuple-element.367), channel_id=1, source_target_pairs={{0,2},{1,3},{2,0},{3,1},{4,6},{5,7},{6,4},{7,5},{8,10},{9,11},{10,... | collective-permute-start | bytes 4718600 | tf_op jit(solution)/shard_map/ppermute | solution.py:1097
  815.3 322.1 %reduce-scatter.8.cloned.1.call-start = ((), (), s32[]{:S(2)}) async-start(), calls=%async_computation.11 | async-start | bytes 15728640 | tf_op jit(solution)/shard_map/reduce_scatter | solution.py:1132
  896.9 406.0 %reduce-scatter.10.cloned.1.call-start = ((), (), s32[]{:S(2)}) async-start(), calls=%async_computation.12 | async-start | bytes 15728640 | tf_op jit(solution)/shard_map/reduce_scatter | solution.py:1132
  1048.4 483.3 %reduce-scatter.12.cloned.1.call-start = ((), (), s32[]{:S(2)}) async-start(), calls=%async_computation.13 | async-start | bytes 5898240 | tf_op jit(solution)/shard_map/reduce_scatter | solution.py:1132
  1048.6 561.5 %collective-permute-start.8 = (bf16[256,3072]{1,0:T(8,128)(2,1)}, bf16[256,3072]{1,0:T(8,128)(2,1)}, u32[]{:S(2)}, u32[]{:S(2)}) collective-permute-start(bf16[256,3072]{1,0:T(8,128)(2,1)} %get-tuple-element.430), channel_id=1, source_target_pairs={{0,2},{1,3},{2,0},{3,1},{4,6},{5,7},{6,4},{7,5},{8,10},{9,11},{10,... | collective-permute-start | bytes 4718600 | tf_op jit(solution)/shard_map/ppermute | solution.py:1097
  1141.2 475.6 %collective-permute-start.7 = (bf16[384,2048]{1,0:T(8,128)(2,1)}, bf16[384,2048]{1,0:T(8,128)(2,1)}, u32[]{:S(2)}, u32[]{:S(2)}) collective-permute-start(bf16[384,2048]{1,0:T(8,128)(2,1)} %get-tuple-element.452), channel_id=1, source_target_pairs={{0,2},{1,3},{2,0},{3,1},{4,6},{5,7},{6,4},{7,5},{8,10},{9,11},{10,... | collective-permute-start | bytes 4718600 | tf_op jit(solution)/shard_map/ppermute | solution.py:1097
  1302.8 406.0 %reduce-scatter.14.cloned.1.call-start = ((), (), s32[]{:S(2)}) async-start(), calls=%async_computation.14 | async-start | bytes 17694720 | tf_op jit(solution)/shard_map/reduce_scatter | solution.py:1132
  1306.8 382.9 %collective-permute-start.10 = (bf16[384,2048]{1,0:T(8,128)(2,1)}, bf16[384,2048]{1,0:T(8,128)(2,1)}, u32[]{:S(2)}, u32[]{:S(2)}) collective-permute-start(bf16[384,2048]{1,0:T(8,128)(2,1)} %get-tuple-element.479), channel_id=1, source_target_pairs={{0,2},{1,3},{2,0},{3,1},{4,6},{5,7},{6,4},{7,5},{8,10},{9,11},{10,... | collective-permute-start | bytes 4718600 | tf_op jit(solution)/shard_map/ppermute | solution.py:1097
  1399.6 286.5 %collective-permute-start.6 = (bf16[256,3072]{1,0:T(8,128)(2,1)}, bf16[256,3072]{1,0:T(8,128)(2,1)}, u32[]{:S(2)}, u32[]{:S(2)}) collective-permute-start(bf16[256,3072]{1,0:T(8,128)(2,1)} %get-tuple-element.589), channel_id=1, source_target_pairs={{0,2},{1,3},{2,0},{3,1},{4,6},{5,7},{6,4},{7,5},{8,10},{9,11},{10,... | collective-permute-start | bytes 4718600 | tf_op jit(solution)/shard_map/ppermute | solution.py:1097
  1595.9 4.0 collective-permute-start.11
  1599.9 7.9 collective-permute-start.12
  1607.9 4.7 collective-permute-start.13
  1610.0 92.6 %collective-permute-start.9 = (bf16[256,3072]{1,0:T(8,128)(2,1)}, bf16[256,3072]{1,0:T(8,128)(2,1)}, u32[]{:S(2)}, u32[]{:S(2)}) collective-permute-start(bf16[256,3072]{1,0:T(8,128)(2,1)} %get-tuple-element.587), channel_id=1, source_target_pairs={{0,2},{1,3},{2,0},{3,1},{4,6},{5,7},{6,4},{7,5},{8,10},{9,11},{10,... | collective-permute-start | bytes 4718600 | tf_op jit(solution)/shard_map/ppermute | solution.py:1097
  1612.7 69.1 %collective-permute-start.14 = (f32[2,192]{1,0:T(2,128)S(1)}, f32[2,192]{1,0:T(2,128)S(1)}, u32[]{:S(2)}, u32[]{:S(2)}) collective-permute-start(f32[2,192]{1,0:T(2,128)S(1)} %bitcast.92), channel_id=1, source_target_pairs={{0,2},{1,3},{2,0},{3,1},{4,6},{5,7},{6,4},{7,5},{8,10},{9,11},{10,... | collective-permute-start | bytes 4616 | tf_op jit(solution)/shard_map/ppermute | solution.py:1158
  (60 other events, 952.0 us)
Sparse Core Ops, SparseCore 0:
  109.4 135.6 all-gather.5
  246.9 57.0 all-gather.7
  305.9 122.5 all-gather.11
  430.1 122.5 all-gather.9
  575.8 123.2 all-gather.13
  815.4 120.3 reduce-scatter.5
  938.9 120.7 reduce-scatter.7
  1062.7 120.7 reduce-scatter.9
  1303.0 56.1 reduce-scatter.11
  1531.8 132.8 reduce-scatter.13

commit v7 on v6

--- a/solution.py
+++ b/solution.py
@@ -646,6 +646,8 @@
     index, place = lax.axis_index("fsdp"), lax.axis_index("tp")
     if kind == "near":
         return (index, place + 1 - 2 * (place % 2))
+    if kind == "core":
+        return sibling_id()
     return (index, place + 2 - 4 * (place // 2))
 
 
@@ -742,7 +744,7 @@
     return exchange_call(
         functools.partial(swap_kernel, kinds), next_key[0], values,
         [jax.ShapeDtypeStruct(value.shape, value.dtype) for value in values],
-        [pltpu.SemaphoreType.DMA((len(pushes),))] * 2, flops=200 * 10**9,
+        [pltpu.SemaphoreType.DMA((len(pushes),))] * 2, flops=40 * 10**9,
     )
 
 
@@ -1189,34 +1191,34 @@
     gate_local, up_local = gate_up_weight[:, 0], gate_up_weight[:, 1]
 
     next_key[0] = 11
-    position_got = swap_far(pick(doc_positions, 1 - far))
-    first, second = place_tokens(doc_positions, position_got)
-    near_both = swap_near(join(first, second))
+    places = jnp.broadcast_to(doc_positions[:, None, :], (2, 8, rows))
 
     def first_norm(part):
         stream = part.astype(jnp.float32)
         return (stream, *rms_pack(stream, gain_one))
 
     s_own, r_own, n_own = act(lambda value: first_norm(pick(value, far)), block_in)
-    near_own, qkv_other = swap(("near", n_own), ("far", qkv_local))
+    near_own, qkv_other, place_got = swap(
+        ("near", n_own), ("far", qkv_local), ("far", pick(places, 1 - far))
+    )
     qkv_full = gather_weight(4, qkv_local, qkv_other)
-    first, second = (
-        join(first, near_both[: first.shape[0]]), join(second, near_both[first.shape[0] :])
-    )
-    core_both = swap_core(join(first, second))
-
-    def make_tables(first, second, both):
-        count = first.shape[0]
-        late = join(second, both[count:])
-        return (*head_tables(join(first, both[:count])), *head_tables(late), late[:, None])
+    places = join(*place_tokens(places, place_got))
+
+    def make_tables(own, other):
+        order = join(own, other)[::8].reshape(2, 2, 2, rows)
+        early, late = order[:, :, 0].reshape(-1), order[:, :, 1].reshape(-1)
+        return (*head_tables(early), *head_tables(late), late[:, None])
 
     c_own = pick(out_cotangent, far)
-    stream_got, c_near_own, out_other = swap(
-        ("far", pick(block_in, 1 - far)), ("near", c_own), ("far", out_weight)
-    )
+    stream_got, c_near_own, out_other, near_places = swap(
+        ("far", pick(block_in, 1 - far)), ("near", c_own), ("far", out_weight), ("near", places)
+    )
+    places = join(places, near_places)
     out_full = gather_weight(3, out_weight, out_other)
     s_got, r_got, n_got = act(first_norm, stream_got)
-    near_got, gate_other = swap(("near", n_got), ("far", gate_local))
+    near_got, gate_other, core_places = swap(
+        ("near", n_got), ("far", gate_local), ("core", places)
+    )
     gate_full = gather_weight(5, gate_local, gate_other)
     h1_first, h1_second = act(core_gather_two, n_own, near_own, n_got, near_got)
     streams = [jnp.where(far == 0, s_own, s_got), jnp.where(far == 0, s_got, s_own)]
@@ -1238,16 +1240,16 @@
 
     up_other = swap_far(chained(up_local, gate_other))
     cos_first, sin_first, cos_second, sin_second, reach = act(
-        make_tables, first, second, core_both
+        make_tables, places, core_places
     )
     tables = [(cos_first, sin_first), (cos_second, sin_second)]
     projected = act(wide_dot, h1_first, qkv_full)
     results = act(attend_first, projected)
+    up_full = gather_weight(5, up_local, up_other)
+    down_other = swap_far(chained(down_weight, up_other))
     saved, lses, mixed_first = [results[:3]], [results[4]], results[3]
     term_first = act(dot_bf16, mixed_first, out_full)
     keep_first, send_first = act(core_reduce, term_first)
-    up_full = gather_weight(5, up_local, up_other)
-    down_other = swap_far(chained(down_weight, up_other))
     projected, branch_first = act(
         wide_dot, h1_second, qkv_full, sends=[("near", send_first)]
     )
@@ -1299,15 +1301,11 @@
             act_grad * (gate * sigmoid_gate),
         )
 
-    def fall(cotangent, weight, gate, up):
+    def fall(cotangent, weight, gate, up, pushes=()):
         return rows_matmul(
             [cotangent], [weight], dot_nt, [jnp.bfloat16] * 2, pick_tile(weight.shape[0]),
-            chunk=512, finish=fall_finish, extras=[gate, up],
-        )
-
-    dg_first, du_first = act(fall, y_first, down_full, gate_first, up_first)
-    dg_second, du_second = act(fall, y_second, down_full, gate_second, up_second)
-    gate_sum = plane_scatter(act(grad_sum, h2_first, dg_first, h2_second, dg_second))
+            chunk=512, finish=fall_finish, extras=[gate, up], pushes=pushes,
+        )
 
     def hidden_grad(gate_grad, up_grad, gate_weight, up_weight, pushes=()):
         return rows_matmul(
@@ -1320,40 +1318,45 @@
         grad = cotangent.astype(jnp.float32) + grad
         return grad, grad.astype(jnp.bfloat16), gain_term
 
+    dg_first, du_first = act(fall, y_first, down_full, gate_first, up_first)
     term_first = act(hidden_grad, dg_first, du_first, gate_full, up_full)
     keep_first, send_first = act(core_reduce, term_first)
-    term_second, back_first = act(
-        hidden_grad, dg_second, du_second, gate_full, up_full, sends=[("near", send_first)]
-    )
-    keep_second, send_second = act(core_reduce, term_second)
+    dg_second, du_second, back_first = act(
+        fall, y_second, down_full, gate_second, up_second, sends=[("near", send_first)]
+    )
     g_first, n_first, gain_two_first = act(
         second_back, m_first, q_first, keep_first, back_first, c_first
     )
+    term_second, near_first = act(
+        hidden_grad, dg_second, du_second, gate_full, up_full, sends=[("near", n_first)]
+    )
+    keep_second, send_second = act(core_reduce, term_second)
+    d_first = act(core_gather, n_first, near_first)
+    grad_gate, back_second = act(
+        grad_sum, h2_first, dg_first, h2_second, dg_second, sends=[("near", send_second)]
+    )
+    gate_sum = plane_scatter(grad_gate)
+    g_second, n_second, gain_two_second = act(
+        second_back, m_second, q_second, keep_second, back_second, c_second
+    )
+    heads_first = act(heads_back, d_first, out_full)
     down_mine, down_away = act(lambda pair: core_split(10, pair), down_sum)
     down_got = swap_far(down_away)
-    grad_up, back_second = act(
-        grad_sum, h2_first, du_first, h2_second, du_second, sends=[("near", send_second)]
+    grad_up, near_second = act(
+        grad_sum, h2_first, du_first, h2_second, du_second, sends=[("near", n_second)]
     )
     up_sum = plane_scatter(grad_up)
-    mlp_first, near_first = act(dot_bf16, a_first, down_full, sends=[("near", n_first)])
-    g_second, n_second, gain_two_second = act(
-        second_back, m_second, q_second, keep_second, back_second, c_second
-    )
-    d_first = act(core_gather, n_first, near_first)
-
+
+    d_second = act(core_gather, n_second, near_second)
+    heads_second = act(heads_back, d_second, out_full)
+    grad_out = act(grad_sum, mixed_first, d_first, mixed_second, d_second)
+    out_sum = plane_scatter(grad_out)
+    mlp_first = act(dot_bf16, a_first, down_full)
+    mlp_keep_first, mlp_send_first = act(core_reduce, mlp_first)
+    mlp_second = act(dot_bf16, a_second, down_full)
+    mlp_keep_second, mlp_send_second = act(core_reduce, mlp_second)
     gate_mine, gate_away = act(lambda pair: core_split(9, pair), gate_sum)
     gate_got = swap_far(gate_away)
-    mlp_second, near_second = act(dot_bf16, a_second, down_full, sends=[("near", n_second)])
-    mlp_keep_first, mlp_send_first = act(core_reduce, mlp_first)
-    heads_first = act(heads_back, d_first, out_full)
-    d_second = act(core_gather, n_second, near_second)
-    heads_second = act(heads_back, d_second, out_full)
-    mlp_keep_second, mlp_send_second = act(core_reduce, mlp_second)
-    grad_out, mlp_branch_first = act(
-        grad_sum, mixed_first, d_first, mixed_second, d_second, sends=[("near", mlp_send_first)]
-    )
-    out_sum = plane_scatter(grad_out)
-    up_mine, up_away = act(lambda pair: core_split(9, pair), up_sum)
 
     def attend_back(heads_first, heads_second, pushes=()):
         return attention_call(
@@ -1368,10 +1371,11 @@
             pushes,
         )
 
+    *grads, mlp_branch_first = act(
+        attend_back, heads_first, heads_second, sends=[("near", mlp_send_first)]
+    )
+    up_mine, up_away = act(lambda pair: core_split(9, pair), up_sum)
     up_got = swap_far(up_away)
-    *grads, mlp_branch_second = act(
-        attend_back, heads_first, heads_second, sends=[("near", mlp_send_second)]
-    )
     p_first, p_second = act(
         lambda *parts: (
             jnp.concatenate(parts[:3], axis=1),
@@ -1385,6 +1389,10 @@
         second = (second + second_keep + second_got.astype(jnp.float32)).astype(jnp.bfloat16)
         return jnp.where(far == 0, first, second), jnp.where(far == 0, second, first)
 
+    grad_qkv, mlp_branch_second = act(
+        grad_sum, h1_first, p_first, h1_second, p_second, sends=[("near", mlp_send_second)]
+    )
+    qkv_sum = plane_scatter(grad_qkv)
     out_keep, out_send = act(
         finish_output,
         m_first, mlp_keep_first, mlp_branch_first, m_second, mlp_keep_second, mlp_branch_second,
@@ -1392,11 +1400,9 @@
     out_got = swap_far(out_send)
     term_first = act(heads_back, p_first, qkv_full)
     keep_first, send_first = act(core_reduce, term_first)
-    grad_qkv, back_first = act(
-        grad_sum, h1_first, p_first, h1_second, p_second, sends=[("near", send_first)]
-    )
-    qkv_sum = plane_scatter(grad_qkv)
-    term_second = act(heads_back, p_second, qkv_full)
+    term_second, back_first = act(
+        heads_back, p_second, qkv_full, sends=[("near", send_first)]
+    )
     keep_second, send_second = act(core_reduce, term_second)
     out_mine, out_away = act(lambda pair: core_split(8, pair), out_sum)
     def settle(keep, got):

time: 1820 us -> 1750 us (0.962)
  Pallas kernels: 1530 us -> 1480 us
    pallas_call x26, Pallas kernels: 1000 us -> 952 us  [grid_call(): pl.pallas_call(kernel, out_shape=outs, grid=grid, in_specs=in_specs, out_...]
    ppermute x2 -> x0, waiting for transfers between devices: 24.1 us -> none  [the longest x1 23 us: swap_near(): return lax.ppermute(value, 'tp', near_pairs)]
    unnamed x127 -> x134, local copies, waits for them, and re-layouts: 38.1 us -> 34.8 us
  transfers between devices with their start and end apart: 26 -> 23, of which waited for: 5 -> 5; matrix products, arithmetic and copies ran while one was open for 6% -> 7% of each run, Pallas kernels for 75% -> 75%
where the time goes in v7:
time: 1750 us; the launch traced here: 1740 us
  Pallas kernels  1480 us (85%)
  other arithmetic  100 us (6%)
  waiting for transfers between devices  77.3 us (4%)
  local copies, waits for them, and re-layouts  58.6 us (3%)
    pallas_call x26, Pallas kernels, grid_call(): pl.pallas_call(kernel, out_shape=outs, grid=grid, in_specs=in_specs, out_...  952 us
    pallas_call x29, Pallas kernels, exchange_call(): pl.pallas_call(kernel, out_shape=outs, in_specs=[anywhere] * len(operands...  526 us
    ppermute x5, waiting for transfers between devices, scatter_gains(): lax.ppermute(sent, axis, [(i, i ^ step) for i in range(size)])  68.7 us
  transfers between devices with their start and end apart: 23, of which 5 were waited for; matrix products, arithmetic and copies ran while one was open for 7% of the time, Pallas kernels for 75%

profile of v7, /device:TPU:0, one launch (start us, length us, event | category | flops | bytes accessed | tf_op | source)
XLA Modules:
  0.0 1744.9 jit_solution(3496536862921942496)
XLA Ops:
  19.1 82.6 %shard_map.152 = (bf16[256,3072]{1,0:T(8,128)(2,1)}, bf16[384,2304]{1,0:T(8,128)(2,1)}, s32[8,256]{1,0:T(8,128)}) custom-call(bf16[256,3072]{1,0:T(8,128)(2,1)} %fusion.4.refs_0_.own_ref, bf16[384,2304]{1,0:T(8,128)(2,1)} %copy.35.refs_1_, s32[8,256]{1,0:T(8,128)} %broadcast_in_dim.11.refs_2_), custom_call_target="tpu_custom_call" | custom-call | flops 67999997952 | bytes 1000 | tf_op jit(solution)/shard_map/pallas_call | solution.py:778
  114.2 96.5 %shard_map.154 = (bf16[256,3072]{1,0:T(8,128)(2,1)}, bf16[256,3072]{1,0:T(8,128)(2,1)}, bf16[96,3072]{1,0:T(8,128)(2,1)}, s32[16,256]{1,0:T(8,128)}) custom-call(bf16[256,3072]{1,0:T(8,128)(2,1)} %get-tuple-element.290.refs_0_, bf16[256,3072]{1,0:T(8,128)(2,1)} %get-tuple-element.379.refs_1_.own_ref, bf16[96,3072]{1,0:T(8,128)(2,1)} %own_ref, ...), custom_call_target="tpu_custom_call" | custom-call | flops 67999997952 | bytes 1000 | tf_op jit(solution)/shard_map/pallas_call | solution.py:778
  229.0 71.5 %shard_map.156 = (bf16[256,3072]{1,0:T(8,128)(2,1)}, bf16[384,2048]{1,0:T(8,128)(2,1)}, s32[32,256]{1,0:T(8,128)}) custom-call(bf16[256,3072]{1,0:T(8,128)(2,1)} %multiply_convert_fusion.2.refs_0_.got_ref, bf16[384,2048]{1,0:T(8,128)(2,1)} %get-tuple-element.307.refs_1_.own_ref, s32[32,256]{1,0:T(8,128)} %pad_add_fusion.1.refs_2_), custom_call_target="tpu_custom_call" | custom-call | flops 67999997952 | bytes 1000 | tf_op jit(solution)/shard_map/pallas_call | solution.py:778
  323.9 21.2 %shard_map.159.q_ref.k_ref.v_ref = f32[1024,2304]{1,0:T(8,128)} custom-call(bf16[1024,3072]{1,0:T(8,128)(2,1)} %get-tuple-element.492.refs_0_, bf16[3072,2304]{1,0:T(8,128)(2,1)} %all-gather.6.cloned.1.call-done.refs_1_), custom_call_target="tpu_custom_call" | custom-call | flops 24642375680 | bytes 1000 | tf_op jit(solution)/shard_map/pallas_call | solution.py:720
  345.1 29.2 %shard_map.160 = (bf16[1024,768]{1,0:T(8,128)(2,1)}, bf16[1024,768]{1,0:T(8,128)(2,1)}, bf16[1024,768]{1,0:T(8,128)(2,1)}, bf16[1024,768]{1,0:T(8,128)(2,1)}, f32[2,1024,4]{2,1,0:T(8,128)}) custom-call(f32[1024,2304]{1,0:T(8,128)} %shard_map.159.q_ref.k_ref.v_ref, f32[1024,2304]{1,0:T(8,128)} %shard_map.159.q_ref.k_ref.v_ref, ...), custom_call_target="tpu_custom_call" | custom-call | flops 8556380160 | bytes 1000 | tf_op jit(solution)/shard_map/pallas_call | solution.py:720
  400.3 76.4 %shard_map.164 = (f32[1024,2304]{1,0:T(8,128)}, bf16[256,3072]{1,0:T(8,128)(2,1)}) custom-call(bf16[1024,3072]{1,0:T(8,128)(2,1)} %get-tuple-element.493.refs_0_.refs_1_, bf16[3072,2304]{1,0:T(8,128)(2,1)} %all-gather.6.cloned.1.call-done.refs_1_, bf16[256,3072]{1,0:T(8,128)(2,1)} %get-tuple-element.333.refs_2_), custom_call_target="tpu_custom_call" | custom-call | flops 45900001280 | bytes 1000 | tf_op jit(solution)/shard_map/pallas_call | solution.py:720
  482.9 40.5 %shard_map.165 = (bf16[1024,768]{1,0:T(8,128)(2,1)}, bf16[1024,768]{1,0:T(8,128)(2,1)}, bf16[1024,768]{1,0:T(8,128)(2,1)}, bf16[1024,768]{1,0:T(8,128)(2,1)}, f3...) custom-call(f32[1024,2304]{1,0:T(8,128)} %get-tuple-element.339.refs_0_.refs_1_.refs_2_, ...), custom_call_target="tpu_custom_call" | custom-call | flops 45900001280 | bytes 1000 | tf_op jit(solution)/shard_map/pallas_call | solution.py:720
  550.7 42.1 %shard_map.170 = (f32[1024,2048]{1,0:T(8,128)}, bf16[256,3072]{1,0:T(8,128)(2,1)}) custom-call(bf16[1024,3072]{1,0:T(8,128)(2,1)} %shard_map.168.refs_0_, bf16[3072,2048]{1,0:T(8,128)(2,1)} %all-gather.12.cloned.1.call-done.refs_1_.refs_2_, bf16[256,3072]{1,0:T(8,128)(2,1)} %get-tuple-element.358.refs_2_), custom_call_target="tpu_custom_call" | custom-call | flops 45900001280 | bytes 1000 | tf_op jit(solution)/shard_map/pallas_call | solution.py:720
  599.2 75.7 %shard_map.171 = (f32[1024,2048]{1,0:T(8,128)}, bf16[1024,2048]{1,0:T(8,128)(2,1)}, bf16[256,3072]{1,0:T(8,128)(2,1)}) custom-call(bf16[1024,3072]{1,0:T(8,128)(2,1)} %shard_map.168.refs_0_, bf16[3072,2048]{1,0:T(8,128)(2,1)} %all-gather.10.cloned.1.call-done.refs_1_.refs_3_, f32[1024,2048]{1,0:T(8,128)} %get-tuple-element.396.refs_2_, ...), custom_call_target="tpu_custom_call" | custom-call | flops 45900001280 | bytes 1000 | tf_op jit(solution)/shard_map/pallas_call | solution.py:720
  681.0 41.9 %shard_map.173 = (f32[1024,2048]{1,0:T(8,128)}, bf16[256,3072]{1,0:T(8,128)(2,1)}) custom-call(bf16[1024,3072]{1,0:T(8,128)(2,1)} %shard_map.172.refs_0_.refs_1_, bf16[3072,2048]{1,0:T(8,128)(2,1)} %all-gather.12.cloned.1.call-done.refs_1_.refs_2_, bf16[256,3072]{1,0:T(8,128)(2,1)} %collective-permute-done.2.refs_2_.got_ref), custom_call_target="tpu_custom_call" | custom-call | flops 45900001280 | bytes 1000 | tf_op jit(solution)/shard_map/pallas_call | solution.py:720
  733.6 20.2 %shard_map.175 = (f32[1024,2048]{1,0:T(8,128)}, bf16[1024,2048]{1,0:T(8,128)(2,1)}) custom-call(bf16[1024,3072]{1,0:T(8,128)(2,1)} %shard_map.172.refs_0_.refs_1_, bf16[3072,2048]{1,0:T(8,128)(2,1)} %all-gather.10.cloned.1.call-done.refs_1_.refs_3_, f32[1024,2048]{1,0:T(8,128)} %get-tuple-element.408.refs_2_), custom_call_target="tpu_custom_call" | custom-call | flops 21904332800 | bytes 1000 | tf_op jit(solution)/shard_map/pallas_call | solution.py:720
  753.8 35.3 %shard_map.176 = bf16[2048,3072]{1,0:T(8,128)(2,1)} custom-call(bf16[1024,2048]{1,0:T(8,128)(2,1)} %get-tuple-element.462.refs_0_, bf16[1024,2048]{1,0:T(8,128)(2,1)} %get-tuple-element.466.refs_1_.refs_0_, bf16[1024,3072]{1,0:T(8,128)(2,1)} %get-tuple-element.394.refs_2_.refs_0_, bf16[1024,3072]{1,0:T(8,128)(2,1)} %get-tuple-element.406.refs_3_.refs_0_), custom_call_target="tpu_custom_call" | custom-call | flops 43808665600 | bytes 1000 | tf_op jit(solution)/shard_map/pallas_call | solution.py:720
  793.8 24.6 %shard_map.177 = (bf16[1024,2048]{1,0:T(8,128)(2,1)}, bf16[1024,2048]{1,0:T(8,128)(2,1)}) custom-call(bf16[1024,3072]{1,0:T(8,128)(2,1)} %get-tuple-element.394.refs_2_.refs_0_, bf16[2048,3072]{1,0:T(8,128)(2,1)} %all-gather.14.cloned.1.call-done.refs_1_, f32[1024,2048]{1,0:T(8,128)} %get-tuple-element.396.refs_2_, f32[1024,2048]{1,0:T(8,128)} %get-tuple-element.397.refs_3_), custom_call_target="tpu_custom_call" | custom-call | flops 21904332800 | bytes 1000 | tf_op jit(solution)/shard_map/pallas_call | solution.py:720
  818.4 33.3 %shard_map.178.term_ref = bf16[1024,3072]{1,0:T(8,128)(2,1)} custom-call(bf16[1024,2048]{1,0:T(8,128)(2,1)} %get-tuple-element.432.refs_0_.refs_2_, bf16[1024,2048]{1,0:T(8,128)(2,1)} %get-tuple-element.449.refs_1_.refs_2_, bf16[3072,2048]{1,0:T(8,128)(2,1)} %all-gather.12.cloned.1.call-done.refs_1_.refs_2_, ...), custom_call_target="tpu_custom_call" | custom-call | flops 43808665600 | bytes 1000 | tf_op jit(solution)/shard_map/pallas_call | solution.py:720
  859.1 44.8 %shard_map.180 = (bf16[1024,2048]{1,0:T(8,128)(2,1)}, bf16[1024,2048]{1,0:T(8,128)(2,1)}, bf16[256,3072]{1,0:T(8,128)(2,1)}) custom-call(bf16[1024,3072]{1,0:T(8,128)(2,1)} %get-tuple-element.406.refs_3_.refs_0_, bf16[2048,3072]{1,0:T(8,128)(2,1)} %all-gather.14.cloned.1.call-done.refs_1_, f32[1024,2048]{1,0:T(8,128)} %get-tuple-element.408.refs_2_, ...), custom_call_target="tpu_custom_call" | custom-call | flops 45900001280 | bytes 1000 | tf_op jit(solution)/shard_map/pallas_call | solution.py:720
  911.9 42.2 %shard_map.181 = (bf16[1024,3072]{1,0:T(8,128)(2,1)}, bf16[256,3072]{1,0:T(8,128)(2,1)}) custom-call(bf16[1024,2048]{1,0:T(8,128)(2,1)} %get-tuple-element.433.refs_0_.refs_3_, bf16[1024,2048]{1,0:T(8,128)(2,1)} %get-tuple-element.450.refs_1_.refs_3_, bf16[3072,2048]{1,0:T(8,128)(2,1)} %all-gather.12.cloned.1.call-done.refs_1_.refs_2_, ...), custom_call_target="tpu_custom_call" | custom-call | flops 45900001280 | bytes 1000 | tf_op jit(solution)/shard_map/pallas_call | solution.py:720
  967.6 42.2 %shard_map.184 = (bf16[3072,2048]{1,0:T(8,128)(2,1)}, bf16[256,3072]{1,0:T(8,128)(2,1)}) custom-call(bf16[1024,3072]{1,0:T(8,128)(2,1)} %shard_map.168.refs_0_, bf16[1024,3072]{1,0:T(8,128)(2,1)} %shard_map.172.refs_0_.refs_1_, bf16[1024,2048]{1,0:T(8,128)(2,1)} %get-tuple-element.432.refs_0_.refs_2_, bf16[1024,2048]{1,0:T(8,128)(2,1)} %get-tuple-element.433.refs_0_.refs_3_, ...), custom_call_target="tpu_custom_call" | custom-call | flops 45900001280 | bytes 1000 | tf_op jit(solution)/shard_map/pallas_call | solution.py:720
  1034.0 42.8 %shard_map.187 = (bf16[3072,2048]{1,0:T(8,128)(2,1)}, bf16[256,3072]{1,0:T(8,128)(2,1)}) custom-call(bf16[1024,3072]{1,0:T(8,128)(2,1)} %shard_map.168.refs_0_, bf16[1024,3072]{1,0:T(8,128)(2,1)} %shard_map.172.refs_0_.refs_1_, bf16[1024,2048]{1,0:T(8,128)(2,1)} %get-tuple-element.449.refs_1_.refs_2_, bf16[1024,2048]{1,0:T(8,128)(2,1)} %get-tuple-element.450.refs_1_.refs_3_, ...), custom_call_target="tpu_custom_call" | custom-call | flops 45900001280 | bytes 1000 | tf_op jit(solution)/shard_map/pallas_call | solution.py:720
  1171.2 74.9 %shard_map.196 = (bf16[1024,768]{1,0:T(8,128)(2,1)}, bf16[1024,768]{1,0:T(8,128)(2,1)}, bf16[1024,768]{1,0:T(8,128)(2,1)}, bf16[1024,768]{1,0:T(8,128)(2,1)}, bf...) custom-call(bf16[1024,768]{1,0:T(8,128)(2,1)} %get-tuple-element.321.refs_0_, ...), custom_call_target="tpu_custom_call" | custom-call | flops 45900001280 | bytes 1000 | tf_op jit(solution)/shard_map/pallas_call | solution.py:720
  1267.6 75.3 %shard_map.198 = (bf16[3072,2304]{1,0:T(8,128)(2,1)}, bf16[256,3072]{1,0:T(8,128)(2,1)}) custom-call(bf16[1024,3072]{1,0:T(8,128)(2,1)} %get-tuple-element.492.refs_0_, bf16[1024,3072]{1,0:T(8,128)(2,1)} %get-tuple-element.493.refs_0_.refs_1_, bf16[1024,2304]{1,0:T(8,128)(2,1)} %constant_dynamic-update-slice_fusion.refs_2_.refs_0_, ...), custom_call_target="tpu_custom_call" | custom-call | flops 49284751360 | bytes 1000 | tf_op jit(solution)/shard_map/pallas_call | solution.py:720
  1381.2 73.5 %shard_map.201 = (bf16[1024,3072]{1,0:T(8,128)(2,1)}, bf16[256,3072]{1,0:T(8,128)(2,1)}) custom-call(bf16[1024,2304]{1,0:T(8,128)(2,1)} %copy-done.43, bf16[3072,2304]{1,0:T(8,128)(2,1)} %all-gather.6.cloned.1.call-done.refs_1_, bf16[256,3072]{1,0:T(8,128)(2,1)} %get-tuple-element.511.refs_2_), custom_call_target="tpu_custom_call" | custom-call | flops 45900001280 | bytes 1000 | tf_op jit(solution)/shard_map/pallas_call | solution.py:720
  1464.6 51.4 %shard_map.204 = (bf16[256,3072]{1,0:T(8,128)(2,1)}, bf16[96,3072]{1,0:T(8,128)(2,1)}) custom-call(bf16[256,3072]{1,0:T(8,128)(2,1)} %get-tuple-element.518.refs_0_, bf16[96,3072]{1,0:T(8,128)(2,1)} %get-tuple-element.519.refs_1_), custom_call_target="tpu_custom_call" | custom-call | flops 67999997952 | bytes 1000 | tf_op jit(solution)/shard_map/pallas_call | solution.py:778
  1547.7 64.8 %collective-permute-done.11 = f32[2,192]{1,0:T(2,128)S(1)} collective-permute-done((f32[2,192]{1,0:T(2,128)S(1)}, f32[2,192]{1,0:T(2,128)S(1)}, u32[]{:S(2)}, u32[]{:S(2)}) %collective-permute-start.11) | collective-permute-done | bytes 1568 | tf_op jit(solution)/shard_map/ppermute | solution.py:1160
  1643.7 83.7 %shard_map.206 = bf16[384,2304]{1,0:T(8,128)(2,1)} custom-call(bf16[384,2304]{1,0:T(8,128)(2,1)} %get-tuple-element.551.refs_0_), custom_call_target="tpu_custom_call" | custom-call | flops 67999997952 | bytes 1000 | tf_op jit(solution)/shard_map/pallas_call | solution.py:778
  (309 shorter events, 442.7 us)
Async XLA Ops:
  7.2 316.7 %all-gather.6.cloned.1.call-start = ((), (), s32[]{:S(2)}) async-start(), calls=%async_computation.5 | async-start | bytes 17694720 | tf_op jit(solution)/shard_map/all_gather | solution.py:1131
  108.2 274.6 %all-gather.8.cloned.1.call-start = ((), (), s32[]{:S(2)}) async-start(), calls=%async_computation.6 | async-start | bytes 5898240 | tf_op jit(solution)/shard_map/all_gather | solution.py:1131
  213.2 337.5 %all-gather.12.cloned.1.call-start = ((), (), s32[]{:S(2)}) async-start(), calls=%async_computation.8 | async-start | bytes 15728640 | tf_op jit(solution)/shard_map/all_gather | solution.py:1131
  304.4 294.8 %all-gather.10.cloned.1.call-start = ((), (), s32[]{:S(2)}) async-start(), calls=%async_computation.7 | async-start | bytes 15728640 | tf_op jit(solution)/shard_map/all_gather | solution.py:1131
  304.6 70.4 %collective-permute-start = (bf16[384,2048]{1,0:T(8,128)(2,1)S(1)}, bf16[384,2048]{1,0:T(8,128)(2,1)S(1)}, u32[]{:S(2)}, u32[]{:S(2)}) collective-permute-start(bf16[384,2048]{1,0:T(8,128)(2,1)S(1)} %get-tuple-element.325.own_ref), channel_id=1, source_target_pairs={{0,2},{1,3},{2,0},{3,1},{4,6},{5,7},{6,4},{7,5},{8,10},{9,11},{10,... | collective-permute-start | bytes 4718600 | tf_op jit(solution)/shard_map/ppermute | solution.py:1099
  380.0 413.9 %all-gather.14.cloned.1.call-start = ((), (), s32[]{:S(2)}) async-start(), calls=%async_computation.9 | async-start | bytes 15728640 | tf_op jit(solution)/shard_map/all_gather | solution.py:1131
  381.1 214.9 %copy-start.41 = (f32[3072]{0:T(1024)}, f32[3072]{0:T(1024)S(1)}, u32[]{:S(2)}) copy-start(f32[3072]{0:T(1024)S(1)} %convert_element_type.136) | copy-start | bytes 36868
  381.1 165.7 %collective-permute-start.1 = (bf16[256,3072]{1,0:T(8,128)(2,1)}, bf16[256,3072]{1,0:T(8,128)(2,1)}, u32[]{:S(2)}, u32[]{:S(2)}) collective-permute-start(bf16[256,3072]{1,0:T(8,128)(2,1)} %own_ref.1), channel_id=1, source_target_pairs={{0,2},{1,3},{2,0},{3,1},{4,6},{5,7},{6,4},{7,5},{8,10},{9,11},{10,... | collective-permute-start | bytes 4718600 | tf_op jit(solution)/shard_map/ppermute | solution.py:1099
  550.7 479.5 %reduce-scatter.6.cloned.1.call-start = ((), (), s32[]{:S(2)}) async-start(), calls=%async_computation.10 | async-start | bytes 15728640 | tf_op jit(solution)/shard_map/reduce_scatter | solution.py:1134
  592.8 88.2 %collective-permute-start.2 = (bf16[256,3072]{1,0:T(8,128)(2,1)}, bf16[256,3072]{1,0:T(8,128)(2,1)}, u32[]{:S(2)}, u32[]{:S(2)}) collective-permute-start(bf16[256,3072]{1,0:T(8,128)(2,1)} %get-tuple-element.369), channel_id=1, source_target_pairs={{0,2},{1,3},{2,0},{3,1},{4,6},{5,7},{6,4},{7,5},{8,10},{9,11},{10,... | collective-permute-start | bytes 4718600 | tf_op jit(solution)/shard_map/ppermute | solution.py:1099
  789.1 375.3 %reduce-scatter.8.cloned.1.call-start = ((), (), s32[]{:S(2)}) async-start(), calls=%async_computation.11 | async-start | bytes 15728640 | tf_op jit(solution)/shard_map/reduce_scatter | solution.py:1134
  1009.8 243.9 %reduce-scatter.10.cloned.1.call-start = ((), (), s32[]{:S(2)}) async-start(), calls=%async_computation.12 | async-start | bytes 15728640 | tf_op jit(solution)/shard_map/reduce_scatter | solution.py:1134
  1076.8 385.3 %reduce-scatter.12.cloned.1.call-start = ((), (), s32[]{:S(2)}) async-start(), calls=%async_computation.13 | async-start | bytes 5898240 | tf_op jit(solution)/shard_map/reduce_scatter | solution.py:1134
  1078.1 462.9 %collective-permute-start.5 = (bf16[256,3072]{1,0:T(8,128)(2,1)}, bf16[256,3072]{1,0:T(8,128)(2,1)}, u32[]{:S(2)}, u32[]{:S(2)}) collective-permute-start(bf16[256,3072]{1,0:T(8,128)(2,1)} %get-tuple-element.446), channel_id=1, source_target_pairs={{0,2},{1,3},{2,0},{3,1},{4,6},{5,7},{6,4},{7,5},{8,10},{9,11},{10,... | collective-permute-start | bytes 4718600 | tf_op jit(solution)/shard_map/ppermute | solution.py:1099
  1168.2 379.5 %collective-permute-start.4 = (bf16[384,2048]{1,0:T(8,128)(2,1)}, bf16[384,2048]{1,0:T(8,128)(2,1)}, u32[]{:S(2)}, u32[]{:S(2)}) collective-permute-start(bf16[384,2048]{1,0:T(8,128)(2,1)} %get-tuple-element.472), channel_id=1, source_target_pairs={{0,2},{1,3},{2,0},{3,1},{4,6},{5,7},{6,4},{7,5},{8,10},{9,11},{10,... | collective-permute-start | bytes 4718600 | tf_op jit(solution)/shard_map/ppermute | solution.py:1099
  1171.2 468.4 %reduce-scatter.14.cloned.1.call-start = ((), (), s32[]{:S(2)}) async-start(), calls=%async_computation.14 | async-start | bytes 17694720 | tf_op jit(solution)/shard_map/reduce_scatter | solution.py:1134
  1257.5 362.8 %collective-permute-start.7 = (bf16[384,2048]{1,0:T(8,128)(2,1)}, bf16[384,2048]{1,0:T(8,128)(2,1)}, u32[]{:S(2)}, u32[]{:S(2)}) collective-permute-start(bf16[384,2048]{1,0:T(8,128)(2,1)} %get-tuple-element.485), channel_id=1, source_target_pairs={{0,2},{1,3},{2,0},{3,1},{4,6},{5,7},{6,4},{7,5},{8,10},{9,11},{10,... | collective-permute-start | bytes 4718600 | tf_op jit(solution)/shard_map/ppermute | solution.py:1099
  1350.8 266.0 %collective-permute-start.3 = (bf16[256,3072]{1,0:T(8,128)(2,1)}, bf16[256,3072]{1,0:T(8,128)(2,1)}, u32[]{:S(2)}, u32[]{:S(2)}) collective-permute-start(bf16[256,3072]{1,0:T(8,128)(2,1)} %get-tuple-element.588), channel_id=1, source_target_pairs={{0,2},{1,3},{2,0},{3,1},{4,6},{5,7},{6,4},{7,5},{8,10},{9,11},{10,... | collective-permute-start | bytes 4718600 | tf_op jit(solution)/shard_map/ppermute | solution.py:1099
  1527.3 3.8 collective-permute-start.8
  1531.2 7.6 collective-permute-start.9
  1538.8 3.6 collective-permute-start.10
  1541.0 92.4 %collective-permute-start.6 = (bf16[256,3072]{1,0:T(8,128)(2,1)}, bf16[256,3072]{1,0:T(8,128)(2,1)}, u32[]{:S(2)}, u32[]{:S(2)}) collective-permute-start(bf16[256,3072]{1,0:T(8,128)(2,1)} %get-tuple-element.586), channel_id=1, source_target_pairs={{0,2},{1,3},{2,0},{3,1},{4,6},{5,7},{6,4},{7,5},{8,10},{9,11},{10,... | collective-permute-start | bytes 4718600 | tf_op jit(solution)/shard_map/ppermute | solution.py:1099
  1542.5 70.0 %collective-permute-start.11 = (f32[2,192]{1,0:T(2,128)S(1)}, f32[2,192]{1,0:T(2,128)S(1)}, u32[]{:S(2)}, u32[]{:S(2)}) collective-permute-start(f32[2,192]{1,0:T(2,128)S(1)} %bitcast.100), channel_id=1, source_target_pairs={{0,2},{1,3},{2,0},{3,1},{4,6},{5,7},{6,4},{7,5},{8,10},{9,11},{10,... | collective-permute-start | bytes 4616 | tf_op jit(solution)/shard_map/ppermute | solution.py:1160
  1612.6 3.6 collective-permute-start.12
  (60 other events, 884.2 us)
Sparse Core Ops, SparseCore 0:
  108.3 135.6 all-gather.5
  245.8 57.0 all-gather.7
  304.7 122.5 all-gather.11
  429.0 122.5 all-gather.9
  553.2 122.5 all-gather.13
  789.2 119.5 reduce-scatter.5
  1009.9 119.8 reduce-scatter.7
  1133.0 120.7 reduce-scatter.9
  1256.7 57.0 reduce-scatter.11
  1351.9 132.5 reduce-scatter.13

commit v8 on v7

--- a/solution.py
+++ b/solution.py
@@ -744,7 +744,7 @@
     return exchange_call(
         functools.partial(swap_kernel, kinds), next_key[0], values,
         [jax.ShapeDtypeStruct(value.shape, value.dtype) for value in values],
-        [pltpu.SemaphoreType.DMA((len(pushes),))] * 2, flops=40 * 10**9,
+        [pltpu.SemaphoreType.DMA((len(pushes),))] * 2, flops=110 * 10**9,
     )
 
 
@@ -1355,9 +1355,6 @@
     mlp_keep_first, mlp_send_first = act(core_reduce, mlp_first)
     mlp_second = act(dot_bf16, a_second, down_full)
     mlp_keep_second, mlp_send_second = act(core_reduce, mlp_second)
-    gate_mine, gate_away = act(lambda pair: core_split(9, pair), gate_sum)
-    gate_got = swap_far(gate_away)
-
     def attend_back(heads_first, heads_second, pushes=()):
         return attention_call(
             backward_both,
@@ -1371,11 +1368,12 @@
             pushes,
         )
 
-    *grads, mlp_branch_first = act(
-        attend_back, heads_first, heads_second, sends=[("near", mlp_send_first)]
-    )
-    up_mine, up_away = act(lambda pair: core_split(9, pair), up_sum)
-    up_got = swap_far(up_away)
+    *grads, mlp_branch_first, mlp_branch_second = act(
+        attend_back, heads_first, heads_second,
+        sends=[("near", mlp_send_first), ("near", mlp_send_second)],
+    )
+    gate_mine, gate_away = act(lambda pair: core_split(9, pair), gate_sum)
+    gate_got = swap_far(gate_away)
     p_first, p_second = act(
         lambda *parts: (
             jnp.concatenate(parts[:3], axis=1),
@@ -1389,15 +1387,15 @@
         second = (second + second_keep + second_got.astype(jnp.float32)).astype(jnp.bfloat16)
         return jnp.where(far == 0, first, second), jnp.where(far == 0, second, first)
 
-    grad_qkv, mlp_branch_second = act(
-        grad_sum, h1_first, p_first, h1_second, p_second, sends=[("near", mlp_send_second)]
-    )
+    grad_qkv = act(grad_sum, h1_first, p_first, h1_second, p_second)
     qkv_sum = plane_scatter(grad_qkv)
     out_keep, out_send = act(
         finish_output,
         m_first, mlp_keep_first, mlp_branch_first, m_second, mlp_keep_second, mlp_branch_second,
     )
     out_got = swap_far(out_send)
+    up_mine, up_away = act(lambda pair: core_split(9, pair), up_sum)
+    up_got = swap_far(up_away)
     term_first = act(heads_back, p_first, qkv_full)
     keep_first, send_first = act(core_reduce, term_first)
     term_second, back_first = act(
@@ -1421,6 +1419,8 @@
         )
 
     back_second, out_back = swap(("near", send_second), ("far", out_away))
+    qkv_mine, qkv_away = act(lambda pair: core_split(0, pair), qkv_sum)
+    qkv_back = swap_far(qkv_away)
     i_first, gain_one_first = act(
         first_back, streams[0], scales_one[0], keep_first, back_first, g_first
     )
@@ -1438,8 +1438,6 @@
         jnp.stack([gain_one_first + gain_one_second, gain_two_first + gain_two_second])
     )
     in_grad = act(lambda keep, got: settle(keep, got.astype(jnp.float32)), in_keep, in_got)
-    qkv_mine, qkv_away = act(lambda pair: core_split(0, pair), qkv_sum)
-    qkv_back = swap(("far", qkv_away))
     qkv_owned = act(add_wide, qkv_mine, qkv_back)
     return (
         block_out,

time: 1750 us -> 1710 us (0.977)
  Pallas kernels: 1480 us -> 1400 us
  waiting for transfers between devices: 77.3 us -> 102 us
    pallas_call x29 -> x28, Pallas kernels: 526 us -> 441 us  [exchange_call(): pl.pallas_call(kernel, out_shape=outs, in_specs=[anywhere] * len(operands...]
    ppermute x5, waiting for transfers between devices: 68.7 us -> 101 us  [scatter_gains(): lax.ppermute(sent, axis, [(i, i ^ step) for i in range(size)])]
    unnamed x134 -> x148, local copies, waits for them, and re-layouts: 34.8 us -> 42.4 us
  transfers between devices with their start and end apart: 23 -> 24, of which waited for: 5 -> 2; matrix products, arithmetic and copies ran while one was open for 7% -> 7% of each run, Pallas kernels for 75% -> 77%
where the time goes in v8:
time: 1710 us
  Pallas kernels  1400 us (82%)
  other arithmetic  104 us (6%)
  waiting for transfers between devices  102 us (6%)
  local copies, waits for them, and re-layouts  68.8 us (4%)
  starting transfers between devices  18.1 us (1%)
    pallas_call x26, Pallas kernels, grid_call(): pl.pallas_call(kernel, out_shape=outs, grid=grid, in_specs=in_specs, out_...  959 us
    pallas_call x28, Pallas kernels, exchange_call(): pl.pallas_call(kernel, out_shape=outs, in_specs=[anywhere] * len(operands...  441 us
    ppermute x5, waiting for transfers between devices, scatter_gains(): lax.ppermute(sent, axis, [(i, i ^ step) for i in range(size)])  101 us
    unnamed x148, local copies, waits for them, and re-layouts  42.4 us
  transfers between devices with their start and end apart: 24, of which 2 were waited for; matrix products, arithmetic and copies ran while one was open for 7% of the time, Pallas kernels for 77%

profile of v8, /device:TPU:0, one launch (start us, length us, event | category | flops | bytes accessed | tf_op | source)
XLA Modules:
  0.0 1707.9 jit_solution(16734733851313342615)
XLA Ops:
  20.3 82.6 %shard_map.152 = (bf16[256,3072]{1,0:T(8,128)(2,1)}, bf16[384,2304]{1,0:T(8,128)(2,1)}, s32[8,256]{1,0:T(8,128)}) custom-call(bf16[256,3072]{1,0:T(8,128)(2,1)} %fusion.4.refs_0_.own_ref, bf16[384,2304]{1,0:T(8,128)(2,1)} %copy.35.refs_1_, s32[8,256]{1,0:T(8,128)} %broadcast_in_dim.11.refs_2_), custom_call_target="tpu_custom_call" | custom-call | flops 186999996416 | bytes 1000 | tf_op jit(solution)/shard_map/pallas_call | solution.py:778
  117.0 96.5 %shard_map.154 = (bf16[256,3072]{1,0:T(8,128)(2,1)}, bf16[256,3072]{1,0:T(8,128)(2,1)}, bf16[96,3072]{1,0:T(8,128)(2,1)}, s32[16,256]{1,0:T(8,128)}) custom-call(bf16[256,3072]{1,0:T(8,128)(2,1)} %get-tuple-element.288.refs_0_, bf16[256,3072]{1,0:T(8,128)(2,1)} %get-tuple-element.377.refs_1_.own_ref, bf16[96,3072]{1,0:T(8,128)(2,1)} %own_ref, ...), custom_call_target="tpu_custom_call" | custom-call | flops 186999996416 | bytes 1000 | tf_op jit(solution)/shard_map/pallas_call | solution.py:778
  232.4 71.6 %shard_map.156 = (bf16[256,3072]{1,0:T(8,128)(2,1)}, bf16[384,2048]{1,0:T(8,128)(2,1)}, s32[32,256]{1,0:T(8,128)}) custom-call(bf16[256,3072]{1,0:T(8,128)(2,1)} %multiply_convert_fusion.2.refs_0_.got_ref, bf16[384,2048]{1,0:T(8,128)(2,1)} %get-tuple-element.305.refs_1_.own_ref, s32[32,256]{1,0:T(8,128)} %pad_add_fusion.1.refs_2_), custom_call_target="tpu_custom_call" | custom-call | flops 186999996416 | bytes 1000 | tf_op jit(solution)/shard_map/pallas_call | solution.py:778
  328.3 21.7 %shard_map.159.q_ref.k_ref.v_ref = f32[1024,2304]{1,0:T(8,128)} custom-call(bf16[1024,3072]{1,0:T(8,128)(2,1)} %get-tuple-element.489.refs_0_, bf16[3072,2304]{1,0:T(8,128)(2,1)} %all-gather.6.cloned.1.call-done.refs_1_), custom_call_target="tpu_custom_call" | custom-call | flops 24642375680 | bytes 1000 | tf_op jit(solution)/shard_map/pallas_call | solution.py:720
  350.0 29.2 %shard_map.160 = (bf16[1024,768]{1,0:T(8,128)(2,1)}, bf16[1024,768]{1,0:T(8,128)(2,1)}, bf16[1024,768]{1,0:T(8,128)(2,1)}, bf16[1024,768]{1,0:T(8,128)(2,1)}, f32[2,1024,4]{2,1,0:T(8,128)}) custom-call(f32[1024,2304]{1,0:T(8,128)} %shard_map.159.q_ref.k_ref.v_ref, f32[1024,2304]{1,0:T(8,128)} %shard_map.159.q_ref.k_ref.v_ref, ...), custom_call_target="tpu_custom_call" | custom-call | flops 8556380160 | bytes 1000 | tf_op jit(solution)/shard_map/pallas_call | solution.py:720
  405.0 75.9 %shard_map.164 = (f32[1024,2304]{1,0:T(8,128)}, bf16[256,3072]{1,0:T(8,128)(2,1)}) custom-call(bf16[1024,3072]{1,0:T(8,128)(2,1)} %get-tuple-element.490.refs_0_.refs_1_, bf16[3072,2304]{1,0:T(8,128)(2,1)} %all-gather.6.cloned.1.call-done.refs_1_, bf16[256,3072]{1,0:T(8,128)(2,1)} %get-tuple-element.331.refs_2_), custom_call_target="tpu_custom_call" | custom-call | flops 45900001280 | bytes 1000 | tf_op jit(solution)/shard_map/pallas_call | solution.py:720
  487.6 39.8 %shard_map.165 = (bf16[1024,768]{1,0:T(8,128)(2,1)}, bf16[1024,768]{1,0:T(8,128)(2,1)}, bf16[1024,768]{1,0:T(8,128)(2,1)}, bf16[1024,768]{1,0:T(8,128)(2,1)}, f3...) custom-call(f32[1024,2304]{1,0:T(8,128)} %get-tuple-element.337.refs_0_.refs_1_.refs_2_, ...), custom_call_target="tpu_custom_call" | custom-call | flops 45900001280 | bytes 1000 | tf_op jit(solution)/shard_map/pallas_call | solution.py:720
  554.7 42.1 %shard_map.170 = (f32[1024,2048]{1,0:T(8,128)}, bf16[256,3072]{1,0:T(8,128)(2,1)}) custom-call(bf16[1024,3072]{1,0:T(8,128)(2,1)} %shard_map.168.refs_0_, bf16[3072,2048]{1,0:T(8,128)(2,1)} %all-gather.12.cloned.1.call-done.refs_1_.refs_2_, bf16[256,3072]{1,0:T(8,128)(2,1)} %get-tuple-element.356.refs_2_), custom_call_target="tpu_custom_call" | custom-call | flops 45900001280 | bytes 1000 | tf_op jit(solution)/shard_map/pallas_call | solution.py:720
  603.8 75.5 %shard_map.171 = (f32[1024,2048]{1,0:T(8,128)}, bf16[1024,2048]{1,0:T(8,128)(2,1)}, bf16[256,3072]{1,0:T(8,128)(2,1)}) custom-call(bf16[1024,3072]{1,0:T(8,128)(2,1)} %shard_map.168.refs_0_, bf16[3072,2048]{1,0:T(8,128)(2,1)} %all-gather.10.cloned.1.call-done.refs_1_.refs_3_, f32[1024,2048]{1,0:T(8,128)} %get-tuple-element.394.refs_2_, ...), custom_call_target="tpu_custom_call" | custom-call | flops 45900001280 | bytes 1000 | tf_op jit(solution)/shard_map/pallas_call | solution.py:720
  685.4 42.0 %shard_map.173 = (f32[1024,2048]{1,0:T(8,128)}, bf16[256,3072]{1,0:T(8,128)(2,1)}) custom-call(bf16[1024,3072]{1,0:T(8,128)(2,1)} %shard_map.172.refs_0_.refs_1_, bf16[3072,2048]{1,0:T(8,128)(2,1)} %all-gather.12.cloned.1.call-done.refs_1_.refs_2_, bf16[256,3072]{1,0:T(8,128)(2,1)} %collective-permute-done.2.refs_2_.got_ref), custom_call_target="tpu_custom_call" | custom-call | flops 45900001280 | bytes 1000 | tf_op jit(solution)/shard_map/pallas_call | solution.py:720
  738.1 20.2 %shard_map.175 = (f32[1024,2048]{1,0:T(8,128)}, bf16[1024,2048]{1,0:T(8,128)(2,1)}) custom-call(bf16[1024,3072]{1,0:T(8,128)(2,1)} %shard_map.172.refs_0_.refs_1_, bf16[3072,2048]{1,0:T(8,128)(2,1)} %all-gather.10.cloned.1.call-done.refs_1_.refs_3_, f32[1024,2048]{1,0:T(8,128)} %get-tuple-element.406.refs_2_), custom_call_target="tpu_custom_call" | custom-call | flops 21904332800 | bytes 1000 | tf_op jit(solution)/shard_map/pallas_call | solution.py:720
  758.2 35.3 %shard_map.176 = bf16[2048,3072]{1,0:T(8,128)(2,1)} custom-call(bf16[1024,2048]{1,0:T(8,128)(2,1)} %get-tuple-element.460.refs_0_, bf16[1024,2048]{1,0:T(8,128)(2,1)} %get-tuple-element.464.refs_1_.refs_0_, bf16[1024,3072]{1,0:T(8,128)(2,1)} %get-tuple-element.392.refs_2_.refs_0_, bf16[1024,3072]{1,0:T(8,128)(2,1)} %get-tuple-element.404.refs_3_.refs_0_), custom_call_target="tpu_custom_call" | custom-call | flops 43808665600 | bytes 1000 | tf_op jit(solution)/shard_map/pallas_call | solution.py:720
  798.2 25.0 %shard_map.177 = (bf16[1024,2048]{1,0:T(8,128)(2,1)}, bf16[1024,2048]{1,0:T(8,128)(2,1)}) custom-call(bf16[1024,3072]{1,0:T(8,128)(2,1)} %get-tuple-element.392.refs_2_.refs_0_, bf16[2048,3072]{1,0:T(8,128)(2,1)} %all-gather.14.cloned.1.call-done.refs_1_, f32[1024,2048]{1,0:T(8,128)} %get-tuple-element.394.refs_2_, f32[1024,2048]{1,0:T(8,128)} %get-tuple-element.395.refs_3_), custom_call_target="tpu_custom_call" | custom-call | flops 21904332800 | bytes 1000 | tf_op jit(solution)/shard_map/pallas_call | solution.py:720
  823.2 33.3 %shard_map.178.term_ref = bf16[1024,3072]{1,0:T(8,128)(2,1)} custom-call(bf16[1024,2048]{1,0:T(8,128)(2,1)} %get-tuple-element.430.refs_0_.refs_2_, bf16[1024,2048]{1,0:T(8,128)(2,1)} %get-tuple-element.447.refs_1_.refs_2_, bf16[3072,2048]{1,0:T(8,128)(2,1)} %all-gather.12.cloned.1.call-done.refs_1_.refs_2_, ...), custom_call_target="tpu_custom_call" | custom-call | flops 43808665600 | bytes 1000 | tf_op jit(solution)/shard_map/pallas_call | solution.py:720
  863.9 44.7 %shard_map.180 = (bf16[1024,2048]{1,0:T(8,128)(2,1)}, bf16[1024,2048]{1,0:T(8,128)(2,1)}, bf16[256,3072]{1,0:T(8,128)(2,1)}) custom-call(bf16[1024,3072]{1,0:T(8,128)(2,1)} %get-tuple-element.404.refs_3_.refs_0_, bf16[2048,3072]{1,0:T(8,128)(2,1)} %all-gather.14.cloned.1.call-done.refs_1_, f32[1024,2048]{1,0:T(8,128)} %get-tuple-element.406.refs_2_, ...), custom_call_target="tpu_custom_call" | custom-call | flops 45900001280 | bytes 1000 | tf_op jit(solution)/shard_map/pallas_call | solution.py:720
  916.6 41.9 %shard_map.181 = (bf16[1024,3072]{1,0:T(8,128)(2,1)}, bf16[256,3072]{1,0:T(8,128)(2,1)}) custom-call(bf16[1024,2048]{1,0:T(8,128)(2,1)} %get-tuple-element.431.refs_0_.refs_3_, bf16[1024,2048]{1,0:T(8,128)(2,1)} %get-tuple-element.448.refs_1_.refs_3_, bf16[3072,2048]{1,0:T(8,128)(2,1)} %all-gather.12.cloned.1.call-done.refs_1_.refs_2_, ...), custom_call_target="tpu_custom_call" | custom-call | flops 45900001280 | bytes 1000 | tf_op jit(solution)/shard_map/pallas_call | solution.py:720
  972.0 42.2 %shard_map.184 = (bf16[3072,2048]{1,0:T(8,128)(2,1)}, bf16[256,3072]{1,0:T(8,128)(2,1)}) custom-call(bf16[1024,3072]{1,0:T(8,128)(2,1)} %shard_map.168.refs_0_, bf16[1024,3072]{1,0:T(8,128)(2,1)} %shard_map.172.refs_0_.refs_1_, bf16[1024,2048]{1,0:T(8,128)(2,1)} %get-tuple-element.430.refs_0_.refs_2_, bf16[1024,2048]{1,0:T(8,128)(2,1)} %get-tuple-element.431.refs_0_.refs_3_, ...), custom_call_target="tpu_custom_call" | custom-call | flops 45900001280 | bytes 1000 | tf_op jit(solution)/shard_map/pallas_call | solution.py:720
  1038.0 43.0 %shard_map.187 = (bf16[3072,2048]{1,0:T(8,128)(2,1)}, bf16[256,3072]{1,0:T(8,128)(2,1)}) custom-call(bf16[1024,3072]{1,0:T(8,128)(2,1)} %shard_map.168.refs_0_, bf16[1024,3072]{1,0:T(8,128)(2,1)} %shard_map.172.refs_0_.refs_1_, bf16[1024,2048]{1,0:T(8,128)(2,1)} %get-tuple-element.447.refs_1_.refs_2_, bf16[1024,2048]{1,0:T(8,128)(2,1)} %get-tuple-element.448.refs_1_.refs_3_, ...), custom_call_target="tpu_custom_call" | custom-call | flops 45900001280 | bytes 1000 | tf_op jit(solution)/shard_map/pallas_call | solution.py:720
  1169.5 74.8 %shard_map.195 = (bf16[1024,768]{1,0:T(8,128)(2,1)}, bf16[1024,768]{1,0:T(8,128)(2,1)}, bf16[1024,768]{1,0:T(8,128)(2,1)}, bf16[1024,768]{1,0:T(8,128)(2,1)}, bf...) custom-call(bf16[1024,768]{1,0:T(8,128)(2,1)} %get-tuple-element.319, ...), custom_call_target="tpu_custom_call" | custom-call | flops 45900001280 | bytes 1000 | tf_op jit(solution)/shard_map/pallas_call | solution.py:720
  1257.8 39.0 %shard_map.197 = bf16[3072,2304]{1,0:T(8,128)(2,1)} custom-call(bf16[1024,3072]{1,0:T(8,128)(2,1)} %get-tuple-element.489.refs_0_, bf16[1024,3072]{1,0:T(8,128)(2,1)} %get-tuple-element.490.refs_0_.refs_1_, bf16[1024,2304]{1,0:T(8,128)(2,1)} %constant_dynamic-update-slice_fusion.refs_2_.refs_0_, bf16[1024,2304]{1,0:T(8,128)(2,1)} %copy-done.45), custom_call_target="tpu_custom_call" | custom-call | flops 49284751360 | bytes 1000 | tf_op jit(solution)/shard_map/pallas_call | solution.py:720
  1315.3 19.9 %shard_map.199.term_ref = bf16[1024,3072]{1,0:T(8,128)(2,1)} custom-call(bf16[1024,2304]{1,0:T(8,128)(2,1)} %constant_dynamic-update-slice_fusion.refs_2_.refs_0_, bf16[3072,2304]{1,0:T(8,128)(2,1)} %all-gather.6.cloned.1.call-done.refs_1_), custom_call_target="tpu_custom_call" | custom-call | flops 24642375680 | bytes 1000 | tf_op jit(solution)/shard_map/pallas_call | solution.py:720
  1342.6 118.2 %shard_map.201 = (bf16[1024,3072]{1,0:T(8,128)(2,1)}, bf16[256,3072]{1,0:T(8,128)(2,1)}) custom-call(bf16[1024,2304]{1,0:T(8,128)(2,1)} %copy-done.45, bf16[3072,2304]{1,0:T(8,128)(2,1)} %all-gather.6.cloned.1.call-done.refs_1_, bf16[256,3072]{1,0:T(8,128)(2,1)} %get-tuple-element.508.refs_2_), custom_call_target="tpu_custom_call" | custom-call | flops 45900001280 | bytes 1000 | tf_op jit(solution)/shard_map/pallas_call | solution.py:720
  1470.7 49.6 %shard_map.204 = (bf16[256,3072]{1,0:T(8,128)(2,1)}, bf16[96,3072]{1,0:T(8,128)(2,1)}) custom-call(bf16[256,3072]{1,0:T(8,128)(2,1)} %get-tuple-element.515.refs_0_, bf16[96,3072]{1,0:T(8,128)(2,1)} %get-tuple-element.516.refs_1_), custom_call_target="tpu_custom_call" | custom-call | flops 186999996416 | bytes 1000 | tf_op jit(solution)/shard_map/pallas_call | solution.py:778
  1570.6 101.0 %collective-permute-done.11 = f32[2,192]{1,0:T(2,128)S(1)} collective-permute-done((f32[2,192]{1,0:T(2,128)S(1)}, f32[2,192]{1,0:T(2,128)S(1)}, u32[]{:S(2)}, u32[]{:S(2)}) %collective-permute-start.11) | collective-permute-done | bytes 1568 | tf_op jit(solution)/shard_map/ppermute | solution.py:1160
  (324 shorter events, 427.4 us)
Async XLA Ops:
  7.2 321.2 %all-gather.6.cloned.1.call-start = ((), (), s32[]{:S(2)}) async-start(), calls=%async_computation.5 | async-start | bytes 17694720 | tf_op jit(solution)/shard_map/all_gather | solution.py:1131
  110.9 276.8 %all-gather.8.cloned.1.call-start = ((), (), s32[]{:S(2)}) async-start(), calls=%async_computation.6 | async-start | bytes 5898240 | tf_op jit(solution)/shard_map/all_gather | solution.py:1131
  215.9 338.7 %all-gather.12.cloned.1.call-start = ((), (), s32[]{:S(2)}) async-start(), calls=%async_computation.8 | async-start | bytes 15728640 | tf_op jit(solution)/shard_map/all_gather | solution.py:1131
  307.9 295.9 %all-gather.10.cloned.1.call-start = ((), (), s32[]{:S(2)}) async-start(), calls=%async_computation.7 | async-start | bytes 15728640 | tf_op jit(solution)/shard_map/all_gather | solution.py:1131
  309.3 70.1 %collective-permute-start = (bf16[384,2048]{1,0:T(8,128)(2,1)S(1)}, bf16[384,2048]{1,0:T(8,128)(2,1)S(1)}, u32[]{:S(2)}, u32[]{:S(2)}) collective-permute-start(bf16[384,2048]{1,0:T(8,128)(2,1)S(1)} %copy-done.30), channel_id=1, source_target_pairs={{0,2},{1,3},{2,0},{3,1},{4,6},{5,7},{6,4},{7,5},{8,10},{9,11},{10,... | collective-permute-start | bytes 4718600 | tf_op jit(solution)/shard_map/ppermute | solution.py:1099
  384.4 413.8 %all-gather.14.cloned.1.call-start = ((), (), s32[]{:S(2)}) async-start(), calls=%async_computation.9 | async-start | bytes 15728640 | tf_op jit(solution)/shard_map/all_gather | solution.py:1131
  385.5 165.3 %collective-permute-start.1 = (bf16[256,3072]{1,0:T(8,128)(2,1)}, bf16[256,3072]{1,0:T(8,128)(2,1)}, u32[]{:S(2)}, u32[]{:S(2)}) collective-permute-start(bf16[256,3072]{1,0:T(8,128)(2,1)} %own_ref.1), channel_id=1, source_target_pairs={{0,2},{1,3},{2,0},{3,1},{4,6},{5,7},{6,4},{7,5},{8,10},{9,11},{10,... | collective-permute-start | bytes 4718600 | tf_op jit(solution)/shard_map/ppermute | solution.py:1099
  554.7 479.5 %reduce-scatter.6.cloned.1.call-start = ((), (), s32[]{:S(2)}) async-start(), calls=%async_computation.10 | async-start | bytes 15728640 | tf_op jit(solution)/shard_map/reduce_scatter | solution.py:1134
  596.9 88.5 %collective-permute-start.2 = (bf16[256,3072]{1,0:T(8,128)(2,1)}, bf16[256,3072]{1,0:T(8,128)(2,1)}, u32[]{:S(2)}, u32[]{:S(2)}) collective-permute-start(bf16[256,3072]{1,0:T(8,128)(2,1)} %get-tuple-element.367), channel_id=1, source_target_pairs={{0,2},{1,3},{2,0},{3,1},{4,6},{5,7},{6,4},{7,5},{8,10},{9,11},{10,... | collective-permute-start | bytes 4718600 | tf_op jit(solution)/shard_map/ppermute | solution.py:1099
  793.5 450.8 %reduce-scatter.8.cloned.1.call-start = ((), (), s32[]{:S(2)}) async-start(), calls=%async_computation.11 | async-start | bytes 15728640 | tf_op jit(solution)/shard_map/reduce_scatter | solution.py:1134
  1014.2 294.3 %reduce-scatter.10.cloned.1.call-start = ((), (), s32[]{:S(2)}) async-start(), calls=%async_computation.12 | async-start | bytes 15728640 | tf_op jit(solution)/shard_map/reduce_scatter | solution.py:1134
  1081.1 387.2 %reduce-scatter.12.cloned.1.call-start = ((), (), s32[]{:S(2)}) async-start(), calls=%async_computation.13 | async-start | bytes 5898240 | tf_op jit(solution)/shard_map/reduce_scatter | solution.py:1134
  1082.3 458.9 %collective-permute-start.5 = (bf16[256,3072]{1,0:T(8,128)(2,1)}, bf16[256,3072]{1,0:T(8,128)(2,1)}, u32[]{:S(2)}, u32[]{:S(2)}) collective-permute-start(bf16[256,3072]{1,0:T(8,128)(2,1)} %get-tuple-element.444), channel_id=1, source_target_pairs={{0,2},{1,3},{2,0},{3,1},{4,6},{5,7},{6,4},{7,5},{8,10},{9,11},{10,... | collective-permute-start | bytes 4718600 | tf_op jit(solution)/shard_map/ppermute | solution.py:1099
  1169.4 350.9 %reduce-scatter.14.cloned.1.call-start = ((), (), s32[]{:S(2)}) async-start(), calls=%async_computation.14 | async-start | bytes 17694720 | tf_op jit(solution)/shard_map/reduce_scatter | solution.py:1134
  1248.2 298.6 %collective-permute-start.4 = (bf16[384,2048]{1,0:T(8,128)(2,1)}, bf16[384,2048]{1,0:T(8,128)(2,1)}, u32[]{:S(2)}, u32[]{:S(2)}) collective-permute-start(bf16[384,2048]{1,0:T(8,128)(2,1)} %get-tuple-element.482), channel_id=1, source_target_pairs={{0,2},{1,3},{2,0},{3,1},{4,6},{5,7},{6,4},{7,5},{8,10},{9,11},{10,... | collective-permute-start | bytes 4718600 | tf_op jit(solution)/shard_map/ppermute | solution.py:1099
  1307.2 241.5 %collective-permute-start.3 = (bf16[256,3072]{1,0:T(8,128)(2,1)}, bf16[256,3072]{1,0:T(8,128)(2,1)}, u32[]{:S(2)}, u32[]{:S(2)}) collective-permute-start(bf16[256,3072]{1,0:T(8,128)(2,1)} %get-tuple-element.584), channel_id=1, source_target_pairs={{0,2},{1,3},{2,0},{3,1},{4,6},{5,7},{6,4},{7,5},{8,10},{9,11},{10,... | collective-permute-start | bytes 4718600 | tf_op jit(solution)/shard_map/ppermute | solution.py:1099
  1312.3 247.9 %collective-permute-start.7 = (bf16[384,2048]{1,0:T(8,128)(2,1)}, bf16[384,2048]{1,0:T(8,128)(2,1)}, u32[]{:S(2)}, u32[]{:S(2)}) collective-permute-start(bf16[384,2048]{1,0:T(8,128)(2,1)} %get-tuple-element.501), channel_id=1, source_target_pairs={{0,2},{1,3},{2,0},{3,1},{4,6},{5,7},{6,4},{7,5},{8,10},{9,11},{10,... | collective-permute-start | bytes 4718600 | tf_op jit(solution)/shard_map/ppermute | solution.py:1099
  1524.5 166.3 %collective-permute-start.13 = (bf16[384,2304]{1,0:T(8,128)(2,1)}, bf16[384,2304]{1,0:T(8,128)(2,1)}, u32[]{:S(2)}, u32[]{:S(2)}) collective-permute-start(bf16[384,2304]{1,0:T(8,128)(2,1)} %get-tuple-element.522), channel_id=1, source_target_pairs={{0,2},{1,3},{2,0},{3,1},{4,6},{5,7},{6,4},{7,5},{8,10},{9,11},{10,... | collective-permute-start | bytes 5308424 | tf_op jit(solution)/shard_map/ppermute | solution.py:1099
  1541.2 144.1 %collective-permute-start.6 = (bf16[256,3072]{1,0:T(8,128)(2,1)}, bf16[256,3072]{1,0:T(8,128)(2,1)}, u32[]{:S(2)}, u32[]{:S(2)}) collective-permute-start(bf16[256,3072]{1,0:T(8,128)(2,1)} %get-tuple-element.582), channel_id=1, source_target_pairs={{0,2},{1,3},{2,0},{3,1},{4,6},{5,7},{6,4},{7,5},{8,10},{9,11},{10,... | collective-permute-start | bytes 4718600 | tf_op jit(solution)/shard_map/ppermute | solution.py:1099
  1548.8 5.5 collective-permute-start.8
  1554.4 5.8 collective-permute-start.9
  1560.2 3.8 collective-permute-start.10
  1564.1 107.4 %collective-permute-start.11 = (f32[2,192]{1,0:T(2,128)S(1)}, f32[2,192]{1,0:T(2,128)S(1)}, u32[]{:S(2)}, u32[]{:S(2)}) collective-permute-start(f32[2,192]{1,0:T(2,128)S(1)} %bitcast.100), channel_id=1, source_target_pairs={{0,2},{1,3},{2,0},{3,1},{4,6},{5,7},{6,4},{7,5},{8,10},{9,11},{10,... | collective-permute-start | bytes 4616 | tf_op jit(solution)/shard_map/ppermute | solution.py:1160
  1671.6 13.1 collective-permute-start.12
  (68 other events, 759.9 us)
Sparse Core Ops, SparseCore 0:
  111.0 135.6 all-gather.5
  248.5 57.0 all-gather.7
  308.0 121.9 all-gather.11
  431.7 122.5 all-gather.9
  556.0 122.5 all-gather.13
  793.6 120.5 reduce-scatter.5
  1014.3 120.5 reduce-scatter.7
  1138.1 120.7 reduce-scatter.9
  1261.8 57.0 reduce-scatter.11
  1321.9 133.6 reduce-scatter.13

commit v9 on v8

--- a/solution.py
+++ b/solution.py
@@ -744,7 +744,7 @@
     return exchange_call(
         functools.partial(swap_kernel, kinds), next_key[0], values,
         [jax.ShapeDtypeStruct(value.shape, value.dtype) for value in values],
-        [pltpu.SemaphoreType.DMA((len(pushes),))] * 2, flops=110 * 10**9,
+        [pltpu.SemaphoreType.DMA((len(pushes),))] * 2, flops=130 * 10**9,
     )
 
 
@@ -1250,20 +1250,20 @@
     saved, lses, mixed_first = [results[:3]], [results[4]], results[3]
     term_first = act(dot_bf16, mixed_first, out_full)
     keep_first, send_first = act(core_reduce, term_first)
-    projected, branch_first = act(
-        wide_dot, h1_second, qkv_full, sends=[("near", send_first)]
-    )
+    projected = act(wide_dot, h1_second, qkv_full)
 
     def second_norm(stream, keep, got):
         middle = stream + keep + got.astype(jnp.float32)
         return (middle, *rms_pack(middle, gain_two))
 
-    m_first, q_first, n_first = act(second_norm, streams[0], keep_first, branch_first)
-    *results, near_first = act(attend_second, projected, sends=[("near", n_first)])
+    *results, branch_first = act(attend_second, projected, sends=[("near", send_first)])
     saved.append(results[:3])
     lses.append(results[4])
     mixed_second = results[3]
-    term_second = act(dot_bf16, mixed_second, out_full)
+    m_first, q_first, n_first = act(second_norm, streams[0], keep_first, branch_first)
+    term_second, near_first = act(
+        dot_bf16, mixed_second, out_full, sends=[("near", n_first)]
+    )
     keep_second, send_second = act(core_reduce, term_second)
     h2_first = act(core_gather, n_first, near_first)
     down_full_pair = act(lambda own, got: core_pair(6, own, got), down_weight, down_other)
@@ -1353,6 +1353,8 @@
     out_sum = plane_scatter(grad_out)
     mlp_first = act(dot_bf16, a_first, down_full)
     mlp_keep_first, mlp_send_first = act(core_reduce, mlp_first)
+    gate_mine, gate_away = act(lambda pair: core_split(9, pair), gate_sum)
+    gate_got = swap_far(gate_away)
     mlp_second = act(dot_bf16, a_second, down_full)
     mlp_keep_second, mlp_send_second = act(core_reduce, mlp_second)
     def attend_back(heads_first, heads_second, pushes=()):
@@ -1372,8 +1374,6 @@
         attend_back, heads_first, heads_second,
         sends=[("near", mlp_send_first), ("near", mlp_send_second)],
     )
-    gate_mine, gate_away = act(lambda pair: core_split(9, pair), gate_sum)
-    gate_got = swap_far(gate_away)
     p_first, p_second = act(
         lambda *parts: (
             jnp.concatenate(parts[:3], axis=1),
@@ -1387,6 +1387,8 @@
         second = (second + second_keep + second_got.astype(jnp.float32)).astype(jnp.bfloat16)
         return jnp.where(far == 0, first, second), jnp.where(far == 0, second, first)
 
+    up_mine, up_away = act(lambda pair: core_split(9, pair), up_sum)
+    up_got = swap_far(up_away)
     grad_qkv = act(grad_sum, h1_first, p_first, h1_second, p_second)
     qkv_sum = plane_scatter(grad_qkv)
     out_keep, out_send = act(
@@ -1394,15 +1396,12 @@
         m_first, mlp_keep_first, mlp_branch_first, m_second, mlp_keep_second, mlp_branch_second,
     )
     out_got = swap_far(out_send)
-    up_mine, up_away = act(lambda pair: core_split(9, pair), up_sum)
-    up_got = swap_far(up_away)
     term_first = act(heads_back, p_first, qkv_full)
     keep_first, send_first = act(core_reduce, term_first)
     term_second, back_first = act(
         heads_back, p_second, qkv_full, sends=[("near", send_first)]
     )
     keep_second, send_second = act(core_reduce, term_second)
-    out_mine, out_away = act(lambda pair: core_split(8, pair), out_sum)
     def settle(keep, got):
         return jnp.stack([jnp.where(far == 0, keep, got), jnp.where(far == 0, got, keep)])
 
@@ -1418,6 +1417,7 @@
             gain_term,
         )
 
+    out_mine, out_away = act(lambda pair: core_split(8, pair), out_sum)
     back_second, out_back = swap(("near", send_second), ("far", out_away))
     qkv_mine, qkv_away = act(lambda pair: core_split(0, pair), qkv_sum)
     qkv_back = swap_far(qkv_away)

time: 1710 us -> 1730 us (1.012)
    unnamed x148 -> x146, local copies, waits for them, and re-layouts: 42.4 us -> 42.6 us
where the time goes in v9:
time: 1730 us; the launch traced here: 1720 us
  Pallas kernels  1410 us (82%)
  other arithmetic  103 us (6%)
  waiting for transfers between devices  102 us (6%)
  local copies, waits for them, and re-layouts  69.1 us (4%)
  starting transfers between devices  18.3 us (1%)
    pallas_call x26, Pallas kernels, grid_call(): pl.pallas_call(kernel, out_shape=outs, grid=grid, in_specs=in_specs, out_...  970 us
    pallas_call x28, Pallas kernels, exchange_call(): pl.pallas_call(kernel, out_shape=outs, in_specs=[anywhere] * len(operands...  441 us
    ppermute x5, waiting for transfers between devices, scatter_gains(): lax.ppermute(sent, axis, [(i, i ^ step) for i in range(size)])  101 us
    unnamed x146, local copies, waits for them, and re-layouts  42.6 us
  transfers between devices with their start and end apart: 24, of which 2 were waited for; matrix products, arithmetic and copies ran while one was open for 7% of the time, Pallas kernels for 77%

profile of v9, /device:TPU:0, one launch (start us, length us, event | category | flops | bytes accessed | tf_op | source)
XLA Modules:
  0.0 1718.3 jit_solution(16305649514943978625)
XLA Ops:
  20.3 82.6 %shard_map.152 = (bf16[256,3072]{1,0:T(8,128)(2,1)}, bf16[384,2304]{1,0:T(8,128)(2,1)}, s32[8,256]{1,0:T(8,128)}) custom-call(bf16[256,3072]{1,0:T(8,128)(2,1)} %fusion.4.refs_0_.own_ref, bf16[384,2304]{1,0:T(8,128)(2,1)} %copy.35.refs_1_, s32[8,256]{1,0:T(8,128)} %broadcast_in_dim.11.refs_2_), custom_call_target="tpu_custom_call" | custom-call | flops 221000007680 | bytes 1000 | tf_op jit(solution)/shard_map/pallas_call | solution.py:778
  118.2 96.5 %shard_map.154 = (bf16[256,3072]{1,0:T(8,128)(2,1)}, bf16[256,3072]{1,0:T(8,128)(2,1)}, bf16[96,3072]{1,0:T(8,128)(2,1)}, s32[16,256]{1,0:T(8,128)}) custom-call(bf16[256,3072]{1,0:T(8,128)(2,1)} %get-tuple-element.295.refs_0_, bf16[256,3072]{1,0:T(8,128)(2,1)} %get-tuple-element.384.refs_1_.own_ref, bf16[96,3072]{1,0:T(8,128)(2,1)} %own_ref, ...), custom_call_target="tpu_custom_call" | custom-call | flops 221000007680 | bytes 1000 | tf_op jit(solution)/shard_map/pallas_call | solution.py:778
  233.6 71.6 %shard_map.156 = (bf16[256,3072]{1,0:T(8,128)(2,1)}, bf16[384,2048]{1,0:T(8,128)(2,1)}, s32[32,256]{1,0:T(8,128)}) custom-call(bf16[256,3072]{1,0:T(8,128)(2,1)} %multiply_convert_fusion.2.refs_0_.got_ref, bf16[384,2048]{1,0:T(8,128)(2,1)} %get-tuple-element.312.refs_1_.own_ref, s32[32,256]{1,0:T(8,128)} %pad_add_fusion.1.refs_2_), custom_call_target="tpu_custom_call" | custom-call | flops 221000007680 | bytes 1000 | tf_op jit(solution)/shard_map/pallas_call | solution.py:778
  329.6 21.7 %shard_map.159.q_ref.k_ref.v_ref = f32[1024,2304]{1,0:T(8,128)} custom-call(bf16[1024,3072]{1,0:T(8,128)(2,1)} %get-tuple-element.499.refs_0_, bf16[3072,2304]{1,0:T(8,128)(2,1)} %all-gather.6.cloned.1.call-done.refs_1_), custom_call_target="tpu_custom_call" | custom-call | flops 24642375680 | bytes 1000 | tf_op jit(solution)/shard_map/pallas_call | solution.py:720
  351.3 29.2 %shard_map.160 = (bf16[1024,768]{1,0:T(8,128)(2,1)}, bf16[1024,768]{1,0:T(8,128)(2,1)}, bf16[1024,768]{1,0:T(8,128)(2,1)}, bf16[1024,768]{1,0:T(8,128)(2,1)}, f32[2,1024,4]{2,1,0:T(8,128)}) custom-call(f32[1024,2304]{1,0:T(8,128)} %shard_map.159.q_ref.k_ref.v_ref, f32[1024,2304]{1,0:T(8,128)} %shard_map.159.q_ref.k_ref.v_ref, ...), custom_call_target="tpu_custom_call" | custom-call | flops 8556380160 | bytes 1000 | tf_op jit(solution)/shard_map/pallas_call | solution.py:720
  406.2 21.2 %shard_map.164.refs_0_.refs_1_.refs_2_ = f32[1024,2304]{1,0:T(8,128)} custom-call(bf16[1024,3072]{1,0:T(8,128)(2,1)} %get-tuple-element.500.refs_0_.refs_1_, bf16[3072,2304]{1,0:T(8,128)(2,1)} %all-gather.6.cloned.1.call-done.refs_1_), custom_call_target="tpu_custom_call" | custom-call | flops 24642375680 | bytes 1000 | tf_op jit(solution)/shard_map/pallas_call | solution.py:720
  427.4 65.7 %shard_map.165 = (bf16[1024,768]{1,0:T(8,128)(2,1)}, bf16[1024,768]{1,0:T(8,128)(2,1)}, bf16[1024,768]{1,0:T(8,128)(2,1)}, bf16[1024,768]{1,0:T(8,128)(2,1)}, f3...) custom-call(f32[1024,2304]{1,0:T(8,128)} %shard_map.164.refs_0_.refs_1_.refs_2_, ...), custom_call_target="tpu_custom_call" | custom-call | flops 45900001280 | bytes 1000 | tf_op jit(solution)/shard_map/pallas_call | solution.py:720
  499.4 39.6 %shard_map.166 = (bf16[1024,3072]{1,0:T(8,128)(2,1)}, bf16[256,3072]{1,0:T(8,128)(2,1)}) custom-call(bf16[1024,768]{1,0:T(8,128)(2,1)} %get-tuple-element.464.refs_0_.refs_1_, bf16[768,3072]{1,0:T(8,128)(2,1)} %all-gather.8.cloned.1.call-done.refs_1_, bf16[256,3072]{1,0:T(8,128)(2,1)} %multiply_convert_fusion.1.refs_2_.own_ref), custom_call_target="tpu_custom_call" | custom-call | flops 45900001280 | bytes 1000 | tf_op jit(solution)/shard_map/pallas_call | solution.py:720
  556.4 42.1 %shard_map.170 = (f32[1024,2048]{1,0:T(8,128)}, bf16[256,3072]{1,0:T(8,128)(2,1)}) custom-call(bf16[1024,3072]{1,0:T(8,128)(2,1)} %shard_map.168.refs_0_, bf16[3072,2048]{1,0:T(8,128)(2,1)} %all-gather.12.cloned.1.call-done.refs_1_.refs_2_, bf16[256,3072]{1,0:T(8,128)(2,1)} %get-tuple-element.363.refs_2_), custom_call_target="tpu_custom_call" | custom-call | flops 45900001280 | bytes 1000 | tf_op jit(solution)/shard_map/pallas_call | solution.py:720
  606.0 75.5 %shard_map.171 = (f32[1024,2048]{1,0:T(8,128)}, bf16[1024,2048]{1,0:T(8,128)(2,1)}, bf16[256,3072]{1,0:T(8,128)(2,1)}) custom-call(bf16[1024,3072]{1,0:T(8,128)(2,1)} %shard_map.168.refs_0_, bf16[3072,2048]{1,0:T(8,128)(2,1)} %all-gather.10.cloned.1.call-done.refs_1_.refs_3_, f32[1024,2048]{1,0:T(8,128)} %get-tuple-element.401.refs_2_, ...), custom_call_target="tpu_custom_call" | custom-call | flops 45900001280 | bytes 1000 | tf_op jit(solution)/shard_map/pallas_call | solution.py:720
  687.6 41.9 %shard_map.173 = (f32[1024,2048]{1,0:T(8,128)}, bf16[256,3072]{1,0:T(8,128)(2,1)}) custom-call(bf16[1024,3072]{1,0:T(8,128)(2,1)} %shard_map.172.refs_0_.refs_1_, bf16[3072,2048]{1,0:T(8,128)(2,1)} %all-gather.12.cloned.1.call-done.refs_1_.refs_2_, bf16[256,3072]{1,0:T(8,128)(2,1)} %collective-permute-done.2.refs_2_.got_ref), custom_call_target="tpu_custom_call" | custom-call | flops 45900001280 | bytes 1000 | tf_op jit(solution)/shard_map/pallas_call | solution.py:720
  740.3 20.1 %shard_map.175 = (f32[1024,2048]{1,0:T(8,128)}, bf16[1024,2048]{1,0:T(8,128)(2,1)}) custom-call(bf16[1024,3072]{1,0:T(8,128)(2,1)} %shard_map.172.refs_0_.refs_1_, bf16[3072,2048]{1,0:T(8,128)(2,1)} %all-gather.10.cloned.1.call-done.refs_1_.refs_3_, f32[1024,2048]{1,0:T(8,128)} %get-tuple-element.413.refs_2_), custom_call_target="tpu_custom_call" | custom-call | flops 21904332800 | bytes 1000 | tf_op jit(solution)/shard_map/pallas_call | solution.py:720
  760.4 35.3 %shard_map.176 = bf16[2048,3072]{1,0:T(8,128)(2,1)} custom-call(bf16[1024,2048]{1,0:T(8,128)(2,1)} %get-tuple-element.467.refs_0_, bf16[1024,2048]{1,0:T(8,128)(2,1)} %get-tuple-element.474.refs_1_.refs_0_, bf16[1024,3072]{1,0:T(8,128)(2,1)} %get-tuple-element.399.refs_2_.refs_0_, bf16[1024,3072]{1,0:T(8,128)(2,1)} %get-tuple-element.411.refs_3_.refs_0_), custom_call_target="tpu_custom_call" | custom-call | flops 43808665600 | bytes 1000 | tf_op jit(solution)/shard_map/pallas_call | solution.py:720
  800.4 24.9 %shard_map.177 = (bf16[1024,2048]{1,0:T(8,128)(2,1)}, bf16[1024,2048]{1,0:T(8,128)(2,1)}) custom-call(bf16[1024,3072]{1,0:T(8,128)(2,1)} %get-tuple-element.399.refs_2_.refs_0_, bf16[2048,3072]{1,0:T(8,128)(2,1)} %all-gather.14.cloned.1.call-done.refs_1_, f32[1024,2048]{1,0:T(8,128)} %get-tuple-element.401.refs_2_, f32[1024,2048]{1,0:T(8,128)} %get-tuple-element.402.refs_3_), custom_call_target="tpu_custom_call" | custom-call | flops 21904332800 | bytes 1000 | tf_op jit(solution)/shard_map/pallas_call | solution.py:720
  825.3 33.3 %shard_map.178.term_ref = bf16[1024,3072]{1,0:T(8,128)(2,1)} custom-call(bf16[1024,2048]{1,0:T(8,128)(2,1)} %get-tuple-element.437.refs_0_.refs_2_, bf16[1024,2048]{1,0:T(8,128)(2,1)} %get-tuple-element.454.refs_1_.refs_2_, bf16[3072,2048]{1,0:T(8,128)(2,1)} %all-gather.12.cloned.1.call-done.refs_1_.refs_2_, ...), custom_call_target="tpu_custom_call" | custom-call | flops 43808665600 | bytes 1000 | tf_op jit(solution)/shard_map/pallas_call | solution.py:720
  865.9 44.7 %shard_map.180 = (bf16[1024,2048]{1,0:T(8,128)(2,1)}, bf16[1024,2048]{1,0:T(8,128)(2,1)}, bf16[256,3072]{1,0:T(8,128)(2,1)}) custom-call(bf16[1024,3072]{1,0:T(8,128)(2,1)} %get-tuple-element.411.refs_3_.refs_0_, bf16[2048,3072]{1,0:T(8,128)(2,1)} %all-gather.14.cloned.1.call-done.refs_1_, f32[1024,2048]{1,0:T(8,128)} %get-tuple-element.413.refs_2_, ...), custom_call_target="tpu_custom_call" | custom-call | flops 45900001280 | bytes 1000 | tf_op jit(solution)/shard_map/pallas_call | solution.py:720
  918.7 41.9 %shard_map.181 = (bf16[1024,3072]{1,0:T(8,128)(2,1)}, bf16[256,3072]{1,0:T(8,128)(2,1)}) custom-call(bf16[1024,2048]{1,0:T(8,128)(2,1)} %get-tuple-element.438.refs_0_.refs_3_, bf16[1024,2048]{1,0:T(8,128)(2,1)} %get-tuple-element.455.refs_1_.refs_3_, bf16[3072,2048]{1,0:T(8,128)(2,1)} %all-gather.12.cloned.1.call-done.refs_1_.refs_2_, ...), custom_call_target="tpu_custom_call" | custom-call | flops 45900001280 | bytes 1000 | tf_op jit(solution)/shard_map/pallas_call | solution.py:720
  974.1 42.2 %shard_map.184 = (bf16[3072,2048]{1,0:T(8,128)(2,1)}, bf16[256,3072]{1,0:T(8,128)(2,1)}) custom-call(bf16[1024,3072]{1,0:T(8,128)(2,1)} %shard_map.168.refs_0_, bf16[1024,3072]{1,0:T(8,128)(2,1)} %shard_map.172.refs_0_.refs_1_, bf16[1024,2048]{1,0:T(8,128)(2,1)} %get-tuple-element.437.refs_0_.refs_2_, bf16[1024,2048]{1,0:T(8,128)(2,1)} %get-tuple-element.438.refs_0_.refs_3_, ...), custom_call_target="tpu_custom_call" | custom-call | flops 45900001280 | bytes 1000 | tf_op jit(solution)/shard_map/pallas_call | solution.py:720
  1040.2 43.0 %shard_map.187 = (bf16[3072,2048]{1,0:T(8,128)(2,1)}, bf16[256,3072]{1,0:T(8,128)(2,1)}) custom-call(bf16[1024,3072]{1,0:T(8,128)(2,1)} %shard_map.168.refs_0_, bf16[1024,3072]{1,0:T(8,128)(2,1)} %shard_map.172.refs_0_.refs_1_, bf16[1024,2048]{1,0:T(8,128)(2,1)} %get-tuple-element.454.refs_1_.refs_2_, bf16[1024,2048]{1,0:T(8,128)(2,1)} %get-tuple-element.455.refs_1_.refs_3_, ...), custom_call_target="tpu_custom_call" | custom-call | flops 45900001280 | bytes 1000 | tf_op jit(solution)/shard_map/pallas_call | solution.py:720
  1176.6 109.6 %shard_map.196 = (bf16[1024,768]{1,0:T(8,128)(2,1)}, bf16[1024,768]{1,0:T(8,128)(2,1)}, bf16[1024,768]{1,0:T(8,128)(2,1)}, bf16[1024,768]{1,0:T(8,128)(2,1)}, bf...) custom-call(bf16[1024,768]{1,0:T(8,128)(2,1)} %get-tuple-element.326, ...), custom_call_target="tpu_custom_call" | custom-call | flops 45900001280 | bytes 1000 | tf_op jit(solution)/shard_map/pallas_call | solution.py:720
  1298.7 39.1 %shard_map.198 = bf16[3072,2304]{1,0:T(8,128)(2,1)} custom-call(bf16[1024,3072]{1,0:T(8,128)(2,1)} %get-tuple-element.499.refs_0_, bf16[1024,3072]{1,0:T(8,128)(2,1)} %get-tuple-element.500.refs_0_.refs_1_, bf16[1024,2304]{1,0:T(8,128)(2,1)} %constant_dynamic-update-slice_fusion.refs_2_.refs_0_, bf16[1024,2304]{1,0:T(8,128)(2,1)} %copy-done.44), custom_call_target="tpu_custom_call" | custom-call | flops 49284751360 | bytes 1000 | tf_op jit(solution)/shard_map/pallas_call | solution.py:720
  1376.9 94.4 %shard_map.201 = (bf16[1024,3072]{1,0:T(8,128)(2,1)}, bf16[256,3072]{1,0:T(8,128)(2,1)}) custom-call(bf16[1024,2304]{1,0:T(8,128)(2,1)} %copy-done.44, bf16[3072,2304]{1,0:T(8,128)(2,1)} %all-gather.6.cloned.1.call-done.refs_1_, bf16[256,3072]{1,0:T(8,128)(2,1)} %get-tuple-element.515.refs_2_), custom_call_target="tpu_custom_call" | custom-call | flops 45900001280 | bytes 1000 | tf_op jit(solution)/shard_map/pallas_call | solution.py:720
  1481.1 49.5 %shard_map.204 = (bf16[256,3072]{1,0:T(8,128)(2,1)}, bf16[96,3072]{1,0:T(8,128)(2,1)}) custom-call(bf16[256,3072]{1,0:T(8,128)(2,1)} %get-tuple-element.522.refs_0_, bf16[96,3072]{1,0:T(8,128)(2,1)} %get-tuple-element.523.refs_1_), custom_call_target="tpu_custom_call" | custom-call | flops 221000007680 | bytes 1000 | tf_op jit(solution)/shard_map/pallas_call | solution.py:778
  1580.5 101.5 %collective-permute-done.11 = f32[2,192]{1,0:T(2,128)S(1)} collective-permute-done((f32[2,192]{1,0:T(2,128)S(1)}, f32[2,192]{1,0:T(2,128)S(1)}, u32[]{:S(2)}, u32[]{:S(2)}) %collective-permute-start.11) | collective-permute-done | bytes 1568 | tf_op jit(solution)/shard_map/ppermute | solution.py:1160
  (322 shorter events, 435.8 us)
Async XLA Ops:
  7.2 322.4 %all-gather.6.cloned.1.call-start = ((), (), s32[]{:S(2)}) async-start(), calls=%async_computation.5 | async-start | bytes 17694720 | tf_op jit(solution)/shard_map/all_gather | solution.py:1131
  110.9 278.1 %all-gather.8.cloned.1.call-start = ((), (), s32[]{:S(2)}) async-start(), calls=%async_computation.6 | async-start | bytes 5898240 | tf_op jit(solution)/shard_map/all_gather | solution.py:1131
  217.1 339.1 %all-gather.12.cloned.1.call-start = ((), (), s32[]{:S(2)}) async-start(), calls=%async_computation.8 | async-start | bytes 15728640 | tf_op jit(solution)/shard_map/all_gather | solution.py:1131
  309.1 296.9 %all-gather.10.cloned.1.call-start = ((), (), s32[]{:S(2)}) async-start(), calls=%async_computation.7 | async-start | bytes 15728640 | tf_op jit(solution)/shard_map/all_gather | solution.py:1131
  310.5 70.1 %collective-permute-start = (bf16[384,2048]{1,0:T(8,128)(2,1)S(1)}, bf16[384,2048]{1,0:T(8,128)(2,1)S(1)}, u32[]{:S(2)}, u32[]{:S(2)}) collective-permute-start(bf16[384,2048]{1,0:T(8,128)(2,1)S(1)} %copy-done.30), channel_id=1, source_target_pairs={{0,2},{1,3},{2,0},{3,1},{4,6},{5,7},{6,4},{7,5},{8,10},{9,11},{10,... | collective-permute-start | bytes 4718600 | tf_op jit(solution)/shard_map/ppermute | solution.py:1099
  385.6 414.8 %all-gather.14.cloned.1.call-start = ((), (), s32[]{:S(2)}) async-start(), calls=%async_computation.9 | async-start | bytes 15728640 | tf_op jit(solution)/shard_map/all_gather | solution.py:1131
  386.7 165.7 %collective-permute-start.1 = (bf16[256,3072]{1,0:T(8,128)(2,1)}, bf16[256,3072]{1,0:T(8,128)(2,1)}, u32[]{:S(2)}, u32[]{:S(2)}) collective-permute-start(bf16[256,3072]{1,0:T(8,128)(2,1)} %own_ref.1), channel_id=1, source_target_pairs={{0,2},{1,3},{2,0},{3,1},{4,6},{5,7},{6,4},{7,5},{8,10},{9,11},{10,... | collective-permute-start | bytes 4718600 | tf_op jit(solution)/shard_map/ppermute | solution.py:1099
  556.3 480.1 %reduce-scatter.6.cloned.1.call-start = ((), (), s32[]{:S(2)}) async-start(), calls=%async_computation.10 | async-start | bytes 15728640 | tf_op jit(solution)/shard_map/reduce_scatter | solution.py:1134
  598.5 89.1 %collective-permute-start.2 = (bf16[256,3072]{1,0:T(8,128)(2,1)}, bf16[256,3072]{1,0:T(8,128)(2,1)}, u32[]{:S(2)}, u32[]{:S(2)}) collective-permute-start(bf16[256,3072]{1,0:T(8,128)(2,1)} %get-tuple-element.374), channel_id=1, source_target_pairs={{0,2},{1,3},{2,0},{3,1},{4,6},{5,7},{6,4},{7,5},{8,10},{9,11},{10,... | collective-permute-start | bytes 4718600 | tf_op jit(solution)/shard_map/ppermute | solution.py:1099
  795.7 349.1 %reduce-scatter.8.cloned.1.call-start = ((), (), s32[]{:S(2)}) async-start(), calls=%async_computation.11 | async-start | bytes 15728640 | tf_op jit(solution)/shard_map/reduce_scatter | solution.py:1134
  1016.3 278.5 %reduce-scatter.10.cloned.1.call-start = ((), (), s32[]{:S(2)}) async-start(), calls=%async_computation.12 | async-start | bytes 15728640 | tf_op jit(solution)/shard_map/reduce_scatter | solution.py:1134
  1083.3 395.4 %reduce-scatter.12.cloned.1.call-start = ((), (), s32[]{:S(2)}) async-start(), calls=%async_computation.13 | async-start | bytes 5898240 | tf_op jit(solution)/shard_map/reduce_scatter | solution.py:1134
  1084.6 467.1 %collective-permute-start.5 = (bf16[256,3072]{1,0:T(8,128)(2,1)}, bf16[256,3072]{1,0:T(8,128)(2,1)}, u32[]{:S(2)}, u32[]{:S(2)}) collective-permute-start(bf16[256,3072]{1,0:T(8,128)(2,1)} %get-tuple-element.451), channel_id=1, source_target_pairs={{0,2},{1,3},{2,0},{3,1},{4,6},{5,7},{6,4},{7,5},{8,10},{9,11},{10,... | collective-permute-start | bytes 4718600 | tf_op jit(solution)/shard_map/ppermute | solution.py:1099
  1148.7 408.3 %collective-permute-start.4 = (bf16[384,2048]{1,0:T(8,128)(2,1)}, bf16[384,2048]{1,0:T(8,128)(2,1)}, u32[]{:S(2)}, u32[]{:S(2)}) collective-permute-start(bf16[384,2048]{1,0:T(8,128)(2,1)} %get-tuple-element.473), channel_id=1, source_target_pairs={{0,2},{1,3},{2,0},{3,1},{4,6},{5,7},{6,4},{7,5},{8,10},{9,11},{10,... | collective-permute-start | bytes 4718600 | tf_op jit(solution)/shard_map/ppermute | solution.py:1099
  1176.6 354.1 %reduce-scatter.14.cloned.1.call-start = ((), (), s32[]{:S(2)}) async-start(), calls=%async_computation.14 | async-start | bytes 17694720 | tf_op jit(solution)/shard_map/reduce_scatter | solution.py:1134
  1298.6 271.6 %collective-permute-start.7 = (bf16[384,2048]{1,0:T(8,128)(2,1)}, bf16[384,2048]{1,0:T(8,128)(2,1)}, u32[]{:S(2)}, u32[]{:S(2)}) collective-permute-start(bf16[384,2048]{1,0:T(8,128)(2,1)} %get-tuple-element.498), channel_id=1, source_target_pairs={{0,2},{1,3},{2,0},{3,1},{4,6},{5,7},{6,4},{7,5},{8,10},{9,11},{10,... | collective-permute-start | bytes 4718600 | tf_op jit(solution)/shard_map/ppermute | solution.py:1099
  1345.4 213.6 %collective-permute-start.3 = (bf16[256,3072]{1,0:T(8,128)(2,1)}, bf16[256,3072]{1,0:T(8,128)(2,1)}, u32[]{:S(2)}, u32[]{:S(2)}) collective-permute-start(bf16[256,3072]{1,0:T(8,128)(2,1)} %get-tuple-element.591), channel_id=1, source_target_pairs={{0,2},{1,3},{2,0},{3,1},{4,6},{5,7},{6,4},{7,5},{8,10},{9,11},{10,... | collective-permute-start | bytes 4718600 | tf_op jit(solution)/shard_map/ppermute | solution.py:1099
  1534.8 166.4 %collective-permute-start.13 = (bf16[384,2304]{1,0:T(8,128)(2,1)}, bf16[384,2304]{1,0:T(8,128)(2,1)}, u32[]{:S(2)}, u32[]{:S(2)}) collective-permute-start(bf16[384,2304]{1,0:T(8,128)(2,1)} %get-tuple-element.529), channel_id=1, source_target_pairs={{0,2},{1,3},{2,0},{3,1},{4,6},{5,7},{6,4},{7,5},{8,10},{9,11},{10,... | collective-permute-start | bytes 5308424 | tf_op jit(solution)/shard_map/ppermute | solution.py:1099
  1551.6 144.1 %collective-permute-start.6 = (bf16[256,3072]{1,0:T(8,128)(2,1)}, bf16[256,3072]{1,0:T(8,128)(2,1)}, u32[]{:S(2)}, u32[]{:S(2)}) collective-permute-start(bf16[256,3072]{1,0:T(8,128)(2,1)} %get-tuple-element.589), channel_id=1, source_target_pairs={{0,2},{1,3},{2,0},{3,1},{4,6},{5,7},{6,4},{7,5},{8,10},{9,11},{10,... | collective-permute-start | bytes 4718600 | tf_op jit(solution)/shard_map/ppermute | solution.py:1099
  1559.1 6.1 collective-permute-start.8
  1565.3 4.9 collective-permute-start.9
  1570.2 3.8 collective-permute-start.10
  1574.1 107.9 %collective-permute-start.11 = (f32[2,192]{1,0:T(2,128)S(1)}, f32[2,192]{1,0:T(2,128)S(1)}, u32[]{:S(2)}, u32[]{:S(2)}) collective-permute-start(f32[2,192]{1,0:T(2,128)S(1)} %bitcast.100), channel_id=1, source_target_pairs={{0,2},{1,3},{2,0},{3,1},{4,6},{5,7},{6,4},{7,5},{8,10},{9,11},{10,... | collective-permute-start | bytes 4616 | tf_op jit(solution)/shard_map/ppermute | solution.py:1160
  1682.1 13.1 collective-permute-start.12
  (67 other events, 789.6 us)
Sparse Core Ops, SparseCore 0:
  111.0 135.6 all-gather.5
  248.5 57.0 all-gather.7
  309.2 121.6 all-gather.11
  432.6 122.5 all-gather.9
  556.8 122.5 all-gather.13
  795.8 119.8 reduce-scatter.5
  1016.4 120.0 reduce-scatter.7
  1139.7 120.7 reduce-scatter.9
  1263.4 57.0 reduce-scatter.11
  1349.8 132.2 reduce-scatter.13

commit v10 on v8

--- a/solution.py
+++ b/solution.py
@@ -744,7 +744,7 @@
     return exchange_call(
         functools.partial(swap_kernel, kinds), next_key[0], values,
         [jax.ShapeDtypeStruct(value.shape, value.dtype) for value in values],
-        [pltpu.SemaphoreType.DMA((len(pushes),))] * 2, flops=110 * 10**9,
+        [pltpu.SemaphoreType.DMA((len(pushes),))] * 2, flops=130 * 10**9,
     )
 
 
@@ -1393,7 +1393,6 @@
         finish_output,
         m_first, mlp_keep_first, mlp_branch_first, m_second, mlp_keep_second, mlp_branch_second,
     )
-    out_got = swap_far(out_send)
     up_mine, up_away = act(lambda pair: core_split(9, pair), up_sum)
     up_got = swap_far(up_away)
     term_first = act(heads_back, p_first, qkv_full)
@@ -1401,6 +1400,7 @@
     term_second, back_first = act(
         heads_back, p_second, qkv_full, sends=[("near", send_first)]
     )
+    out_got = swap_far(chained(out_send, term_second))
     keep_second, send_second = act(core_reduce, term_second)
     out_mine, out_away = act(lambda pair: core_split(8, pair), out_sum)
     def settle(keep, got):

time: 1710 us -> 1720 us (level)
    pallas_call x28, Pallas kernels: 441 us -> 487 us  [exchange_call(): pl.pallas_call(kernel, out_shape=outs, in_specs=[anywhere] * len(operands...]
    pallas_call x26, Pallas kernels: 959 us -> 921 us  [grid_call(): pl.pallas_call(kernel, out_shape=outs, grid=grid, in_specs=in_specs, out_...]
where the time goes in v10:
time: 1720 us; the launch traced here: 1710 us
  Pallas kernels  1410 us (82%)
  other arithmetic  104 us (6%)
  waiting for transfers between devices  102 us (6%)
  local copies, waits for them, and re-layouts  70 us (4%)
    pallas_call x26, Pallas kernels, grid_call(): pl.pallas_call(kernel, out_shape=outs, grid=grid, in_specs=in_specs, out_...  921 us
    pallas_call x28, Pallas kernels, exchange_call(): pl.pallas_call(kernel, out_shape=outs, in_specs=[anywhere] * len(operands...  487 us
    ppermute x5, waiting for transfers between devices, scatter_gains(): lax.ppermute(sent, axis, [(i, i ^ step) for i in range(size)])  102 us
    unnamed x148, local copies, waits for them, and re-layouts  43.5 us
  transfers between devices with their start and end apart: 24, of which 2 were waited for; matrix products, arithmetic and copies ran while one was open for 7% of the time, Pallas kernels for 77%

profile of v10, /device:TPU:0, one launch (start us, length us, event | category | flops | bytes accessed | tf_op | source)
XLA Modules:
  0.0 1713.7 jit_solution(17308614411093617)
XLA Ops:
  20.3 82.6 %shard_map.152 = (bf16[256,3072]{1,0:T(8,128)(2,1)}, bf16[384,2304]{1,0:T(8,128)(2,1)}, s32[8,256]{1,0:T(8,128)}) custom-call(bf16[256,3072]{1,0:T(8,128)(2,1)} %fusion.4.refs_0_.own_ref, bf16[384,2304]{1,0:T(8,128)(2,1)} %copy.35.refs_1_, s32[8,256]{1,0:T(8,128)} %broadcast_in_dim.11.refs_2_), custom_call_target="tpu_custom_call" | custom-call | flops 221000007680 | bytes 1000 | tf_op jit(solution)/shard_map/pallas_call | solution.py:778
  118.2 96.5 %shard_map.154 = (bf16[256,3072]{1,0:T(8,128)(2,1)}, bf16[256,3072]{1,0:T(8,128)(2,1)}, bf16[96,3072]{1,0:T(8,128)(2,1)}, s32[16,256]{1,0:T(8,128)}) custom-call(bf16[256,3072]{1,0:T(8,128)(2,1)} %get-tuple-element.289.refs_0_, bf16[256,3072]{1,0:T(8,128)(2,1)} %get-tuple-element.378.refs_1_.own_ref, bf16[96,3072]{1,0:T(8,128)(2,1)} %own_ref, ...), custom_call_target="tpu_custom_call" | custom-call | flops 221000007680 | bytes 1000 | tf_op jit(solution)/shard_map/pallas_call | solution.py:778
  233.6 71.6 %shard_map.156 = (bf16[256,3072]{1,0:T(8,128)(2,1)}, bf16[384,2048]{1,0:T(8,128)(2,1)}, s32[32,256]{1,0:T(8,128)}) custom-call(bf16[256,3072]{1,0:T(8,128)(2,1)} %multiply_convert_fusion.2.refs_0_.got_ref, bf16[384,2048]{1,0:T(8,128)(2,1)} %get-tuple-element.306.refs_1_.own_ref, s32[32,256]{1,0:T(8,128)} %pad_add_fusion.1.refs_2_), custom_call_target="tpu_custom_call" | custom-call | flops 221000007680 | bytes 1000 | tf_op jit(solution)/shard_map/pallas_call | solution.py:778
  329.6 21.7 %shard_map.159.q_ref.k_ref.v_ref = f32[1024,2304]{1,0:T(8,128)} custom-call(bf16[1024,3072]{1,0:T(8,128)(2,1)} %get-tuple-element.490.refs_0_, bf16[3072,2304]{1,0:T(8,128)(2,1)} %all-gather.6.cloned.1.call-done.refs_1_), custom_call_target="tpu_custom_call" | custom-call | flops 24642375680 | bytes 1000 | tf_op jit(solution)/shard_map/pallas_call | solution.py:720
  351.2 29.2 %shard_map.160 = (bf16[1024,768]{1,0:T(8,128)(2,1)}, bf16[1024,768]{1,0:T(8,128)(2,1)}, bf16[1024,768]{1,0:T(8,128)(2,1)}, bf16[1024,768]{1,0:T(8,128)(2,1)}, f32[2,1024,4]{2,1,0:T(8,128)}) custom-call(f32[1024,2304]{1,0:T(8,128)} %shard_map.159.q_ref.k_ref.v_ref, f32[1024,2304]{1,0:T(8,128)} %shard_map.159.q_ref.k_ref.v_ref, ...), custom_call_target="tpu_custom_call" | custom-call | flops 8556380160 | bytes 1000 | tf_op jit(solution)/shard_map/pallas_call | solution.py:720
  406.2 75.9 %shard_map.164 = (f32[1024,2304]{1,0:T(8,128)}, bf16[256,3072]{1,0:T(8,128)(2,1)}) custom-call(bf16[1024,3072]{1,0:T(8,128)(2,1)} %get-tuple-element.491.refs_0_.refs_1_, bf16[3072,2304]{1,0:T(8,128)(2,1)} %all-gather.6.cloned.1.call-done.refs_1_, bf16[256,3072]{1,0:T(8,128)(2,1)} %get-tuple-element.332.refs_2_), custom_call_target="tpu_custom_call" | custom-call | flops 45900001280 | bytes 1000 | tf_op jit(solution)/shard_map/pallas_call | solution.py:720
  488.8 39.7 %shard_map.165 = (bf16[1024,768]{1,0:T(8,128)(2,1)}, bf16[1024,768]{1,0:T(8,128)(2,1)}, bf16[1024,768]{1,0:T(8,128)(2,1)}, bf16[1024,768]{1,0:T(8,128)(2,1)}, f3...) custom-call(f32[1024,2304]{1,0:T(8,128)} %get-tuple-element.338.refs_0_.refs_1_.refs_2_, ...), custom_call_target="tpu_custom_call" | custom-call | flops 45900001280 | bytes 1000 | tf_op jit(solution)/shard_map/pallas_call | solution.py:720
  555.8 42.1 %shard_map.170 = (f32[1024,2048]{1,0:T(8,128)}, bf16[256,3072]{1,0:T(8,128)(2,1)}) custom-call(bf16[1024,3072]{1,0:T(8,128)(2,1)} %shard_map.168.refs_0_, bf16[3072,2048]{1,0:T(8,128)(2,1)} %all-gather.12.cloned.1.call-done.refs_1_.refs_2_, bf16[256,3072]{1,0:T(8,128)(2,1)} %get-tuple-element.357.refs_2_), custom_call_target="tpu_custom_call" | custom-call | flops 45900001280 | bytes 1000 | tf_op jit(solution)/shard_map/pallas_call | solution.py:720
  605.0 75.5 %shard_map.171 = (f32[1024,2048]{1,0:T(8,128)}, bf16[1024,2048]{1,0:T(8,128)(2,1)}, bf16[256,3072]{1,0:T(8,128)(2,1)}) custom-call(bf16[1024,3072]{1,0:T(8,128)(2,1)} %shard_map.168.refs_0_, bf16[3072,2048]{1,0:T(8,128)(2,1)} %all-gather.10.cloned.1.call-done.refs_1_.refs_3_, f32[1024,2048]{1,0:T(8,128)} %get-tuple-element.395.refs_2_, ...), custom_call_target="tpu_custom_call" | custom-call | flops 45900001280 | bytes 1000 | tf_op jit(solution)/shard_map/pallas_call | solution.py:720
  686.6 42.0 %shard_map.173 = (f32[1024,2048]{1,0:T(8,128)}, bf16[256,3072]{1,0:T(8,128)(2,1)}) custom-call(bf16[1024,3072]{1,0:T(8,128)(2,1)} %shard_map.172.refs_0_.refs_1_, bf16[3072,2048]{1,0:T(8,128)(2,1)} %all-gather.12.cloned.1.call-done.refs_1_.refs_2_, bf16[256,3072]{1,0:T(8,128)(2,1)} %collective-permute-done.2.refs_2_.got_ref), custom_call_target="tpu_custom_call" | custom-call | flops 45900001280 | bytes 1000 | tf_op jit(solution)/shard_map/pallas_call | solution.py:720
  739.3 20.2 %shard_map.175 = (f32[1024,2048]{1,0:T(8,128)}, bf16[1024,2048]{1,0:T(8,128)(2,1)}) custom-call(bf16[1024,3072]{1,0:T(8,128)(2,1)} %shard_map.172.refs_0_.refs_1_, bf16[3072,2048]{1,0:T(8,128)(2,1)} %all-gather.10.cloned.1.call-done.refs_1_.refs_3_, f32[1024,2048]{1,0:T(8,128)} %get-tuple-element.407.refs_2_), custom_call_target="tpu_custom_call" | custom-call | flops 21904332800 | bytes 1000 | tf_op jit(solution)/shard_map/pallas_call | solution.py:720
  759.4 35.2 %shard_map.176 = bf16[2048,3072]{1,0:T(8,128)(2,1)} custom-call(bf16[1024,2048]{1,0:T(8,128)(2,1)} %get-tuple-element.461.refs_0_, bf16[1024,2048]{1,0:T(8,128)(2,1)} %get-tuple-element.465.refs_1_.refs_0_, bf16[1024,3072]{1,0:T(8,128)(2,1)} %get-tuple-element.393.refs_2_.refs_0_, bf16[1024,3072]{1,0:T(8,128)(2,1)} %get-tuple-element.405.refs_3_.refs_0_), custom_call_target="tpu_custom_call" | custom-call | flops 43808665600 | bytes 1000 | tf_op jit(solution)/shard_map/pallas_call | solution.py:720
  799.4 25.0 %shard_map.177 = (bf16[1024,2048]{1,0:T(8,128)(2,1)}, bf16[1024,2048]{1,0:T(8,128)(2,1)}) custom-call(bf16[1024,3072]{1,0:T(8,128)(2,1)} %get-tuple-element.393.refs_2_.refs_0_, bf16[2048,3072]{1,0:T(8,128)(2,1)} %all-gather.14.cloned.1.call-done.refs_1_, f32[1024,2048]{1,0:T(8,128)} %get-tuple-element.395.refs_2_, f32[1024,2048]{1,0:T(8,128)} %get-tuple-element.396.refs_3_), custom_call_target="tpu_custom_call" | custom-call | flops 21904332800 | bytes 1000 | tf_op jit(solution)/shard_map/pallas_call | solution.py:720
  824.4 33.3 %shard_map.178.term_ref = bf16[1024,3072]{1,0:T(8,128)(2,1)} custom-call(bf16[1024,2048]{1,0:T(8,128)(2,1)} %get-tuple-element.431.refs_0_.refs_2_, bf16[1024,2048]{1,0:T(8,128)(2,1)} %get-tuple-element.448.refs_1_.refs_2_, bf16[3072,2048]{1,0:T(8,128)(2,1)} %all-gather.12.cloned.1.call-done.refs_1_.refs_2_, ...), custom_call_target="tpu_custom_call" | custom-call | flops 43808665600 | bytes 1000 | tf_op jit(solution)/shard_map/pallas_call | solution.py:720
  865.1 44.7 %shard_map.180 = (bf16[1024,2048]{1,0:T(8,128)(2,1)}, bf16[1024,2048]{1,0:T(8,128)(2,1)}, bf16[256,3072]{1,0:T(8,128)(2,1)}) custom-call(bf16[1024,3072]{1,0:T(8,128)(2,1)} %get-tuple-element.405.refs_3_.refs_0_, bf16[2048,3072]{1,0:T(8,128)(2,1)} %all-gather.14.cloned.1.call-done.refs_1_, f32[1024,2048]{1,0:T(8,128)} %get-tuple-element.407.refs_2_, ...), custom_call_target="tpu_custom_call" | custom-call | flops 45900001280 | bytes 1000 | tf_op jit(solution)/shard_map/pallas_call | solution.py:720
  917.8 41.8 %shard_map.181 = (bf16[1024,3072]{1,0:T(8,128)(2,1)}, bf16[256,3072]{1,0:T(8,128)(2,1)}) custom-call(bf16[1024,2048]{1,0:T(8,128)(2,1)} %get-tuple-element.432.refs_0_.refs_3_, bf16[1024,2048]{1,0:T(8,128)(2,1)} %get-tuple-element.449.refs_1_.refs_3_, bf16[3072,2048]{1,0:T(8,128)(2,1)} %all-gather.12.cloned.1.call-done.refs_1_.refs_2_, ...), custom_call_target="tpu_custom_call" | custom-call | flops 45900001280 | bytes 1000 | tf_op jit(solution)/shard_map/pallas_call | solution.py:720
  973.2 42.2 %shard_map.184 = (bf16[3072,2048]{1,0:T(8,128)(2,1)}, bf16[256,3072]{1,0:T(8,128)(2,1)}) custom-call(bf16[1024,3072]{1,0:T(8,128)(2,1)} %shard_map.168.refs_0_, bf16[1024,3072]{1,0:T(8,128)(2,1)} %shard_map.172.refs_0_.refs_1_, bf16[1024,2048]{1,0:T(8,128)(2,1)} %get-tuple-element.431.refs_0_.refs_2_, bf16[1024,2048]{1,0:T(8,128)(2,1)} %get-tuple-element.432.refs_0_.refs_3_, ...), custom_call_target="tpu_custom_call" | custom-call | flops 45900001280 | bytes 1000 | tf_op jit(solution)/shard_map/pallas_call | solution.py:720
  1039.2 43.0 %shard_map.187 = (bf16[3072,2048]{1,0:T(8,128)(2,1)}, bf16[256,3072]{1,0:T(8,128)(2,1)}) custom-call(bf16[1024,3072]{1,0:T(8,128)(2,1)} %shard_map.168.refs_0_, bf16[1024,3072]{1,0:T(8,128)(2,1)} %shard_map.172.refs_0_.refs_1_, bf16[1024,2048]{1,0:T(8,128)(2,1)} %get-tuple-element.448.refs_1_.refs_2_, bf16[1024,2048]{1,0:T(8,128)(2,1)} %get-tuple-element.449.refs_1_.refs_3_, ...), custom_call_target="tpu_custom_call" | custom-call | flops 45900001280 | bytes 1000 | tf_op jit(solution)/shard_map/pallas_call | solution.py:720
  1170.5 74.8 %shard_map.195 = (bf16[1024,768]{1,0:T(8,128)(2,1)}, bf16[1024,768]{1,0:T(8,128)(2,1)}, bf16[1024,768]{1,0:T(8,128)(2,1)}, bf16[1024,768]{1,0:T(8,128)(2,1)}, bf...) custom-call(bf16[1024,768]{1,0:T(8,128)(2,1)} %get-tuple-element.320, ...), custom_call_target="tpu_custom_call" | custom-call | flops 45900001280 | bytes 1000 | tf_op jit(solution)/shard_map/pallas_call | solution.py:720
  1259.0 39.0 %shard_map.197 = bf16[3072,2304]{1,0:T(8,128)(2,1)} custom-call(bf16[1024,3072]{1,0:T(8,128)(2,1)} %get-tuple-element.490.refs_0_, bf16[1024,3072]{1,0:T(8,128)(2,1)} %get-tuple-element.491.refs_0_.refs_1_, bf16[1024,2304]{1,0:T(8,128)(2,1)} %constant_dynamic-update-slice_fusion.refs_2_.refs_0_, bf16[1024,2304]{1,0:T(8,128)(2,1)} %copy-done.45), custom_call_target="tpu_custom_call" | custom-call | flops 49284751360 | bytes 1000 | tf_op jit(solution)/shard_map/pallas_call | solution.py:720
  1313.6 19.9 %shard_map.199.term_ref = bf16[1024,3072]{1,0:T(8,128)(2,1)} custom-call(bf16[1024,2304]{1,0:T(8,128)(2,1)} %constant_dynamic-update-slice_fusion.refs_2_.refs_0_, bf16[3072,2304]{1,0:T(8,128)(2,1)} %all-gather.6.cloned.1.call-done.refs_1_), custom_call_target="tpu_custom_call" | custom-call | flops 24642375680 | bytes 1000 | tf_op jit(solution)/shard_map/pallas_call | solution.py:720
  1340.8 79.8 %shard_map.201 = (bf16[1024,3072]{1,0:T(8,128)(2,1)}, bf16[256,3072]{1,0:T(8,128)(2,1)}) custom-call(bf16[1024,2304]{1,0:T(8,128)(2,1)} %copy-done.45, bf16[3072,2304]{1,0:T(8,128)(2,1)} %all-gather.6.cloned.1.call-done.refs_1_, bf16[256,3072]{1,0:T(8,128)(2,1)} %get-tuple-element.509.refs_2_), custom_call_target="tpu_custom_call" | custom-call | flops 45900001280 | bytes 1000 | tf_op jit(solution)/shard_map/pallas_call | solution.py:720
  1430.9 96.0 %shard_map.204 = (bf16[256,3072]{1,0:T(8,128)(2,1)}, bf16[96,3072]{1,0:T(8,128)(2,1)}) custom-call(bf16[256,3072]{1,0:T(8,128)(2,1)} %get-tuple-element.519.refs_0_, bf16[96,3072]{1,0:T(8,128)(2,1)} %get-tuple-element.520.refs_1_), custom_call_target="tpu_custom_call" | custom-call | flops 221000007680 | bytes 1000 | tf_op jit(solution)/shard_map/pallas_call | solution.py:778
  1575.9 101.5 %collective-permute-done.11 = f32[2,192]{1,0:T(2,128)S(1)} collective-permute-done((f32[2,192]{1,0:T(2,128)S(1)}, f32[2,192]{1,0:T(2,128)S(1)}, u32[]{:S(2)}, u32[]{:S(2)}) %collective-permute-start.11) | collective-permute-done | bytes 1568 | tf_op jit(solution)/shard_map/ppermute | solution.py:1160
  (324 shorter events, 424.9 us)
Async XLA Ops:
  7.2 322.4 %all-gather.6.cloned.1.call-start = ((), (), s32[]{:S(2)}) async-start(), calls=%async_computation.5 | async-start | bytes 17694720 | tf_op jit(solution)/shard_map/all_gather | solution.py:1131
  110.9 278.0 %all-gather.8.cloned.1.call-start = ((), (), s32[]{:S(2)}) async-start(), calls=%async_computation.6 | async-start | bytes 5898240 | tf_op jit(solution)/shard_map/all_gather | solution.py:1131
  217.2 338.5 %all-gather.12.cloned.1.call-start = ((), (), s32[]{:S(2)}) async-start(), calls=%async_computation.8 | async-start | bytes 15728640 | tf_op jit(solution)/shard_map/all_gather | solution.py:1131
  309.1 295.9 %all-gather.10.cloned.1.call-start = ((), (), s32[]{:S(2)}) async-start(), calls=%async_computation.7 | async-start | bytes 15728640 | tf_op jit(solution)/shard_map/all_gather | solution.py:1131
  310.5 70.1 %collective-permute-start = (bf16[384,2048]{1,0:T(8,128)(2,1)S(1)}, bf16[384,2048]{1,0:T(8,128)(2,1)S(1)}, u32[]{:S(2)}, u32[]{:S(2)}) collective-permute-start(bf16[384,2048]{1,0:T(8,128)(2,1)S(1)} %copy-done.30), channel_id=1, source_target_pairs={{0,2},{1,3},{2,0},{3,1},{4,6},{5,7},{6,4},{7,5},{8,10},{9,11},{10,... | collective-permute-start | bytes 4718600 | tf_op jit(solution)/shard_map/ppermute | solution.py:1099
  385.6 413.8 %all-gather.14.cloned.1.call-start = ((), (), s32[]{:S(2)}) async-start(), calls=%async_computation.9 | async-start | bytes 15728640 | tf_op jit(solution)/shard_map/all_gather | solution.py:1131
  386.7 165.1 %collective-permute-start.1 = (bf16[256,3072]{1,0:T(8,128)(2,1)}, bf16[256,3072]{1,0:T(8,128)(2,1)}, u32[]{:S(2)}, u32[]{:S(2)}) collective-permute-start(bf16[256,3072]{1,0:T(8,128)(2,1)} %own_ref.1), channel_id=1, source_target_pairs={{0,2},{1,3},{2,0},{3,1},{4,6},{5,7},{6,4},{7,5},{8,10},{9,11},{10,... | collective-permute-start | bytes 4718600 | tf_op jit(solution)/shard_map/ppermute | solution.py:1099
  555.7 479.7 %reduce-scatter.6.cloned.1.call-start = ((), (), s32[]{:S(2)}) async-start(), calls=%async_computation.10 | async-start | bytes 15728640 | tf_op jit(solution)/shard_map/reduce_scatter | solution.py:1134
  597.9 88.7 %collective-permute-start.2 = (bf16[256,3072]{1,0:T(8,128)(2,1)}, bf16[256,3072]{1,0:T(8,128)(2,1)}, u32[]{:S(2)}, u32[]{:S(2)}) collective-permute-start(bf16[256,3072]{1,0:T(8,128)(2,1)} %get-tuple-element.368), channel_id=1, source_target_pairs={{0,2},{1,3},{2,0},{3,1},{4,6},{5,7},{6,4},{7,5},{8,10},{9,11},{10,... | collective-permute-start | bytes 4718600 | tf_op jit(solution)/shard_map/ppermute | solution.py:1099
  794.7 450.6 %reduce-scatter.8.cloned.1.call-start = ((), (), s32[]{:S(2)}) async-start(), calls=%async_computation.11 | async-start | bytes 15728640 | tf_op jit(solution)/shard_map/reduce_scatter | solution.py:1134
  1015.4 294.3 %reduce-scatter.10.cloned.1.call-start = ((), (), s32[]{:S(2)}) async-start(), calls=%async_computation.12 | async-start | bytes 15728640 | tf_op jit(solution)/shard_map/reduce_scatter | solution.py:1134
  1082.3 345.8 %reduce-scatter.12.cloned.1.call-start = ((), (), s32[]{:S(2)}) async-start(), calls=%async_computation.13 | async-start | bytes 5898240 | tf_op jit(solution)/shard_map/reduce_scatter | solution.py:1134
  1083.5 463.3 %collective-permute-start.5 = (bf16[256,3072]{1,0:T(8,128)(2,1)}, bf16[256,3072]{1,0:T(8,128)(2,1)}, u32[]{:S(2)}, u32[]{:S(2)}) collective-permute-start(bf16[256,3072]{1,0:T(8,128)(2,1)} %get-tuple-element.445), channel_id=1, source_target_pairs={{0,2},{1,3},{2,0},{3,1},{4,6},{5,7},{6,4},{7,5},{8,10},{9,11},{10,... | collective-permute-start | bytes 4718600 | tf_op jit(solution)/shard_map/ppermute | solution.py:1099
  1170.5 356.5 %reduce-scatter.14.cloned.1.call-start = ((), (), s32[]{:S(2)}) async-start(), calls=%async_computation.14 | async-start | bytes 17694720 | tf_op jit(solution)/shard_map/reduce_scatter | solution.py:1134
  1249.2 304.2 %collective-permute-start.4 = (bf16[384,2048]{1,0:T(8,128)(2,1)}, bf16[384,2048]{1,0:T(8,128)(2,1)}, u32[]{:S(2)}, u32[]{:S(2)}) collective-permute-start(bf16[384,2048]{1,0:T(8,128)(2,1)} %get-tuple-element.483), channel_id=1, source_target_pairs={{0,2},{1,3},{2,0},{3,1},{4,6},{5,7},{6,4},{7,5},{8,10},{9,11},{10,... | collective-permute-start | bytes 4718600 | tf_op jit(solution)/shard_map/ppermute | solution.py:1099
  1313.5 253.1 %collective-permute-start.7 = (bf16[384,2048]{1,0:T(8,128)(2,1)}, bf16[384,2048]{1,0:T(8,128)(2,1)}, u32[]{:S(2)}, u32[]{:S(2)}) collective-permute-start(bf16[384,2048]{1,0:T(8,128)(2,1)} %get-tuple-element.502), channel_id=1, source_target_pairs={{0,2},{1,3},{2,0},{3,1},{4,6},{5,7},{6,4},{7,5},{8,10},{9,11},{10,... | collective-permute-start | bytes 4718600 | tf_op jit(solution)/shard_map/ppermute | solution.py:1099
  1430.5 124.9 %collective-permute-start.3 = (bf16[256,3072]{1,0:T(8,128)(2,1)}, bf16[256,3072]{1,0:T(8,128)(2,1)}, u32[]{:S(2)}, u32[]{:S(2)}) collective-permute-start(bf16[256,3072]{1,0:T(8,128)(2,1)} %get-tuple-element.511), channel_id=1, source_target_pairs={{0,2},{1,3},{2,0},{3,1},{4,6},{5,7},{6,4},{7,5},{8,10},{9,11},{10,... | collective-permute-start | bytes 4718600 | tf_op jit(solution)/shard_map/ppermute | solution.py:1099
  1531.1 165.5 %collective-permute-start.13 = (bf16[384,2304]{1,0:T(8,128)(2,1)}, bf16[384,2304]{1,0:T(8,128)(2,1)}, u32[]{:S(2)}, u32[]{:S(2)}) collective-permute-start(bf16[384,2304]{1,0:T(8,128)(2,1)} %get-tuple-element.525), channel_id=1, source_target_pairs={{0,2},{1,3},{2,0},{3,1},{4,6},{5,7},{6,4},{7,5},{8,10},{9,11},{10,... | collective-permute-start | bytes 5308424 | tf_op jit(solution)/shard_map/ppermute | solution.py:1099
  1546.8 144.3 %collective-permute-start.6 = (bf16[256,3072]{1,0:T(8,128)(2,1)}, bf16[256,3072]{1,0:T(8,128)(2,1)}, u32[]{:S(2)}, u32[]{:S(2)}) collective-permute-start(bf16[256,3072]{1,0:T(8,128)(2,1)} %get-tuple-element.585), channel_id=1, source_target_pairs={{0,2},{1,3},{2,0},{3,1},{4,6},{5,7},{6,4},{7,5},{8,10},{9,11},{10,... | collective-permute-start | bytes 4718600 | tf_op jit(solution)/shard_map/ppermute | solution.py:1099
  1555.5 5.0 collective-permute-start.8
  1560.6 6.0 collective-permute-start.9
  1566.6 3.8 collective-permute-start.10
  1570.5 106.9 %collective-permute-start.11 = (f32[2,192]{1,0:T(2,128)S(1)}, f32[2,192]{1,0:T(2,128)S(1)}, u32[]{:S(2)}, u32[]{:S(2)}) collective-permute-start(f32[2,192]{1,0:T(2,128)S(1)} %bitcast.100), channel_id=1, source_target_pairs={{0,2},{1,3},{2,0},{3,1},{4,6},{5,7},{6,4},{7,5},{8,10},{9,11},{10,... | collective-permute-start | bytes 4616 | tf_op jit(solution)/shard_map/ppermute | solution.py:1160
  1677.5 13.1 collective-permute-start.12
  (68 other events, 766.9 us)
Sparse Core Ops, SparseCore 0:
  111.0 135.6 all-gather.5
  248.5 57.0 all-gather.7
  309.2 121.6 all-gather.11
  432.6 122.4 all-gather.9
  556.8 122.5 all-gather.13
  794.8 120.3 reduce-scatter.5
  1015.5 120.4 reduce-scatter.7
  1139.1 120.7 reduce-scatter.9
  1262.8 57.0 reduce-scatter.11
  1322.9 133.6 reduce-scatter.13

commit v11 on v10

--- a/solution.py
+++ b/solution.py
@@ -1349,12 +1349,16 @@
 
     d_second = act(core_gather, n_second, near_second)
     heads_second = act(heads_back, d_second, out_full)
+    mlp_first = act(dot_bf16, a_first, down_full)
+    mlp_keep_first, mlp_send_first = act(core_reduce, mlp_first)
+    mlp_second, mlp_branch_first = act(
+        dot_bf16, a_second, down_full, sends=[("near", mlp_send_first)]
+    )
+    mlp_keep_second, mlp_send_second = act(core_reduce, mlp_second)
+    gate_mine, gate_away = act(lambda pair: core_split(9, pair), gate_sum)
+    gate_got = swap_far(gate_away)
     grad_out = act(grad_sum, mixed_first, d_first, mixed_second, d_second)
     out_sum = plane_scatter(grad_out)
-    mlp_first = act(dot_bf16, a_first, down_full)
-    mlp_keep_first, mlp_send_first = act(core_reduce, mlp_first)
-    mlp_second = act(dot_bf16, a_second, down_full)
-    mlp_keep_second, mlp_send_second = act(core_reduce, mlp_second)
     def attend_back(heads_first, heads_second, pushes=()):
         return attention_call(
             backward_both,
@@ -1368,12 +1372,9 @@
             pushes,
         )
 
-    *grads, mlp_branch_first, mlp_branch_second = act(
-        attend_back, heads_first, heads_second,
-        sends=[("near", mlp_send_first), ("near", mlp_send_second)],
-    )
-    gate_mine, gate_away = act(lambda pair: core_split(9, pair), gate_sum)
-    gate_got = swap_far(gate_away)
+    *grads, mlp_branch_second = act(
+        attend_back, heads_first, heads_second, sends=[("near", mlp_send_second)]
+    )
     p_first, p_second = act(
         lambda *parts: (
             jnp.concatenate(parts[:3], axis=1),
@@ -1387,20 +1388,20 @@
         second = (second + second_keep + second_got.astype(jnp.float32)).astype(jnp.bfloat16)
         return jnp.where(far == 0, first, second), jnp.where(far == 0, second, first)
 
+    up_mine, up_away = act(lambda pair: core_split(9, pair), up_sum)
+    up_got = swap_far(up_away)
     grad_qkv = act(grad_sum, h1_first, p_first, h1_second, p_second)
     qkv_sum = plane_scatter(grad_qkv)
     out_keep, out_send = act(
         finish_output,
         m_first, mlp_keep_first, mlp_branch_first, m_second, mlp_keep_second, mlp_branch_second,
     )
-    up_mine, up_away = act(lambda pair: core_split(9, pair), up_sum)
-    up_got = swap_far(up_away)
+    out_got = swap_far(out_send)
     term_first = act(heads_back, p_first, qkv_full)
     keep_first, send_first = act(core_reduce, term_first)
     term_second, back_first = act(
         heads_back, p_second, qkv_full, sends=[("near", send_first)]
     )
-    out_got = swap_far(chained(out_send, term_second))
     keep_second, send_second = act(core_reduce, term_second)
     out_mine, out_away = act(lambda pair: core_split(8, pair), out_sum)
     def settle(keep, got):

time: 1720 us -> 1730 us (level)
    pallas_call x26, Pallas kernels: 921 us -> 978 us  [grid_call(): pl.pallas_call(kernel, out_shape=outs, grid=grid, in_specs=in_specs, out_...]
    pallas_call x28, Pallas kernels: 487 us -> 442 us  [exchange_call(): pl.pallas_call(kernel, out_shape=outs, in_specs=[anywhere] * len(operands...]
    unnamed x148 -> x146, local copies, waits for them, and re-layouts: 43.5 us -> 42.8 us
where the time goes in v11:
time: 1730 us
  Pallas kernels  1420 us (82%)
  other arithmetic  103 us (6%)
  waiting for transfers between devices  102 us (6%)
  local copies, waits for them, and re-layouts  69.2 us (4%)
    pallas_call x26, Pallas kernels, grid_call(): pl.pallas_call(kernel, out_shape=outs, grid=grid, in_specs=in_specs, out_...  978 us
    pallas_call x28, Pallas kernels, exchange_call(): pl.pallas_call(kernel, out_shape=outs, in_specs=[anywhere] * len(operands...  442 us
    ppermute x5, waiting for transfers between devices, scatter_gains(): lax.ppermute(sent, axis, [(i, i ^ step) for i in range(size)])  102 us
    unnamed x146, local copies, waits for them, and re-layouts  42.8 us
  transfers between devices with their start and end apart: 24, of which 2 were waited for; matrix products, arithmetic and copies ran while one was open for 7% of the time, Pallas kernels for 77%

profile of v11, /device:TPU:0, one launch (start us, length us, event | category | flops | bytes accessed | tf_op | source)
XLA Modules:
  0.0 1725.4 jit_solution(10711004005761276072)
XLA Ops:
  20.3 82.6 %shard_map.152 = (bf16[256,3072]{1,0:T(8,128)(2,1)}, bf16[384,2304]{1,0:T(8,128)(2,1)}, s32[8,256]{1,0:T(8,128)}) custom-call(bf16[256,3072]{1,0:T(8,128)(2,1)} %fusion.4.refs_0_.own_ref, bf16[384,2304]{1,0:T(8,128)(2,1)} %copy.35.refs_1_, s32[8,256]{1,0:T(8,128)} %broadcast_in_dim.11.refs_2_), custom_call_target="tpu_custom_call" | custom-call | flops 221000007680 | bytes 1000 | tf_op jit(solution)/shard_map/pallas_call | solution.py:778
  118.2 96.5 %shard_map.154 = (bf16[256,3072]{1,0:T(8,128)(2,1)}, bf16[256,3072]{1,0:T(8,128)(2,1)}, bf16[96,3072]{1,0:T(8,128)(2,1)}, s32[16,256]{1,0:T(8,128)}) custom-call(bf16[256,3072]{1,0:T(8,128)(2,1)} %get-tuple-element.296.refs_0_, bf16[256,3072]{1,0:T(8,128)(2,1)} %get-tuple-element.385.refs_1_.own_ref, bf16[96,3072]{1,0:T(8,128)(2,1)} %own_ref, ...), custom_call_target="tpu_custom_call" | custom-call | flops 221000007680 | bytes 1000 | tf_op jit(solution)/shard_map/pallas_call | solution.py:778
  233.6 71.7 %shard_map.156 = (bf16[256,3072]{1,0:T(8,128)(2,1)}, bf16[384,2048]{1,0:T(8,128)(2,1)}, s32[32,256]{1,0:T(8,128)}) custom-call(bf16[256,3072]{1,0:T(8,128)(2,1)} %multiply_convert_fusion.2.refs_0_.got_ref, bf16[384,2048]{1,0:T(8,128)(2,1)} %get-tuple-element.313.refs_1_.own_ref, s32[32,256]{1,0:T(8,128)} %pad_add_fusion.1.refs_2_), custom_call_target="tpu_custom_call" | custom-call | flops 221000007680 | bytes 1000 | tf_op jit(solution)/shard_map/pallas_call | solution.py:778
  329.6 21.7 %shard_map.159.q_ref.k_ref.v_ref = f32[1024,2304]{1,0:T(8,128)} custom-call(bf16[1024,3072]{1,0:T(8,128)(2,1)} %get-tuple-element.501.refs_0_, bf16[3072,2304]{1,0:T(8,128)(2,1)} %all-gather.6.cloned.1.call-done.refs_1_), custom_call_target="tpu_custom_call" | custom-call | flops 24642375680 | bytes 1000 | tf_op jit(solution)/shard_map/pallas_call | solution.py:720
  351.2 29.2 %shard_map.160 = (bf16[1024,768]{1,0:T(8,128)(2,1)}, bf16[1024,768]{1,0:T(8,128)(2,1)}, bf16[1024,768]{1,0:T(8,128)(2,1)}, bf16[1024,768]{1,0:T(8,128)(2,1)}, f32[2,1024,4]{2,1,0:T(8,128)}) custom-call(f32[1024,2304]{1,0:T(8,128)} %shard_map.159.q_ref.k_ref.v_ref, f32[1024,2304]{1,0:T(8,128)} %shard_map.159.q_ref.k_ref.v_ref, ...), custom_call_target="tpu_custom_call" | custom-call | flops 8556380160 | bytes 1000 | tf_op jit(solution)/shard_map/pallas_call | solution.py:720
  406.2 75.9 %shard_map.164 = (f32[1024,2304]{1,0:T(8,128)}, bf16[256,3072]{1,0:T(8,128)(2,1)}) custom-call(bf16[1024,3072]{1,0:T(8,128)(2,1)} %get-tuple-element.502.refs_0_.refs_1_, bf16[3072,2304]{1,0:T(8,128)(2,1)} %all-gather.6.cloned.1.call-done.refs_1_, bf16[256,3072]{1,0:T(8,128)(2,1)} %get-tuple-element.339.refs_2_), custom_call_target="tpu_custom_call" | custom-call | flops 45900001280 | bytes 1000 | tf_op jit(solution)/shard_map/pallas_call | solution.py:720
  488.8 39.7 %shard_map.165 = (bf16[1024,768]{1,0:T(8,128)(2,1)}, bf16[1024,768]{1,0:T(8,128)(2,1)}, bf16[1024,768]{1,0:T(8,128)(2,1)}, bf16[1024,768]{1,0:T(8,128)(2,1)}, f3...) custom-call(f32[1024,2304]{1,0:T(8,128)} %get-tuple-element.345.refs_0_.refs_1_.refs_2_, ...), custom_call_target="tpu_custom_call" | custom-call | flops 45900001280 | bytes 1000 | tf_op jit(solution)/shard_map/pallas_call | solution.py:720
  555.8 42.1 %shard_map.170 = (f32[1024,2048]{1,0:T(8,128)}, bf16[256,3072]{1,0:T(8,128)(2,1)}) custom-call(bf16[1024,3072]{1,0:T(8,128)(2,1)} %shard_map.168.refs_0_, bf16[3072,2048]{1,0:T(8,128)(2,1)} %all-gather.12.cloned.1.call-done.refs_1_.refs_2_, bf16[256,3072]{1,0:T(8,128)(2,1)} %get-tuple-element.364.refs_2_), custom_call_target="tpu_custom_call" | custom-call | flops 45900001280 | bytes 1000 | tf_op jit(solution)/shard_map/pallas_call | solution.py:720
  605.0 75.5 %shard_map.171 = (f32[1024,2048]{1,0:T(8,128)}, bf16[1024,2048]{1,0:T(8,128)(2,1)}, bf16[256,3072]{1,0:T(8,128)(2,1)}) custom-call(bf16[1024,3072]{1,0:T(8,128)(2,1)} %shard_map.168.refs_0_, bf16[3072,2048]{1,0:T(8,128)(2,1)} %all-gather.10.cloned.1.call-done.refs_1_.refs_3_, f32[1024,2048]{1,0:T(8,128)} %get-tuple-element.402.refs_2_, ...), custom_call_target="tpu_custom_call" | custom-call | flops 45900001280 | bytes 1000 | tf_op jit(solution)/shard_map/pallas_call | solution.py:720
  686.6 42.0 %shard_map.173 = (f32[1024,2048]{1,0:T(8,128)}, bf16[256,3072]{1,0:T(8,128)(2,1)}) custom-call(bf16[1024,3072]{1,0:T(8,128)(2,1)} %shard_map.172.refs_0_.refs_1_, bf16[3072,2048]{1,0:T(8,128)(2,1)} %all-gather.12.cloned.1.call-done.refs_1_.refs_2_, bf16[256,3072]{1,0:T(8,128)(2,1)} %collective-permute-done.2.refs_2_.got_ref), custom_call_target="tpu_custom_call" | custom-call | flops 45900001280 | bytes 1000 | tf_op jit(solution)/shard_map/pallas_call | solution.py:720
  739.3 20.2 %shard_map.175 = (f32[1024,2048]{1,0:T(8,128)}, bf16[1024,2048]{1,0:T(8,128)(2,1)}) custom-call(bf16[1024,3072]{1,0:T(8,128)(2,1)} %shard_map.172.refs_0_.refs_1_, bf16[3072,2048]{1,0:T(8,128)(2,1)} %all-gather.10.cloned.1.call-done.refs_1_.refs_3_, f32[1024,2048]{1,0:T(8,128)} %get-tuple-element.414.refs_2_), custom_call_target="tpu_custom_call" | custom-call | flops 21904332800 | bytes 1000 | tf_op jit(solution)/shard_map/pallas_call | solution.py:720
  759.4 35.3 %shard_map.176 = bf16[2048,3072]{1,0:T(8,128)(2,1)} custom-call(bf16[1024,2048]{1,0:T(8,128)(2,1)} %get-tuple-element.464.refs_0_, bf16[1024,2048]{1,0:T(8,128)(2,1)} %get-tuple-element.468.refs_1_.refs_0_, bf16[1024,3072]{1,0:T(8,128)(2,1)} %get-tuple-element.400.refs_2_.refs_0_, bf16[1024,3072]{1,0:T(8,128)(2,1)} %get-tuple-element.412.refs_3_.refs_0_), custom_call_target="tpu_custom_call" | custom-call | flops 43808665600 | bytes 1000 | tf_op jit(solution)/shard_map/pallas_call | solution.py:720
  799.4 25.0 %shard_map.177 = (bf16[1024,2048]{1,0:T(8,128)(2,1)}, bf16[1024,2048]{1,0:T(8,128)(2,1)}) custom-call(bf16[1024,3072]{1,0:T(8,128)(2,1)} %get-tuple-element.400.refs_2_.refs_0_, bf16[2048,3072]{1,0:T(8,128)(2,1)} %all-gather.14.cloned.1.call-done.refs_1_, f32[1024,2048]{1,0:T(8,128)} %get-tuple-element.402.refs_2_, f32[1024,2048]{1,0:T(8,128)} %get-tuple-element.403.refs_3_), custom_call_target="tpu_custom_call" | custom-call | flops 21904332800 | bytes 1000 | tf_op jit(solution)/shard_map/pallas_call | solution.py:720
  824.4 33.3 %shard_map.178.term_ref = bf16[1024,3072]{1,0:T(8,128)(2,1)} custom-call(bf16[1024,2048]{1,0:T(8,128)(2,1)} %get-tuple-element.438.refs_0_.refs_2_, bf16[1024,2048]{1,0:T(8,128)(2,1)} %get-tuple-element.455.refs_1_.refs_2_, bf16[3072,2048]{1,0:T(8,128)(2,1)} %all-gather.12.cloned.1.call-done.refs_1_.refs_2_, ...), custom_call_target="tpu_custom_call" | custom-call | flops 43808665600 | bytes 1000 | tf_op jit(solution)/shard_map/pallas_call | solution.py:720
  865.1 44.6 %shard_map.180 = (bf16[1024,2048]{1,0:T(8,128)(2,1)}, bf16[1024,2048]{1,0:T(8,128)(2,1)}, bf16[256,3072]{1,0:T(8,128)(2,1)}) custom-call(bf16[1024,3072]{1,0:T(8,128)(2,1)} %get-tuple-element.412.refs_3_.refs_0_, bf16[2048,3072]{1,0:T(8,128)(2,1)} %all-gather.14.cloned.1.call-done.refs_1_, f32[1024,2048]{1,0:T(8,128)} %get-tuple-element.414.refs_2_, ...), custom_call_target="tpu_custom_call" | custom-call | flops 45900001280 | bytes 1000 | tf_op jit(solution)/shard_map/pallas_call | solution.py:720
  917.8 41.8 %shard_map.181 = (bf16[1024,3072]{1,0:T(8,128)(2,1)}, bf16[256,3072]{1,0:T(8,128)(2,1)}) custom-call(bf16[1024,2048]{1,0:T(8,128)(2,1)} %get-tuple-element.439.refs_0_.refs_3_, bf16[1024,2048]{1,0:T(8,128)(2,1)} %get-tuple-element.456.refs_1_.refs_3_, bf16[3072,2048]{1,0:T(8,128)(2,1)} %all-gather.12.cloned.1.call-done.refs_1_.refs_2_, ...), custom_call_target="tpu_custom_call" | custom-call | flops 45900001280 | bytes 1000 | tf_op jit(solution)/shard_map/pallas_call | solution.py:720
  973.1 42.2 %shard_map.184 = (bf16[3072,2048]{1,0:T(8,128)(2,1)}, bf16[256,3072]{1,0:T(8,128)(2,1)}) custom-call(bf16[1024,3072]{1,0:T(8,128)(2,1)} %shard_map.168.refs_0_, bf16[1024,3072]{1,0:T(8,128)(2,1)} %shard_map.172.refs_0_.refs_1_, bf16[1024,2048]{1,0:T(8,128)(2,1)} %get-tuple-element.438.refs_0_.refs_2_, bf16[1024,2048]{1,0:T(8,128)(2,1)} %get-tuple-element.439.refs_0_.refs_3_, ...), custom_call_target="tpu_custom_call" | custom-call | flops 45900001280 | bytes 1000 | tf_op jit(solution)/shard_map/pallas_call | solution.py:720
  1039.2 43.0 %shard_map.187 = (bf16[3072,2048]{1,0:T(8,128)(2,1)}, bf16[256,3072]{1,0:T(8,128)(2,1)}) custom-call(bf16[1024,3072]{1,0:T(8,128)(2,1)} %shard_map.168.refs_0_, bf16[1024,3072]{1,0:T(8,128)(2,1)} %shard_map.172.refs_0_.refs_1_, bf16[1024,2048]{1,0:T(8,128)(2,1)} %get-tuple-element.455.refs_1_.refs_2_, bf16[1024,2048]{1,0:T(8,128)(2,1)} %get-tuple-element.456.refs_1_.refs_3_, ...), custom_call_target="tpu_custom_call" | custom-call | flops 45900001280 | bytes 1000 | tf_op jit(solution)/shard_map/pallas_call | solution.py:720
  1125.9 62.8 %shard_map.192 = (bf16[1024,3072]{1,0:T(8,128)(2,1)}, bf16[256,3072]{1,0:T(8,128)(2,1)}) custom-call(bf16[1024,2048]{1,0:T(8,128)(2,1)} %get-tuple-element.468.refs_1_.refs_0_, bf16[2048,3072]{1,0:T(8,128)(2,1)} %all-gather.14.cloned.1.call-done.refs_1_, bf16[256,3072]{1,0:T(8,128)(2,1)} %get-tuple-element.470.refs_2_), custom_call_target="tpu_custom_call" | custom-call | flops 45900001280 | bytes 1000 | tf_op jit(solution)/shard_map/pallas_call | solution.py:720
  1218.5 74.6 %shard_map.196 = (bf16[1024,768]{1,0:T(8,128)(2,1)}, bf16[1024,768]{1,0:T(8,128)(2,1)}, bf16[1024,768]{1,0:T(8,128)(2,1)}, bf16[1024,768]{1,0:T(8,128)(2,1)}, bf...) custom-call(bf16[1024,768]{1,0:T(8,128)(2,1)} %get-tuple-element.327.refs_0_, ...), custom_call_target="tpu_custom_call" | custom-call | flops 45900001280 | bytes 1000 | tf_op jit(solution)/shard_map/pallas_call | solution.py:720
  1306.1 39.1 %shard_map.198 = bf16[3072,2304]{1,0:T(8,128)(2,1)} custom-call(bf16[1024,3072]{1,0:T(8,128)(2,1)} %get-tuple-element.501.refs_0_, bf16[1024,3072]{1,0:T(8,128)(2,1)} %get-tuple-element.502.refs_0_.refs_1_, bf16[1024,2304]{1,0:T(8,128)(2,1)} %constant_dynamic-update-slice_fusion.refs_2_.refs_0_, bf16[1024,2304]{1,0:T(8,128)(2,1)} %copy-done.44), custom_call_target="tpu_custom_call" | custom-call | flops 49284751360 | bytes 1000 | tf_op jit(solution)/shard_map/pallas_call | solution.py:720
  1383.7 93.6 %shard_map.201 = (bf16[1024,3072]{1,0:T(8,128)(2,1)}, bf16[256,3072]{1,0:T(8,128)(2,1)}) custom-call(bf16[1024,2304]{1,0:T(8,128)(2,1)} %copy-done.44, bf16[3072,2304]{1,0:T(8,128)(2,1)} %all-gather.6.cloned.1.call-done.refs_1_, bf16[256,3072]{1,0:T(8,128)(2,1)} %get-tuple-element.517.refs_2_), custom_call_target="tpu_custom_call" | custom-call | flops 45900001280 | bytes 1000 | tf_op jit(solution)/shard_map/pallas_call | solution.py:720
  1487.2 50.6 %shard_map.204 = (bf16[256,3072]{1,0:T(8,128)(2,1)}, bf16[96,3072]{1,0:T(8,128)(2,1)}) custom-call(bf16[256,3072]{1,0:T(8,128)(2,1)} %get-tuple-element.524.refs_0_, bf16[96,3072]{1,0:T(8,128)(2,1)} %get-tuple-element.525.refs_1_), custom_call_target="tpu_custom_call" | custom-call | flops 221000007680 | bytes 1000 | tf_op jit(solution)/shard_map/pallas_call | solution.py:778
  1587.1 102.0 %collective-permute-done.11 = f32[2,192]{1,0:T(2,128)S(1)} collective-permute-done((f32[2,192]{1,0:T(2,128)S(1)}, f32[2,192]{1,0:T(2,128)S(1)}, u32[]{:S(2)}, u32[]{:S(2)}) %collective-permute-start.11) | collective-permute-done | bytes 1568 | tf_op jit(solution)/shard_map/ppermute | solution.py:1160
  (322 shorter events, 425.0 us)
Async XLA Ops:
  7.2 322.4 %all-gather.6.cloned.1.call-start = ((), (), s32[]{:S(2)}) async-start(), calls=%async_computation.5 | async-start | bytes 17694720 | tf_op jit(solution)/shard_map/all_gather | solution.py:1131
  110.9 278.1 %all-gather.8.cloned.1.call-start = ((), (), s32[]{:S(2)}) async-start(), calls=%async_computation.6 | async-start | bytes 5898240 | tf_op jit(solution)/shard_map/all_gather | solution.py:1131
  217.1 338.5 %all-gather.12.cloned.1.call-start = ((), (), s32[]{:S(2)}) async-start(), calls=%async_computation.8 | async-start | bytes 15728640 | tf_op jit(solution)/shard_map/all_gather | solution.py:1131
  309.1 295.9 %all-gather.10.cloned.1.call-start = ((), (), s32[]{:S(2)}) async-start(), calls=%async_computation.7 | async-start | bytes 15728640 | tf_op jit(solution)/shard_map/all_gather | solution.py:1131
  310.5 70.1 %collective-permute-start = (bf16[384,2048]{1,0:T(8,128)(2,1)S(1)}, bf16[384,2048]{1,0:T(8,128)(2,1)S(1)}, u32[]{:S(2)}, u32[]{:S(2)}) collective-permute-start(bf16[384,2048]{1,0:T(8,128)(2,1)S(1)} %copy-done.30), channel_id=1, source_target_pairs={{0,2},{1,3},{2,0},{3,1},{4,6},{5,7},{6,4},{7,5},{8,10},{9,11},{10,... | collective-permute-start | bytes 4718600 | tf_op jit(solution)/shard_map/ppermute | solution.py:1099
  385.6 413.8 %all-gather.14.cloned.1.call-start = ((), (), s32[]{:S(2)}) async-start(), calls=%async_computation.9 | async-start | bytes 15728640 | tf_op jit(solution)/shard_map/all_gather | solution.py:1131
  386.7 165.1 %collective-permute-start.1 = (bf16[256,3072]{1,0:T(8,128)(2,1)}, bf16[256,3072]{1,0:T(8,128)(2,1)}, u32[]{:S(2)}, u32[]{:S(2)}) collective-permute-start(bf16[256,3072]{1,0:T(8,128)(2,1)} %own_ref.1), channel_id=1, source_target_pairs={{0,2},{1,3},{2,0},{3,1},{4,6},{5,7},{6,4},{7,5},{8,10},{9,11},{10,... | collective-permute-start | bytes 4718600 | tf_op jit(solution)/shard_map/ppermute | solution.py:1099
  555.7 479.7 %reduce-scatter.6.cloned.1.call-start = ((), (), s32[]{:S(2)}) async-start(), calls=%async_computation.10 | async-start | bytes 15728640 | tf_op jit(solution)/shard_map/reduce_scatter | solution.py:1134
  597.9 88.7 %collective-permute-start.2 = (bf16[256,3072]{1,0:T(8,128)(2,1)}, bf16[256,3072]{1,0:T(8,128)(2,1)}, u32[]{:S(2)}, u32[]{:S(2)}) collective-permute-start(bf16[256,3072]{1,0:T(8,128)(2,1)} %get-tuple-element.375), channel_id=1, source_target_pairs={{0,2},{1,3},{2,0},{3,1},{4,6},{5,7},{6,4},{7,5},{8,10},{9,11},{10,... | collective-permute-start | bytes 4718600 | tf_op jit(solution)/shard_map/ppermute | solution.py:1099
  794.7 401.5 %reduce-scatter.8.cloned.1.call-start = ((), (), s32[]{:S(2)}) async-start(), calls=%async_computation.11 | async-start | bytes 15728640 | tf_op jit(solution)/shard_map/reduce_scatter | solution.py:1134
  1015.4 286.2 %reduce-scatter.10.cloned.1.call-start = ((), (), s32[]{:S(2)}) async-start(), calls=%async_computation.12 | async-start | bytes 15728640 | tf_op jit(solution)/shard_map/reduce_scatter | solution.py:1134
  1082.2 402.5 %reduce-scatter.12.cloned.1.call-start = ((), (), s32[]{:S(2)}) async-start(), calls=%async_computation.13 | async-start | bytes 5898240 | tf_op jit(solution)/shard_map/reduce_scatter | solution.py:1134
  1083.5 474.6 %collective-permute-start.5 = (bf16[256,3072]{1,0:T(8,128)(2,1)}, bf16[256,3072]{1,0:T(8,128)(2,1)}, u32[]{:S(2)}, u32[]{:S(2)}) collective-permute-start(bf16[256,3072]{1,0:T(8,128)(2,1)} %get-tuple-element.452), channel_id=1, source_target_pairs={{0,2},{1,3},{2,0},{3,1},{4,6},{5,7},{6,4},{7,5},{8,10},{9,11},{10,... | collective-permute-start | bytes 4718600 | tf_op jit(solution)/shard_map/ppermute | solution.py:1099
  1200.0 364.2 %collective-permute-start.4 = (bf16[384,2048]{1,0:T(8,128)(2,1)}, bf16[384,2048]{1,0:T(8,128)(2,1)}, u32[]{:S(2)}, u32[]{:S(2)}) collective-permute-start(bf16[384,2048]{1,0:T(8,128)(2,1)} %get-tuple-element.477), channel_id=1, source_target_pairs={{0,2},{1,3},{2,0},{3,1},{4,6},{5,7},{6,4},{7,5},{8,10},{9,11},{10,... | collective-permute-start | bytes 4718600 | tf_op jit(solution)/shard_map/ppermute | solution.py:1099
  1218.4 319.4 %reduce-scatter.14.cloned.1.call-start = ((), (), s32[]{:S(2)}) async-start(), calls=%async_computation.14 | async-start | bytes 17694720 | tf_op jit(solution)/shard_map/reduce_scatter | solution.py:1134
  1305.4 271.5 %collective-permute-start.7 = (bf16[384,2048]{1,0:T(8,128)(2,1)}, bf16[384,2048]{1,0:T(8,128)(2,1)}, u32[]{:S(2)}, u32[]{:S(2)}) collective-permute-start(bf16[384,2048]{1,0:T(8,128)(2,1)} %get-tuple-element.500), channel_id=1, source_target_pairs={{0,2},{1,3},{2,0},{3,1},{4,6},{5,7},{6,4},{7,5},{8,10},{9,11},{10,... | collective-permute-start | bytes 4718600 | tf_op jit(solution)/shard_map/ppermute | solution.py:1099
  1352.8 213.4 %collective-permute-start.3 = (bf16[256,3072]{1,0:T(8,128)(2,1)}, bf16[256,3072]{1,0:T(8,128)(2,1)}, u32[]{:S(2)}, u32[]{:S(2)}) collective-permute-start(bf16[256,3072]{1,0:T(8,128)(2,1)} %get-tuple-element.593), channel_id=1, source_target_pairs={{0,2},{1,3},{2,0},{3,1},{4,6},{5,7},{6,4},{7,5},{8,10},{9,11},{10,... | collective-permute-start | bytes 4718600 | tf_op jit(solution)/shard_map/ppermute | solution.py:1099
  1542.0 166.3 %collective-permute-start.13 = (bf16[384,2304]{1,0:T(8,128)(2,1)}, bf16[384,2304]{1,0:T(8,128)(2,1)}, u32[]{:S(2)}, u32[]{:S(2)}) collective-permute-start(bf16[384,2304]{1,0:T(8,128)(2,1)} %get-tuple-element.531), channel_id=1, source_target_pairs={{0,2},{1,3},{2,0},{3,1},{4,6},{5,7},{6,4},{7,5},{8,10},{9,11},{10,... | collective-permute-start | bytes 5308424 | tf_op jit(solution)/shard_map/ppermute | solution.py:1099
  1558.1 144.7 %collective-permute-start.6 = (bf16[256,3072]{1,0:T(8,128)(2,1)}, bf16[256,3072]{1,0:T(8,128)(2,1)}, u32[]{:S(2)}, u32[]{:S(2)}) collective-permute-start(bf16[256,3072]{1,0:T(8,128)(2,1)} %get-tuple-element.591), channel_id=1, source_target_pairs={{0,2},{1,3},{2,0},{3,1},{4,6},{5,7},{6,4},{7,5},{8,10},{9,11},{10,... | collective-permute-start | bytes 4718600 | tf_op jit(solution)/shard_map/ppermute | solution.py:1099
  1566.3 5.0 collective-permute-start.8
  1571.4 5.5 collective-permute-start.9
  1576.9 3.8 collective-permute-start.10
  1580.8 108.2 %collective-permute-start.11 = (f32[2,192]{1,0:T(2,128)S(1)}, f32[2,192]{1,0:T(2,128)S(1)}, u32[]{:S(2)}, u32[]{:S(2)}) collective-permute-start(f32[2,192]{1,0:T(2,128)S(1)} %bitcast.100), channel_id=1, source_target_pairs={{0,2},{1,3},{2,0},{3,1},{4,6},{5,7},{6,4},{7,5},{8,10},{9,11},{10,... | collective-permute-start | bytes 4616 | tf_op jit(solution)/shard_map/ppermute | solution.py:1160
  1689.1 13.1 collective-permute-start.12
  (67 other events, 798.0 us)
Sparse Core Ops, SparseCore 0:
  111.0 135.6 all-gather.5
  248.5 57.0 all-gather.7
  309.2 121.6 all-gather.11
  432.6 122.4 all-gather.9
  556.8 122.5 all-gather.13
  794.8 120.3 reduce-scatter.5
  1015.5 120.4 reduce-scatter.7
  1139.1 120.7 reduce-scatter.9
  1262.8 57.0 reduce-scatter.11
  1356.6 133.5 reduce-scatter.13

commit v12 on v8

--- a/solution.py
+++ b/solution.py
@@ -933,6 +933,7 @@
             pltpu.VMEM((pieces // 2, count, width), term.dtype),
         ]
         + [pltpu.SemaphoreType.DMA((pieces,))] * 4,
+        flops=58 * 10**9,
     )
 
 
@@ -1418,9 +1419,9 @@
             gain_term,
         )
 
-    back_second, out_back = swap(("near", send_second), ("far", out_away))
     qkv_mine, qkv_away = act(lambda pair: core_split(0, pair), qkv_sum)
     qkv_back = swap_far(qkv_away)
+    back_second, out_back = swap(("near", send_second), ("far", out_away))
     i_first, gain_one_first = act(
         first_back, streams[0], scales_one[0], keep_first, back_first, g_first
     )

time: 1710 us -> 1750 us (1.023)
  Pallas kernels: 1400 us -> 1450 us
    ppermute x5, waiting for transfers between devices: 101 us -> 41.8 us  [scatter_gains(): lax.ppermute(sent, axis, [(i, i ^ step) for i in range(size)])]
    pallas_call x28, Pallas kernels: 441 us -> 495 us  [exchange_call(): pl.pallas_call(kernel, out_shape=outs, in_specs=[anywhere] * len(operands...]
    ppermute x9, waiting for transfers between devices: 0.25 us -> 49.4 us  [swap_far(): return lax.ppermute(value, 'tp', far_pairs)]
    unnamed x148 -> x152, local copies, waits for them, and re-layouts: 42.4 us -> 39.8 us
  transfers between devices with their start and end apart: 24 -> 24, of which waited for: 2 -> 2; matrix products, arithmetic and copies ran while one was open for 7% -> 7% of each run, Pallas kernels for 77% -> 78%
where the time goes in v12:
time: 1750 us; the launch traced here: 1740 us
  Pallas kernels  1450 us (83%)
  other arithmetic  104 us (6%)
  waiting for transfers between devices  91.5 us (5%)
  local copies, waits for them, and re-layouts  66.2 us (4%)
    pallas_call x26, Pallas kernels, grid_call(): pl.pallas_call(kernel, out_shape=outs, grid=grid, in_specs=in_specs, out_...  959 us
    pallas_call x28, Pallas kernels, exchange_call(): pl.pallas_call(kernel, out_shape=outs, in_specs=[anywhere] * len(operands...  495 us
    ppermute x9, waiting for transfers between devices, swap_far(): return lax.ppermute(value, 'tp', far_pairs)  49.4 us
    ppermute x5, waiting for transfers between devices, scatter_gains(): lax.ppermute(sent, axis, [(i, i ^ step) for i in range(size)])  41.8 us
    unnamed x152, local copies, waits for them, and re-layouts  39.8 us
  transfers between devices with their start and end apart: 24, of which 2 were waited for; matrix products, arithmetic and copies ran while one was open for 7% of the time, Pallas kernels for 78%

profile of v12, /device:TPU:0, one launch (start us, length us, event | category | flops | bytes accessed | tf_op | source)
XLA Modules:
  0.0 1743.8 jit_solution(13798346608767469715)
XLA Ops:
  20.3 82.6 %shard_map.152 = (bf16[256,3072]{1,0:T(8,128)(2,1)}, bf16[384,2304]{1,0:T(8,128)(2,1)}, s32[8,256]{1,0:T(8,128)}) custom-call(bf16[256,3072]{1,0:T(8,128)(2,1)} %fusion.4.refs_0_.own_ref, bf16[384,2304]{1,0:T(8,128)(2,1)} %copy.35.refs_1_, s32[8,256]{1,0:T(8,128)} %broadcast_in_dim.11.refs_2_), custom_call_target="tpu_custom_call" | custom-call | flops 186999996416 | bytes 1000 | tf_op jit(solution)/shard_map/pallas_call | solution.py:778
  116.9 96.5 %shard_map.154 = (bf16[256,3072]{1,0:T(8,128)(2,1)}, bf16[256,3072]{1,0:T(8,128)(2,1)}, bf16[96,3072]{1,0:T(8,128)(2,1)}, s32[16,256]{1,0:T(8,128)}) custom-call(bf16[256,3072]{1,0:T(8,128)(2,1)} %get-tuple-element.288.refs_0_, bf16[256,3072]{1,0:T(8,128)(2,1)} %get-tuple-element.377.refs_1_.own_ref, bf16[96,3072]{1,0:T(8,128)(2,1)} %own_ref, ...), custom_call_target="tpu_custom_call" | custom-call | flops 186999996416 | bytes 1000 | tf_op jit(solution)/shard_map/pallas_call | solution.py:778
  232.3 71.6 %shard_map.156 = (bf16[256,3072]{1,0:T(8,128)(2,1)}, bf16[384,2048]{1,0:T(8,128)(2,1)}, s32[32,256]{1,0:T(8,128)}) custom-call(bf16[256,3072]{1,0:T(8,128)(2,1)} %multiply_convert_fusion.2.refs_0_.got_ref, bf16[384,2048]{1,0:T(8,128)(2,1)} %get-tuple-element.305.refs_1_.own_ref, s32[32,256]{1,0:T(8,128)} %pad_add_fusion.1.refs_2_), custom_call_target="tpu_custom_call" | custom-call | flops 186999996416 | bytes 1000 | tf_op jit(solution)/shard_map/pallas_call | solution.py:778
  329.9 49.4 %collective-permute-done.refs_0_ = bf16[384,2048]{1,0:T(8,128)(2,1)S(1)} collective-permute-done((bf16[384,2048]{1,0:T(8,128)(2,1)S(1)}, bf16[384,2048]{1,0:T(8,128)(2,1)S(1)}, u32[]{:S(2)}, u32[]{:S(2)}) %collective-permute-start) | collective-permute-done | bytes 1572896 | tf_op jit(solution)/shard_map/ppermute | solution.py:1100
  379.3 21.6 %shard_map.159.q_ref.k_ref.v_ref = f32[1024,2304]{1,0:T(8,128)} custom-call(bf16[1024,3072]{1,0:T(8,128)(2,1)} %get-tuple-element.489.refs_0_, bf16[3072,2304]{1,0:T(8,128)(2,1)} %all-gather.6.cloned.1.call-done.refs_1_), custom_call_target="tpu_custom_call" | custom-call | flops 24642375680 | bytes 1000 | tf_op jit(solution)/shard_map/pallas_call | solution.py:720
  400.9 29.2 %shard_map.160 = (bf16[1024,768]{1,0:T(8,128)(2,1)}, bf16[1024,768]{1,0:T(8,128)(2,1)}, bf16[1024,768]{1,0:T(8,128)(2,1)}, bf16[1024,768]{1,0:T(8,128)(2,1)}, f32[2,1024,4]{2,1,0:T(8,128)}) custom-call(f32[1024,2304]{1,0:T(8,128)} %shard_map.159.q_ref.k_ref.v_ref, f32[1024,2304]{1,0:T(8,128)} %shard_map.159.q_ref.k_ref.v_ref, ...), custom_call_target="tpu_custom_call" | custom-call | flops 8556380160 | bytes 1000 | tf_op jit(solution)/shard_map/pallas_call | solution.py:720
  451.1 44.2 %shard_map.164 = (f32[1024,2304]{1,0:T(8,128)}, bf16[256,3072]{1,0:T(8,128)(2,1)}) custom-call(bf16[1024,3072]{1,0:T(8,128)(2,1)} %get-tuple-element.490.refs_0_.refs_1_, bf16[3072,2304]{1,0:T(8,128)(2,1)} %all-gather.6.cloned.1.call-done.refs_1_, bf16[256,3072]{1,0:T(8,128)(2,1)} %get-tuple-element.331.refs_2_), custom_call_target="tpu_custom_call" | custom-call | flops 45900001280 | bytes 1000 | tf_op jit(solution)/shard_map/pallas_call | solution.py:720
  501.6 39.7 %shard_map.165 = (bf16[1024,768]{1,0:T(8,128)(2,1)}, bf16[1024,768]{1,0:T(8,128)(2,1)}, bf16[1024,768]{1,0:T(8,128)(2,1)}, bf16[1024,768]{1,0:T(8,128)(2,1)}, f3...) custom-call(f32[1024,2304]{1,0:T(8,128)} %get-tuple-element.337.refs_0_.refs_1_.refs_2_, ...), custom_call_target="tpu_custom_call" | custom-call | flops 45900001280 | bytes 1000 | tf_op jit(solution)/shard_map/pallas_call | solution.py:720
  570.1 74.5 %shard_map.170 = (f32[1024,2048]{1,0:T(8,128)}, bf16[256,3072]{1,0:T(8,128)(2,1)}) custom-call(bf16[1024,3072]{1,0:T(8,128)(2,1)} %shard_map.168.refs_0_, bf16[3072,2048]{1,0:T(8,128)(2,1)} %all-gather.12.cloned.1.call-done.refs_1_.refs_2_, bf16[256,3072]{1,0:T(8,128)(2,1)} %get-tuple-element.356.refs_2_), custom_call_target="tpu_custom_call" | custom-call | flops 45900001280 | bytes 1000 | tf_op jit(solution)/shard_map/pallas_call | solution.py:720
  654.1 41.7 %shard_map.171 = (f32[1024,2048]{1,0:T(8,128)}, bf16[1024,2048]{1,0:T(8,128)(2,1)}, bf16[256,3072]{1,0:T(8,128)(2,1)}) custom-call(bf16[1024,3072]{1,0:T(8,128)(2,1)} %shard_map.168.refs_0_, bf16[3072,2048]{1,0:T(8,128)(2,1)} %all-gather.10.cloned.1.call-done.refs_1_.refs_3_, f32[1024,2048]{1,0:T(8,128)} %get-tuple-element.394.refs_2_, ...), custom_call_target="tpu_custom_call" | custom-call | flops 45900001280 | bytes 1000 | tf_op jit(solution)/shard_map/pallas_call | solution.py:720
  701.9 41.9 %shard_map.173 = (f32[1024,2048]{1,0:T(8,128)}, bf16[256,3072]{1,0:T(8,128)(2,1)}) custom-call(bf16[1024,3072]{1,0:T(8,128)(2,1)} %shard_map.172.refs_0_.refs_1_, bf16[3072,2048]{1,0:T(8,128)(2,1)} %all-gather.12.cloned.1.call-done.refs_1_.refs_2_, bf16[256,3072]{1,0:T(8,128)(2,1)} %collective-permute-done.2.refs_2_.got_ref), custom_call_target="tpu_custom_call" | custom-call | flops 45900001280 | bytes 1000 | tf_op jit(solution)/shard_map/pallas_call | solution.py:720
  774.7 35.3 %shard_map.176 = bf16[2048,3072]{1,0:T(8,128)(2,1)} custom-call(bf16[1024,2048]{1,0:T(8,128)(2,1)} %get-tuple-element.460.refs_0_, bf16[1024,2048]{1,0:T(8,128)(2,1)} %get-tuple-element.464.refs_1_.refs_0_, bf16[1024,3072]{1,0:T(8,128)(2,1)} %get-tuple-element.392.refs_2_.refs_0_, bf16[1024,3072]{1,0:T(8,128)(2,1)} %get-tuple-element.404.refs_3_.refs_0_), custom_call_target="tpu_custom_call" | custom-call | flops 43808665600 | bytes 1000 | tf_op jit(solution)/shard_map/pallas_call | solution.py:720
  810.1 23.8 %shard_map.177 = (bf16[1024,2048]{1,0:T(8,128)(2,1)}, bf16[1024,2048]{1,0:T(8,128)(2,1)}) custom-call(bf16[1024,3072]{1,0:T(8,128)(2,1)} %get-tuple-element.392.refs_2_.refs_0_, bf16[2048,3072]{1,0:T(8,128)(2,1)} %all-gather.14.cloned.1.call-done.refs_1_, f32[1024,2048]{1,0:T(8,128)} %get-tuple-element.394.refs_2_, f32[1024,2048]{1,0:T(8,128)} %get-tuple-element.395.refs_3_), custom_call_target="tpu_custom_call" | custom-call | flops 21904332800 | bytes 1000 | tf_op jit(solution)/shard_map/pallas_call | solution.py:720
  833.9 33.3 %shard_map.178.term_ref = bf16[1024,3072]{1,0:T(8,128)(2,1)} custom-call(bf16[1024,2048]{1,0:T(8,128)(2,1)} %get-tuple-element.430.refs_0_.refs_2_, bf16[1024,2048]{1,0:T(8,128)(2,1)} %get-tuple-element.447.refs_1_.refs_2_, bf16[3072,2048]{1,0:T(8,128)(2,1)} %all-gather.12.cloned.1.call-done.refs_1_.refs_2_, ...), custom_call_target="tpu_custom_call" | custom-call | flops 43808665600 | bytes 1000 | tf_op jit(solution)/shard_map/pallas_call | solution.py:720
  874.6 44.6 %shard_map.180 = (bf16[1024,2048]{1,0:T(8,128)(2,1)}, bf16[1024,2048]{1,0:T(8,128)(2,1)}, bf16[256,3072]{1,0:T(8,128)(2,1)}) custom-call(bf16[1024,3072]{1,0:T(8,128)(2,1)} %get-tuple-element.404.refs_3_.refs_0_, bf16[2048,3072]{1,0:T(8,128)(2,1)} %all-gather.14.cloned.1.call-done.refs_1_, f32[1024,2048]{1,0:T(8,128)} %get-tuple-element.406.refs_2_, ...), custom_call_target="tpu_custom_call" | custom-call | flops 45900001280 | bytes 1000 | tf_op jit(solution)/shard_map/pallas_call | solution.py:720
  927.3 41.9 %shard_map.181 = (bf16[1024,3072]{1,0:T(8,128)(2,1)}, bf16[256,3072]{1,0:T(8,128)(2,1)}) custom-call(bf16[1024,2048]{1,0:T(8,128)(2,1)} %get-tuple-element.431.refs_0_.refs_3_, bf16[1024,2048]{1,0:T(8,128)(2,1)} %get-tuple-element.448.refs_1_.refs_3_, bf16[3072,2048]{1,0:T(8,128)(2,1)} %all-gather.12.cloned.1.call-done.refs_1_.refs_2_, ...), custom_call_target="tpu_custom_call" | custom-call | flops 45900001280 | bytes 1000 | tf_op jit(solution)/shard_map/pallas_call | solution.py:720
  982.6 42.2 %shard_map.184 = (bf16[3072,2048]{1,0:T(8,128)(2,1)}, bf16[256,3072]{1,0:T(8,128)(2,1)}) custom-call(bf16[1024,3072]{1,0:T(8,128)(2,1)} %shard_map.168.refs_0_, bf16[1024,3072]{1,0:T(8,128)(2,1)} %shard_map.172.refs_0_.refs_1_, bf16[1024,2048]{1,0:T(8,128)(2,1)} %get-tuple-element.430.refs_0_.refs_2_, bf16[1024,2048]{1,0:T(8,128)(2,1)} %get-tuple-element.431.refs_0_.refs_3_, ...), custom_call_target="tpu_custom_call" | custom-call | flops 45900001280 | bytes 1000 | tf_op jit(solution)/shard_map/pallas_call | solution.py:720
  1050.9 76.2 %shard_map.187 = (bf16[3072,2048]{1,0:T(8,128)(2,1)}, bf16[256,3072]{1,0:T(8,128)(2,1)}) custom-call(bf16[1024,3072]{1,0:T(8,128)(2,1)} %shard_map.168.refs_0_, bf16[1024,3072]{1,0:T(8,128)(2,1)} %shard_map.172.refs_0_.refs_1_, bf16[1024,2048]{1,0:T(8,128)(2,1)} %get-tuple-element.447.refs_1_.refs_2_, bf16[1024,2048]{1,0:T(8,128)(2,1)} %get-tuple-element.448.refs_1_.refs_3_, ...), custom_call_target="tpu_custom_call" | custom-call | flops 45900001280 | bytes 1000 | tf_op jit(solution)/shard_map/pallas_call | solution.py:720
  1213.1 74.9 %shard_map.195 = (bf16[1024,768]{1,0:T(8,128)(2,1)}, bf16[1024,768]{1,0:T(8,128)(2,1)}, bf16[1024,768]{1,0:T(8,128)(2,1)}, bf16[1024,768]{1,0:T(8,128)(2,1)}, bf...) custom-call(bf16[1024,768]{1,0:T(8,128)(2,1)} %get-tuple-element.319, ...), custom_call_target="tpu_custom_call" | custom-call | flops 45900001280 | bytes 1000 | tf_op jit(solution)/shard_map/pallas_call | solution.py:720
  1300.3 39.0 %shard_map.197 = bf16[3072,2304]{1,0:T(8,128)(2,1)} custom-call(bf16[1024,3072]{1,0:T(8,128)(2,1)} %get-tuple-element.489.refs_0_, bf16[1024,3072]{1,0:T(8,128)(2,1)} %get-tuple-element.490.refs_0_.refs_1_, bf16[1024,2304]{1,0:T(8,128)(2,1)} %constant_dynamic-update-slice_fusion.refs_2_.refs_0_, bf16[1024,2304]{1,0:T(8,128)(2,1)} %copy-done.47), custom_call_target="tpu_custom_call" | custom-call | flops 49284751360 | bytes 1000 | tf_op jit(solution)/shard_map/pallas_call | solution.py:720
  1357.5 20.3 %shard_map.199.term_ref = bf16[1024,3072]{1,0:T(8,128)(2,1)} custom-call(bf16[1024,2304]{1,0:T(8,128)(2,1)} %constant_dynamic-update-slice_fusion.refs_2_.refs_0_, bf16[3072,2304]{1,0:T(8,128)(2,1)} %all-gather.6.cloned.1.call-done.refs_1_), custom_call_target="tpu_custom_call" | custom-call | flops 24642375680 | bytes 1000 | tf_op jit(solution)/shard_map/pallas_call | solution.py:720
  1385.2 119.8 %shard_map.201 = (bf16[1024,3072]{1,0:T(8,128)(2,1)}, bf16[256,3072]{1,0:T(8,128)(2,1)}) custom-call(bf16[1024,2304]{1,0:T(8,128)(2,1)} %copy-done.47, bf16[3072,2304]{1,0:T(8,128)(2,1)} %all-gather.6.cloned.1.call-done.refs_1_, bf16[256,3072]{1,0:T(8,128)(2,1)} %get-tuple-element.508.refs_2_), custom_call_target="tpu_custom_call" | custom-call | flops 45900001280 | bytes 1000 | tf_op jit(solution)/shard_map/pallas_call | solution.py:720
  1519.1 104.0 %shard_map.205 = (bf16[256,3072]{1,0:T(8,128)(2,1)}, bf16[96,3072]{1,0:T(8,128)(2,1)}) custom-call(bf16[256,3072]{1,0:T(8,128)(2,1)} %get-tuple-element.518.refs_0_, bf16[96,3072]{1,0:T(8,128)(2,1)} %get-tuple-element.519.refs_1_), custom_call_target="tpu_custom_call" | custom-call | flops 186999996416 | bytes 1000 | tf_op jit(solution)/shard_map/pallas_call | solution.py:778
  1665.7 41.8 %collective-permute-done.11 = f32[2,192]{1,0:T(2,128)S(1)} collective-permute-done((f32[2,192]{1,0:T(2,128)S(1)}, f32[2,192]{1,0:T(2,128)S(1)}, u32[]{:S(2)}, u32[]{:S(2)}) %collective-permute-start.11) | collective-permute-done | bytes 1568 | tf_op jit(solution)/shard_map/ppermute | solution.py:1161
  (328 shorter events, 438.0 us)
Async XLA Ops:
  7.2 372.1 %all-gather.6.cloned.1.call-start = ((), (), s32[]{:S(2)}) async-start(), calls=%async_computation.5 | async-start | bytes 17694720 | tf_op jit(solution)/shard_map/all_gather | solution.py:1132
  110.9 323.0 %all-gather.8.cloned.1.call-start = ((), (), s32[]{:S(2)}) async-start(), calls=%async_computation.6 | async-start | bytes 5898240 | tf_op jit(solution)/shard_map/all_gather | solution.py:1132
  215.9 352.6 %all-gather.12.cloned.1.call-start = ((), (), s32[]{:S(2)}) async-start(), calls=%async_computation.8 | async-start | bytes 15728640 | tf_op jit(solution)/shard_map/all_gather | solution.py:1132
  307.8 346.3 %all-gather.10.cloned.1.call-start = ((), (), s32[]{:S(2)}) async-start(), calls=%async_computation.7 | async-start | bytes 15728640 | tf_op jit(solution)/shard_map/all_gather | solution.py:1132
  309.2 70.1 %collective-permute-start = (bf16[384,2048]{1,0:T(8,128)(2,1)S(1)}, bf16[384,2048]{1,0:T(8,128)(2,1)S(1)}, u32[]{:S(2)}, u32[]{:S(2)}) collective-permute-start(bf16[384,2048]{1,0:T(8,128)(2,1)S(1)} %copy-done.30), channel_id=1, source_target_pairs={{0,2},{1,3},{2,0},{3,1},{4,6},{5,7},{6,4},{7,5},{8,10},{9,11},{10,... | collective-permute-start | bytes 4718600 | tf_op jit(solution)/shard_map/ppermute | solution.py:1100
  379.3 185.3 %collective-permute-start.1 = (bf16[256,3072]{1,0:T(8,128)(2,1)}, bf16[256,3072]{1,0:T(8,128)(2,1)}, u32[]{:S(2)}, u32[]{:S(2)}) collective-permute-start(bf16[256,3072]{1,0:T(8,128)(2,1)} %own_ref.1), channel_id=1, source_target_pairs={{0,2},{1,3},{2,0},{3,1},{4,6},{5,7},{6,4},{7,5},{8,10},{9,11},{10,... | collective-permute-start | bytes 4718600 | tf_op jit(solution)/shard_map/ppermute | solution.py:1100
  451.0 359.1 %all-gather.14.cloned.1.call-start = ((), (), s32[]{:S(2)}) async-start(), calls=%async_computation.9 | async-start | bytes 15728640 | tf_op jit(solution)/shard_map/all_gather | solution.py:1132
  568.5 82.3 %collective-permute-start.2 = (bf16[256,3072]{1,0:T(8,128)(2,1)}, bf16[256,3072]{1,0:T(8,128)(2,1)}, u32[]{:S(2)}, u32[]{:S(2)}) collective-permute-start(bf16[256,3072]{1,0:T(8,128)(2,1)} %get-tuple-element.367), channel_id=1, source_target_pairs={{0,2},{1,3},{2,0},{3,1},{4,6},{5,7},{6,4},{7,5},{8,10},{9,11},{10,... | collective-permute-start | bytes 4718600 | tf_op jit(solution)/shard_map/ppermute | solution.py:1100
  570.0 475.5 %reduce-scatter.6.cloned.1.call-start = ((), (), s32[]{:S(2)}) async-start(), calls=%async_computation.10 | async-start | bytes 15728640 | tf_op jit(solution)/shard_map/reduce_scatter | solution.py:1135
  810.0 478.0 %reduce-scatter.8.cloned.1.call-start = ((), (), s32[]{:S(2)}) async-start(), calls=%async_computation.11 | async-start | bytes 15728640 | tf_op jit(solution)/shard_map/reduce_scatter | solution.py:1135
  1024.9 327.3 %reduce-scatter.10.cloned.1.call-start = ((), (), s32[]{:S(2)}) async-start(), calls=%async_computation.12 | async-start | bytes 15728640 | tf_op jit(solution)/shard_map/reduce_scatter | solution.py:1135
  1049.3 589.5 %collective-permute-start.5 = (bf16[256,3072]{1,0:T(8,128)(2,1)}, bf16[256,3072]{1,0:T(8,128)(2,1)}, u32[]{:S(2)}, u32[]{:S(2)}) collective-permute-start(bf16[256,3072]{1,0:T(8,128)(2,1)} %get-tuple-element.444), channel_id=1, source_target_pairs={{0,2},{1,3},{2,0},{3,1},{4,6},{5,7},{6,4},{7,5},{8,10},{9,11},{10,... | collective-permute-start | bytes 4718600 | tf_op jit(solution)/shard_map/ppermute | solution.py:1100
  1127.1 385.3 %reduce-scatter.12.cloned.1.call-start = ((), (), s32[]{:S(2)}) async-start(), calls=%async_computation.13 | async-start | bytes 5898240 | tf_op jit(solution)/shard_map/reduce_scatter | solution.py:1135
  1213.0 301.9 %reduce-scatter.14.cloned.1.call-start = ((), (), s32[]{:S(2)}) async-start(), calls=%async_computation.14 | async-start | bytes 17694720 | tf_op jit(solution)/shard_map/reduce_scatter | solution.py:1135
  1291.8 350.8 %collective-permute-start.4 = (bf16[384,2048]{1,0:T(8,128)(2,1)}, bf16[384,2048]{1,0:T(8,128)(2,1)}, u32[]{:S(2)}, u32[]{:S(2)}) collective-permute-start(bf16[384,2048]{1,0:T(8,128)(2,1)} %get-tuple-element.482), channel_id=1, source_target_pairs={{0,2},{1,3},{2,0},{3,1},{4,6},{5,7},{6,4},{7,5},{8,10},{9,11},{10,... | collective-permute-start | bytes 4718600 | tf_op jit(solution)/shard_map/ppermute | solution.py:1100
  1349.4 295.1 %collective-permute-start.3 = (bf16[256,3072]{1,0:T(8,128)(2,1)}, bf16[256,3072]{1,0:T(8,128)(2,1)}, u32[]{:S(2)}, u32[]{:S(2)}) collective-permute-start(bf16[256,3072]{1,0:T(8,128)(2,1)} %get-tuple-element.584), channel_id=1, source_target_pairs={{0,2},{1,3},{2,0},{3,1},{4,6},{5,7},{6,4},{7,5},{8,10},{9,11},{10,... | collective-permute-start | bytes 4718600 | tf_op jit(solution)/shard_map/ppermute | solution.py:1100
  1356.0 297.7 %collective-permute-start.7 = (bf16[384,2048]{1,0:T(8,128)(2,1)}, bf16[384,2048]{1,0:T(8,128)(2,1)}, u32[]{:S(2)}, u32[]{:S(2)}) collective-permute-start(bf16[384,2048]{1,0:T(8,128)(2,1)} %get-tuple-element.501), channel_id=1, source_target_pairs={{0,2},{1,3},{2,0},{3,1},{4,6},{5,7},{6,4},{7,5},{8,10},{9,11},{10,... | collective-permute-start | bytes 4718600 | tf_op jit(solution)/shard_map/ppermute | solution.py:1100
  1519.0 207.7 %collective-permute-start.13 = (bf16[384,2304]{1,0:T(8,128)(2,1)}, bf16[384,2304]{1,0:T(8,128)(2,1)}, u32[]{:S(2)}, u32[]{:S(2)}) collective-permute-start(bf16[384,2304]{1,0:T(8,128)(2,1)} %get-tuple-element.517), channel_id=1, source_target_pairs={{0,2},{1,3},{2,0},{3,1},{4,6},{5,7},{6,4},{7,5},{8,10},{9,11},{10,... | collective-permute-start | bytes 5308424 | tf_op jit(solution)/shard_map/ppermute | solution.py:1100
  1638.8 82.4 %collective-permute-start.6 = (bf16[256,3072]{1,0:T(8,128)(2,1)}, bf16[256,3072]{1,0:T(8,128)(2,1)}, u32[]{:S(2)}, u32[]{:S(2)}) collective-permute-start(bf16[256,3072]{1,0:T(8,128)(2,1)} %get-tuple-element.582), channel_id=1, source_target_pairs={{0,2},{1,3},{2,0},{3,1},{4,6},{5,7},{6,4},{7,5},{8,10},{9,11},{10,... | collective-permute-start | bytes 4718600 | tf_op jit(solution)/shard_map/ppermute | solution.py:1100
  1644.7 4.8 collective-permute-start.8
  1649.5 4.2 collective-permute-start.9
  1653.7 3.8 collective-permute-start.10
  1657.6 49.8 %collective-permute-start.11 = (f32[2,192]{1,0:T(2,128)S(1)}, f32[2,192]{1,0:T(2,128)S(1)}, u32[]{:S(2)}, u32[]{:S(2)}) collective-permute-start(f32[2,192]{1,0:T(2,128)S(1)} %bitcast.100), channel_id=1, source_target_pairs={{0,2},{1,3},{2,0},{3,1},{4,6},{5,7},{6,4},{7,5},{8,10},{9,11},{10,... | collective-permute-start | bytes 4616 | tf_op jit(solution)/shard_map/ppermute | solution.py:1161
  1707.5 13.1 collective-permute-start.12
  (70 other events, 809.8 us)
Sparse Core Ops, SparseCore 0:
  111.0 135.6 all-gather.5
  248.5 57.0 all-gather.7
  307.9 121.9 all-gather.11
  451.1 123.0 all-gather.9
  575.9 122.5 all-gather.13
  810.1 120.6 reduce-scatter.5
  1025.0 120.6 reduce-scatter.7
  1148.8 120.7 reduce-scatter.9
  1272.6 57.0 reduce-scatter.11
  1339.5 132.9 reduce-scatter.13
